TPU v7x, 32 devices: a whole 2x2x4 slice. The times are simulated.
32 devices in a mesh: head: 4 (over x, core), blk: 8 (over z, y).
Axes of the slice: x: 2, y: 2, z: 4, core: 2. Of those that a mesh axis runs over, the one named last changes fastest.
Arguments:
- inputs: bfloat16 [4096, 1024], P(('blk', 'head')), may hold values from -60 to 60
- cotangent: bfloat16 [4096, 1024], P(('blk', 'head')), may hold values from -6 to 6
- attn_gain: float32 [1024], replicated, may hold values from 0.5 to 1.5
- ffn_gain: float32 [1024], replicated, may hold values from 0.5 to 1.5
- query_gain: float32 [64], replicated, may hold values from 0.25 to 1.75
- key_gain: float32 [64], replicated, may hold values from 0.25 to 1.75
- variate_bias: float32 [2, 16], replicated, may hold values from -4 to 4
- qkv_weight: bfloat16 [1024, 3072], P(('blk', 'head')), may hold values from -0.1875 to 0.1875
- out_weight: bfloat16 [1024, 1024], P(('blk', 'head')), may hold values from -1 to 1
- expand_weight: bfloat16 [1024, 8192], P(('blk', 'head')), may hold values from -0.1875 to 0.1875
- down_weight: bfloat16 [4096, 1024], P(('blk', 'head')), may hold values from -0.09375 to 0.09375
- seq_lengths: int32 [8], replicated, may hold values from 1 to 2048, 3584 in all
- variate_ids: int32 [4096], replicated, may hold values from 0 to 3
- block_order: int32 [32], replicated, may hold values from 0 to 31, each once
Outputs:
- outputs: bfloat16 [4096, 1024], P(('blk', 'head'))
- grad_inputs: float32 [4096, 1024], P(('blk', 'head'))
- grad_qkv: float32 [1024, 3072], P(('blk', 'head'))
- grad_out: float32 [1024, 1024], P(('blk', 'head'))
- grad_expand: float32 [1024, 8192], P(('blk', 'head'))
- grad_down: float32 [4096, 1024], P(('blk', 'head'))
- grad_attn: float32 [1024], replicated
- grad_ffn: float32 [1024], replicated
- grad_query: float32 [64], replicated
- grad_key: float32 [64], replicated
- grad_bias: float32 [2, 16], replicated
- root_means: float32 [3], replicated
Inputs may be any that keep to these rules, and one draw needn't show every extreme that they name: `seq_lengths`: the lengths sum to 3584; the last 512 packed positions are padding, which is one more segment. `block_order`: each block number once.
All inputs are finite; a program needn't handle non-finite values.
Results may differ from a plain program's by a relative error of at most 0.02.
Values may be sent and summed in bfloat16 or wider, within the bound.
No kernel may reach another device: no remote copies, remote signals or barrier semaphores. Data moves between devices by JAX's collectives and lax.ppermute only.
A program may use at most 192 MiB of HBM per device.

v0:
```python
from functools import partial

import jax
import jax.numpy as jnp
from jax import lax
from jax.sharding import PartitionSpec as P

D = 1024
H = 16
HD = 64
BLOCK = 128


EPSILON = 1e-05
THETA = 10000.0


def from_behind(shard, axis, by):
    length = lax.axis_size(axis)
    return lax.ppermute(shard, axis, [(i, (i + by) % length) for i in range(length)])


def norm_rows(values, gain):
    factor = lax.rsqrt(jnp.mean(values * values, axis=-1, keepdims=True) + EPSILON)
    return values * factor * gain


def rotate(values, position):
    halfway = values.shape[-1] // 2
    freqs = THETA ** (-jnp.arange(halfway, dtype=jnp.float32) / halfway)
    angles = position.astype(jnp.float32)[:, None] * freqs[None, :]
    cosine = jnp.cos(angles)[:, None, :]
    sine = jnp.sin(angles)[:, None, :]
    first = values[..., :halfway]
    latter = values[..., halfway:]
    return jnp.concatenate(
        [first * cosine - latter * sine, latter * cosine + first * sine], axis=-1
    )


def token_meta(seq_lengths, block_order):
    blocks = block_order.shape[0]
    packed_at = jnp.repeat(block_order, BLOCK) * BLOCK + jnp.tile(
        jnp.arange(BLOCK, dtype=jnp.int32), blocks
    )
    ends = jnp.cumsum(seq_lengths)
    after = packed_at[:, None] >= ends[None, :]
    segment = jnp.sum(after.astype(jnp.int32), axis=1)
    begin = jnp.max(jnp.where(after, ends[None, :], jnp.zeros_like(ends)[None, :]), axis=1)
    return (segment, packed_at - begin)


def project_heads(both, query_gain, key_gain, position):
    rows = both.shape[0]
    width = both.shape[1] // 2
    heads = width // HD
    queries = rotate(norm_rows(both[:, :width].reshape(rows, heads, HD), query_gain), position)
    keys = rotate(norm_rows(both[:, width:].reshape(rows, heads, HD), key_gain), position)
    return (queries.reshape(rows, width), keys.reshape(rows, width))


def swiglu(expand):
    half = expand.shape[1] // 2
    return jax.nn.silu(expand[:, :half]) * expand[:, half:]


def exponent(query_heads, key_heads, key_first, context):
    row_segment, row_variate, bias_here, segment, variate_ids = context
    key_count = key_heads.shape[0]
    key_segment = lax.dynamic_slice_in_dim(segment, key_first, key_count)
    key_variate = lax.dynamic_slice_in_dim(variate_ids, key_first, key_count)
    dots = jnp.einsum("qhd,khd->hqk", query_heads, key_heads, preferred_element_type=jnp.float32)
    same_variate = (row_variate[:, None] == key_variate[None, :])[None]
    scores = dots * HD ** (-0.5) + jnp.where(
        same_variate, bias_here[1][:, None, None], bias_here[0][:, None, None]
    )
    same_segment = (row_segment[:, None] == key_segment[None, :])[None]
    return (jnp.where(same_segment, jnp.exp(scores), 0.0), same_variate)


def body(
    inputs,
    cotangent,
    attn_gain,
    ffn_gain,
    query_gain,
    key_gain,
    variate_bias,
    qkv_weight,
    out_weight,
    expand_weight,
    down_weight,
    seq_lengths,
    variate_ids,
    block_order,
):
    head_ways = lax.axis_size("head")
    group_count = lax.axis_size("blk")
    group_index = lax.axis_index("blk")
    head_index = lax.axis_index("head")
    tok_rows = inputs.shape[0]
    group_rows = tok_rows * head_ways
    head_group = H // head_ways
    own_width = head_group * HD
    segment, position = token_meta(seq_lengths, block_order)
    token_first = (group_index * head_ways + head_index) * tok_rows
    group_first = group_index * group_rows
    own_position = lax.dynamic_slice_in_dim(position, token_first, tok_rows)
    row_segment = lax.dynamic_slice_in_dim(segment, group_first, group_rows)
    row_variate = lax.dynamic_slice_in_dim(variate_ids, group_first, group_rows)
    bias_here = lax.dynamic_slice_in_dim(variate_bias, head_index * head_group, head_group, 1)
    context = (row_segment, row_variate, bias_here, segment, variate_ids)
    out_full = lax.all_gather(out_weight, ("blk", "head"), axis=0, tiled=True)
    residual = inputs.astype(jnp.float32)
    normed, first_back = jax.vjp(norm_rows, residual, attn_gain)
    normed_low = normed.astype(jnp.bfloat16)
    qkv_full, expand_full, down_full = (
        lax.all_gather(qkv_weight, ("blk", "head"), axis=0, tiled=True),
        lax.all_gather(expand_weight, ("blk", "head"), axis=0, tiled=True),
        lax.all_gather(down_weight, ("blk", "head"), axis=0, tiled=True),
    )
    project = jnp.dot(normed_low, qkv_full, preferred_element_type=jnp.float32)
    (query_rot, key_rot), rotate_back = jax.vjp(
        partial(project_heads, position=own_position), project[:, : 2 * D], query_gain, key_gain
    )
    queries, key_rows, value_rows = (
        lax.all_to_all(
            query_rot.astype(jnp.bfloat16), "head", split_axis=1, concat_axis=0, tiled=True
        ),
        lax.all_to_all(
            key_rot.astype(jnp.bfloat16), "head", split_axis=1, concat_axis=0, tiled=True
        ),
        lax.all_to_all(
            project[:, 2 * D :].astype(jnp.bfloat16),
            "head",
            split_axis=1,
            concat_axis=0,
            tiled=True,
        ),
    )
    query_heads = queries.reshape(group_rows, head_group, HD)
    pieces = (
        lax.all_gather(key_rows, "blk", axis=0, tiled=True),
        lax.all_gather(value_rows, "blk", axis=0, tiled=True),
    )
    key_count = pieces[0].shape[0]
    key_stack = pieces[0].reshape(key_count // group_rows, group_rows, head_group, HD)
    value_stack = pieces[1].reshape(key_count // group_rows, group_rows, head_group, HD)

    def one_block(current, stacked):
        totals, accumulated = current
        block_index, key_heads, value_heads = stacked
        expo, same_variate = exponent(query_heads, key_heads, block_index * group_rows, context)
        totals = totals + jnp.sum(expo, axis=2)
        accumulated = accumulated + jnp.einsum(
            "hqk,khd->qhd",
            expo.astype(jnp.bfloat16),
            value_heads,
            preferred_element_type=jnp.float32,
        )
        return ((totals, accumulated), None)

    result, unused = lax.scan(
        one_block,
        (
            jnp.zeros((head_group, group_rows), jnp.float32),
            jnp.zeros((group_rows, head_group, HD), jnp.float32),
        ),
        (jnp.arange(key_count // group_rows, dtype=jnp.int32), key_stack, value_stack),
    )
    totals, accumulated = result
    attended = accumulated / totals.T[:, :, None]
    merged = lax.all_to_all(
        attended.reshape(group_rows, own_width).astype(jnp.bfloat16),
        "head",
        split_axis=0,
        concat_axis=1,
        tiled=True,
    )
    attn_branch = jnp.dot(merged, out_full, preferred_element_type=jnp.float32)
    middle = residual + attn_branch
    second, second_back = jax.vjp(norm_rows, middle, ffn_gain)
    second_low = second.astype(jnp.bfloat16)
    expand = jnp.dot(second_low, expand_full, preferred_element_type=jnp.float32)
    hidden, swiglu_back = jax.vjp(swiglu, expand)
    hidden_low = hidden.astype(jnp.bfloat16)
    ffn_branch = jnp.dot(hidden_low, down_full, preferred_element_type=jnp.float32)
    outputs = (middle + ffn_branch).astype(jnp.bfloat16)
    grad_down_full = jnp.einsum(
        "tf,td->fd", hidden_low, cotangent, preferred_element_type=jnp.float32
    )
    grad_hidden = jnp.einsum("td,fd->tf", cotangent, down_full, preferred_element_type=jnp.float32)
    grad_expand_rows = swiglu_back(grad_hidden)[0].astype(jnp.bfloat16)
    grad_expand_full = jnp.einsum(
        "td,tc->dc", second_low, grad_expand_rows, preferred_element_type=jnp.float32
    )
    grad_second = jnp.einsum(
        "tc,dc->td", grad_expand_rows, expand_full, preferred_element_type=jnp.float32
    )
    grad_middle_norm, grad_ffn_gain = second_back(grad_second)
    grad_middle = cotangent.astype(jnp.float32) + grad_middle_norm
    branch_grad = grad_middle.astype(jnp.bfloat16)
    grad_out_full = jnp.einsum("td,tc->dc", merged, branch_grad, preferred_element_type=jnp.float32)
    grad_merged = jnp.einsum(
        "tc,dc->td", branch_grad, out_full, preferred_element_type=jnp.float32
    ).astype(jnp.bfloat16)
    grad_attended = lax.all_to_all(
        grad_merged, "head", split_axis=1, concat_axis=0, tiled=True
    ).reshape(group_rows, head_group, HD)
    grad_float = grad_attended.astype(jnp.float32)
    accum_grad = (grad_float / totals.T[:, :, None]).astype(jnp.bfloat16)
    center = jnp.sum(grad_float * attended, axis=2).T / totals

    def two_steps(turn_index, carried):
        key_now, value_now, key_grad, value_grad, query_grad, bias_grad = carried
        for offset in range(2):
            source = (group_index - 2 * turn_index - offset) % group_count
            expo, same_variate = exponent(query_heads, key_now, source * group_rows, context)
            prob_grad = jnp.einsum(
                "qhd,khd->hqk", accum_grad, value_now, preferred_element_type=jnp.float32
            )
            score_grad = expo * (prob_grad - center[:, :, None])
            other_sum = jnp.sum(jnp.where(same_variate, 0.0, score_grad), axis=(1, 2))
            same_sum = jnp.sum(jnp.where(same_variate, score_grad, 0.0), axis=(1, 2))
            bias_grad = bias_grad + jnp.stack([other_sum, same_sum])
            dot_grad = (score_grad * HD ** (-0.5)).astype(jnp.bfloat16)
            query_grad = query_grad + jnp.einsum(
                "hqk,khd->qhd", dot_grad, key_now, preferred_element_type=jnp.float32
            )
            key_grad = key_grad + jnp.einsum(
                "hqk,qhd->khd", dot_grad, query_heads, preferred_element_type=jnp.float32
            )
            value_grad = value_grad + jnp.einsum(
                "hqk,qhd->khd",
                expo.astype(jnp.bfloat16),
                accum_grad,
                preferred_element_type=jnp.float32,
            )
            key_now, value_now = from_behind((key_now, value_now), "blk", 1)
            key_grad, value_grad = from_behind((key_grad, value_grad), "blk", 1)
        return (key_now, value_now, key_grad, value_grad, query_grad, bias_grad)

    empty_heads = jnp.zeros((group_rows, head_group, HD), jnp.float32)
    carried = lax.fori_loop(
        0,
        group_count // 2,
        two_steps,
        (
            key_rows.reshape(group_rows, head_group, HD),
            value_rows.reshape(group_rows, head_group, HD),
            empty_heads,
            empty_heads,
            empty_heads,
            jnp.zeros((2, head_group), jnp.float32),
        ),
    )
    key_grad, value_grad, query_grad, bias_grad = (carried[2], carried[3], carried[4], carried[5])
    query_low = query_grad.reshape(group_rows, own_width).astype(jnp.bfloat16)
    key_low = key_grad.reshape(group_rows, own_width).astype(jnp.bfloat16)
    value_low = value_grad.reshape(group_rows, own_width).astype(jnp.bfloat16)
    grad_query_tok, grad_key_tok, grad_value_tok = (
        lax.all_to_all(query_low, "head", split_axis=0, concat_axis=1, tiled=True),
        lax.all_to_all(key_low, "head", split_axis=0, concat_axis=1, tiled=True),
        lax.all_to_all(value_low, "head", split_axis=0, concat_axis=1, tiled=True),
    )
    grad_query_key, grad_query_gain, grad_key_gain = rotate_back(
        (grad_query_tok.astype(jnp.float32), grad_key_tok.astype(jnp.float32))
    )
    grad_project = jnp.concatenate(
        [grad_query_key, grad_value_tok.astype(jnp.float32)], axis=1
    ).astype(jnp.bfloat16)
    grad_qkv_full = jnp.einsum(
        "td,tc->dc", normed_low, grad_project, preferred_element_type=jnp.float32
    )
    grad_normed = jnp.einsum(
        "tc,dc->td", grad_project, qkv_full, preferred_element_type=jnp.float32
    )
    grad_qkv, grad_expand, grad_down = (
        lax.psum_scatter(grad_qkv_full, ("blk", "head"), scatter_dimension=0, tiled=True),
        lax.psum_scatter(grad_expand_full, ("blk", "head"), scatter_dimension=0, tiled=True),
        lax.psum_scatter(grad_down_full, ("blk", "head"), scatter_dimension=0, tiled=True),
    )
    grad_first, grad_attn_gain = first_back(grad_normed)
    grad_inputs = grad_middle + grad_first
    grad_out = lax.psum_scatter(grad_out_full, ("blk", "head"), scatter_dimension=0, tiled=True)
    bias_full = lax.dynamic_update_slice(
        jnp.zeros((2, H), jnp.float32), bias_grad, (0, head_index * head_group)
    )
    squares = jnp.stack(
        [
            jnp.sum(residual * residual),
            jnp.sum(attn_branch * attn_branch),
            jnp.sum(ffn_branch * ffn_branch),
        ]
    )
    summed = lax.psum(
        (grad_attn_gain, grad_ffn_gain, grad_query_gain, grad_key_gain, bias_full, squares),
        ("blk", "head"),
    )
    entries = tok_rows * group_count * head_ways * D
    root_means = jnp.sqrt(summed[5] / entries)
    return (
        outputs,
        grad_inputs,
        grad_qkv,
        grad_out,
        grad_expand,
        grad_down,
        summed[0],
        summed[1],
        summed[2],
        summed[3],
        summed[4],
        root_means,
    )


def solution(mesh):
    return jax.shard_map(
        body,
        mesh=mesh,
        in_specs=(
            P(("blk", "head"), None),
            P(("blk", "head"), None),
            P(),
            P(),
            P(),
            P(),
            P(),
            P(("blk", "head"), None),
            P(("blk", "head"), None),
            P(("blk", "head"), None),
            P(("blk", "head"), None),
            P(),
            P(),
            P(),
        ),
        out_specs=(
            P(("blk", "head"), None),
            P(("blk", "head"), None),
            P(("blk", "head"), None),
            P(("blk", "head"), None),
            P(("blk", "head"), None),
            P(("blk", "head"), None),
            P(),
            P(),
            P(),
            P(),
            P(),
            P(),
        ),
        check_vma=False,
    )
```

profile of v0, /device:TPU:0, one launch (start us, length us, event | category | flops | bytes accessed | tf_op | source)
XLA Modules:
  0.0 1547.2 jit_solution(6861388137210778783)
XLA Ops:
  11.1 71.7 %all-gather.7.cloned.1.call-done = bf16[1024,3072]{1,0:T(8,128)(2,1)} async-done(((bf16[32,3072]{1,0:T(8,128)(2,1)}), bf16[1024,3072]{1,0:T(8,128)(2,1)}) %all-gather.7.cloned.1.call-update) | async-done | bytes 6291472 | tf_op jit(solution)/shard_map/all_gather | solution.py:118
  119.2 26.3 %all-gather.9.cloned.1.call-done = bf16[4096,256]{1,0:T(8,128)(2,1)} async-done(((bf16[512,256]{1,0:T(8,128)(2,1)}), bf16[4096,256]{1,0:T(8,128)(2,1)}) %all-gather.9.cloned.1.call-update) | async-done | bytes 2097168 | tf_op jit(solution)/shard_map/all_gather | solution.py:143
  159.5 35.7 %all-gather.11.cloned.1.call-done = bf16[4096,256]{1,0:T(8,128)(2,1)} async-done(((bf16[512,256]{1,0:T(8,128)(2,1)}), bf16[4096,256]{1,0:T(8,128)(2,1)}) %all-gather.11.cloned.1.call-update) | async-done | bytes 2097168 | tf_op jit(solution)/shard_map/all_gather | solution.py:144
  209.3 83.3 %while.39 = (s32[]{:T(128)}, f32[4,512]{1,0:T(4,128)S(1)}, f32[512,4,64]{0,2,1:T(8,128)S(1)}, s32[512]{0:T(512)S(1)}, s32[8]{0:T(128)S(1)}, /*index=5*/s32[4096]...) while((s32[]{:T(128)}, f32[4,512]{1,0:T(4,128)S(1)}, ...), condition=%wide.region_8.9_spmd.clone, body=%wide.region_6.8_spmd.clone.sunk | while | flops 279709696 | bytes 11847010 | solution.py:163
  306.4 65.3 %all-gather.15.cloned.1.call-done = bf16[1024,8192]{1,0:T(8,128)(2,1)} async-done(((bf16[32,8192]{1,0:T(8,128)(2,1)}), bf16[1024,8192]{1,0:T(8,128)(2,1)}) %all-gather.15.cloned.1.call-update) | async-done | bytes 16777232 | tf_op jit(solution)/shard_map/all_gather | solution.py:119
  371.7 10.2 fusion.87
  381.9 67.8 %all-gather.17.cloned.1.call-done = bf16[4096,1024]{1,0:T(8,128)(2,1)} async-done(((bf16[128,1024]{1,0:T(8,128)(2,1)}), bf16[4096,1024]{1,0:T(8,128)(2,1)}) %all-gather.17.cloned.1.call-update) | async-done | bytes 8388624 | tf_op jit(solution)/shard_map/all_gather | solution.py:120
  449.7 10.3 fusion.68
  460.0 13.4 multiply_reduce_fusion.4
  494.2 305.0 %while.40 = (s32[]{:T(128)}, bf16[512,4,64]{0,2,1:T(8,128)(2,1)S(1)}, bf16[512,4,64]{0,2,1:T(8,128)(2,1)}, f32[512,4,64]{0,2,1:T(8,128)S(1)}, f32[512,4,64]{0,2,...) while((s32[]{:T(128)}, ...), condition=%wide.region_17.18_spmd.clone, body=%wide.region_12.17_spmd.clone.sunk | while | flops 1383989248 | bytes 100185528 | solution.py:244
  530.1 10.1 collective-permute-done.4
  553.9 12.7 collective-permute-done.7
  566.7 11.2 collective-permute-done.5
  613.6 9.6 collective-permute-done.4
  636.1 13.0 collective-permute-done.7
  649.1 9.3 collective-permute-done.5
  709.8 11.1 collective-permute-done.7
  780.5 11.1 collective-permute-done.7
  800.1 13.4 all-to-all-start.5
  855.1 17.5 %fusion.66 = f32[1024,8192]{1,0:T(8,128)} fusion(f32[128,4096]{1,0:T(8,128)} %get-tuple-element.726, f32[128,4096]{1,0:T(8,128)} %get-tuple-element.725, f32[128,1024]{1,0:T(8,128)S(1)} %get-tuple-element.704, f32[1024]{0:T(1024)S(1)} %copy-done.20, f32[128]{0:T(128)S(1)} %fusion.82), kind=kOutput, calls=%fused_computation.115 | convolution fusion | flops 2149974016 | bytes 38277632 | tf_op jit(solution)/shard_map/td,tc->dc/dot_general | solution.py:194
  880.9 40.9 %all-reduce.8 = (f32[1024]{0:T(1024)}, f32[1024]{0:T(1024)}, f32[64]{0:T(128)}, f32[64]{0:T(128)}, f32[2,16]{1,0:T(2,128)}, /*index=5*/f32[3]{0:T(128)S(1)}) all-reduce(f32[1024]{0:T(1024)S(1)} %get-tuple-element.632, f32[1024]{0:T(1024)S(1)} %copy-done.37, ...), channel_id=1, replica_groups=mesh['head'=4,'blk'=8] {'blk','head'}, use_global_device_ids=true, to_apply=%region_26.27 | all-reduce | flops 2211 | bytes 17688 | tf_op jit(solution)/shard_map/psum | solution.py:296
  923.3 73.2 %reduce-scatter.5.cloned.1.call-done = f32[32,3072]{1,0:T(8,128)} async-done(((f32[1024,3072]{1,0:T(8,128)}), f32[32,3072]{1,0:T(8,128)}) %reduce-scatter.5.cloned.1.call-update) | async-done | bytes 393232 | tf_op jit(solution)/shard_map/reduce_scatter | solution.py:279
  996.5 184.8 %reduce-scatter.11.cloned.1.call-done = f32[128,1024]{1,0:T(8,128)} async-done(((f32[4096,1024]{1,0:T(8,128)}), f32[128,1024]{1,0:T(8,128)}) %reduce-scatter.11.cloned.1.call-update) | async-done | bytes 524304 | tf_op jit(solution)/shard_map/reduce_scatter | solution.py:281
  1181.3 358.8 %reduce-scatter.9.cloned.1.call-done = f32[32,8192]{1,0:T(8,128)} async-done(((f32[1024,8192]{1,0:T(8,128)}), f32[32,8192]{1,0:T(8,128)}) %reduce-scatter.9.cloned.1.call-update) | async-done | bytes 1048592 | tf_op jit(solution)/shard_map/reduce_scatter | solution.py:280
  (430 shorter events, 448.1 us)
Async XLA Ops:
  7.2 75.6 %all-gather.7.cloned.1.call-start = ((), (), s32[]{:S(2)}) async-start(), calls=%async_computation.12 | async-start | bytes 6488064 | tf_op jit(solution)/shard_map/all_gather | solution.py:118
  7.9 137.6 %all-gather.9.cloned.1.call-start = ((), (), s32[]{:S(2)}) async-start(), calls=%async_computation.13 | async-start | bytes 2359296 | tf_op jit(solution)/shard_map/all_gather | solution.py:143
  97.8 97.5 %all-gather.11.cloned.1.call-start = ((), (), s32[]{:S(2)}) async-start(), calls=%async_computation.14 | async-start | bytes 2359296 | tf_op jit(solution)/shard_map/all_gather | solution.py:144
  107.0 191.8 %all-gather.13.cloned.1.call-start = ((), (), s32[]{:S(2)}) async-start(), calls=%async_computation.15 | async-start | bytes 2162688 | tf_op jit(solution)/shard_map/all_gather | solution.py:113
  107.6 264.1 %all-gather.15.cloned.1.call-start = ((), (), s32[]{:S(2)}) async-start(), calls=%async_computation.16 | async-start | bytes 17301504 | tf_op jit(solution)/shard_map/all_gather | solution.py:119
  108.2 341.5 %all-gather.17.cloned.1.call-start = ((), (), s32[]{:S(2)}) async-start(), calls=%async_computation.17 | async-start | bytes 8650752 | tf_op jit(solution)/shard_map/all_gather | solution.py:120
  484.9 438.4 %reduce-scatter.7.cloned.1.call-start = ((), (), s32[]{:S(2)}) async-start(), calls=%async_computation.19 | async-start | bytes 4325376 | tf_op jit(solution)/shard_map/reduce_scatter | solution.py:285
  509.4 30.8 %collective-permute-start.4 = (f32[512,4,64]{0,2,1:T(8,128)S(1)}, f32[512,4,64]{0,2,1:T(8,128)S(1)}, u32[]{:S(2)}, u32[]{:S(2)}) collective-permute-start(f32[512,4,64]{0,2,1:T(8,128)S(1)} %fusion.179), channel_id=1, source_target_pairs={{0,1},{1,2},{2,3},{3,4},{4,5},{5,6},{6,7},{7,0},{8,9},{9,10},{10,1... | collective-permute-start | bytes 1572872 | tf_op jit(solution)/shard_map/while/body/eval_jaxpr/ppermute | solution.py:20
  513.5 33.5 %collective-permute-start.1 = (bf16[512,4,64]{0,2,1:T(8,128)(2,1)S(1)}, bf16[512,4,64]{0,2,1:T(8,128)(2,1)S(1)}, u32[]{:S(2)}, u32[]{:S(2)}) collective-permute-start(bf16[512,4,64]{0,2,1:T(8,128)(2,1)S(1)} %collective-permute-done), channel_id=1, source_target_pairs={{0,1},{1,2},{2,3},{3,4},{4,5},{5,6},{6,7},{7,0},{8,9},{9,10},{10,1... | collective-permute-start | bytes 786440 | tf_op jit(solution)/shard_map/while/body/eval_jaxpr/ppermute | solution.py:20
  515.8 38.1 %collective-permute-start.3 = (bf16[512,4,64]{0,2,1:T(8,128)(2,1)}, bf16[512,4,64]{0,2,1:T(8,128)(2,1)}, u32[]{:S(2)}, u32[]{:S(2)}) collective-permute-start(bf16[512,4,64]{0,2,1:T(8,128)(2,1)} %collective-permute-done.2), channel_id=1, source_target_pairs={{0,1},{1,2},{2,3},{3,4},{4,5},{5,6},{6,7},{7,0},{8,9},{9,10},{10,1... | collective-permute-start | bytes 786440 | tf_op jit(solution)/shard_map/while/body/eval_jaxpr/ppermute | solution.py:20
  530.0 36.7 %collective-permute-start.7 = (f32[512,4,64]{0,2,1:T(8,128)S(1)}, f32[512,4,64]{0,2,1:T(8,128)S(1)}, u32[]{:S(2)}, u32[]{:S(2)}) collective-permute-start(f32[512,4,64]{0,2,1:T(8,128)S(1)} %fusion.183), channel_id=1, source_target_pairs={{0,1},{1,2},{2,3},{3,4},{4,5},{5,6},{6,7},{7,0},{8,9},{9,10},{10,1... | collective-permute-start | bytes 1572872 | tf_op jit(solution)/shard_map/while/body/eval_jaxpr/ppermute | solution.py:20
  540.7 37.2 %collective-permute-start.5 = (f32[512,4,64]{0,2,1:T(8,128)S(1)}, f32[512,4,64]{0,2,1:T(8,128)S(1)}, u32[]{:S(2)}, u32[]{:S(2)}) collective-permute-start(f32[512,4,64]{0,2,1:T(8,128)S(1)} %fusion.181), channel_id=1, source_target_pairs={{0,1},{1,2},{2,3},{3,4},{4,5},{5,6},{6,7},{7,0},{8,9},{9,10},{10,1... | collective-permute-start | bytes 1572872 | tf_op jit(solution)/shard_map/while/body/eval_jaxpr/ppermute | solution.py:20
  599.6 30.3 %collective-permute-start.1 = (bf16[512,4,64]{0,2,1:T(8,128)(2,1)S(1)}, bf16[512,4,64]{0,2,1:T(8,128)(2,1)S(1)}, u32[]{:S(2)}, u32[]{:S(2)}) collective-permute-start(bf16[512,4,64]{0,2,1:T(8,128)(2,1)S(1)} %collective-permute-done), channel_id=1, source_target_pairs={{0,1},{1,2},{2,3},{3,4},{4,5},{5,6},{6,7},{7,0},{8,9},{9,10},{10,1... | collective-permute-start | bytes 786440 | tf_op jit(solution)/shard_map/while/body/eval_jaxpr/ppermute | solution.py:20
  602.4 33.8 %collective-permute-start.3 = (bf16[512,4,64]{0,2,1:T(8,128)(2,1)}, bf16[512,4,64]{0,2,1:T(8,128)(2,1)}, u32[]{:S(2)}, u32[]{:S(2)}) collective-permute-start(bf16[512,4,64]{0,2,1:T(8,128)(2,1)} %collective-permute-done.2), channel_id=1, source_target_pairs={{0,1},{1,2},{2,3},{3,4},{4,5},{5,6},{6,7},{7,0},{8,9},{9,10},{10,1... | collective-permute-start | bytes 786440 | tf_op jit(solution)/shard_map/while/body/eval_jaxpr/ppermute | solution.py:20
  612.8 36.4 %collective-permute-start.7 = (f32[512,4,64]{0,2,1:T(8,128)S(1)}, f32[512,4,64]{0,2,1:T(8,128)S(1)}, u32[]{:S(2)}, u32[]{:S(2)}) collective-permute-start(f32[512,4,64]{0,2,1:T(8,128)S(1)} %fusion.183), channel_id=1, source_target_pairs={{0,1},{1,2},{2,3},{3,4},{4,5},{5,6},{6,7},{7,0},{8,9},{9,10},{10,1... | collective-permute-start | bytes 1572872 | tf_op jit(solution)/shard_map/while/body/eval_jaxpr/ppermute | solution.py:20
  623.7 34.8 %collective-permute-start.5 = (f32[512,4,64]{0,2,1:T(8,128)S(1)}, f32[512,4,64]{0,2,1:T(8,128)S(1)}, u32[]{:S(2)}, u32[]{:S(2)}) collective-permute-start(f32[512,4,64]{0,2,1:T(8,128)S(1)} %fusion.181), channel_id=1, source_target_pairs={{0,1},{1,2},{2,3},{3,4},{4,5},{5,6},{6,7},{7,0},{8,9},{9,10},{10,1... | collective-permute-start | bytes 1572872 | tf_op jit(solution)/shard_map/while/body/eval_jaxpr/ppermute | solution.py:20
  676.1 33.7 %collective-permute-start.3 = (bf16[512,4,64]{0,2,1:T(8,128)(2,1)}, bf16[512,4,64]{0,2,1:T(8,128)(2,1)}, u32[]{:S(2)}, u32[]{:S(2)}) collective-permute-start(bf16[512,4,64]{0,2,1:T(8,128)(2,1)} %collective-permute-done.2), channel_id=1, source_target_pairs={{0,1},{1,2},{2,3},{3,4},{4,5},{5,6},{6,7},{7,0},{8,9},{9,10},{10,1... | collective-permute-start | bytes 786440 | tf_op jit(solution)/shard_map/while/body/eval_jaxpr/ppermute | solution.py:20
  689.9 31.0 %collective-permute-start.7 = (f32[512,4,64]{0,2,1:T(8,128)S(1)}, f32[512,4,64]{0,2,1:T(8,128)S(1)}, u32[]{:S(2)}, u32[]{:S(2)}) collective-permute-start(f32[512,4,64]{0,2,1:T(8,128)S(1)} %fusion.183), channel_id=1, source_target_pairs={{0,1},{1,2},{2,3},{3,4},{4,5},{5,6},{6,7},{7,0},{8,9},{9,10},{10,1... | collective-permute-start | bytes 1572872 | tf_op jit(solution)/shard_map/while/body/eval_jaxpr/ppermute | solution.py:20
  744.2 30.6 %collective-permute-start.1 = (bf16[512,4,64]{0,2,1:T(8,128)(2,1)S(1)}, bf16[512,4,64]{0,2,1:T(8,128)(2,1)S(1)}, u32[]{:S(2)}, u32[]{:S(2)}) collective-permute-start(bf16[512,4,64]{0,2,1:T(8,128)(2,1)S(1)} %collective-permute-done), channel_id=1, source_target_pairs={{0,1},{1,2},{2,3},{3,4},{4,5},{5,6},{6,7},{7,0},{8,9},{9,10},{10,1... | collective-permute-start | bytes 786440 | tf_op jit(solution)/shard_map/while/body/eval_jaxpr/ppermute | solution.py:20
  746.8 33.7 %collective-permute-start.3 = (bf16[512,4,64]{0,2,1:T(8,128)(2,1)}, bf16[512,4,64]{0,2,1:T(8,128)(2,1)}, u32[]{:S(2)}, u32[]{:S(2)}) collective-permute-start(bf16[512,4,64]{0,2,1:T(8,128)(2,1)} %collective-permute-done.2), channel_id=1, source_target_pairs={{0,1},{1,2},{2,3},{3,4},{4,5},{5,6},{6,7},{7,0},{8,9},{9,10},{10,1... | collective-permute-start | bytes 786440 | tf_op jit(solution)/shard_map/while/body/eval_jaxpr/ppermute | solution.py:20
  760.6 31.0 %collective-permute-start.7 = (f32[512,4,64]{0,2,1:T(8,128)S(1)}, f32[512,4,64]{0,2,1:T(8,128)S(1)}, u32[]{:S(2)}, u32[]{:S(2)}) collective-permute-start(f32[512,4,64]{0,2,1:T(8,128)S(1)} %fusion.183), channel_id=1, source_target_pairs={{0,1},{1,2},{2,3},{3,4},{4,5},{5,6},{6,7},{7,0},{8,9},{9,10},{10,1... | collective-permute-start | bytes 1572872 | tf_op jit(solution)/shard_map/while/body/eval_jaxpr/ppermute | solution.py:20
  832.3 164.1 %reduce-scatter.5.cloned.1.call-start = ((), (), s32[]{:S(2)}) async-start(), calls=%async_computation.18 | async-start | bytes 12976128 | tf_op jit(solution)/shard_map/reduce_scatter | solution.py:279
  844.7 336.6 %reduce-scatter.11.cloned.1.call-start = ((), (), s32[]{:S(2)}) async-start(), calls=%async_computation.21 | async-start | bytes 17301504 | tf_op jit(solution)/shard_map/reduce_scatter | solution.py:281
  855.0 685.1 %reduce-scatter.9.cloned.1.call-start = ((), (), s32[]{:S(2)}) async-start(), calls=%async_computation.20 | async-start | bytes 34603008 | tf_op jit(solution)/shard_map/reduce_scatter | solution.py:280
  (88 other events, 2426.0 us)
Sparse Core Ops, SparseCore 0:
  10.9 71.8 all-gather.6
  97.9 47.5 all-gather.8
  147.6 47.6 all-gather.10
  198.0 54.7 all-gather.12
  255.5 116.1 all-gather.14
  374.4 75.2 all-gather.16
  488.5 159.9 reduce-scatter.6
  844.9 151.5 reduce-scatter.4
  999.3 181.9 reduce-scatter.10
  1184.0 356.0 reduce-scatter.8
where the time goes:
time: 1560 us; the launch traced here: 1550 us
  waiting for transfers between devices  1100 us (71%)
  matrix products  232 us (15%)
  starting transfers between devices  60.4 us (4%)
  blocking collectives  58.4 us (4%)
  local copies, waits for them, and re-layouts  53.1 us (3%)
  other arithmetic  21 us (1%)
    reduce_scatter x1, waiting for transfers between devices, body(): lax.psum_scatter(grad_expand_full, ('blk', 'head'), scatter_dimension=0,...  359 us
    ppermute x32, waiting for transfers between devices, from_behind(): lax.ppermute(shard, axis, [(i, (i + by) % length) for i in range(length)])  188 us
    reduce_scatter x1, waiting for transfers between devices, body(): lax.psum_scatter(grad_down_full, ('blk', 'head'), scatter_dimension=0, ti...  185 us
    reduce_scatter x1, waiting for transfers between devices, body(): lax.psum_scatter(grad_qkv_full, ('blk', 'head'), scatter_dimension=0, til...  73.2 us
    all_gather x1, waiting for transfers between devices, body(): lax.all_gather(qkv_weight, ('blk', 'head'), axis=0, tiled=True)  71.7 us
    all_gather x1, waiting for transfers between devices, body(): lax.all_gather(down_weight, ('blk', 'head'), axis=0, tiled=True)  67.8 us
    all_gather x1, waiting for transfers between devices, body(): lax.all_gather(expand_weight, ('blk', 'head'), axis=0, tiled=True)  65.3 us
    dot_general x16, matrix products, exponent(): jnp.einsum('qhd,khd->hqk', query_heads, key_heads, preferred_element_type...  44.3 us
  transfers between devices with their start and end apart: 48, of which 40 were waited for; matrix products, arithmetic and copies ran while one was open for 17% of the time, Pallas kernels for 0%

commit v1 on v0

v1 whole, which is shorter than its diff:
```python
from functools import partial

import jax
import jax.numpy as jnp
from jax import lax
from jax.experimental import pallas as pl
from jax.experimental.pallas import tpu as pltpu
from jax.sharding import Mesh
from jax.sharding import PartitionSpec as P

D = 1024
H = 16
HD = 64
BLOCK = 128
NVAR = 4
EPSILON = 1e-05
THETA = 10000.0

DEVICES = ("bz", "by", "hx", "core")
CHIPS = ("bz", "by", "hx")
PLANE = ("by", "hx", "core")

SEGMENT_LANE = 64
VARIATE_LANE = 76
MASK = -512.0
QUERY_TILE = 256
KEY_TILE = 256

bf16 = jnp.bfloat16
f32 = jnp.float32


def dot(left, right, dims):
    return lax.dot_general(left, right, (dims, ((), ())), preferred_element_type=f32)


def norm_rows(values, gain):
    factor = lax.rsqrt(jnp.mean(values * values, axis=-1, keepdims=True) + EPSILON)
    return values * factor * gain


def norm_back(values, gain, grad):
    factor = lax.rsqrt(jnp.mean(values * values, axis=-1, keepdims=True) + EPSILON)
    scaled = grad * gain
    inner = jnp.mean(scaled * values, axis=-1, keepdims=True)
    grad_values = factor * (scaled - values * (factor * factor) * inner)
    return grad_values, grad * values * factor


def swiglu(expand):
    half = expand.shape[1] // 2
    return jax.nn.silu(expand[:, :half]) * expand[:, half:]


def swap(shard, axis):
    return lax.ppermute(shard, axis, [(0, 1), (1, 0)])


def plane_gather(shard):
    half = shard.shape[0] // 2
    across_x = swap(shard, "hx")
    across_y = swap(shard, "by")
    corner_a = swap(across_y[:half], "hx")
    corner_b = swap(across_x[half:], "by")
    mine = jnp.concatenate([shard, across_x, across_y, corner_a, corner_b], axis=0)
    return jnp.concatenate([mine, swap(mine, "core")], axis=0)


def plane_scatter(partial_low):
    rows = partial_low.shape[0] // 8
    half = rows // 2
    other = swap(partial_low[4 * rows :], "core")
    mine = partial_low[: 4 * rows].astype(f32) + other.astype(f32)
    corner = mine[3 * rows :].astype(bf16)
    for_y = swap(corner[:half], "hx").astype(f32)
    for_x = swap(corner[half:], "by").astype(f32)
    to_x = mine[rows : 2 * rows]
    to_y = mine[2 * rows : 3 * rows]
    to_x = jnp.concatenate([to_x[:half], to_x[half:] + for_x], axis=0).astype(bf16)
    to_y = jnp.concatenate([to_y[:half] + for_y, to_y[half:]], axis=0).astype(bf16)
    from_x = swap(to_x, "hx")
    from_y = swap(to_y, "by")
    return mine[:rows] + from_x.astype(f32) + from_y.astype(f32)


def plane_members():
    by, hx, core = lax.axis_index("by"), lax.axis_index("hx"), lax.axis_index("core")
    members = []
    for core_flip in (0, 1):
        for x_flip, y_flip in ((0, 0), (1, 0), (0, 1), (1, 1)):
            members.append((by ^ y_flip) * 4 + (hx ^ x_flip) * 2 + (core ^ core_flip))
    return members


def lanes(shape):
    return lax.broadcasted_iota(jnp.int32, shape, len(shape) - 1)


def half_mean(values, lane):
    low = jnp.sum(jnp.where(lane < HD, values, 0.0), axis=-1, keepdims=True)
    high = jnp.sum(jnp.where(lane < HD, 0.0, values), axis=-1, keepdims=True)
    return jnp.where(lane < HD, low, high) * (1.0 / HD)


def swap_halves(values, lane):
    return jnp.where(
        (lane & (HD - 1)) < HD // 2, pltpu.roll(values, 96, 1), pltpu.roll(values, 32, 1)
    )


def project_kernel(
    core_ref,
    x_ref,
    gain_ref,
    weight_ref,
    cosine_ref,
    sine_ref,
    gains_ref,
    hot_ref,
    normed_ref,
    raw_ref,
    query_ref,
    kv_ref,
):
    x = x_ref[0, 0].astype(f32)
    normed = norm_rows(x, gain_ref[...]).astype(bf16)
    normed_ref[...] = normed
    project = dot(normed, weight_ref[...], ((1,), (0,)))
    both = project[:, : 2 * HD]
    value = project[:, 2 * HD :]
    raw_ref[...] = both
    lane = lanes(both.shape)
    scaled = both * lax.rsqrt(half_mean(both * both, lane) + EPSILON) * gains_ref[...]
    turned = scaled * cosine_ref[...] + swap_halves(scaled, lane) * sine_ref[...]
    turned = turned.astype(bf16).astype(f32)
    query_ref[...] = jnp.where(lane < HD, turned, hot_ref[...].astype(f32)).astype(bf16)
    kv_ref[...] = jnp.where(lane < HD, value, turned * HD ** (-0.5)).astype(bf16)


def project(core, gathered, gain, weight, cosine, sine, gains, hot):
    blocks = gathered.shape[0]
    rows = blocks * BLOCK
    row_spec = lambda width: pl.BlockSpec((BLOCK, width), lambda j, core: (j, 0))
    whole = lambda array: pl.BlockSpec(array.shape, lambda j, core: (0, 0))
    return pl.pallas_call(
        project_kernel,
        grid_spec=pltpu.PrefetchScalarGridSpec(
            num_scalar_prefetch=1,
            grid=(blocks,),
            in_specs=[
                pl.BlockSpec((1, 1, BLOCK, D), lambda j, core: (j, core[0], 0, 0)),
                whole(gain),
                whole(weight),
                row_spec(128),
                row_spec(128),
                whole(gains),
                row_spec(128),
            ],
            out_specs=[row_spec(D), row_spec(128), row_spec(128), row_spec(128)],
        ),
        out_shape=[
            jax.ShapeDtypeStruct((rows, D), bf16),
            jax.ShapeDtypeStruct((rows, 128), f32),
            jax.ShapeDtypeStruct((rows, 128), bf16),
            jax.ShapeDtypeStruct((rows, 128), bf16),
        ],
        name="project",
    )(core, gathered, gain, weight, cosine, sine, gains, hot)


def sort_keys(place_ref, own_ref, other_ref, mask_ref, key_ref, value_ref):
    blocks = own_ref.shape[0] // BLOCK
    lane = lanes((BLOCK, 128))
    ones = jnp.where((lane >= HD) & (lane < HD + 3), 1.0, 0.0)
    for half, source_ref in ((0, own_ref), (1, other_ref)):

        def put(j, unused, half=half, source_ref=source_ref):
            source = pl.multiple_of(j * BLOCK, BLOCK)
            tail = pl.multiple_of((half * blocks + j) * BLOCK, BLOCK)
            target = pl.multiple_of(place_ref[half * blocks + j] * BLOCK, BLOCK)
            both = source_ref[pl.ds(source, BLOCK), :].astype(f32)
            mask = mask_ref[pl.ds(tail, BLOCK), :].astype(f32)
            key_ref[pl.ds(target, BLOCK), :] = jnp.where(
                lane < HD, pltpu.roll(both, HD, 1), mask
            ).astype(bf16)
            value_ref[pl.ds(target, BLOCK), :] = jnp.where(lane < HD, both, ones).astype(bf16)
            return unused

        lax.fori_loop(0, blocks, put, 0)


def tile_rows(order_ref, tile):
    count = QUERY_TILE // BLOCK
    return [pl.multiple_of(order_ref[tile * count + i] * BLOCK, BLOCK) for i in range(count)]


def load_rows(ref, starts):
    return jnp.concatenate([ref[pl.ds(start, BLOCK), :] for start in starts], axis=0)


def attend_kernel(
    order_ref,
    place_ref,
    low_ref,
    high_ref,
    query_ref,
    own_ref,
    other_ref,
    mask_ref,
    kept_ref,
    attended_ref,
    key_ref,
    value_ref,
):
    tile = pl.program_id(0)

    @pl.when(tile == 0)
    def _():
        sort_keys(place_ref, own_ref, other_ref, mask_ref, key_ref, value_ref)
        kept_ref[...] = jnp.zeros_like(kept_ref)
        attended_ref[...] = jnp.zeros_like(attended_ref)

    starts = tile_rows(order_ref, tile)
    query = load_rows(query_ref, starts)

    def chunk(index, accumulated):
        first = pl.multiple_of(index * KEY_TILE, KEY_TILE)
        key = key_ref[pl.ds(first, KEY_TILE), :]
        value = value_ref[pl.ds(first, KEY_TILE), :]
        expo = jnp.exp(dot(query, key, ((1,), (1,))))
        return accumulated + dot(expo.astype(bf16), value, ((1,), (0,)))

    accumulated = lax.fori_loop(
        low_ref[tile], high_ref[tile], chunk, jnp.zeros((QUERY_TILE, 128), f32)
    )
    totals = accumulated[:, HD : HD + 1]
    lane = lanes(accumulated.shape)
    kept = jnp.where(lane < HD, accumulated / totals, totals)
    for i, start in enumerate(starts):
        piece = kept[i * BLOCK : (i + 1) * BLOCK]
        kept_ref[pl.ds(start, BLOCK), :] = piece
        attended_ref[pl.ds(start, BLOCK), :] = piece[:, :HD].astype(bf16)


def fixed(array, prefetched):
    return pl.BlockSpec(
        array.shape, lambda *unused: (0,) * len(array.shape), pipeline_mode=pl.Buffered(1)
    )


def attend(order, place, low, high, query, own, other, mask):
    rows = query.shape[0]
    operands = (query, own, other, mask)
    outs = (jax.ShapeDtypeStruct((rows, 128), f32), jax.ShapeDtypeStruct((rows, HD), bf16))
    return pl.pallas_call(
        attend_kernel,
        grid_spec=pltpu.PrefetchScalarGridSpec(
            num_scalar_prefetch=4,
            grid=(low.shape[0],),
            in_specs=[fixed(array, 4) for array in operands],
            out_specs=[fixed(array, 4) for array in outs],
            scratch_shapes=[pltpu.VMEM((2 * rows, 128), bf16), pltpu.VMEM((2 * rows, 128), bf16)],
        ),
        out_shape=list(outs),
        name="attend",
    )(order, place, low, high, *operands)


def attend_back_kernel(
    order_ref,
    place_ref,
    low_ref,
    high_ref,
    query_ref,
    own_ref,
    other_ref,
    mask_ref,
    hot_ref,
    kept_ref,
    grad_ref,
    query_grad_ref,
    own_grad_ref,
    other_grad_ref,
    bias_ref,
    key_ref,
    value_ref,
    key_grad_ref,
    value_grad_ref,
):
    tile = pl.program_id(0)

    @pl.when(tile == 0)
    def _():
        sort_keys(place_ref, own_ref, other_ref, mask_ref, key_ref, value_ref)
        query_grad_ref[...] = jnp.zeros_like(query_grad_ref)
        key_grad_ref[...] = jnp.zeros_like(key_grad_ref)
        value_grad_ref[...] = jnp.zeros_like(value_grad_ref)

    starts = tile_rows(order_ref, tile)
    query = load_rows(query_ref, starts)
    kept = load_rows(kept_ref, starts)
    grad = load_rows(grad_ref, starts).astype(f32)
    grad = jnp.concatenate([grad, jnp.zeros_like(grad)], axis=1)
    lane = lanes(kept.shape)
    totals = kept[:, HD : HD + 1]
    center = jnp.sum(jnp.where(lane < HD, grad * kept, 0.0), axis=1, keepdims=True) / totals
    center_high = center.astype(bf16).astype(f32)
    center_rest = center - center_high
    center_mid = center_rest.astype(bf16).astype(f32)
    center_low = center_rest - center_mid
    wide = jnp.where(lane == HD, -center_high, 0.0)
    wide = jnp.where(lane == HD + 1, -center_mid, wide)
    wide = jnp.where(lane == HD + 2, -center_low, wide)
    wide = jnp.where(lane < HD, grad / totals, wide).astype(bf16)

    def chunk(index, query_grad):
        first = pl.multiple_of(index * KEY_TILE, KEY_TILE)
        window = pl.ds(first, KEY_TILE)
        key = key_ref[window, :]
        value = value_ref[window, :]
        expo = jnp.exp(dot(key, query, ((1,), (1,))))
        score_grad = expo * dot(value, wide, ((1,), (1,)))
        score_low = score_grad.astype(bf16)
        value_grad_ref[window, :] += dot(expo.astype(bf16), wide, ((1,), (0,)))
        key_grad_ref[window, :] += dot(score_low, query, ((1,), (0,)))
        return query_grad + dot(score_low, key, ((0,), (0,)))

    query_grad = lax.fori_loop(
        low_ref[tile], high_ref[tile], chunk, jnp.zeros((QUERY_TILE, 128), f32)
    )
    for i, start in enumerate(starts):
        query_grad_ref[pl.ds(start, BLOCK), :] = query_grad[i * BLOCK : (i + 1) * BLOCK]

    @pl.when(tile == pl.num_programs(0) - 1)
    def _():
        blocks = own_ref.shape[0] // BLOCK
        block_lane = lanes((BLOCK, 128))
        variate = (block_lane >= VARIATE_LANE) & (block_lane < VARIATE_LANE + NVAR)
        sums = (jnp.zeros((BLOCK, 128), f32), jnp.zeros((BLOCK, 128), f32))
        for half, target_ref in ((0, own_grad_ref), (1, other_grad_ref)):

            def take(j, sums, half=half, target_ref=target_ref):
                target = pl.multiple_of(j * BLOCK, BLOCK)
                tail = pl.multiple_of((half * blocks + j) * BLOCK, BLOCK)
                source = pl.multiple_of(place_ref[half * blocks + j] * BLOCK, BLOCK)
                key_grad = key_grad_ref[pl.ds(source, BLOCK), :]
                value_grad = value_grad_ref[pl.ds(source, BLOCK), :]
                target_ref[pl.ds(target, BLOCK), :] = jnp.where(
                    block_lane < HD, value_grad, pltpu.roll(key_grad, HD, 1) * HD ** (-0.5)
                )
                every = jnp.where(variate, key_grad, 0.0)
                hot = hot_ref[pl.ds(tail, BLOCK), :].astype(f32)
                return (sums[0] + every, sums[1] + every * hot)

            sums = lax.fori_loop(0, blocks, take, sums)
        every = jnp.sum(sums[0], keepdims=True)
        same = jnp.sum(sums[1], keepdims=True)
        bias_lane = lanes((8, 128))
        bias_ref[...] = jnp.where(bias_lane == 0, every - same, jnp.where(bias_lane == 1, same, 0.0))


def attend_back(order, place, low, high, query, own, other, mask, hot, kept, grad):
    rows = query.shape[0]
    operands = (query, own, other, mask, hot, kept, grad)
    outs = tuple(jax.ShapeDtypeStruct((rows, 128), f32) for unused in range(3)) + (
        jax.ShapeDtypeStruct((8, 128), f32),
    )
    return pl.pallas_call(
        attend_back_kernel,
        grid_spec=pltpu.PrefetchScalarGridSpec(
            num_scalar_prefetch=4,
            grid=(low.shape[0],),
            in_specs=[fixed(array, 4) for array in operands],
            out_specs=[fixed(array, 4) for array in outs],
            scratch_shapes=[
                pltpu.VMEM((2 * rows, 128), bf16),
                pltpu.VMEM((2 * rows, 128), bf16),
                pltpu.VMEM((2 * rows, 128), f32),
                pltpu.VMEM((2 * rows, 128), f32),
            ],
        ),
        out_shape=list(outs),
        name="attend_back",
    )(order, place, low, high, *operands)


def project_back_kernel(
    query_grad_ref,
    own_ref,
    other_ref,
    raw_ref,
    cosine_ref,
    sine_ref,
    gains_ref,
    normed_ref,
    grad_ref,
    weight_grad_ref,
    gain_grad_ref,
    weight_ref,
    gain_ref,
):
    step = pl.program_id(0)

    @pl.when(step == 0)
    def _():
        weight_ref[...] = jnp.zeros_like(weight_ref)
        gain_ref[...] = jnp.zeros_like(gain_ref)

    kv_grad = (own_ref[...] + other_ref[...]).astype(bf16).astype(f32)
    lane = lanes(kv_grad.shape)
    turned = jnp.where(lane < HD, query_grad_ref[...].astype(bf16).astype(f32), kv_grad)
    grad = turned * cosine_ref[...] - swap_halves(turned, lane) * sine_ref[...]
    raw = raw_ref[...]
    factor = lax.rsqrt(half_mean(raw * raw, lane) + EPSILON)
    scaled = grad * gains_ref[...]
    inner = half_mean(scaled * raw, lane)
    both = (factor * (scaled - raw * (factor * factor) * inner)).astype(bf16)
    gain_ref[...] += jnp.sum(grad * raw * factor, axis=0, keepdims=True)
    value = jnp.where(lane < HD, kv_grad, 0.0).astype(bf16)
    full = jnp.concatenate([both, value], axis=1)
    grad_ref[...] = full[:, : 3 * HD]
    weight_ref[...] += dot(normed_ref[...], full, ((0,), (0,)))

    @pl.when(step == pl.num_programs(0) - 1)
    def _():
        weight_grad_ref[...] = weight_ref[:, : 3 * HD].astype(bf16)
        gain_grad_ref[...] = jnp.broadcast_to(gain_ref[...], gain_grad_ref.shape)


def project_back(query_grad, own, other, raw, cosine, sine, gains, normed):
    rows = query_grad.shape[0]
    step_rows = 2 * BLOCK
    row_spec = lambda width: pl.BlockSpec((step_rows, width), lambda j: (j, 0))
    whole = lambda shape: pl.BlockSpec(shape, lambda j: (0, 0))
    return pl.pallas_call(
        project_back_kernel,
        grid=(rows // step_rows,),
        in_specs=[row_spec(128)] * 6 + [whole(gains.shape), row_spec(D)],
        out_specs=[row_spec(3 * HD), whole((D, 3 * HD)), whole((8, 128))],
        out_shape=[
            jax.ShapeDtypeStruct((rows, 3 * HD), bf16),
            jax.ShapeDtypeStruct((D, 3 * HD), bf16),
            jax.ShapeDtypeStruct((8, 128), f32),
        ],
        scratch_shapes=[pltpu.VMEM((D, 4 * HD), f32), pltpu.VMEM((1, 128), f32)],
        name="project_back",
    )(query_grad, own, other, raw, cosine, sine, gains, normed)


def token_meta(seq_lengths, block_order):
    blocks = block_order.shape[0]
    packed_at = jnp.repeat(block_order, BLOCK) * BLOCK + jnp.tile(
        jnp.arange(BLOCK, dtype=jnp.int32), blocks
    )
    ends = jnp.cumsum(seq_lengths)
    after = packed_at[:, None] >= ends[None, :]
    segment = jnp.sum(after.astype(jnp.int32), axis=1)
    begin = jnp.max(jnp.where(after, ends[None, :], jnp.zeros_like(ends)[None, :]), axis=1)
    return (segment, packed_at - begin, ends)


def both_cores(array, core):
    pairs = array.reshape((-1, 2, BLOCK) + array.shape[1:])
    shape = (-1,) + array.shape[1:]
    own = lax.dynamic_index_in_dim(pairs, core, 1, keepdims=False).reshape(shape)
    other = lax.dynamic_index_in_dim(pairs, 1 - core, 1, keepdims=False).reshape(shape)
    return own, other


def one_hot_rows(segment, variate, segments):
    lane = jnp.arange(128, dtype=jnp.int32)[None, :]
    hot = lane == SEGMENT_LANE + segment[:, None]
    for copy in range(3):
        hot = hot | (lane == VARIATE_LANE + copy * NVAR + variate[:, None])
    return hot.astype(bf16)


def mask_rows(segment, variate, segments, bias):
    lane = jnp.arange(128, dtype=jnp.int32)[None, :]
    here = lane - SEGMENT_LANE
    rows = jnp.where(
        (here >= 0) & (here < segments) & (here != segment[:, None]), jnp.float32(MASK), 0.0
    )
    high = lax.reduce_precision(bias, 8, 7)
    mid = lax.reduce_precision(bias - high, 8, 7)
    low = bias - high - mid
    for copy, part in enumerate((high, mid, low)):
        here = lane - VARIATE_LANE - copy * NVAR
        value = jnp.where(here == variate[:, None], part[1], part[0])
        rows = jnp.where((here >= 0) & (here < NVAR), value, rows)
    return rows.astype(bf16)


def sum_everywhere(vector, devices):
    copies = jnp.broadcast_to(vector[None], (devices,) + vector.shape)
    return jnp.sum(lax.all_to_all(copies, DEVICES, 0, 0, tiled=True), axis=0)


def body(
    inputs,
    cotangent,
    attn_gain,
    ffn_gain,
    query_gain,
    key_gain,
    variate_bias,
    qkv_weight,
    out_weight,
    expand_weight,
    down_weight,
    seq_lengths,
    variate_ids,
    block_order,
):
    depth = lax.axis_size("bz")
    chips = depth * 4
    devices = chips * 2
    sharers = chips // H
    core = lax.axis_index("core")
    chip = (lax.axis_index("bz") * 2 + lax.axis_index("by")) * 2 + lax.axis_index("hx")
    head = chip // sharers
    share = chip % sharers
    rows = qkv_weight.shape[0]
    hidden_rows = down_weight.shape[0]
    segments = seq_lengths.shape[0] + 1
    tokens = variate_ids.shape[0]

    gathered = lax.all_gather(
        jnp.concatenate([inputs, out_weight], axis=0), DEVICES, axis=0, tiled=True
    ).reshape(chips, 2, BLOCK + rows, D)

    by_head = qkv_weight.reshape(rows, 3, H, HD)
    to_heads = jnp.repeat(
        by_head.transpose(2, 0, 1, 3).reshape(H, rows, 3 * HD), 2 * sharers, axis=0
    )
    own_qkv = lax.all_to_all(to_heads, DEVICES, 0, 0, tiled=True).reshape(D, 3 * HD)
    own_qkv = jnp.pad(own_qkv, ((0, 0), (0, HD)))
    to_plane = (
        expand_weight.reshape(rows, 2, depth, 8, hidden_rows)
        .transpose(3, 0, 1, 2, 4)
        .reshape(8, rows, 2 * depth * hidden_rows)
    )
    expand_part = lax.all_to_all(to_plane, PLANE, 0, 0, tiled=True).reshape(8 * rows, -1)
    cotangent_plane = plane_gather(cotangent)

    segment, position, ends = token_meta(seq_lengths, block_order)
    own_segment, other_segment = both_cores(segment, core)
    own_variate, other_variate = both_cores(variate_ids, core)
    own_position = both_cores(position, core)[0]
    all_segment = jnp.concatenate([own_segment, other_segment])
    all_variate = jnp.concatenate([own_variate, other_variate])
    bias = lax.dynamic_index_in_dim(variate_bias, head, 1, keepdims=False)
    hot = one_hot_rows(all_segment, all_variate, segments)
    mask = mask_rows(all_segment, all_variate, segments, bias)
    freqs = THETA ** (-jnp.arange(HD // 2, dtype=f32) / (HD // 2))
    angles = own_position.astype(f32)[:, None] * freqs[None, :]
    cosine = jnp.tile(jnp.cos(angles), (1, 4))
    sine = jnp.sin(angles)
    sine = jnp.tile(jnp.concatenate([-sine, sine], axis=1), (1, 2))
    pairs = block_order.reshape(chips, 2)
    own_place = lax.dynamic_index_in_dim(pairs, core, 1, keepdims=False)
    other_place = lax.dynamic_index_in_dim(pairs, 1 - core, 1, keepdims=False)
    place = jnp.concatenate([own_place, other_place])
    rank = jnp.sum((own_place[None, :] < own_place[:, None]).astype(jnp.int32), axis=1)
    taken = chips // sharers
    wanted = share * taken + jnp.arange(taken, dtype=jnp.int32)
    chosen = (rank[None, :] == wanted[:, None]).astype(jnp.int32)
    order = jnp.sum(chosen * jnp.arange(chips, dtype=jnp.int32)[None, :], axis=1)
    sorted_place = jnp.sum(chosen * own_place[None, :], axis=1).reshape(-1, QUERY_TILE // BLOCK)
    first_token = sorted_place[:, 0] * BLOCK
    last_token = sorted_place[:, -1] * BLOCK + BLOCK - 1
    begins = jnp.max(jnp.where(ends[None, :] <= first_token[:, None], ends[None, :], 0), axis=1)
    finish = jnp.min(jnp.where(ends[None, :] > last_token[:, None], ends[None, :], tokens), axis=1)
    low = begins // KEY_TILE
    high = (finish + KEY_TILE - 1) // KEY_TILE
    gains = jnp.concatenate([query_gain, key_gain])[None, :]

    gathered, expand_part, down_part = lax.optimization_barrier(
        (gathered, expand_part, down_weight)
    )
    expand_own = lax.all_gather(expand_part, "bz", axis=0, tiled=True)
    down_own = lax.all_gather(down_part, "bz", axis=0, tiled=True)
    out_full = gathered[:, :, BLOCK:, :].reshape(D, D)

    normed_low, raw, query, own_kv = project(
        core[None], gathered, attn_gain[None], own_qkv, cosine, sine, gains, hot
    )
    other_kv = swap(own_kv, "core")
    kept, attended = attend(order, place, low, high, query, own_kv, other_kv, mask)
    merged = lax.all_to_all(attended.reshape(chips, BLOCK, HD), CHIPS, 0, 0, tiled=True)
    merged = merged.reshape(H, sharers, BLOCK, HD)
    merged = merged[:, 0] if sharers == 1 else jnp.sum(merged, axis=1)
    merged = merged.transpose(1, 0, 2).reshape(BLOCK, D)

    residual = inputs.astype(f32)
    attn_branch = jnp.dot(merged, out_full, preferred_element_type=f32)
    middle = residual + attn_branch
    second_low = plane_gather(norm_rows(middle, ffn_gain).astype(bf16))

    expand = jnp.dot(second_low, expand_own, preferred_element_type=f32)
    hidden, swiglu_back = jax.vjp(swiglu, expand)
    hidden_low = hidden.astype(bf16)
    ffn_part = jnp.dot(hidden_low, down_own, preferred_element_type=f32).astype(bf16)
    grad_hidden = dot(cotangent_plane, down_own, ((1,), (1,)))
    grad_down_part = dot(hidden_low, cotangent_plane, ((0,), (0,))).astype(bf16)
    grad_expand_rows = swiglu_back(grad_hidden)[0].astype(bf16)
    grad_second_part = dot(grad_expand_rows, expand_own, ((1,), (1,))).astype(bf16)
    grad_expand_part = dot(second_low, grad_expand_rows, ((0,), (0,))).astype(bf16)
    grad_second = plane_scatter(grad_second_part)
    grad_middle, grad_ffn_rows = norm_back(middle, ffn_gain, grad_second)
    grad_middle = cotangent.astype(f32) + grad_middle
    branch_grad = grad_middle.astype(bf16)
    grad_merged = dot(branch_grad, out_full, ((1,), (1,))).astype(bf16)
    to_chips = jnp.repeat(grad_merged.reshape(BLOCK, H, HD).transpose(1, 0, 2), sharers, axis=0)
    grad_attended = lax.all_to_all(to_chips, CHIPS, 0, 0, tiled=True).reshape(-1, HD)

    ffn_branch = plane_scatter(ffn_part)
    outputs = (middle + ffn_branch).astype(bf16)
    grad_down = lax.psum_scatter(grad_down_part, "bz", scatter_dimension=0, tiled=True)
    grad_expand = lax.psum_scatter(grad_expand_part, "bz", scatter_dimension=0, tiled=True)
    grad_expand = (
        lax.all_to_all(grad_expand.reshape(8, rows, -1), PLANE, 0, 0, tiled=True)
        .reshape(8, rows, 2, depth, hidden_rows)
        .transpose(1, 2, 3, 0, 4)
        .reshape(rows, -1)
        .astype(f32)
    )

    grad_out_full = dot(merged, branch_grad, ((0,), (0,))).astype(bf16)
    grad_out_rows = grad_out_full.reshape(depth, 8, rows, D)
    grad_out_rows = jnp.concatenate(
        [
            lax.dynamic_index_in_dim(grad_out_rows, member, 1, keepdims=False).reshape(-1, D)
            for member in plane_members()
        ],
        axis=0,
    )
    grad_out_part = plane_scatter(grad_out_rows).astype(bf16)
    grad_out = lax.psum_scatter(grad_out_part, "bz", scatter_dimension=0, tiled=True).astype(f32)

    query_grad, own_grad, other_grad, bias_grad = attend_back(
        order, place, low, high, query, own_kv, other_kv, mask, hot, kept, grad_attended
    )
    grad_project, grad_qkv_part, gain_grad = project_back(
        query_grad, own_grad, swap(other_grad, "core"), raw, cosine, sine, gains, normed_low
    )
    grad_qkv = lax.all_to_all(
        grad_qkv_part.reshape(devices, rows, 3 * HD), DEVICES, 0, 0, tiled=True
    )
    grad_qkv = jnp.sum(grad_qkv.reshape(H, 2 * sharers, rows, 3, HD).astype(f32), axis=1)
    grad_qkv = grad_qkv.transpose(1, 2, 0, 3).reshape(rows, 3 * D)
    qkv_full = lax.all_gather(
        by_head.transpose(0, 2, 1, 3).reshape(rows, 3 * D), DEVICES, axis=0, tiled=True
    )
    grad_rows = lax.all_to_all(
        grad_project.reshape(chips, BLOCK, 3 * HD), CHIPS, 0, 0, tiled=True
    ).reshape(H, sharers, BLOCK, 3 * HD)
    if sharers == 1:
        grad_rows = grad_rows[:, 0]
    else:
        grad_rows = jnp.sum(grad_rows.astype(f32), axis=1).astype(bf16)
    grad_rows = grad_rows.transpose(1, 0, 2).reshape(BLOCK, 3 * D)
    grad_normed = dot(grad_rows, qkv_full, ((1,), (1,)))
    grad_first, grad_attn_rows = norm_back(residual, attn_gain, grad_normed)
    grad_inputs = grad_middle + grad_first

    bias_part = jnp.where(
        jnp.arange(H)[None, :] == head, bias_grad[0, :2][:, None], jnp.zeros((2, H), f32)
    )
    squares = jnp.stack(
        [
            jnp.sum(residual * residual),
            jnp.sum(attn_branch * attn_branch),
            jnp.sum(ffn_branch * ffn_branch),
        ]
    )
    packed = jnp.concatenate(
        [
            jnp.sum(grad_attn_rows, axis=0),
            jnp.sum(grad_ffn_rows, axis=0),
            gain_grad[0],
            bias_part.reshape(-1),
            squares,
            jnp.zeros((93,), f32),
        ]
    )
    summed = sum_everywhere(packed, devices)
    at = 2 * D + 2 * HD
    root_means = jnp.sqrt(summed[at + 2 * H : at + 2 * H + 3] / (tokens * D))
    return (
        outputs,
        grad_inputs,
        grad_qkv,
        grad_out,
        grad_expand,
        grad_down.astype(f32),
        summed[:D],
        summed[D : 2 * D],
        summed[2 * D : 2 * D + HD],
        summed[2 * D + HD : at],
        summed[at : at + 2 * H].reshape(2, H),
        root_means,
    )


def solution(mesh):
    grid = mesh.devices if mesh.axis_names == ("head", "blk") else mesh.devices.T
    heads, blks = grid.shape
    mesh = Mesh(grid.reshape(heads // 2, 2, blks // 2, 2), ("hx", "core", "bz", "by"))
    split = P(DEVICES, None)
    return jax.shard_map(
        body,
        mesh=mesh,
        in_specs=(split,) * 2 + (P(),) * 5 + (split,) * 4 + (P(),) * 3,
        out_specs=(split,) * 6 + (P(),) * 6,
        check_vma=False,
    )
```

time: 1560 us -> 435 us (0.28)
  waiting for transfers between devices: 1100 us -> 127 us
  matrix products: 232 us -> 38.5 us
  Pallas kernels: 0 us -> 87 us
  blocking collectives: 58.4 us -> 0 us
  other arithmetic: 21 us -> 37 us
    reduce_scatter x4 -> x3, waiting for transfers between devices: 617 us -> 0.02 us  [the longest x1 0.02 us: body(): lax.psum_scatter(grad_down_part, 'bz', scatter_dimension=0, tiled=True)]
    dot_general x68 -> x10, matrix products: 232 us -> 38.5 us  [the longest x7 29.3 us: dot(): lax.dot_general(left, right, (dims, ((), ())), preferred_element_type=f32)]
    all_gather x6 -> x4, waiting for transfers between devices: 267 us -> 82.8 us  [the longest x1 66.6 us: body(): lax.all_gather(jnp.concatenate([inputs, out_weight], axis=0), DEVICES, ax...]
    ppermute x32 -> x27, waiting for transfers between devices: 188 us -> 21.4 us  [swap(): return lax.ppermute(shard, axis, [(0, 1), (1, 0)])]
    pallas_call x0 -> x4, Pallas kernels: none -> 87 us  [the longest x1 38.7 us: attend_back(): pl.pallas_call(attend_back_kernel, grid_spec=pltpu.PrefetchScalarGridSpec...]
    psum x1 -> x0, blocking collectives: 40.9 us -> none  [body(): lax.psum((grad_attn_gain, grad_ffn_gain, grad_query_gain, grad_key_gain,...]
    all_to_all x2 -> x0, blocking collectives: 17.6 us -> none  [the longest x1 9.06 us: body(): lax.all_to_all(project[:, 2 * D:].astype(jnp.bfloat16), 'head', split_axi...]
    all_to_all x6 -> x8, starting transfers between devices: 30.9 us -> 35.3 us  [the longest x1 6.24 us: body(): lax.all_to_all(to_heads, DEVICES, 0, 0, tiled=True).reshape(D, 3 * HD)]
  transfers between devices with their start and end apart: 48 -> 42, of which waited for: 40 -> 21; matrix products, arithmetic and copies ran while one was open for 17% -> 25% of each run, Pallas kernels for 0% -> 20%
where the time goes in v1:
time: 435 us; the launch traced here: 430 us
  waiting for transfers between devices  127 us (29%)
  Pallas kernels  87 us (20%)
  starting transfers between devices  69.2 us (16%)
  local copies, waits for them, and re-layouts  56.2 us (13%)
  matrix products  38.5 us (9%)
  other arithmetic  37 us (9%)
  between operations  14.9 us (3%)
    all_gather x1, waiting for transfers between devices, body(): lax.all_gather(jnp.concatenate([inputs, out_weight], axis=0), DEVICES, ax...  66.6 us
    pallas_call x1, Pallas kernels, attend_back(): pl.pallas_call(attend_back_kernel, grid_spec=pltpu.PrefetchScalarGridSpec...  38.7 us
    ppermute x27, starting transfers between devices, swap(): return lax.ppermute(shard, axis, [(0, 1), (1, 0)])  32.9 us
    dot_general x7, matrix products, dot(): lax.dot_general(left, right, (dims, ((), ())), preferred_element_type=f32)  29.3 us
    pallas_call x1, Pallas kernels, attend(): pl.pallas_call(attend_kernel, grid_spec=pltpu.PrefetchScalarGridSpec(num_...  24.6 us
    ppermute x27, waiting for transfers between devices, swap(): return lax.ppermute(shard, axis, [(0, 1), (1, 0)])  21.4 us
    unnamed x68, local copies, waits for them, and re-layouts  16.2 us
    all_gather x1, waiting for transfers between devices, body(): down_own = lax.all_gather(down_part, 'bz', axis=0, tiled=True)  16.2 us
  transfers between devices with their start and end apart: 42, of which 21 were waited for; matrix products, arithmetic and copies ran while one was open for 25% of the time, Pallas kernels for 20%

profile of v1, /device:TPU:0, one launch (start us, length us, event | category | flops | bytes accessed | tf_op | source)
XLA Modules:
  0.0 430.3 jit_solution(6593943581384818049)
XLA Ops:
  22.2 6.4 %select_convert_fusion.mask_ref = bf16[4096,128]{1,0:T(8,128)(2,1)} fusion(s32[128]{0:T(128)S(1)} %get-tuple-element.164, bf16[]{:T(256)} %bitcast.27, bf16[]{:T(256)} %bitcast.26, s32[128]{0:T(128)S(1)} %get-tuple-element.165, bf16[]{:T(256)} %bitcast.25, bf16[]{:T(256)} %bitcast.24, s32[128]{0:T(128)S(1)} %get-tuple-element.166, bf16[]{:T(256)} %bitcast.23, ...), kind=kLoop, calls=%fused_computation.10 | loop fusion | flops 6291456 | bytes 1083916 | tf_op jit(solution)/shard_map/convert_element_type | solution.py:491
  28.5 4.6 %fusion.6.hot_ref = bf16[4096,128]{1,0:T(8,128)(2,1)} fusion(s32[4096]{0:T(1024)S(1)} %get-tuple-element.126, s32[4096]{0:T(1024)S(1)} %get-tuple-element.125, s32[4096]{0:T(1024)S(1)} %get-tuple-element.124, s32[4096]{0:T(1024)S(1)} %get-tuple-element.128), kind=kLoop, calls=%fused_computation.18 | loop fusion | flops 4194304 | bytes 1114112 | tf_op jit(solution)/shard_map/convert_element_type | solution.py:475
  35.8 6.2 %all-to-all-start.1 = ((bf16[32,32,192]{2,1,0:T(8,128)(2,1)}), bf16[32,32,192]{2,1,0:T(8,128)(2,1)S(1)}, u32[]{:S(2)}, u32[]{:S(2)}) async-start(bf16[32,32,192]{2,1,0:T(8,128)(2,1)} %bitcast.8), calls=%async_computation.1 | async-start | bytes 1048576 | tf_op jit(solution)/shard_map/all_to_all | solution.py:536
  44.6 66.6 %all-gather.5.cloned.1.call-done = bf16[5120,1024]{1,0:T(8,128)(2,1)} async-done(((bf16[160,1024]{1,0:T(8,128)(2,1)}), bf16[5120,1024]{1,0:T(8,128)(2,1)}) %all-gather.5.cloned.1.call-update) | async-done | bytes 10485776 | tf_op jit(solution)/shard_map/all_gather | solution.py:528
  114.2 13.9 %project.1 = (bf16[2048,1024]{1,0:T(8,128)(2,1)}, f32[2048,128]{1,0:T(8,128)}, bf16[2048,128]{1,0:T(8,128)(2,1)}, bf16[2048,128]{1,0:T(8,128)(2,1)}) custom-call(s32[1]{0:T(128)} %bitcast.2.core_ref, bf16[16,2,160,1024]{3,2,1,0:T(8,128)(2,1)} %bitcast.98, f32[1,1024]{1,0:T(1,128)} %bitcast.130, bf16[1024,256]{1,0:T(8,128)(2,1)} %pad.10.weight_ref, ...), custom_call_target="tpu_custom_call" | custom-call | tf_op jit(solution)/shard_map/project/pallas_call | solution.py:145
  131.2 24.6 %attend.1 = (f32[2048,128]{1,0:T(8,128)}, bf16[2048,64]{1,0:T(8,128)(2,1)}) custom-call(s32[16]{0:T(128)} %get-tuple-element.59.order_ref, s32[32]{0:T(128)} %pad_add_fusion.2.place_ref, s32[8]{0:T(128)} %get-tuple-element.159.low_ref, s32[8]{0:T(128)} %get-tuple-element.158.high_ref, bf16[2048,128]{1,0:T(8,128)(2,1)} %get-tuple-element.29.query_ref, ...), custom_call_target="tpu_custom_call" | custom-call | tf_op jit(solution)/shard_map/attend/pallas_call | solution.py:255
  157.7 4.2 all-to-all-start.2
  194.5 6.7 %fusion.50 = f32[1024,1024]{1,0:T(8,128)} fusion(bf16[1024,1024]{1,0:T(8,128)(2,1)} %constant_dynamic-update-slice_fusion.5, bf16[1024,1024]{1,0:T(8,128)(2,1)} %all-gather.7.cloned.1.call-done), kind=kOutput, calls=%fused_computation.194 | convolution fusion | flops 2147483648 | bytes 8388608 | tf_op jit(solution)/shard_map/dot_general | solution.py:600
  201.2 16.2 %all-gather.9.cloned.1.call-done = bf16[512,1024]{1,0:T(8,128)(2,1)} async-done(((bf16[128,1024]{1,0:T(8,128)(2,1)}), bf16[512,1024]{1,0:T(8,128)(2,1)}) %all-gather.9.cloned.1.call-update) | async-done | bytes 1048592 | tf_op jit(solution)/shard_map/all_gather | solution.py:582
  217.4 6.4 %fusion.26 = (f32[1024,512]{1,0:T(8,128)S(1)}, f32[1024,512]{1,0:T(8,128)S(1)}, bf16[1024,512]{1,0:T(8,128)(2,1)}) fusion(f32[1024,1024]{1,0:T(8,128)} %fusion.50, bf16[1024,1024]{1,0:T(8,128)(2,1)} %constant_dynamic-update-slice_fusion.16, bf16[512,1024]{1,0:T(8,128)(2,1)} %all-gather.9.cloned.1.call-done), kind=kOutput, calls=%fused_computation.81 | convolution fusion | flops 1081081856 | bytes 12582912 | tf_op jit(solution)/shard_map/dot_general | solution.py:34
  225.8 5.3 %convolution_convert_fusion = bf16[1024,1024]{1,0:T(8,128)(2,1)} fusion(bf16[1024,1024]{1,0:T(8,128)(2,1)} %constant_dynamic-update-slice_fusion.5, f32[1024,512]{1,0:T(8,128)S(1)} %get-tuple-element.65, f32[1024,512]{1,0:T(8,128)S(1)} %get-tuple-element.64), kind=kOutput, calls=%fused_computation.19 | convolution fusion | flops 2150629376 | bytes 8388608 | tf_op jit(solution)/shard_map/dot_general | solution.py:34
  235.4 5.6 %convolution_convert_fusion.1 = bf16[1024,1024]{1,0:T(8,128)(2,1)S(1)} fusion(bf16[1024,1024]{1,0:T(8,128)(2,1)} %all-gather.7.cloned.1.call-done, f32[1024,512]{1,0:T(8,128)} %copy-done.28, f32[1024,512]{1,0:T(8,128)} %copy-done.27), kind=kOutput, calls=%fused_computation.20 | convolution fusion | flops 2150629376 | bytes 8388608 | tf_op jit(solution)/shard_map/dot_general | solution.py:34
  256.8 4.7 %collective-permute-done.20 = bf16[128,1024]{1,0:T(8,128)(2,1)S(1)} collective-permute-done((bf16[128,1024]{1,0:T(8,128)(2,1)S(1)}, bf16[128,1024]{1,0:T(8,128)(2,1)S(1)}, u32[]{:S(2)}, u32[]{:S(2)}) %collective-permute-start.20) | collective-permute-done | bytes 262176 | tf_op jit(solution)/shard_map/ppermute | solution.py:56
  269.0 4.7 %all-to-all-start.3 = ((bf16[16,128,64]{1,2,0:T(8,128)(2,1)}), bf16[16,128,64]{1,2,0:T(8,128)(2,1)S(1)}, u32[]{:S(2)}, u32[]{:S(2)}) async-start(bf16[16,128,64]{1,2,0:T(8,128)(2,1)} %bitcast.33), calls=%async_computation.3 | async-start | bytes 524288 | tf_op jit(solution)/shard_map/all_to_all | solution.py:615
  273.8 8.4 %all-to-all-done.3 = bf16[16,128,64]{1,2,0:T(8,128)(2,1)S(1)} async-done(((bf16[16,128,64]{1,2,0:T(8,128)(2,1)}), bf16[16,128,64]{1,2,0:T(8,128)(2,1)S(1)}, u32[]{:S(2)}, u32[]{:S(2)}) %all-to-all-start.3) | async-done | bytes 262176 | tf_op jit(solution)/shard_map/all_to_all | solution.py:615
  283.2 38.7 %attend_back.1 = (f32[2048,128]{1,0:T(8,128)}, f32[2048,128]{1,0:T(8,128)}, f32[2048,128]{1,0:T(8,128)}, f32[8,128]{1,0:T(8,128)}) custom-call(s32[16]{0:T(128)} %get-tuple-element.59.order_ref, s32[32]{0:T(128)} %pad_add_fusion.2.place_ref, s32[8]{0:T(128)} %get-tuple-element.159.low_ref, s32[8]{0:T(128)} %get-tuple-element.158.high_ref, ...), custom_call_target="tpu_custom_call" | custom-call | tf_op jit(solution)/shard_map/attend_back/pallas_call | solution.py:368
  327.2 9.7 %project_back.1 = (bf16[2048,192]{1,0:T(8,128)(2,1)}, bf16[1024,192]{1,0:T(8,128)(2,1)}, f32[8,128]{1,0:T(8,128)}) custom-call(f32[2048,128]{1,0:T(8,128)} %get-tuple-element.35.query_grad_ref, f32[2048,128]{1,0:T(8,128)} %get-tuple-element.36.own_ref, f32[2048,128]{1,0:T(8,128)} %collective-permute-done.21.other_ref, ...), custom_call_target="tpu_custom_call" | custom-call | tf_op jit(solution)/shard_map/project_back/pallas_call | solution.py:435
  336.9 3.8 all-to-all-start.5
  341.0 4.3 %convolution_convert_fusion.4 = bf16[512,1024]{1,0:T(8,128)(2,1)} fusion(bf16[1024,512]{1,0:T(8,128)(2,1)} %get-tuple-element.66, bf16[1024,1024]{1,0:T(8,128)(2,1)} %constant_dynamic-update-slice_fusion.16), kind=kOutput, calls=%fused_computation.23 | convolution fusion | flops 1074266112 | bytes 4194304 | tf_op jit(solution)/shard_map/dot_general | solution.py:34
  356.3 4.3 all-to-all-start.4
  368.7 5.2 %collective-permute-done.26 = bf16[128,1024]{1,0:T(8,128)(2,1)} collective-permute-done((bf16[128,1024]{1,0:T(8,128)(2,1)}, bf16[128,1024]{1,0:T(8,128)(2,1)}, u32[]{:S(2)}, u32[]{:S(2)}) %collective-permute-start.26) | collective-permute-done | bytes 262176 | tf_op jit(solution)/shard_map/ppermute | solution.py:56
  376.8 11.5 %all-to-all-done.4 = bf16[16,128,192]{1,2,0:T(8,128)(2,1)} async-done(((bf16[16,128,192]{1,2,0:T(8,128)(2,1)}), bf16[16,128,192]{1,2,0:T(8,128)(2,1)}, u32[]{:S(2)}, u32[]{:S(2)}) %all-to-all-start.4) | async-done | bytes 786464 | tf_op jit(solution)/shard_map/all_to_all | solution.py:655
  391.8 6.1 %fusion.15 = (f32[1024]{0:T(1024)S(1)}, f32[128]{0:T(128)S(1)}, f32[128,1024]{1,0:T(8,128)}) fusion(bf16[128,1024]{1,0:T(8,128)(2,1)S(1)} %copy-done.2, f32[128]{0:T(128)S(1)} %get-tuple-element.141, f32[1024]{0:T(1024)S(1)} %copy-done.18, bf16[128,3072]{0,1:T(8,128)(2,1)} %bitcast.37, bf16[1024,3072]{1,0:T(8,128)(2,1)} %all-gather.11.cloned.1.call-done), kind=kOutput, calls=%fused_computation.40 | convolution fusion | flops 806222720 | bytes 7873536 | tf_op jit(solution)/shard_map/dot_general | solution.py:34
  402.4 5.0 %all-to-all-start.7 = ((f32[32,1,2304]{2,1,0:T(1,128)}), f32[32,1,2304]{2,1,0:T(1,128)}, u32[]{:S(2)}, u32[]{:S(2)}) async-start(f32[32,1,2304]{2,1,0:T(1,128)} %broadcast_in_dim.184), calls=%async_computation.10 | async-start | bytes 589824 | tf_op jit(solution)/shard_map/all_to_all | solution.py:496
  (259 shorter events, 142.1 us)
Async XLA Ops:
  7.2 104.0 %all-gather.5.cloned.1.call-start = ((), (), s32[]{:S(2)}) async-start(), calls=%async_computation.11 | async-start | bytes 10813440 | tf_op jit(solution)/shard_map/all_gather | solution.py:528
  9.0 156.5 %collective-permute-start.11 = (bf16[128,1024]{1,0:T(8,128)(2,1)}, bf16[128,1024]{1,0:T(8,128)(2,1)S(1)}, u32[]{:S(2)}, u32[]{:S(2)}) collective-permute-start(bf16[128,1024]{1,0:T(8,128)(2,1)} %param.15), channel_id=1, source_target_pairs={{0,16},{16,0},{1,17},{17,1},{2,18},{18,2},{3,19},{19,3},{4,20},{20... | collective-permute-start | bytes 786440 | tf_op jit(solution)/shard_map/ppermute | solution.py:56
  12.0 150.8 %collective-permute-start.12 = (bf16[128,1024]{1,0:T(8,128)(2,1)}, bf16[128,1024]{1,0:T(8,128)(2,1)S(1)}, u32[]{:S(2)}, u32[]{:S(2)}) collective-permute-start(bf16[128,1024]{1,0:T(8,128)(2,1)} %param.15), channel_id=1, source_target_pairs={{0,1},{1,0},{2,3},{3,2},{4,5},{5,4},{6,7},{7,6},{8,9},{9,8},{10,11... | collective-permute-start | bytes 786440 | tf_op jit(solution)/shard_map/ppermute | solution.py:56
  16.1 18.8 %all-to-all-start = ((bf16[8,32,1024]{2,1,0:T(8,128)(2,1)}), bf16[8,32,1024]{2,1,0:T(8,128)(2,1)S(1)}, u32[]{:S(2)}, u32[]{:S(2)}) async-start(bf16[8,32,1024]{2,1,0:T(8,128)(2,1)} %reshape.433), calls=%async_computation | async-start | bytes 1048576 | tf_op jit(solution)/shard_map/all_to_all | solution.py:543
  35.8 77.5 %all-to-all-start.1 = ((bf16[32,32,192]{2,1,0:T(8,128)(2,1)}), bf16[32,32,192]{2,1,0:T(8,128)(2,1)S(1)}, u32[]{:S(2)}, u32[]{:S(2)}) async-start(bf16[32,32,192]{2,1,0:T(8,128)(2,1)} %bitcast.8), calls=%async_computation.1 | async-start | bytes 1048576 | tf_op jit(solution)/shard_map/all_to_all | solution.py:536
  42.1 152.4 %all-gather.7.cloned.1.call-start = ((), (), s32[]{:S(2)}) async-start(), calls=%async_computation.12 | async-start | bytes 2621440 | tf_op jit(solution)/shard_map/all_gather | solution.py:581
  157.7 13.5 %all-to-all-start.2 = ((bf16[16,128,64]{1,2,0:T(8,128)(2,1)}), bf16[16,128,64]{1,2,0:T(8,128)(2,1)S(1)}, u32[]{:S(2)}, u32[]{:S(2)}) async-start(bf16[16,128,64]{1,2,0:T(8,128)(2,1)} %copy.82), calls=%async_computation.2 | async-start | bytes 524288 | tf_op jit(solution)/shard_map/all_to_all | solution.py:590
  161.9 55.5 %all-gather.9.cloned.1.call-start = ((), (), s32[]{:S(2)}) async-start(), calls=%async_computation.13 | async-start | bytes 1310720 | tf_op jit(solution)/shard_map/all_gather | solution.py:582
  163.5 10.5 %collective-permute-start.13 = (bf16[64,1024]{1,0:T(8,128)(2,1)}, bf16[64,1024]{1,0:T(8,128)(2,1)}, u32[]{:S(2)}, u32[]{:S(2)}) collective-permute-start(bf16[64,1024]{1,0:T(8,128)(2,1)} %slice.253), channel_id=1, source_target_pairs={{0,16},{16,0},{1,17},{17,1},{2,18},{18,2},{3,19},{19,3},{4,20},{20... | collective-permute-start | bytes 393224 | tf_op jit(solution)/shard_map/ppermute | solution.py:56
  176.5 13.4 %collective-permute-start.15 = (bf16[512,1024]{1,0:T(8,128)(2,1)}, bf16[512,1024]{1,0:T(8,128)(2,1)}, u32[]{:S(2)}, u32[]{:S(2)}) collective-permute-start(bf16[512,1024]{1,0:T(8,128)(2,1)} %get-tuple-element.115), channel_id=1, source_target_pairs={{0,8},{8,0},{1,9},{9,1},{2,10},{10,2},{3,11},{11,3},{4,12},{12,4},... | collective-permute-start | bytes 3145736 | tf_op jit(solution)/shard_map/ppermute | solution.py:56
  189.7 187.1 %reduce-scatter.6.cloned.1.call-start = ((), (), s32[]{:S(2)}) async-start(), calls=%async_computation.16 | async-start | bytes 2621440 | tf_op jit(solution)/shard_map/reduce_scatter | solution.py:620
  231.1 160.7 %all-gather.11.cloned.1.call-start = ((), (), s32[]{:S(2)}) async-start(), calls=%async_computation.14 | async-start | bytes 6488064 | tf_op jit(solution)/shard_map/all_gather | solution.py:652
  254.8 10.3 %collective-permute-start.10 = (bf16[128,1024]{1,0:T(8,128)(2,1)S(1)}, bf16[128,1024]{1,0:T(8,128)(2,1)S(1)}, u32[]{:S(2)}, u32[]{:S(2)}) collective-permute-start(bf16[128,1024]{1,0:T(8,128)(2,1)S(1)} %pad_maximum_fusion.4), channel_id=1, source_target_pairs={{0,1},{1,0},{2,3},{3,2},{4,5},{5,4},{6,7},{7,6},{8,9},{9,8},{10,11... | collective-permute-start | bytes 786440 | tf_op jit(solution)/shard_map/ppermute | solution.py:56
  269.0 13.2 %all-to-all-start.3 = ((bf16[16,128,64]{1,2,0:T(8,128)(2,1)}), bf16[16,128,64]{1,2,0:T(8,128)(2,1)S(1)}, u32[]{:S(2)}, u32[]{:S(2)}) async-start(bf16[16,128,64]{1,2,0:T(8,128)(2,1)} %bitcast.33), calls=%async_computation.3 | async-start | bytes 524288 | tf_op jit(solution)/shard_map/all_to_all | solution.py:615
  326.3 19.1 %collective-permute-start.22 = (bf16[512,1024]{1,0:T(8,128)(2,1)S(1)}, bf16[512,1024]{1,0:T(8,128)(2,1)S(1)}, u32[]{:S(2)}, u32[]{:S(2)}) collective-permute-start(bf16[512,1024]{1,0:T(8,128)(2,1)S(1)} %pad_maximum_fusion), channel_id=1, source_target_pairs={{0,8},{8,0},{1,9},{9,1},{2,10},{10,2},{3,11},{11,3},{4,12},{12,4},... | collective-permute-start | bytes 3145736 | tf_op jit(solution)/shard_map/ppermute | solution.py:56
  336.9 19.4 %all-to-all-start.5 = ((bf16[32,32,192]{2,1,0:T(8,128)(2,1)}), bf16[32,32,192]{2,1,0:T(8,128)(2,1)S(1)}, u32[]{:S(2)}, u32[]{:S(2)}) async-start(bf16[32,32,192]{2,1,0:T(8,128)(2,1)} %bitcast.127), calls=%async_computation.5 | async-start | bytes 1048576 | tf_op jit(solution)/shard_map/all_to_all | solution.py:647
  340.7 66.7 %reduce-scatter.8.cloned.1.call-start = ((), (), s32[]{:S(2)}) async-start(), calls=%async_computation.17 | async-start | bytes 1310720 | tf_op jit(solution)/shard_map/reduce_scatter | solution.py:619
  349.1 12.1 %collective-permute-start.23 = (bf16[64,1024]{1,0:T(8,128)(2,1)}, bf16[64,1024]{1,0:T(8,128)(2,1)}, u32[]{:S(2)}, u32[]{:S(2)}) collective-permute-start(bf16[64,1024]{1,0:T(8,128)(2,1)} %get-tuple-element.92), channel_id=1, source_target_pairs={{0,1},{1,0},{2,3},{3,2},{4,5},{5,4},{6,7},{7,6},{8,9},{9,8},{10,11... | collective-permute-start | bytes 393224 | tf_op jit(solution)/shard_map/ppermute | solution.py:56
  350.9 10.3 %collective-permute-start.25 = (bf16[64,1024]{1,0:T(8,128)(2,1)}, bf16[64,1024]{1,0:T(8,128)(2,1)}, u32[]{:S(2)}, u32[]{:S(2)}) collective-permute-start(bf16[64,1024]{1,0:T(8,128)(2,1)} %get-tuple-element.91), channel_id=1, source_target_pairs={{0,16},{16,0},{1,17},{17,1},{2,18},{18,2},{3,19},{19,3},{4,20},{20... | collective-permute-start | bytes 393224 | tf_op jit(solution)/shard_map/ppermute | solution.py:56
  356.3 32.0 %all-to-all-start.4 = ((bf16[16,128,192]{1,2,0:T(8,128)(2,1)}), bf16[16,128,192]{1,2,0:T(8,128)(2,1)}, u32[]{:S(2)}, u32[]{:S(2)}) async-start(bf16[16,128,192]{1,2,0:T(8,128)(2,1)} %copy.87), calls=%async_computation.4 | async-start | bytes 1572864 | tf_op jit(solution)/shard_map/all_to_all | solution.py:655
  360.6 48.6 %reduce-scatter.4.cloned.1.call-start = ((), (), s32[]{:S(2)}) async-start(), calls=%async_computation.15 | async-start | bytes 327680 | tf_op jit(solution)/shard_map/reduce_scatter | solution.py:639
  363.9 9.9 %collective-permute-start.26 = (bf16[128,1024]{1,0:T(8,128)(2,1)}, bf16[128,1024]{1,0:T(8,128)(2,1)}, u32[]{:S(2)}, u32[]{:S(2)}) collective-permute-start(bf16[128,1024]{1,0:T(8,128)(2,1)} %pad_maximum_fusion.8), channel_id=1, source_target_pairs={{0,1},{1,0},{2,3},{3,2},{4,5},{5,4},{6,7},{7,6},{8,9},{9,8},{10,11... | collective-permute-start | bytes 786440 | tf_op jit(solution)/shard_map/ppermute | solution.py:56
  388.3 13.1 %all-to-all-start.6 = ((bf16[8,32,1024]{2,1,0:T(8,128)(2,1)}), bf16[8,32,1024]{2,1,0:T(8,128)(2,1)S(1)}, u32[]{:S(2)}, u32[]{:S(2)}) async-start(bf16[8,32,1024]{2,1,0:T(8,128)(2,1)} %bitcast.126), calls=%async_computation.8 | async-start | bytes 1048576 | tf_op jit(solution)/shard_map/all_to_all | solution.py:622
  402.4 17.5 %all-to-all-start.7 = ((f32[32,1,2304]{2,1,0:T(1,128)}), f32[32,1,2304]{2,1,0:T(1,128)}, u32[]{:S(2)}, u32[]{:S(2)}) async-start(f32[32,1,2304]{2,1,0:T(1,128)} %broadcast_in_dim.184), calls=%async_computation.10 | async-start | bytes 589824 | tf_op jit(solution)/shard_map/all_to_all | solution.py:496
  (47 other events, 355.7 us)
Sparse Core Ops, SparseCore 0:
  11.4 99.6 all-gather.4
  112.7 44.1 all-gather.6
  189.8 27.5 all-gather.8
  231.3 43.0 reduce-scatter.5
  277.0 68.4 all-gather.10
  347.7 35.8 reduce-scatter.7
  386.5 20.5 reduce-scatter.3

commit v2 on v1

--- a/solution.py
+++ b/solution.py
@@ -47,30 +47,44 @@
     return grad_values, grad * values * factor
 
 
-def swiglu(expand):
-    half = expand.shape[1] // 2
-    return jax.nn.silu(expand[:, :half]) * expand[:, half:]
-
-
 def swap(shard, axis):
     return lax.ppermute(shard, axis, [(0, 1), (1, 0)])
 
 
 def plane_gather(shard):
+    mine = jnp.concatenate(quarters(shard), axis=0)
+    return mine, swap(mine, "core")
+
+
+def chip_gather(shard):
+    depth = lax.axis_size("bz")
+    chips = depth * 4
+    z, y, x = lax.axis_index("bz"), lax.axis_index("by"), lax.axis_index("hx")
+    at = jnp.arange(chips, dtype=jnp.int32)
+    if depth > 4:
+        return lax.all_gather(shard, CHIPS, axis=0, tiled=True).reshape(chips, BLOCK, D), at
+    shifted = [
+        lax.ppermute(shard, "bz", [(i, (i + by) % depth) for i in range(depth)])
+        for by in range(1, depth)
+    ]
+    pieces = quarters(shard) + quarters(jnp.concatenate(shifted, axis=0))
+    back = (z - at // 4) % depth
+    flips = ((at % 2) ^ x) + 2 * (((at // 2) % 2) ^ y)
+    where = jnp.where(back == 0, flips, 4 + flips * (depth - 1) + back - 1)
+    return jnp.concatenate(pieces, axis=0).reshape(chips, BLOCK, D), where.astype(jnp.int32)
+
+
+def quarters(shard):
     half = shard.shape[0] // 2
     across_x = swap(shard, "hx")
     across_y = swap(shard, "by")
-    corner_a = swap(across_y[:half], "hx")
-    corner_b = swap(across_x[half:], "by")
-    mine = jnp.concatenate([shard, across_x, across_y, corner_a, corner_b], axis=0)
-    return jnp.concatenate([mine, swap(mine, "core")], axis=0)
-
-
-def plane_scatter(partial_low):
-    rows = partial_low.shape[0] // 8
+    return [shard, across_x, across_y, swap(across_y[:half], "hx"), swap(across_x[half:], "by")]
+
+
+def plane_scatter(mine, other):
+    rows = mine.shape[0] // 4
     half = rows // 2
-    other = swap(partial_low[4 * rows :], "core")
-    mine = partial_low[: 4 * rows].astype(f32) + other.astype(f32)
+    mine = mine.astype(f32) + swap(other, "core").astype(f32)
     corner = mine[3 * rows :].astype(bf16)
     for_y = swap(corner[:half], "hx").astype(f32)
     for_x = swap(corner[half:], "by").astype(f32)
@@ -109,7 +123,7 @@
 
 
 def project_kernel(
-    core_ref,
+    where_ref,
     x_ref,
     gain_ref,
     weight_ref,
@@ -122,7 +136,7 @@
     query_ref,
     kv_ref,
 ):
-    x = x_ref[0, 0].astype(f32)
+    x = x_ref[0].astype(f32)
     normed = norm_rows(x, gain_ref[...]).astype(bf16)
     normed_ref[...] = normed
     project = dot(normed, weight_ref[...], ((1,), (0,)))
@@ -137,18 +151,18 @@
     kv_ref[...] = jnp.where(lane < HD, value, turned * HD ** (-0.5)).astype(bf16)
 
 
-def project(core, gathered, gain, weight, cosine, sine, gains, hot):
+def project(where, gathered, gain, weight, cosine, sine, gains, hot):
     blocks = gathered.shape[0]
     rows = blocks * BLOCK
-    row_spec = lambda width: pl.BlockSpec((BLOCK, width), lambda j, core: (j, 0))
-    whole = lambda array: pl.BlockSpec(array.shape, lambda j, core: (0, 0))
+    row_spec = lambda width: pl.BlockSpec((BLOCK, width), lambda j, where: (j, 0))
+    whole = lambda array: pl.BlockSpec(array.shape, lambda j, where: (0, 0))
     return pl.pallas_call(
         project_kernel,
         grid_spec=pltpu.PrefetchScalarGridSpec(
             num_scalar_prefetch=1,
             grid=(blocks,),
             in_specs=[
-                pl.BlockSpec((1, 1, BLOCK, D), lambda j, core: (j, core[0], 0, 0)),
+                pl.BlockSpec((1, BLOCK, D), lambda j, where: (where[j], 0, 0)),
                 whole(gain),
                 whole(weight),
                 row_spec(128),
@@ -165,7 +179,7 @@
             jax.ShapeDtypeStruct((rows, 128), bf16),
         ],
         name="project",
-    )(core, gathered, gain, weight, cosine, sine, gains, hot)
+    )(where, gathered, gain, weight, cosine, sine, gains, hot)
 
 
 def sort_keys(place_ref, own_ref, other_ref, mask_ref, key_ref, value_ref):
@@ -445,6 +459,98 @@
         scratch_shapes=[pltpu.VMEM((D, 4 * HD), f32), pltpu.VMEM((1, 128), f32)],
         name="project_back",
     )(query_grad, own, other, raw, cosine, sine, gains, normed)
+
+
+def feed_kernel(
+    second_mine_ref,
+    second_other_ref,
+    grad_mine_ref,
+    grad_other_ref,
+    weight_ref,
+    ffn_mine_ref,
+    ffn_other_ref,
+    back_mine_ref,
+    back_other_ref,
+    weight_grad_ref,
+    expand_ref,
+    down_ref,
+    expand_grad_ref,
+    down_grad_ref,
+):
+    step = pl.program_id(0)
+    half = pl.num_programs(0) // 2
+    depth, both_rows, width = weight_ref.shape
+    down_rows = down_ref.shape[0] // depth
+    expand_rows = both_rows - down_rows
+
+    @pl.when(step == 0)
+    def _():
+        for z in range(depth):
+            expand_ref[z * expand_rows : (z + 1) * expand_rows] = weight_ref[z, :expand_rows]
+            down_ref[z * down_rows : (z + 1) * down_rows] = weight_ref[z, expand_rows:]
+        expand_grad_ref[...] = jnp.zeros_like(expand_grad_ref)
+        down_grad_ref[...] = jnp.zeros_like(down_grad_ref)
+
+    second = jnp.where(step < half, second_mine_ref[...], second_other_ref[...])
+    grad = jnp.where(step < half, grad_mine_ref[...], grad_other_ref[...])
+    expand = dot(second, expand_ref[...], ((1,), (0,)))
+    gate = expand[:, : width // 2]
+    up = expand[:, width // 2 :]
+    sigmoid = 1.0 / (1.0 + jnp.exp(-gate))
+    silu = gate * sigmoid
+    hidden = (silu * up).astype(bf16)
+    grad_hidden = dot(grad, down_ref[...], ((1,), (1,)))
+    grad_gate = grad_hidden * up * (sigmoid * (1.0 + gate * (1.0 - sigmoid)))
+    rows = jnp.concatenate([grad_gate, grad_hidden * silu], axis=1).astype(bf16)
+    ffn = dot(hidden, down_ref[...], ((1,), (0,))).astype(bf16)
+    back = dot(rows, expand_ref[...], ((1,), (1,))).astype(bf16)
+    expand_grad_ref[...] += dot(second, rows, ((0,), (0,)))
+    down_grad_ref[...] += dot(hidden, grad, ((0,), (0,)))
+
+    @pl.when(step < half)
+    def _():
+        ffn_mine_ref[...] = ffn
+        back_mine_ref[...] = back
+
+    @pl.when(step >= half)
+    def _():
+        ffn_other_ref[...] = ffn
+        back_other_ref[...] = back
+
+    @pl.when(step == pl.num_programs(0) - 1)
+    def _():
+        for z in range(depth):
+            weight_grad_ref[z, :expand_rows] = expand_grad_ref[
+                z * expand_rows : (z + 1) * expand_rows
+            ].astype(bf16)
+            weight_grad_ref[z, expand_rows:] = down_grad_ref[
+                z * down_rows : (z + 1) * down_rows
+            ].astype(bf16)
+
+
+def feed(second, grad, weight, down_rows):
+    rows = second[0].shape[0]
+    tile = 256
+    steps = rows // tile
+    depth, both_rows, width = weight.shape
+    mine = pl.BlockSpec((tile, D), lambda i: (jnp.minimum(i, steps - 1), 0))
+    other = pl.BlockSpec((tile, D), lambda i: (jnp.maximum(i - steps, 0), 0))
+    whole = pl.BlockSpec(weight.shape, lambda i: (0, 0, 0), pipeline_mode=pl.Buffered(1))
+    token_rows = jax.ShapeDtypeStruct((rows, D), bf16)
+    return pl.pallas_call(
+        feed_kernel,
+        grid=(2 * steps,),
+        in_specs=[mine, other, mine, other, whole],
+        out_specs=[mine, other, mine, other, whole],
+        out_shape=[token_rows] * 4 + [jax.ShapeDtypeStruct(weight.shape, bf16)],
+        scratch_shapes=[
+            pltpu.VMEM((depth * (both_rows - down_rows), width), bf16),
+            pltpu.VMEM((depth * down_rows, D), bf16),
+            pltpu.VMEM((depth * (both_rows - down_rows), width), f32),
+            pltpu.VMEM((depth * down_rows, D), f32),
+        ],
+        name="feed",
+    )(*second, *grad, weight)
 
 
 def token_meta(seq_lengths, block_order):
@@ -525,9 +631,8 @@
     segments = seq_lengths.shape[0] + 1
     tokens = variate_ids.shape[0]
 
-    gathered = lax.all_gather(
-        jnp.concatenate([inputs, out_weight], axis=0), DEVICES, axis=0, tiled=True
-    ).reshape(chips, 2, BLOCK + rows, D)
+    gathered, where = chip_gather(inputs)
+    out_full = lax.all_gather(out_weight, DEVICES, axis=0, tiled=True)
 
     by_head = qkv_weight.reshape(rows, 3, H, HD)
     to_heads = jnp.repeat(
@@ -541,7 +646,6 @@
         .reshape(8, rows, 2 * depth * hidden_rows)
     )
     expand_part = lax.all_to_all(to_plane, PLANE, 0, 0, tiled=True).reshape(8 * rows, -1)
-    cotangent_plane = plane_gather(cotangent)
 
     segment, position, ends = token_meta(seq_lengths, block_order)
     own_segment, other_segment = both_cores(segment, core)
@@ -575,15 +679,15 @@
     high = (finish + KEY_TILE - 1) // KEY_TILE
     gains = jnp.concatenate([query_gain, key_gain])[None, :]
 
-    gathered, expand_part, down_part = lax.optimization_barrier(
-        (gathered, expand_part, down_weight)
-    )
-    expand_own = lax.all_gather(expand_part, "bz", axis=0, tiled=True)
-    down_own = lax.all_gather(down_part, "bz", axis=0, tiled=True)
-    out_full = gathered[:, :, BLOCK:, :].reshape(D, D)
+    feed_part = jnp.concatenate([expand_part, down_weight], axis=0)
+    gathered, late_cotangent, out_full, feed_part = lax.optimization_barrier(
+        (gathered, cotangent, out_full, feed_part)
+    )
+    feed_own = lax.all_gather(feed_part[None], "bz", axis=0, tiled=True)
+    cotangent_plane = plane_gather(late_cotangent)
 
     normed_low, raw, query, own_kv = project(
-        core[None], gathered, attn_gain[None], own_qkv, cosine, sine, gains, hot
+        where, gathered, attn_gain[None], own_qkv, cosine, sine, gains, hot
     )
     other_kv = swap(own_kv, "core")
     kept, attended = attend(order, place, low, high, query, own_kv, other_kv, mask)
@@ -597,16 +701,10 @@
     middle = residual + attn_branch
     second_low = plane_gather(norm_rows(middle, ffn_gain).astype(bf16))
 
-    expand = jnp.dot(second_low, expand_own, preferred_element_type=f32)
-    hidden, swiglu_back = jax.vjp(swiglu, expand)
-    hidden_low = hidden.astype(bf16)
-    ffn_part = jnp.dot(hidden_low, down_own, preferred_element_type=f32).astype(bf16)
-    grad_hidden = dot(cotangent_plane, down_own, ((1,), (1,)))
-    grad_down_part = dot(hidden_low, cotangent_plane, ((0,), (0,))).astype(bf16)
-    grad_expand_rows = swiglu_back(grad_hidden)[0].astype(bf16)
-    grad_second_part = dot(grad_expand_rows, expand_own, ((1,), (1,))).astype(bf16)
-    grad_expand_part = dot(second_low, grad_expand_rows, ((0,), (0,))).astype(bf16)
-    grad_second = plane_scatter(grad_second_part)
+    ffn_mine, ffn_other, back_mine, back_other, feed_grad = feed(
+        second_low, cotangent_plane, feed_own, hidden_rows
+    )
+    grad_second = plane_scatter(back_mine, back_other)
     grad_middle, grad_ffn_rows = norm_back(middle, ffn_gain, grad_second)
     grad_middle = cotangent.astype(f32) + grad_middle
     branch_grad = grad_middle.astype(bf16)
@@ -614,12 +712,12 @@
     to_chips = jnp.repeat(grad_merged.reshape(BLOCK, H, HD).transpose(1, 0, 2), sharers, axis=0)
     grad_attended = lax.all_to_all(to_chips, CHIPS, 0, 0, tiled=True).reshape(-1, HD)
 
-    ffn_branch = plane_scatter(ffn_part)
+    ffn_branch = plane_scatter(ffn_mine, ffn_other)
     outputs = (middle + ffn_branch).astype(bf16)
-    grad_down = lax.psum_scatter(grad_down_part, "bz", scatter_dimension=0, tiled=True)
-    grad_expand = lax.psum_scatter(grad_expand_part, "bz", scatter_dimension=0, tiled=True)
+    feed_grad = lax.psum_scatter(feed_grad, "bz", scatter_dimension=0, tiled=True)[0]
+    grad_down = feed_grad[8 * rows :].astype(f32)
     grad_expand = (
-        lax.all_to_all(grad_expand.reshape(8, rows, -1), PLANE, 0, 0, tiled=True)
+        lax.all_to_all(feed_grad[: 8 * rows].reshape(8, rows, -1), PLANE, 0, 0, tiled=True)
         .reshape(8, rows, 2, depth, hidden_rows)
         .transpose(1, 2, 3, 0, 4)
         .reshape(rows, -1)
@@ -635,7 +733,9 @@
         ],
         axis=0,
     )
-    grad_out_part = plane_scatter(grad_out_rows).astype(bf16)
+    middle_row = grad_out_rows.shape[0] // 2
+    grad_out_part = plane_scatter(grad_out_rows[:middle_row], grad_out_rows[middle_row:])
+    grad_out_part = grad_out_part.astype(bf16)
     grad_out = lax.psum_scatter(grad_out_part, "bz", scatter_dimension=0, tiled=True).astype(f32)
 
     query_grad, own_grad, other_grad, bias_grad = attend_back(
@@ -644,17 +744,18 @@
     grad_project, grad_qkv_part, gain_grad = project_back(
         query_grad, own_grad, swap(other_grad, "core"), raw, cosine, sine, gains, normed_low
     )
-    grad_qkv = lax.all_to_all(
-        grad_qkv_part.reshape(devices, rows, 3 * HD), DEVICES, 0, 0, tiled=True
-    )
-    grad_qkv = jnp.sum(grad_qkv.reshape(H, 2 * sharers, rows, 3, HD).astype(f32), axis=1)
-    grad_qkv = grad_qkv.transpose(1, 2, 0, 3).reshape(rows, 3 * D)
     qkv_full = lax.all_gather(
         by_head.transpose(0, 2, 1, 3).reshape(rows, 3 * D), DEVICES, axis=0, tiled=True
     )
     grad_rows = lax.all_to_all(
         grad_project.reshape(chips, BLOCK, 3 * HD), CHIPS, 0, 0, tiled=True
     ).reshape(H, sharers, BLOCK, 3 * HD)
+    grad_rows, grad_qkv_part = lax.optimization_barrier((grad_rows, grad_qkv_part))
+    grad_qkv = lax.all_to_all(
+        grad_qkv_part.reshape(devices, rows, 3 * HD), DEVICES, 0, 0, tiled=True
+    )
+    grad_qkv = jnp.sum(grad_qkv.reshape(H, 2 * sharers, rows, 3, HD).astype(f32), axis=1)
+    grad_qkv = grad_qkv.transpose(1, 2, 0, 3).reshape(rows, 3 * D)
     if sharers == 1:
         grad_rows = grad_rows[:, 0]
     else:
@@ -693,7 +794,7 @@
         grad_qkv,
         grad_out,
         grad_expand,
-        grad_down.astype(f32),
+        grad_down,
         summed[:D],
         summed[D : 2 * D],
         summed[2 * D : 2 * D + HD],

time: 435 us -> 437 us (level); the launches traced: 430 us -> 437 us
  matrix products: 38.5 us -> 7.89 us
  Pallas kernels: 87 us -> 112 us
  blocking collectives: 0 us -> 15.7 us
  waiting for transfers between devices: 127 us -> 138 us
  local copies, waits for them, and re-layouts: 56.2 us -> 49.7 us
  other arithmetic: 37 us -> 30.9 us
    all_gather x3 -> x2, waiting for transfers between devices: 82.8 us -> 1.11 us  [the longest x1 1.11 us: body(): out_full = lax.all_gather(out_weight, DEVICES, axis=0, tiled=True)]
    ppermute x27 -> x35, waiting for transfers between devices: 21.4 us -> 71.4 us  [swap(): return lax.ppermute(shard, axis, [(0, 1), (1, 0)])]
    dot_general x7 -> x3, matrix products: 29.3 us -> 6.65 us  [dot(): lax.dot_general(left, right, (dims, ((), ())), preferred_element_type=f32)]
    pallas_call x0 -> x1, Pallas kernels: none -> 18.5 us  [feed(): pl.pallas_call(feed_kernel, grid=(2 * steps,), in_specs=[mine, other, min...]
    all_to_all x0 -> x1, blocking collectives: none -> 15.7 us  [body(): lax.all_to_all(to_chips, CHIPS, 0, 0, tiled=True).reshape(-1, HD)]
    all_to_all x1, waiting for transfers between devices: 0.01 us -> 9.86 us  [sum_everywhere(): return jnp.sum(lax.all_to_all(copies, DEVICES, 0, 0, tiled=True), axis=0)]
    all_to_all x1, waiting for transfers between devices: 1.64 us -> 10.6 us  [body(): lax.all_to_all(grad_qkv_part.reshape(devices, rows, 3 * HD), DEVICES, 0,...]
    dot_general x2 -> x0, matrix products: 7.91 us -> none  [the longest x1 6.66 us: body(): expand = jnp.dot(second_low, expand_own, preferred_element_type=f32)]
  transfers between devices with their start and end apart: 42 -> 50, of which waited for: 21 -> 34; matrix products, arithmetic and copies ran while one was open for 25% -> 19% of each run, Pallas kernels for 20% -> 26%
where the time goes in v2:
time: 437 us
  waiting for transfers between devices  138 us (32%)
  Pallas kernels  112 us (26%)
  starting transfers between devices  68.5 us (16%)
  local copies, waits for them, and re-layouts  49.7 us (11%)
  other arithmetic  30.9 us (7%)
  blocking collectives  15.7 us (4%)
  between operations  14.5 us (3%)
  matrix products  7.89 us (2%)
    ppermute x35, waiting for transfers between devices, swap(): return lax.ppermute(shard, axis, [(0, 1), (1, 0)])  71.4 us
    pallas_call x1, Pallas kernels, attend_back(): pl.pallas_call(attend_back_kernel, grid_spec=pltpu.PrefetchScalarGridSpec...  41.8 us
    ppermute x35, starting transfers between devices, swap(): return lax.ppermute(shard, axis, [(0, 1), (1, 0)])  33.1 us
    pallas_call x1, Pallas kernels, attend(): pl.pallas_call(attend_kernel, grid_spec=pltpu.PrefetchScalarGridSpec(num_...  27 us
    pallas_call x1, Pallas kernels, feed(): pl.pallas_call(feed_kernel, grid=(2 * steps,), in_specs=[mine, other, min...  18.5 us
    all_to_all x1, waiting for transfers between devices, body(): lax.all_to_all(grad_project.reshape(chips, BLOCK, 3 * HD), CHIPS, 0, 0, t...  18.5 us
    unnamed x63, local copies, waits for them, and re-layouts  16.2 us
    all_to_all x1, blocking collectives, body(): lax.all_to_all(to_chips, CHIPS, 0, 0, tiled=True).reshape(-1, HD)  15.7 us
  transfers between devices with their start and end apart: 50, of which 34 were waited for; matrix products, arithmetic and copies ran while one was open for 19% of the time, Pallas kernels for 26%

profile of v2, /device:TPU:0, one launch (start us, length us, event | category | flops | bytes accessed | tf_op | source)
XLA Modules:
  0.0 437.3 jit_solution(4644056180252413829)
XLA Ops:
  27.3 7.1 %collective-permute-done.5 = bf16[128,1024]{1,0:T(8,128)(2,1)S(1)} collective-permute-done((bf16[128,1024]{1,0:T(8,128)(2,1)}, bf16[128,1024]{1,0:T(8,128)(2,1)S(1)}, u32[]{:S(2)}, u32[]{:S(2)}) %collective-permute-start.5) | collective-permute-done | bytes 262176 | tf_op jit(solution)/shard_map/ppermute | solution.py:67
  42.5 15.3 %collective-permute-done.8 = bf16[384,1024]{1,0:T(8,128)(2,1)S(1)} collective-permute-done((bf16[384,1024]{1,0:T(8,128)(2,1)}, bf16[384,1024]{1,0:T(8,128)(2,1)S(1)}, u32[]{:S(2)}, u32[]{:S(2)}) %collective-permute-start.8) | collective-permute-done | bytes 786464 | tf_op jit(solution)/shard_map/ppermute | solution.py:51
  61.4 6.8 %all-to-all-done = bf16[8,32,1024]{2,1,0:T(8,128)(2,1)S(1)} async-done(((bf16[8,32,1024]{2,1,0:T(8,128)(2,1)}), bf16[8,32,1024]{2,1,0:T(8,128)(2,1)S(1)}, u32[]{:S(2)}, u32[]{:S(2)}) %all-to-all-start) | async-done | bytes 524320 | tf_op jit(solution)/shard_map/all_to_all | solution.py:648
  71.1 4.5 %collective-permute-done.9 = bf16[192,1024]{1,0:T(8,128)(2,1)S(1)} collective-permute-done((bf16[192,1024]{1,0:T(8,128)(2,1)S(1)}, bf16[192,1024]{1,0:T(8,128)(2,1)S(1)}, u32[]{:S(2)}, u32[]{:S(2)}) %collective-permute-start.9) | collective-permute-done | bytes 393248 | tf_op jit(solution)/shard_map/ppermute | solution.py:51
  80.1 6.1 %all-to-all-start.1 = ((bf16[32,32,192]{2,1,0:T(8,128)(2,1)}), bf16[32,32,192]{2,1,0:T(8,128)(2,1)S(1)}, u32[]{:S(2)}, u32[]{:S(2)}) async-start(bf16[32,32,192]{2,1,0:T(8,128)(2,1)} %bitcast.7), calls=%async_computation.1 | async-start | bytes 1048576 | tf_op jit(solution)/shard_map/all_to_all | solution.py:641
  91.3 4.6 %fusion.3.hot_ref = bf16[4096,128]{1,0:T(8,128)(2,1)} fusion(s32[4096]{0:T(1024)S(1)} %get-tuple-element.127, s32[4096]{0:T(1024)S(1)} %get-tuple-element.126, s32[4096]{0:T(1024)S(1)} %get-tuple-element.125, s32[4096]{0:T(1024)S(1)} %get-tuple-element.129), kind=kLoop, calls=%fused_computation.11 | loop fusion | flops 4194304 | bytes 1114112 | tf_op jit(solution)/shard_map/convert_element_type | solution.py:581
  100.6 6.4 %select_convert_fusion.mask_ref = bf16[4096,128]{1,0:T(8,128)(2,1)} fusion(s32[128]{0:T(128)S(1)} %get-tuple-element.165, bf16[]{:T(256)} %bitcast.26, bf16[]{:T(256)} %bitcast.25, s32[128]{0:T(128)S(1)} %get-tuple-element.166, bf16[]{:T(256)} %bitcast.24, bf16[]{:T(256)} %bitcast.23, s32[128]{0:T(128)S(1)} %get-tuple-element.167, bf16[]{:T(256)} %bitcast.22, ...), kind=kLoop, calls=%fused_computation.3 | loop fusion | flops 6291456 | bytes 1083916 | tf_op jit(solution)/shard_map/convert_element_type | solution.py:597
  107.0 7.4 %all-to-all-done.1 = bf16[32,32,192]{2,1,0:T(8,128)(2,1)S(1)} async-done(((bf16[32,32,192]{2,1,0:T(8,128)(2,1)}), bf16[32,32,192]{2,1,0:T(8,128)(2,1)S(1)}, u32[]{:S(2)}, u32[]{:S(2)}) %all-to-all-start.1) | async-done | bytes 393248 | tf_op jit(solution)/shard_map/all_to_all | solution.py:641
  115.3 14.8 %project.1 = (bf16[2048,1024]{1,0:T(8,128)(2,1)}, f32[2048,128]{1,0:T(8,128)}, bf16[2048,128]{1,0:T(8,128)(2,1)}, bf16[2048,128]{1,0:T(8,128)(2,1)}) custom-call(s32[16]{0:T(128)} %compare_select_fusion.5.where_ref, bf16[16,128,1024]{2,1,0:T(8,128)(2,1)} %bitcast.2.x_ref, f32[1,1024]{1,0:T(1,128)} %bitcast.123, bf16[1024,256]{1,0:T(8,128)(2,1)} %pad.4.weight_ref, ...), custom_call_target="tpu_custom_call" | custom-call | tf_op jit(solution)/shard_map/project/pallas_call | solution.py:159
  133.0 27.0 %attend.1 = (f32[2048,128]{1,0:T(8,128)}, bf16[2048,64]{1,0:T(8,128)(2,1)}) custom-call(s32[16]{0:T(128)} %get-tuple-element.75.order_ref, s32[32]{0:T(128)} %pad_add_fusion.2.place_ref, s32[8]{0:T(128)} %get-tuple-element.160.low_ref, s32[8]{0:T(128)} %get-tuple-element.159.high_ref, bf16[2048,128]{1,0:T(8,128)(2,1)} %get-tuple-element.37.query_ref, ...), custom_call_target="tpu_custom_call" | custom-call | tf_op jit(solution)/shard_map/attend/pallas_call | solution.py:269
  162.2 5.1 %all-to-all-start.2 = ((bf16[16,128,64]{1,2,0:T(8,128)(2,1)}), bf16[16,128,64]{1,2,0:T(8,128)(2,1)S(1)}, u32[]{:S(2)}, u32[]{:S(2)}) async-start(bf16[16,128,64]{1,2,0:T(8,128)(2,1)} %copy.82), calls=%async_computation.2 | async-start | bytes 524288 | tf_op jit(solution)/shard_map/all_to_all | solution.py:694
  171.7 5.5 %collective-permute-done.18 = bf16[128,1024]{1,0:T(8,128)(2,1)S(1)} collective-permute-done((bf16[128,1024]{1,0:T(8,128)(2,1)S(1)}, bf16[128,1024]{1,0:T(8,128)(2,1)S(1)}, u32[]{:S(2)}, u32[]{:S(2)}) %collective-permute-start.18) | collective-permute-done | bytes 262176 | tf_op jit(solution)/shard_map/ppermute | solution.py:51
  204.2 18.5 %feed.1 = (bf16[512,1024]{1,0:T(8,128)(2,1)}, bf16[512,1024]{1,0:T(8,128)(2,1)}, bf16[512,1024]{1,0:T(8,128)(2,1)}, bf16[512,1024]{1,0:T(8,128)(2,1)}, bf16[4,384,1024]{2,1,0:T(8,128)(2,1)}) custom-call(bf16[512,1024]{1,0:T(8,128)(2,1)} %copy-done.7, bf16[512,1024]{1,0:T(8,128)(2,1)} %collective-permute-done.16.second_other_ref, ...), custom_call_target="tpu_custom_call" | custom-call | tf_op jit(solution)/shard_map/feed/pallas_call | solution.py:540
  264.6 4.9 %collective-permute-done.35 = bf16[128,1024]{1,0:T(8,128)(2,1)S(1)} collective-permute-done((bf16[128,1024]{1,0:T(8,128)(2,1)S(1)}, bf16[128,1024]{1,0:T(8,128)(2,1)S(1)}, u32[]{:S(2)}, u32[]{:S(2)}) %collective-permute-start.35) | collective-permute-done | bytes 262176 | tf_op jit(solution)/shard_map/ppermute | solution.py:51
  273.4 15.7 %all_to_all.41 = bf16[16,128,64]{1,2,0:T(8,128)(2,1)S(1)} all-to-all(bf16[16,128,64]{1,2,0:T(8,128)(2,1)S(1)} %bitcast.115), channel_id=1, replica_groups=mesh['hx'=2,'core'=2,'bz'=4,'by'=2] {'bz','by','hx'}, dimensions={0} | all-to-all | bytes 524288 | tf_op jit(solution)/shard_map/all_to_all | solution.py:713
  290.1 41.8 %attend_back.1 = (f32[2048,128]{1,0:T(8,128)}, f32[2048,128]{1,0:T(8,128)}, f32[2048,128]{1,0:T(8,128)}, f32[8,128]{1,0:T(8,128)}) custom-call(s32[16]{0:T(128)} %get-tuple-element.75.order_ref, s32[32]{0:T(128)} %pad_add_fusion.2.place_ref, s32[8]{0:T(128)} %get-tuple-element.160.low_ref, s32[8]{0:T(128)} %get-tuple-element.159.high_ref, ...), custom_call_target="tpu_custom_call" | custom-call | tf_op jit(solution)/shard_map/attend_back/pallas_call | solution.py:382
  335.8 9.8 %project_back.1 = (bf16[2048,192]{1,0:T(8,128)(2,1)}, bf16[1024,192]{1,0:T(8,128)(2,1)}, f32[8,128]{1,0:T(8,128)}) custom-call(f32[2048,128]{1,0:T(8,128)} %get-tuple-element.48.query_grad_ref, f32[2048,128]{1,0:T(8,128)} %get-tuple-element.49.own_ref, f32[2048,128]{1,0:T(8,128)} %copy-done.11, f32[2048,128]{1,0:T(8,128)} %get-tuple-element.51.raw_ref, ...), custom_call_target="tpu_custom_call" | custom-call | tf_op jit(solution)/shard_map/project_back/pallas_call | solution.py:449
  353.0 18.5 %all-to-all-done.4 = bf16[16,128,192]{1,2,0:T(8,128)(2,1)S(1)} async-done(((bf16[16,128,192]{1,2,0:T(8,128)(2,1)}), bf16[16,128,192]{1,2,0:T(8,128)(2,1)S(1)}, u32[]{:S(2)}, u32[]{:S(2)}) %all-to-all-start.4) | async-done | bytes 786464 | tf_op jit(solution)/shard_map/all_to_all | solution.py:750
  371.5 5.1 %fusion.12 = (f32[1024]{0:T(1024)S(1)}, f32[128]{0:T(128)S(1)}, f32[128,1024]{1,0:T(8,128)S(1)}) fusion(bf16[128,1024]{1,0:T(8,128)(2,1)S(1)} %copy-done.3, f32[128]{0:T(128)S(1)} %get-tuple-element.142, f32[1024]{0:T(1024)S(1)} %copy-done.15, bf16[128,3072]{0,1:T(8,128)(2,1)S(1)} %bitcast.99, bf16[1024,3072]{1,0:T(8,128)(2,1)} %all-gather.7.cloned.1.call-done), kind=kOutput, calls=%fused_computation.30 | convolution fusion | flops 806222720 | bytes 7873536 | tf_op jit(solution)/shard_map/dot_general | solution.py:34
  379.5 4.1 all-to-all-start.7
  385.1 9.9 %all-to-all-done.7 = f32[32,1,2304]{2,1,0:T(1,128)S(1)} async-done(((f32[32,1,2304]{2,1,0:T(1,128)}), f32[32,1,2304]{2,1,0:T(1,128)S(1)}, u32[]{:S(2)}, u32[]{:S(2)}) %all-to-all-start.7) | async-done | bytes 294944 | tf_op jit(solution)/shard_map/all_to_all | solution.py:602
  402.6 10.6 %all-to-all-done.5 = bf16[32,32,192]{2,1,0:T(8,128)(2,1)S(1)} async-done(((bf16[32,32,192]{2,1,0:T(8,128)(2,1)}), bf16[32,32,192]{2,1,0:T(8,128)(2,1)S(1)}, u32[]{:S(2)}, u32[]{:S(2)}) %all-to-all-start.5) | async-done | bytes 393248 | tf_op jit(solution)/shard_map/all_to_all | solution.py:754
  413.2 4.1 all-to-all-start.6
  423.0 4.1 all-to-all-done.6
  (267 shorter events, 165.1 us)
Async XLA Ops:
  7.2 71.1 %all-gather.5.cloned.1.call-start = ((), (), s32[]{:S(2)}) async-start(), calls=%async_computation.10 | async-start | bytes 2162688 | tf_op jit(solution)/shard_map/all_gather | solution.py:635
  7.9 11.8 %collective-permute-start.1 = (bf16[128,1024]{1,0:T(8,128)(2,1)}, bf16[128,1024]{1,0:T(8,128)(2,1)S(1)}, u32[]{:S(2)}, u32[]{:S(2)}) collective-permute-start(bf16[128,1024]{1,0:T(8,128)(2,1)} %param.14), channel_id=1, source_target_pairs={{0,1},{1,0},{2,3},{3,2},{4,5},{5,4},{6,7},{7,6},{8,9},{9,8},{10,11... | collective-permute-start | bytes 786440 | tf_op jit(solution)/shard_map/ppermute | solution.py:51
  12.5 14.0 %collective-permute-start.4 = (bf16[128,1024]{1,0:T(8,128)(2,1)}, bf16[128,1024]{1,0:T(8,128)(2,1)S(1)}, u32[]{:S(2)}, u32[]{:S(2)}) collective-permute-start(bf16[128,1024]{1,0:T(8,128)(2,1)} %param.14), channel_id=1, source_target_pairs={{0,2},{2,4},{4,6},{6,0},{1,3},{3,5},{5,7},{7,1},{8,10},{10,12},{12... | collective-permute-start | bytes 786440 | tf_op jit(solution)/shard_map/ppermute | solution.py:67
  14.1 20.4 %collective-permute-start.5 = (bf16[128,1024]{1,0:T(8,128)(2,1)}, bf16[128,1024]{1,0:T(8,128)(2,1)S(1)}, u32[]{:S(2)}, u32[]{:S(2)}) collective-permute-start(bf16[128,1024]{1,0:T(8,128)(2,1)} %param.14), channel_id=1, source_target_pairs={{0,4},{2,6},{4,0},{6,2},{1,5},{3,7},{5,1},{7,3},{8,12},{10,14},{12... | collective-permute-start | bytes 786440 | tf_op jit(solution)/shard_map/ppermute | solution.py:67
  16.6 18.6 %collective-permute-start.6 = (bf16[128,1024]{1,0:T(8,128)(2,1)}, bf16[128,1024]{1,0:T(8,128)(2,1)S(1)}, u32[]{:S(2)}, u32[]{:S(2)}) collective-permute-start(bf16[128,1024]{1,0:T(8,128)(2,1)} %param.14), channel_id=1, source_target_pairs={{0,6},{2,0},{4,2},{6,4},{1,7},{3,1},{5,3},{7,5},{8,14},{10,8},{12,... | collective-permute-start | bytes 786440 | tf_op jit(solution)/shard_map/ppermute | solution.py:67
  36.2 21.6 %collective-permute-start.8 = (bf16[384,1024]{1,0:T(8,128)(2,1)}, bf16[384,1024]{1,0:T(8,128)(2,1)S(1)}, u32[]{:S(2)}, u32[]{:S(2)}) collective-permute-start(bf16[384,1024]{1,0:T(8,128)(2,1)} %get-tuple-element.118), channel_id=1, source_target_pairs={{0,1},{1,0},{2,3},{3,2},{4,5},{5,4},{6,7},{7,6},{8,9},{9,8},{10,11... | collective-permute-start | bytes 2359304 | tf_op jit(solution)/shard_map/ppermute | solution.py:51
  36.6 22.5 %collective-permute-start.7 = (bf16[384,1024]{1,0:T(8,128)(2,1)}, bf16[384,1024]{1,0:T(8,128)(2,1)S(1)}, u32[]{:S(2)}, u32[]{:S(2)}) collective-permute-start(bf16[384,1024]{1,0:T(8,128)(2,1)} %get-tuple-element.118), channel_id=1, source_target_pairs={{0,16},{16,0},{1,17},{17,1},{2,18},{18,2},{3,19},{19,3},{4,20},{20... | collective-permute-start | bytes 2359304 | tf_op jit(solution)/shard_map/ppermute | solution.py:51
  38.6 29.6 %all-to-all-start = ((bf16[8,32,1024]{2,1,0:T(8,128)(2,1)}), bf16[8,32,1024]{2,1,0:T(8,128)(2,1)S(1)}, u32[]{:S(2)}, u32[]{:S(2)}) async-start(bf16[8,32,1024]{2,1,0:T(8,128)(2,1)} %reshape.438), calls=%async_computation | async-start | bytes 1048576 | tf_op jit(solution)/shard_map/all_to_all | solution.py:648
  42.4 161.8 %all-gather.9.cloned.1.call-start = ((), (), s32[]{:S(2)}) async-start(), calls=%async_computation.14 | async-start | bytes 3932160 | tf_op jit(solution)/shard_map/all_gather | solution.py:686
  57.8 17.8 %collective-permute-start.9 = (bf16[192,1024]{1,0:T(8,128)(2,1)S(1)}, bf16[192,1024]{1,0:T(8,128)(2,1)S(1)}, u32[]{:S(2)}, u32[]{:S(2)}) collective-permute-start(bf16[192,1024]{1,0:T(8,128)(2,1)S(1)} %slice.240), channel_id=1, source_target_pairs={{0,16},{16,0},{1,17},{17,1},{2,18},{18,2},{3,19},{19,3},{4,20},{20... | collective-permute-start | bytes 1179656 | tf_op jit(solution)/shard_map/ppermute | solution.py:51
  59.8 16.6 %collective-permute-start.10 = (bf16[192,1024]{1,0:T(8,128)(2,1)}, bf16[192,1024]{1,0:T(8,128)(2,1)S(1)}, u32[]{:S(2)}, u32[]{:S(2)}) collective-permute-start(bf16[192,1024]{1,0:T(8,128)(2,1)} %slice.241), channel_id=1, source_target_pairs={{0,1},{1,0},{2,3},{3,2},{4,5},{5,4},{6,7},{7,6},{8,9},{9,8},{10,11... | collective-permute-start | bytes 1179656 | tf_op jit(solution)/shard_map/ppermute | solution.py:51
  80.1 34.3 %all-to-all-start.1 = ((bf16[32,32,192]{2,1,0:T(8,128)(2,1)}), bf16[32,32,192]{2,1,0:T(8,128)(2,1)S(1)}, u32[]{:S(2)}, u32[]{:S(2)}) async-start(bf16[32,32,192]{2,1,0:T(8,128)(2,1)} %bitcast.7), calls=%async_computation.1 | async-start | bytes 1048576 | tf_op jit(solution)/shard_map/all_to_all | solution.py:641
  86.2 285.3 %all-gather.7.cloned.1.call-start = ((), (), s32[]{:S(2)}) async-start(), calls=%async_computation.11 | async-start | bytes 6488064 | tf_op jit(solution)/shard_map/all_gather | solution.py:747
  162.2 20.4 %all-to-all-start.2 = ((bf16[16,128,64]{1,2,0:T(8,128)(2,1)}), bf16[16,128,64]{1,2,0:T(8,128)(2,1)S(1)}, u32[]{:S(2)}, u32[]{:S(2)}) async-start(bf16[16,128,64]{1,2,0:T(8,128)(2,1)} %copy.82), calls=%async_computation.2 | async-start | bytes 524288 | tf_op jit(solution)/shard_map/all_to_all | solution.py:694
  167.2 216.4 %reduce-scatter.3.cloned.1.call-start = ((), (), s32[]{:S(2)}) async-start(), calls=%async_computation.12 | async-start | bytes 327680 | tf_op jit(solution)/shard_map/reduce_scatter | solution.py:739
  169.5 10.2 %collective-permute-start.17 = (bf16[128,1024]{1,0:T(8,128)(2,1)S(1)}, bf16[128,1024]{1,0:T(8,128)(2,1)S(1)}, u32[]{:S(2)}, u32[]{:S(2)}) collective-permute-start(bf16[128,1024]{1,0:T(8,128)(2,1)S(1)} %copy-done.9), channel_id=1, source_target_pairs={{0,16},{16,0},{1,17},{17,1},{2,18},{18,2},{3,19},{19,3},{4,20},{20... | collective-permute-start | bytes 786440 | tf_op jit(solution)/shard_map/ppermute | solution.py:51
  183.9 11.3 %collective-permute-start.12 = (bf16[128,1024]{1,0:T(8,128)(2,1)S(1)}, bf16[128,1024]{1,0:T(8,128)(2,1)S(1)}, u32[]{:S(2)}, u32[]{:S(2)}) collective-permute-start(bf16[128,1024]{1,0:T(8,128)(2,1)S(1)} %get-tuple-element.77), channel_id=1, source_target_pairs={{0,16},{16,0},{1,17},{17,1},{2,18},{18,2},{3,19},{19,3},{4,20},{20... | collective-permute-start | bytes 786440 | tf_op jit(solution)/shard_map/ppermute | solution.py:51
  190.9 10.6 %collective-permute-start.21 = (bf16[512,1024]{1,0:T(8,128)(2,1)}, bf16[512,1024]{1,0:T(8,128)(2,1)}, u32[]{:S(2)}, u32[]{:S(2)}) collective-permute-start(bf16[512,1024]{1,0:T(8,128)(2,1)} %constant_dynamic-update-slice_fusion.20.grad_mine_ref), channel_id=1, source_target_pairs={{0,8},{8,0},{1,9},{9,1},{2,10},{10,2},{3,11},{11,3},{4,12},{12,4},... | collective-permute-start | bytes 3145736 | tf_op jit(solution)/shard_map/ppermute | solution.py:51
  239.9 10.2 %collective-permute-start.24 = (bf16[128,1024]{1,0:T(8,128)(2,1)S(1)}, bf16[128,1024]{1,0:T(8,128)(2,1)S(1)}, u32[]{:S(2)}, u32[]{:S(2)}) collective-permute-start(bf16[128,1024]{1,0:T(8,128)(2,1)S(1)} %pad_maximum_fusion.3), channel_id=1, source_target_pairs={{0,16},{16,0},{1,17},{17,1},{2,18},{18,2},{3,19},{19,3},{4,20},{20... | collective-permute-start | bytes 786440 | tf_op jit(solution)/shard_map/ppermute | solution.py:51
  271.8 128.9 %reduce-scatter.5.cloned.1.call-start = ((), (), s32[]{:S(2)}) async-start(), calls=%async_computation.13 | async-start | bytes 3932160 | tf_op jit(solution)/shard_map/reduce_scatter | solution.py:717
  347.8 23.7 %all-to-all-start.4 = ((bf16[16,128,192]{1,2,0:T(8,128)(2,1)}), bf16[16,128,192]{1,2,0:T(8,128)(2,1)S(1)}, u32[]{:S(2)}, u32[]{:S(2)}) async-start(bf16[16,128,192]{1,2,0:T(8,128)(2,1)} %copy.87), calls=%async_computation.4 | async-start | bytes 1572864 | tf_op jit(solution)/shard_map/all_to_all | solution.py:750
  379.5 15.5 %all-to-all-start.7 = ((f32[32,1,2304]{2,1,0:T(1,128)}), f32[32,1,2304]{2,1,0:T(1,128)S(1)}, u32[]{:S(2)}, u32[]{:S(2)}) async-start(f32[32,1,2304]{2,1,0:T(1,128)} %broadcast_in_dim.184), calls=%async_computation.9 | async-start | bytes 589824 | tf_op jit(solution)/shard_map/all_to_all | solution.py:602
  395.0 18.2 %all-to-all-start.5 = ((bf16[32,32,192]{2,1,0:T(8,128)(2,1)}), bf16[32,32,192]{2,1,0:T(8,128)(2,1)S(1)}, u32[]{:S(2)}, u32[]{:S(2)}) async-start(bf16[32,32,192]{2,1,0:T(8,128)(2,1)} %bitcast.40), calls=%async_computation.5 | async-start | bytes 1048576 | tf_op jit(solution)/shard_map/all_to_all | solution.py:754
  413.2 13.9 %all-to-all-start.6 = ((bf16[8,32,1024]{2,1,0:T(8,128)(2,1)}), bf16[8,32,1024]{2,1,0:T(8,128)(2,1)}, u32[]{:S(2)}, u32[]{:S(2)}) async-start(bf16[8,32,1024]{2,1,0:T(8,128)(2,1)} %bitcast.52), calls=%async_computation.8 | async-start | bytes 1048576 | tf_op jit(solution)/shard_map/all_to_all | solution.py:720
  (48 other events, 501.0 us)
Sparse Core Ops, SparseCore 0:
  10.9 67.3 all-gather.4
  79.9 72.4 all-gather.8
  155.2 73.9 all-gather.6
  271.9 19.1 reduce-scatter.2
  293.3 58.8 reduce-scatter.4

commit v3 on v2

--- a/solution.py
+++ b/solution.py
@@ -8,6 +8,7 @@
 from jax.sharding import Mesh
 from jax.sharding import PartitionSpec as P
 
+
 D = 1024
 H = 16
 HD = 64
@@ -25,6 +26,7 @@
 MASK = -512.0
 QUERY_TILE = 256
 KEY_TILE = 256
+PROJECT_BLOCKS = 4
 
 bf16 = jnp.bfloat16
 f32 = jnp.float32
@@ -56,22 +58,40 @@
     return mine, swap(mine, "core")
 
 
-def chip_gather(shard):
+def chip_gather(shard, rider, tables):
     depth = lax.axis_size("bz")
     chips = depth * 4
+    rows = shard.shape[0]
     z, y, x = lax.axis_index("bz"), lax.axis_index("by"), lax.axis_index("hx")
     at = jnp.arange(chips, dtype=jnp.int32)
     if depth > 4:
-        return lax.all_gather(shard, CHIPS, axis=0, tiled=True).reshape(chips, BLOCK, D), at
+        gathered = lax.all_gather(shard, CHIPS, axis=0, tiled=True).reshape(chips, rows, D)
+        return gathered, at, jnp.concatenate(quarters(rider), axis=0), tables
     shifted = [
         lax.ppermute(shard, "bz", [(i, (i + by) % depth) for i in range(depth)])
         for by in range(1, depth)
     ]
-    pieces = quarters(shard) + quarters(jnp.concatenate(shifted, axis=0))
+    near = quarters(jnp.concatenate([shard, rider], axis=0))
+    shifted, tables = lax.optimization_barrier((shifted, tables))
+    pieces = [near[0][:rows], near[1][:rows], near[2][:rows], near[3]]
+    riders = [near[0][rows:], near[1][rows:], near[2][rows:], near[4]]
+    pieces = pieces + quarters(jnp.concatenate(shifted, axis=0))
     back = (z - at // 4) % depth
     flips = ((at % 2) ^ x) + 2 * (((at // 2) % 2) ^ y)
-    where = jnp.where(back == 0, flips, 4 + flips * (depth - 1) + back - 1)
-    return jnp.concatenate(pieces, axis=0).reshape(chips, BLOCK, D), where.astype(jnp.int32)
+    where = jnp.where(back == 0, flips, 4 + flips * (depth - 1) + back - 1).astype(jnp.int32)
+    gathered = jnp.concatenate(pieces, axis=0).reshape(chips, rows, D)
+    return gathered, where, jnp.concatenate(riders, axis=0), tables
+
+
+def sum_everywhere(values):
+    for axis in ("core", "hx", "by"):
+        values = values + swap(values, axis)
+    depth = lax.axis_size("bz")
+    step = 1
+    while step < depth:
+        values = values + lax.ppermute(values, "bz", [(i, i ^ step) for i in range(depth)])
+        step *= 2
+    return values
 
 
 def quarters(shard):
@@ -94,7 +114,7 @@
     to_y = jnp.concatenate([to_y[:half] + for_y, to_y[half:]], axis=0).astype(bf16)
     from_x = swap(to_x, "hx")
     from_y = swap(to_y, "by")
-    return mine[:rows] + from_x.astype(f32) + from_y.astype(f32)
+    return mine[:rows], from_x, from_y
 
 
 def plane_members():
@@ -122,21 +142,11 @@
     )
 
 
-def project_kernel(
-    where_ref,
-    x_ref,
-    gain_ref,
-    weight_ref,
-    cosine_ref,
-    sine_ref,
-    gains_ref,
-    hot_ref,
-    normed_ref,
-    raw_ref,
-    query_ref,
-    kv_ref,
-):
-    x = x_ref[0].astype(f32)
+def project_kernel(where_ref, *refs):
+    x_refs = refs[:PROJECT_BLOCKS]
+    gain_ref, weight_ref, cosine_ref, sine_ref, gains_ref, hot_ref = refs[PROJECT_BLOCKS:-4]
+    normed_ref, raw_ref, query_ref, kv_ref = refs[-4:]
+    x = jnp.concatenate([x_ref[0] for x_ref in x_refs], axis=0).astype(f32)
     normed = norm_rows(x, gain_ref[...]).astype(bf16)
     normed_ref[...] = normed
     project = dot(normed, weight_ref[...], ((1,), (0,)))
@@ -154,15 +164,19 @@
 def project(where, gathered, gain, weight, cosine, sine, gains, hot):
     blocks = gathered.shape[0]
     rows = blocks * BLOCK
-    row_spec = lambda width: pl.BlockSpec((BLOCK, width), lambda j, where: (j, 0))
+    step_rows = PROJECT_BLOCKS * BLOCK
+    row_spec = lambda width: pl.BlockSpec((step_rows, width), lambda j, where: (j, 0))
     whole = lambda array: pl.BlockSpec(array.shape, lambda j, where: (0, 0))
+    block = lambda i: pl.BlockSpec(
+        (1, BLOCK, D), lambda j, where: (where[j * PROJECT_BLOCKS + i], 0, 0)
+    )
     return pl.pallas_call(
         project_kernel,
         grid_spec=pltpu.PrefetchScalarGridSpec(
             num_scalar_prefetch=1,
-            grid=(blocks,),
-            in_specs=[
-                pl.BlockSpec((1, BLOCK, D), lambda j, where: (where[j], 0, 0)),
+            grid=(blocks // PROJECT_BLOCKS,),
+            in_specs=[block(i) for i in range(PROJECT_BLOCKS)]
+            + [
                 whole(gain),
                 whole(weight),
                 row_spec(128),
@@ -179,7 +193,7 @@
             jax.ShapeDtypeStruct((rows, 128), bf16),
         ],
         name="project",
-    )(where, gathered, gain, weight, cosine, sine, gains, hot)
+    )(where, *[gathered] * PROJECT_BLOCKS, gain, weight, cosine, sine, gains, hot)
 
 
 def sort_keys(place_ref, own_ref, other_ref, mask_ref, key_ref, value_ref):
@@ -256,7 +270,7 @@
         attended_ref[pl.ds(start, BLOCK), :] = piece[:, :HD].astype(bf16)
 
 
-def fixed(array, prefetched):
+def fixed(array):
     return pl.BlockSpec(
         array.shape, lambda *unused: (0,) * len(array.shape), pipeline_mode=pl.Buffered(1)
     )
@@ -271,8 +285,8 @@
         grid_spec=pltpu.PrefetchScalarGridSpec(
             num_scalar_prefetch=4,
             grid=(low.shape[0],),
-            in_specs=[fixed(array, 4) for array in operands],
-            out_specs=[fixed(array, 4) for array in outs],
+            in_specs=[fixed(array) for array in operands],
+            out_specs=[fixed(array) for array in outs],
             scratch_shapes=[pltpu.VMEM((2 * rows, 128), bf16), pltpu.VMEM((2 * rows, 128), bf16)],
         ),
         out_shape=list(outs),
@@ -376,7 +390,7 @@
 def attend_back(order, place, low, high, query, own, other, mask, hot, kept, grad):
     rows = query.shape[0]
     operands = (query, own, other, mask, hot, kept, grad)
-    outs = tuple(jax.ShapeDtypeStruct((rows, 128), f32) for unused in range(3)) + (
+    outs = tuple(jax.ShapeDtypeStruct((rows, 128), f32) for _ in range(3)) + (
         jax.ShapeDtypeStruct((8, 128), f32),
     )
     return pl.pallas_call(
@@ -384,8 +398,8 @@
         grid_spec=pltpu.PrefetchScalarGridSpec(
             num_scalar_prefetch=4,
             grid=(low.shape[0],),
-            in_specs=[fixed(array, 4) for array in operands],
-            out_specs=[fixed(array, 4) for array in outs],
+            in_specs=[fixed(array) for array in operands],
+            out_specs=[fixed(array) for array in outs],
             scratch_shapes=[
                 pltpu.VMEM((2 * rows, 128), bf16),
                 pltpu.VMEM((2 * rows, 128), bf16),
@@ -407,9 +421,11 @@
     sine_ref,
     gains_ref,
     normed_ref,
+    forward_ref,
     grad_ref,
     weight_grad_ref,
     gain_grad_ref,
+    attn_grad_ref,
     weight_ref,
     gain_ref,
 ):
@@ -439,9 +455,12 @@
     def _():
         weight_grad_ref[...] = weight_ref[:, : 3 * HD].astype(bf16)
         gain_grad_ref[...] = jnp.broadcast_to(gain_ref[...], gain_grad_ref.shape)
-
-
-def project_back(query_grad, own, other, raw, cosine, sine, gains, normed):
+        forward = forward_ref[...].astype(f32)
+        attn = jnp.sum(weight_ref[...] * forward, axis=1, keepdims=True)
+        attn_grad_ref[...] = jnp.broadcast_to(attn, attn_grad_ref.shape)
+
+
+def project_back(query_grad, own, other, raw, cosine, sine, gains, normed, forward):
     rows = query_grad.shape[0]
     step_rows = 2 * BLOCK
     row_spec = lambda width: pl.BlockSpec((step_rows, width), lambda j: (j, 0))
@@ -449,16 +468,17 @@
     return pl.pallas_call(
         project_back_kernel,
         grid=(rows // step_rows,),
-        in_specs=[row_spec(128)] * 6 + [whole(gains.shape), row_spec(D)],
-        out_specs=[row_spec(3 * HD), whole((D, 3 * HD)), whole((8, 128))],
+        in_specs=[row_spec(128)] * 6 + [whole(gains.shape), row_spec(D), whole(forward.shape)],
+        out_specs=[row_spec(3 * HD), whole((D, 3 * HD)), whole((8, 128)), whole((D, 128))],
         out_shape=[
             jax.ShapeDtypeStruct((rows, 3 * HD), bf16),
             jax.ShapeDtypeStruct((D, 3 * HD), bf16),
             jax.ShapeDtypeStruct((8, 128), f32),
+            jax.ShapeDtypeStruct((D, 128), f32),
         ],
         scratch_shapes=[pltpu.VMEM((D, 4 * HD), f32), pltpu.VMEM((1, 128), f32)],
         name="project_back",
-    )(query_grad, own, other, raw, cosine, sine, gains, normed)
+    )(query_grad, own, other, raw, cosine, sine, gains, normed, forward)
 
 
 def feed_kernel(
@@ -553,6 +573,174 @@
     )(*second, *grad, weight)
 
 
+def out_kernel(
+    parts_ref, x_ref, weight_ref, gain_ref, merged_ref, middle_ref, second_ref, squares_ref
+):
+    heads = parts_ref.shape[0]
+    for pair in range(heads // 2):
+        merged_ref[:, pair * 2 * HD : (pair + 1) * 2 * HD] = jnp.concatenate(
+            [parts_ref[2 * pair], parts_ref[2 * pair + 1]], axis=1
+        )
+    branch = dot(merged_ref[...], weight_ref[...], ((1,), (0,)))
+    x = x_ref[...].astype(f32)
+    middle = x + branch
+    middle_ref[...] = middle
+    second_ref[...] = norm_rows(middle, gain_ref[...]).astype(bf16)
+    row = lax.broadcasted_iota(jnp.int32, squares_ref.shape, 0)
+    x_sum = jnp.sum(x * x, keepdims=True)
+    branch_sum = jnp.sum(branch * branch, keepdims=True)
+    squares_ref[...] = jnp.where(row == 0, x_sum, branch_sum)
+
+
+def out_project(parts, x, weight, gain):
+    rows = x.shape[0]
+    return pl.pallas_call(
+        out_kernel,
+        out_shape=[
+            jax.ShapeDtypeStruct((rows, D), bf16),
+            jax.ShapeDtypeStruct((rows, D), f32),
+            jax.ShapeDtypeStruct((rows, D), bf16),
+            jax.ShapeDtypeStruct((8, 128), f32),
+        ],
+        name="out_project",
+    )(parts, x, weight, gain)
+
+
+def middle_back_kernel(
+    own_ref,
+    from_x_ref,
+    from_y_ref,
+    middle_ref,
+    cotangent_ref,
+    gain_ref,
+    weight_ref,
+    grad_middle_ref,
+    branch_ref,
+    parts_ref,
+    gain_grad_ref,
+):
+    grad_second = own_ref[...] + from_x_ref[...].astype(f32) + from_y_ref[...].astype(f32)
+    grad_middle, gain_rows = norm_back(middle_ref[...], gain_ref[...], grad_second)
+    grad_middle = cotangent_ref[...].astype(f32) + grad_middle
+    grad_middle_ref[...] = grad_middle
+    branch = grad_middle.astype(bf16)
+    branch_ref[...] = branch
+    merged = dot(branch, weight_ref[...], ((1,), (1,))).astype(bf16)
+    for head in range(parts_ref.shape[0]):
+        parts_ref[head] = merged[:, head * HD : (head + 1) * HD]
+    gain_grad_ref[...] = jnp.broadcast_to(
+        jnp.sum(gain_rows, axis=0, keepdims=True), gain_grad_ref.shape
+    )
+
+
+def middle_back(own, from_x, from_y, middle, cotangent, gain, weight):
+    rows = middle.shape[0]
+    return pl.pallas_call(
+        middle_back_kernel,
+        out_shape=[
+            jax.ShapeDtypeStruct((rows, D), f32),
+            jax.ShapeDtypeStruct((rows, D), bf16),
+            jax.ShapeDtypeStruct((H, rows, HD), bf16),
+            jax.ShapeDtypeStruct((8, D), f32),
+        ],
+        name="middle_back",
+    )(own, from_x, from_y, middle, cotangent, gain, weight)
+
+
+def out_grad_kernel(
+    members_ref,
+    merged_ref,
+    branch_ref,
+    ffn_mine_ref,
+    ffn_other_ref,
+    mine_ref,
+    other_ref,
+    grad_ref,
+    depth,
+):
+    shard = mine_ref.shape[0] // 4
+    rows = shard // depth
+    grad_ref[...] = dot(merged_ref[...], branch_ref[...], ((0,), (0,)))
+    mine_ref[:, :D] = ffn_mine_ref[...]
+    other_ref[:, :D] = ffn_other_ref[...]
+    for place in range(8):
+        target_ref = mine_ref if place < 4 else other_ref
+        for z in range(depth):
+            source = pl.multiple_of((z * 8 + members_ref[place]) * rows, rows)
+            target = (place % 4) * shard + z * rows
+            target_ref[target : target + rows, D:] = grad_ref[pl.ds(source, rows), :].astype(bf16)
+
+
+def out_grad(members, merged, branch, ffn_mine, ffn_other, depth):
+    joined = jax.ShapeDtypeStruct((ffn_mine.shape[0], 2 * D), bf16)
+    operands = (merged, branch, ffn_mine, ffn_other)
+    return pl.pallas_call(
+        partial(out_grad_kernel, depth=depth),
+        grid_spec=pltpu.PrefetchScalarGridSpec(
+            num_scalar_prefetch=1,
+            grid=(1,),
+            in_specs=[fixed(array) for array in operands],
+            out_specs=[fixed(joined), fixed(joined)],
+            scratch_shapes=[pltpu.VMEM((D, D), f32)],
+        ),
+        out_shape=[joined, joined],
+        name="out_grad",
+    )(members, *operands)
+
+
+def input_back_kernel(
+    joined_ref, weight_ref, x_ref, gain_ref, middle_ref, grad_ref, qkv_ref, wide_ref
+):
+    heads = joined_ref.shape[0]
+    rows = x_ref.shape[0]
+    for pair in range(heads // 2):
+        left = joined_ref[2 * pair]
+        right = joined_ref[2 * pair + 1]
+        wide_ref[:, pair * 6 * HD : (pair + 1) * 6 * HD] = jnp.concatenate(
+            [left[:rows], right[:rows]], axis=1
+        )
+        for part in range(3):
+            at = part * D + pair * 2 * HD
+            window = slice(part * HD, (part + 1) * HD)
+            qkv_ref[:, at : at + 2 * HD] = jnp.concatenate(
+                [left[rows:, window], right[rows:, window]], axis=1
+            ).astype(f32)
+    grad_normed = dot(wide_ref[...], weight_ref[...], ((1,), (1,)))
+    grad, _ = norm_back(x_ref[...].astype(f32), gain_ref[...], grad_normed)
+    grad_ref[...] = middle_ref[...] + grad
+
+
+def input_back(joined, weight, x, gain, middle):
+    rows = x.shape[0]
+    return pl.pallas_call(
+        input_back_kernel,
+        out_shape=[
+            jax.ShapeDtypeStruct((rows, D), f32),
+            jax.ShapeDtypeStruct((joined.shape[1] - rows, 3 * D), f32),
+        ],
+        scratch_shapes=[pltpu.VMEM((rows, 3 * D), bf16)],
+        name="input_back",
+    )(joined, weight, x, gain, middle)
+
+
+def widen_kernel(parts_ref, grad_ref):
+    sources, _, width = parts_ref.shape
+    for source in range(sources):
+        for at in range(width // 128):
+            to = (at * sources + source) * 128
+            grad_ref[:, to : to + 128] = parts_ref[source, :, at * 128 : (at + 1) * 128].astype(f32)
+
+
+def widen(parts, depth, hidden_rows):
+    sources, rows, width = parts.shape
+    if hidden_rows != 128:
+        parts = parts.reshape(sources, rows, 2, depth, hidden_rows)
+        return parts.transpose(1, 2, 3, 0, 4).reshape(rows, -1).astype(f32)
+    return pl.pallas_call(
+        widen_kernel, out_shape=jax.ShapeDtypeStruct((rows, sources * width), f32), name="widen"
+    )(parts)
+
+
 def token_meta(seq_lengths, block_order):
     blocks = block_order.shape[0]
     packed_at = jnp.repeat(block_order, BLOCK) * BLOCK + jnp.tile(
@@ -573,7 +761,7 @@
     return own, other
 
 
-def one_hot_rows(segment, variate, segments):
+def one_hot_rows(segment, variate):
     lane = jnp.arange(128, dtype=jnp.int32)[None, :]
     hot = lane == SEGMENT_LANE + segment[:, None]
     for copy in range(3):
@@ -597,9 +785,11 @@
     return rows.astype(bf16)
 
 
-def sum_everywhere(vector, devices):
-    copies = jnp.broadcast_to(vector[None], (devices,) + vector.shape)
-    return jnp.sum(lax.all_to_all(copies, DEVICES, 0, 0, tiled=True), axis=0)
+def over_sharers(parts, sharers):
+    if sharers == 1:
+        return parts
+    parts = parts.reshape((H, sharers) + parts.shape[1:]).astype(f32)
+    return jnp.sum(parts, axis=1).astype(bf16)
 
 
 def body(
@@ -620,7 +810,6 @@
 ):
     depth = lax.axis_size("bz")
     chips = depth * 4
-    devices = chips * 2
     sharers = chips // H
     core = lax.axis_index("core")
     chip = (lax.axis_index("bz") * 2 + lax.axis_index("by")) * 2 + lax.axis_index("hx")
@@ -631,7 +820,6 @@
     segments = seq_lengths.shape[0] + 1
     tokens = variate_ids.shape[0]
 
-    gathered, where = chip_gather(inputs)
     out_full = lax.all_gather(out_weight, DEVICES, axis=0, tiled=True)
 
     by_head = qkv_weight.reshape(rows, 3, H, HD)
@@ -654,7 +842,7 @@
     all_segment = jnp.concatenate([own_segment, other_segment])
     all_variate = jnp.concatenate([own_variate, other_variate])
     bias = lax.dynamic_index_in_dim(variate_bias, head, 1, keepdims=False)
-    hot = one_hot_rows(all_segment, all_variate, segments)
+    hot = one_hot_rows(all_segment, all_variate)
     mask = mask_rows(all_segment, all_variate, segments, bias)
     freqs = THETA ** (-jnp.arange(HD // 2, dtype=f32) / (HD // 2))
     angles = own_position.astype(f32)[:, None] * freqs[None, :]
@@ -679,113 +867,109 @@
     high = (finish + KEY_TILE - 1) // KEY_TILE
     gains = jnp.concatenate([query_gain, key_gain])[None, :]
 
+    tables = (hot, mask, cosine, sine, place, order, low, high, own_qkv)
+    gathered, where, cotangent_mine, tables = chip_gather(inputs, cotangent, tables)
+    hot, mask, cosine, sine, place, order, low, high, own_qkv = tables
+
     feed_part = jnp.concatenate([expand_part, down_weight], axis=0)
-    gathered, late_cotangent, out_full, feed_part = lax.optimization_barrier(
-        (gathered, cotangent, out_full, feed_part)
-    )
+    gathered, out_full, feed_part = lax.optimization_barrier((gathered, out_full, feed_part))
     feed_own = lax.all_gather(feed_part[None], "bz", axis=0, tiled=True)
-    cotangent_plane = plane_gather(late_cotangent)
+    cotangent_plane = (cotangent_mine, swap(cotangent_mine, "core"))
 
     normed_low, raw, query, own_kv = project(
         where, gathered, attn_gain[None], own_qkv, cosine, sine, gains, hot
     )
     other_kv = swap(own_kv, "core")
     kept, attended = attend(order, place, low, high, query, own_kv, other_kv, mask)
-    merged = lax.all_to_all(attended.reshape(chips, BLOCK, HD), CHIPS, 0, 0, tiled=True)
-    merged = merged.reshape(H, sharers, BLOCK, HD)
-    merged = merged[:, 0] if sharers == 1 else jnp.sum(merged, axis=1)
-    merged = merged.transpose(1, 0, 2).reshape(BLOCK, D)
-
-    residual = inputs.astype(f32)
-    attn_branch = jnp.dot(merged, out_full, preferred_element_type=f32)
-    middle = residual + attn_branch
-    second_low = plane_gather(norm_rows(middle, ffn_gain).astype(bf16))
+    parts = lax.all_to_all(attended.reshape(chips, BLOCK, HD), CHIPS, 0, 0, tiled=True)
+    parts = over_sharers(parts, sharers)
+    merged, middle, second, squares = out_project(parts, inputs, out_full, ffn_gain[None])
+    second_plane = plane_gather(second)
 
     ffn_mine, ffn_other, back_mine, back_other, feed_grad = feed(
-        second_low, cotangent_plane, feed_own, hidden_rows
-    )
-    grad_second = plane_scatter(back_mine, back_other)
-    grad_middle, grad_ffn_rows = norm_back(middle, ffn_gain, grad_second)
-    grad_middle = cotangent.astype(f32) + grad_middle
-    branch_grad = grad_middle.astype(bf16)
-    grad_merged = dot(branch_grad, out_full, ((1,), (1,))).astype(bf16)
-    to_chips = jnp.repeat(grad_merged.reshape(BLOCK, H, HD).transpose(1, 0, 2), sharers, axis=0)
-    grad_attended = lax.all_to_all(to_chips, CHIPS, 0, 0, tiled=True).reshape(-1, HD)
-
-    ffn_branch = plane_scatter(ffn_mine, ffn_other)
-    outputs = (middle + ffn_branch).astype(bf16)
+        second_plane, cotangent_plane, feed_own, hidden_rows
+    )
     feed_grad = lax.psum_scatter(feed_grad, "bz", scatter_dimension=0, tiled=True)[0]
-    grad_down = feed_grad[8 * rows :].astype(f32)
-    grad_expand = (
-        lax.all_to_all(feed_grad[: 8 * rows].reshape(8, rows, -1), PLANE, 0, 0, tiled=True)
-        .reshape(8, rows, 2, depth, hidden_rows)
-        .transpose(1, 2, 3, 0, 4)
-        .reshape(rows, -1)
-        .astype(f32)
-    )
-
-    grad_out_full = dot(merged, branch_grad, ((0,), (0,))).astype(bf16)
-    grad_out_rows = grad_out_full.reshape(depth, 8, rows, D)
-    grad_out_rows = jnp.concatenate(
-        [
-            lax.dynamic_index_in_dim(grad_out_rows, member, 1, keepdims=False).reshape(-1, D)
-            for member in plane_members()
-        ],
-        axis=0,
-    )
-    middle_row = grad_out_rows.shape[0] // 2
-    grad_out_part = plane_scatter(grad_out_rows[:middle_row], grad_out_rows[middle_row:])
-    grad_out_part = grad_out_part.astype(bf16)
-    grad_out = lax.psum_scatter(grad_out_part, "bz", scatter_dimension=0, tiled=True).astype(f32)
+    ffn_mine, late_qkv = lax.optimization_barrier(
+        (ffn_mine, by_head.transpose(0, 2, 1, 3).reshape(rows, 3 * D))
+    )
+    qkv_full = lax.all_gather(late_qkv, DEVICES, axis=0, tiled=True)
+    grad_middle, branch_grad, to_chips, grad_ffn = middle_back(
+        *plane_scatter(back_mine, back_other), middle, cotangent, ffn_gain[None], out_full
+    )
+    grad_attended = lax.all_to_all(jnp.repeat(to_chips, sharers, axis=0), CHIPS, 0, 0, tiled=True)
+    grad_attended = grad_attended.reshape(-1, HD)
+
+    joined_mine, joined_other = out_grad(
+        jnp.stack(plane_members()), merged, branch_grad, ffn_mine, ffn_other, depth
+    )
+    joined = joined_mine.astype(f32) + swap(joined_other, "core").astype(f32)
+    joined = joined.reshape(4, BLOCK, 2 * D)
+    to_x = jnp.concatenate([joined[1], joined[3]], axis=0).astype(bf16)
+    grad_attended, to_x = lax.optimization_barrier((grad_attended, to_x))
+    from_x = swap(to_x, "hx")
 
     query_grad, own_grad, other_grad, bias_grad = attend_back(
         order, place, low, high, query, own_kv, other_kv, mask, hot, kept, grad_attended
     )
-    grad_project, grad_qkv_part, gain_grad = project_back(
-        query_grad, own_grad, swap(other_grad, "core"), raw, cosine, sine, gains, normed_low
-    )
-    qkv_full = lax.all_gather(
-        by_head.transpose(0, 2, 1, 3).reshape(rows, 3 * D), DEVICES, axis=0, tiled=True
-    )
-    grad_rows = lax.all_to_all(
-        grad_project.reshape(chips, BLOCK, 3 * HD), CHIPS, 0, 0, tiled=True
-    ).reshape(H, sharers, BLOCK, 3 * HD)
-    grad_rows, grad_qkv_part = lax.optimization_barrier((grad_rows, grad_qkv_part))
-    grad_qkv = lax.all_to_all(
-        grad_qkv_part.reshape(devices, rows, 3 * HD), DEVICES, 0, 0, tiled=True
-    )
-    grad_qkv = jnp.sum(grad_qkv.reshape(H, 2 * sharers, rows, 3, HD).astype(f32), axis=1)
-    grad_qkv = grad_qkv.transpose(1, 2, 0, 3).reshape(rows, 3 * D)
-    if sharers == 1:
-        grad_rows = grad_rows[:, 0]
-    else:
-        grad_rows = jnp.sum(grad_rows.astype(f32), axis=1).astype(bf16)
-    grad_rows = grad_rows.transpose(1, 0, 2).reshape(BLOCK, 3 * D)
-    grad_normed = dot(grad_rows, qkv_full, ((1,), (1,)))
-    grad_first, grad_attn_rows = norm_back(residual, attn_gain, grad_normed)
-    grad_inputs = grad_middle + grad_first
+    query_grad, from_x, feed_grad = lax.optimization_barrier((query_grad, from_x, feed_grad))
+    from_x = from_x.astype(f32)
+    from_y = swap((joined[2] + from_x[BLOCK:]).astype(bf16), "by")
+    expand_grad = lax.all_to_all(
+        feed_grad[: 8 * rows].reshape(8, rows, -1), PLANE, 0, 0, tiled=True
+    )
+    grad_project, grad_qkv_part, gain_grad, attn_grad = project_back(
+        query_grad,
+        own_grad,
+        swap(other_grad, "core"),
+        raw,
+        cosine,
+        sine,
+        gains,
+        normed_low,
+        own_qkv,
+    )
+    grad_qkv_part, from_y, expand_grad = lax.optimization_barrier(
+        (grad_qkv_part, from_y, expand_grad)
+    )
+    joined = joined[0] + from_x[:BLOCK] + from_y.astype(f32)
+    ffn_branch = joined[:, :D]
+    outputs = (middle + ffn_branch).astype(bf16)
+    grad_out = lax.psum_scatter(joined[:, D:].astype(bf16), "bz", scatter_dimension=0, tiled=True)
+    grad_out = grad_out.astype(f32)
+    grad_qkv_part = grad_qkv_part.reshape(chips, 2, rows, 3 * HD)
+    grad_qkv_own = lax.dynamic_index_in_dim(grad_qkv_part, core, 1, keepdims=False)
+    grad_qkv_other = lax.dynamic_index_in_dim(grad_qkv_part, 1 - core, 1, keepdims=False)
+    grad_qkv_own = grad_qkv_own.astype(f32) + swap(grad_qkv_other, "core").astype(f32)
+    joined = jnp.concatenate(
+        [grad_project.reshape(chips, BLOCK, 3 * HD), grad_qkv_own.astype(bf16)], axis=1
+    )
 
     bias_part = jnp.where(
         jnp.arange(H)[None, :] == head, bias_grad[0, :2][:, None], jnp.zeros((2, H), f32)
     )
-    squares = jnp.stack(
-        [
-            jnp.sum(residual * residual),
-            jnp.sum(attn_branch * attn_branch),
-            jnp.sum(ffn_branch * ffn_branch),
-        ]
-    )
     packed = jnp.concatenate(
         [
-            jnp.sum(grad_attn_rows, axis=0),
-            jnp.sum(grad_ffn_rows, axis=0),
+            attn_grad[:, 0] / attn_gain,
+            grad_ffn[0],
             gain_grad[0],
             bias_part.reshape(-1),
-            squares,
+            squares[:2, 0],
+            jnp.sum(ffn_branch * ffn_branch)[None],
             jnp.zeros((93,), f32),
         ]
     )
-    summed = sum_everywhere(packed, devices)
+    joined, packed = lax.optimization_barrier((joined, packed))
+    joined = lax.all_to_all(joined, CHIPS, 0, 0, tiled=True)
+    summed = sum_everywhere(packed.reshape(-1, 128))
+    grad_down = feed_grad[8 * rows :].astype(f32)
+    grad_expand = widen(expand_grad, depth, hidden_rows)
+    joined, summed, grad_down, grad_expand = lax.optimization_barrier(
+        (joined, summed, grad_down, grad_expand)
+    )
+    joined = over_sharers(joined, sharers)
+    grad_inputs, grad_qkv = input_back(joined, qkv_full, inputs, attn_gain[None], grad_middle)
+    summed = summed.reshape(-1)
     at = 2 * D + 2 * HD
     root_means = jnp.sqrt(summed[at + 2 * H : at + 2 * H + 3] / (tokens * D))
     return (
@@ -809,6 +993,7 @@
     heads, blks = grid.shape
     mesh = Mesh(grid.reshape(heads // 2, 2, blks // 2, 2), ("hx", "core", "bz", "by"))
     split = P(DEVICES, None)
+
     return jax.shard_map(
         body,
         mesh=mesh,

time: 437 us -> 446 us (1.021)
  Pallas kernels: 112 us -> 126 us
  waiting for transfers between devices: 138 us -> 130 us
  matrix products: 7.89 us -> 0 us
  other arithmetic: 30.9 us -> 37.2 us
  starting transfers between devices: 68.5 us -> 63 us
  blocking collectives: 15.7 us -> 21 us
    all_gather x1, waiting for transfers between devices: 0.01 us -> 40.1 us  [body(): qkv_full = lax.all_gather(late_qkv, DEVICES, axis=0, tiled=True)]
    all_to_all x3 -> x1, waiting for transfers between devices: 39 us -> 0.01 us  [body(): joined = lax.all_to_all(joined, CHIPS, 0, 0, tiled=True)]
    pallas_call x0 -> x5, Pallas kernels: none -> 21.6 us  [the longest x1 6.59 us: input_back(): pl.pallas_call(input_back_kernel, out_shape=[jax.ShapeDtypeStruct((rows,...]
    ppermute x35 -> x28, waiting for transfers between devices: 71.4 us -> 54.9 us  [swap(): return lax.ppermute(shard, axis, [(0, 1), (1, 0)])]
    ppermute x0 -> x2, waiting for transfers between devices: none -> 15.9 us  [sum_everywhere(): lax.ppermute(values, 'bz', [(i, i ^ step) for i in range(depth)])]
    all_to_all x1, waiting for transfers between devices: 0.01 us -> 12 us  [body(): lax.all_to_all(attended.reshape(chips, BLOCK, HD), CHIPS, 0, 0, tiled=True)]
    dot_general x4 -> x0, matrix products: 7.89 us -> none  [the longest x3 6.65 us: dot(): lax.dot_general(left, right, (dims, ((), ())), preferred_element_type=f32)]
    ppermute x35 -> x28, starting transfers between devices: 33.1 us -> 25.4 us  [swap(): return lax.ppermute(shard, axis, [(0, 1), (1, 0)])]
  transfers between devices with their start and end apart: 50 -> 43, of which waited for: 34 -> 24; matrix products, arithmetic and copies ran while one was open for 19% -> 19% of each run, Pallas kernels for 26% -> 23%
where the time goes in v3:
time: 446 us; the launch traced here: 444 us
  waiting for transfers between devices  130 us (29%)
  Pallas kernels  126 us (28%)
  starting transfers between devices  63 us (14%)
  local copies, waits for them, and re-layouts  52.6 us (12%)
  other arithmetic  37.2 us (8%)
  blocking collectives  21 us (5%)
  between operations  14.4 us (3%)
    ppermute x28, waiting for transfers between devices, swap(): return lax.ppermute(shard, axis, [(0, 1), (1, 0)])  54.9 us
    pallas_call x1, Pallas kernels, attend_back(): pl.pallas_call(attend_back_kernel, grid_spec=pltpu.PrefetchScalarGridSpec...  41.1 us
    all_gather x1, waiting for transfers between devices, body(): qkv_full = lax.all_gather(late_qkv, DEVICES, axis=0, tiled=True)  40.1 us
    pallas_call x1, Pallas kernels, attend(): pl.pallas_call(attend_kernel, grid_spec=pltpu.PrefetchScalarGridSpec(num_...  26.4 us
    ppermute x28, starting transfers between devices, swap(): return lax.ppermute(shard, axis, [(0, 1), (1, 0)])  25.4 us
    all_to_all x1, blocking collectives, body(): lax.all_to_all(jnp.repeat(to_chips, sharers, axis=0), CHIPS, 0, 0, tiled=...  21 us
    pallas_call x1, Pallas kernels, feed(): pl.pallas_call(feed_kernel, grid=(2 * steps,), in_specs=[mine, other, min...  17.6 us
    unnamed x66, local copies, waits for them, and re-layouts  16.7 us
  transfers between devices with their start and end apart: 43, of which 24 were waited for; matrix products, arithmetic and copies ran while one was open for 19% of the time, Pallas kernels for 23%

profile of v3, /device:TPU:0, one launch (start us, length us, event | category | flops | bytes accessed | tf_op | source)
XLA Modules:
  0.0 444.1 jit_solution(15681896726029742430)
XLA Ops:
  29.7 4.6 %fusion.3.refs_9_.hot_ref = bf16[4096,128]{1,0:T(8,128)(2,1)} fusion(s32[4096]{0:T(1024)S(1)} %get-tuple-element.176, s32[4096]{0:T(1024)S(1)} %get-tuple-element.175, s32[4096]{0:T(1024)S(1)} %get-tuple-element.174, s32[4096]{0:T(1024)S(1)} %get-tuple-element.178), kind=kLoop, calls=%fused_computation.10 | loop fusion | flops 4194304 | bytes 1114112 | tf_op jit(solution)/shard_map/convert_element_type | solution.py:769
  34.3 6.4 %select_convert_fusion.mask_ref = bf16[4096,128]{1,0:T(8,128)(2,1)} fusion(s32[128]{0:T(128)S(1)} %get-tuple-element.208, bf16[]{:T(256)} %bitcast.14, bf16[]{:T(256)} %bitcast.13, s32[128]{0:T(128)S(1)} %get-tuple-element.209, bf16[]{:T(256)} %bitcast.12, bf16[]{:T(256)} %bitcast.11, s32[128]{0:T(128)S(1)} %get-tuple-element.210, bf16[]{:T(256)} %bitcast.10, ...), kind=kLoop, calls=%fused_computation.2 | loop fusion | flops 6291456 | bytes 1083916 | tf_op jit(solution)/shard_map/convert_element_type | solution.py:785
  49.1 4.0 collective-permute-done.5
  68.0 17.0 %collective-permute-done.7 = bf16[384,1024]{1,0:T(8,128)(2,1)} collective-permute-done((bf16[384,1024]{1,0:T(8,128)(2,1)}, bf16[384,1024]{1,0:T(8,128)(2,1)}, u32[]{:S(2)}, u32[]{:S(2)}) %collective-permute-start.7) | collective-permute-done | bytes 786464 | tf_op jit(solution)/shard_map/ppermute | solution.py:53
  105.6 8.5 %project.1 = (bf16[2048,1024]{1,0:T(8,128)(2,1)}, f32[2048,128]{1,0:T(8,128)}, bf16[2048,128]{1,0:T(8,128)(2,1)}, bf16[2048,128]{1,0:T(8,128)(2,1)}) custom-call(s32[16]{0:T(128)} %compare_select_fusion.5.where_ref, bf16[16,128,1024]{2,1,0:T(8,128)(2,1)} %bitcast.77, bf16[16,128,1024]{2,1,0:T(8,128)(2,1)} %bitcast.78, bf16[16,128,1024]{2,1,0:T(8,128)(2,1)} %bitcast.79, ...), custom_call_target="tpu_custom_call" | custom-call | tf_op jit(solution)/shard_map/project/pallas_call | solution.py:173
  117.1 26.4 %attend.1 = (f32[2048,128]{1,0:T(8,128)}, bf16[2048,64]{1,0:T(8,128)(2,1)}) custom-call(s32[16]{0:T(128)} %get-tuple-element.74.order_ref, s32[32]{0:T(128)} %pad_add_fusion.2.place_ref, s32[8]{0:T(128)} %get-tuple-element.76.low_ref, s32[8]{0:T(128)} %get-tuple-element.77.high_ref, bf16[2048,128]{1,0:T(8,128)(2,1)} %get-tuple-element.86.query_ref, ...), custom_call_target="tpu_custom_call" | custom-call | tf_op jit(solution)/shard_map/attend/pallas_call | solution.py:283
  145.4 5.6 %all-to-all-start.2 = ((bf16[16,128,64]{1,2,0:T(8,128)(2,1)}), bf16[16,128,64]{1,2,0:T(8,128)(2,1)S(1)}, u32[]{:S(2)}, u32[]{:S(2)}) async-start(bf16[16,128,64]{1,2,0:T(8,128)(2,1)} %copy.51), calls=%async_computation.2 | async-start | bytes 524288 | tf_op jit(solution)/shard_map/all_to_all | solution.py:884
  153.3 12.0 %all-to-all-done.2 = bf16[16,128,64]{1,2,0:T(8,128)(2,1)S(1)} async-done(((bf16[16,128,64]{1,2,0:T(8,128)(2,1)}), bf16[16,128,64]{1,2,0:T(8,128)(2,1)S(1)}, u32[]{:S(2)}, u32[]{:S(2)}) %all-to-all-start.2) | async-done | bytes 262176 | tf_op jit(solution)/shard_map/all_to_all | solution.py:884
  171.8 5.4 %collective-permute-done.12 = bf16[128,1024]{1,0:T(8,128)(2,1)S(1)} collective-permute-done((bf16[128,1024]{1,0:T(8,128)(2,1)}, bf16[128,1024]{1,0:T(8,128)(2,1)S(1)}, u32[]{:S(2)}, u32[]{:S(2)}) %collective-permute-start.12) | collective-permute-done | bytes 262176 | tf_op jit(solution)/shard_map/ppermute | solution.py:53
  186.9 17.6 %feed.1 = (bf16[512,1024]{1,0:T(8,128)(2,1)}, bf16[512,1024]{1,0:T(8,128)(2,1)}, bf16[512,1024]{1,0:T(8,128)(2,1)}, bf16[512,1024]{1,0:T(8,128)(2,1)}, bf16[4,384,1024]{2,1,0:T(8,128)(2,1)}) custom-call(bf16[512,1024]{1,0:T(8,128)(2,1)} %copy-done.9, bf16[512,1024]{1,0:T(8,128)(2,1)} %collective-permute-done.15.second_other_ref, ...), custom_call_target="tpu_custom_call" | custom-call | tf_op jit(solution)/shard_map/feed/pallas_call | solution.py:560
  227.1 4.2 middle_back.1
  231.3 5.4 %out_grad.1 = (bf16[512,2048]{1,0:T(8,128)(2,1)}, bf16[512,2048]{1,0:T(8,128)(2,1)}) custom-call(s32[8]{0:T(128)} %stack.35.members_ref, bf16[128,1024]{1,0:T(8,128)(2,1)} %get-tuple-element.92.merged_ref, bf16[128,1024]{1,0:T(8,128)(2,1)} %get-tuple-element.97.branch_ref, bf16[512,1024]{1,0:T(8,128)(2,1)} %get-tuple-element.99.ffn_mine_ref, ...), custom_call_target="tpu_custom_call" | custom-call | tf_op jit(solution)/shard_map/out_grad/pallas_call | solution.py:677
  236.9 21.0 %all_to_all.30 = bf16[16,128,64]{1,2,0:T(8,128)(2,1)S(1)} all-to-all(bf16[16,128,64]{1,2,0:T(8,128)(2,1)S(1)} %copy.54), channel_id=1, replica_groups=mesh['hx'=2,'core'=2,'bz'=4,'by'=2] {'bz','by','hx'}, dimensions={0} | all-to-all | bytes 524288 | tf_op jit(solution)/shard_map/all_to_all | solution.py:900
  258.9 4.6 %convert_add_fusion = (f32[512,2048]{1,0:T(8,128)}, bf16[512,2048]{1,0:T(8,128)(2,1)S(1)}) fusion(bf16[512,2048]{1,0:T(8,128)(2,1)} %collective-permute-done.23, bf16[512,2048]{1,0:T(8,128)(2,1)S(1)} %copy-done.5), kind=kLoop, calls=%fused_computation | loop fusion | flops 4194304 | bytes 10485760 | tf_op jit(solution)/shard_map/add | solution.py:906
  265.1 41.1 %attend_back.1 = (f32[2048,128]{1,0:T(8,128)}, f32[2048,128]{1,0:T(8,128)}, f32[2048,128]{1,0:T(8,128)}, f32[8,128]{1,0:T(8,128)}) custom-call(s32[16]{0:T(128)} %get-tuple-element.74.order_ref, s32[32]{0:T(128)} %pad_add_fusion.2.place_ref, s32[8]{0:T(128)} %get-tuple-element.76.low_ref, s32[8]{0:T(128)} %get-tuple-element.77.high_ref, ...), custom_call_target="tpu_custom_call" | custom-call | tf_op jit(solution)/shard_map/attend_back/pallas_call | solution.py:396
  309.6 3.7 all-to-all-start.4
  313.4 10.3 %project_back.1 = (bf16[2048,192]{1,0:T(8,128)(2,1)}, bf16[1024,192]{1,0:T(8,128)(2,1)}, f32[8,128]{1,0:T(8,128)}, f32[1024,128]{1,0:T(8,128)}) custom-call(f32[2048,128]{1,0:T(8,128)} %get-tuple-element.110.query_grad_ref, f32[2048,128]{1,0:T(8,128)} %get-tuple-element.111.own_ref, f32[2048,128]{1,0:T(8,128)} %collective-permute-done.25.other_ref, ...), custom_call_target="tpu_custom_call" | custom-call | tf_op jit(solution)/shard_map/project_back/pallas_call | solution.py:468
  323.8 4.2 all-to-all-done.4.parts_ref
  341.8 8.2 %all-to-all-start.5 = ((bf16[16,160,192]{2,1,0:T(8,128)(2,1)}), bf16[16,160,192]{2,1,0:T(8,128)(2,1)S(1)}, u32[]{:S(2)}, u32[]{:S(2)}) async-start(bf16[16,160,192]{2,1,0:T(8,128)(2,1)} %pad_maximum_fusion), calls=%async_computation.6 | async-start | bytes 2621440 | tf_op jit(solution)/shard_map/all_to_all | solution.py:963
  353.2 3.6 collective-permute-done.29
  362.0 13.2 %collective-permute-done.31 = f32[18,128]{1,0:T(8,128)S(1)} collective-permute-done((f32[18,128]{1,0:T(8,128)S(1)}, f32[18,128]{1,0:T(8,128)S(1)}, u32[]{:S(2)}, u32[]{:S(2)}) %collective-permute-start.31) | collective-permute-done | bytes 9248 | tf_op jit(solution)/shard_map/ppermute | solution.py:92
  375.2 5.0 %collective-permute-start.32 = (f32[18,128]{1,0:T(8,128)S(1)}, f32[18,128]{1,0:T(8,128)S(1)}, u32[]{:S(2)}, u32[]{:S(2)}) collective-permute-start(f32[18,128]{1,0:T(8,128)S(1)} %add.306), channel_id=1, source_target_pairs={{0,4},{2,6},{4,0},{6,2},{1,5},{3,7},{5,1},{7,3},{8,12},{10,14},{12... | collective-permute-start | bytes 27656 | tf_op jit(solution)/shard_map/ppermute | solution.py:92
  390.9 40.1 %all-gather.7.cloned.1.call-done.weight_ref = bf16[1024,3072]{1,0:T(8,128)(2,1)} async-done(((bf16[32,3072]{1,0:T(8,128)(2,1)}), bf16[1024,3072]{1,0:T(8,128)(2,1)}) %all-gather.7.cloned.1.call-update) | async-done | bytes 6291472 | tf_op jit(solution)/shard_map/all_gather | solution.py:896
  431.0 6.6 %input_back.1 = (f32[128,1024]{1,0:T(8,128)}, f32[32,3072]{1,0:T(8,128)}) custom-call(bf16[16,160,192]{2,1,0:T(8,128)(2,1)} %copy-done.2, bf16[1024,3072]{1,0:T(8,128)(2,1)} %all-gather.7.cloned.1.call-done.weight_ref, bf16[128,1024]{1,0:T(8,128)(2,1)} %x_ref.3, f32[1,1024]{1,0:T(1,128)} %bitcast.104, f32[128,1024]{1,0:T(8,128)} %get-tuple-element.130.middle_ref), custom_call_target="tpu_custom_call" | custom-call | tf_op jit(solution)/shard_map/input_back/pallas_call | solution.py:715
  (249 shorter events, 150.8 us)
Async XLA Ops:
  7.2 41.7 %collective-permute-start = (bf16[128,1024]{1,0:T(8,128)(2,1)}, bf16[128,1024]{1,0:T(8,128)(2,1)}, u32[]{:S(2)}, u32[]{:S(2)}) collective-permute-start(bf16[128,1024]{1,0:T(8,128)(2,1)} %x_ref.3), channel_id=1, source_target_pairs={{0,2},{2,4},{4,6},{6,0},{1,3},{3,5},{5,7},{7,1},{8,10},{10,12},{12... | collective-permute-start | bytes 786440 | tf_op jit(solution)/shard_map/ppermute | solution.py:71
  10.3 38.6 %collective-permute-start.1 = (bf16[128,1024]{1,0:T(8,128)(2,1)}, bf16[128,1024]{1,0:T(8,128)(2,1)}, u32[]{:S(2)}, u32[]{:S(2)}) collective-permute-start(bf16[128,1024]{1,0:T(8,128)(2,1)} %x_ref.3), channel_id=1, source_target_pairs={{0,4},{2,6},{4,0},{6,2},{1,5},{3,7},{5,1},{7,3},{8,12},{10,14},{12... | collective-permute-start | bytes 786440 | tf_op jit(solution)/shard_map/ppermute | solution.py:71
  12.9 36.0 %collective-permute-start.2 = (bf16[128,1024]{1,0:T(8,128)(2,1)}, bf16[128,1024]{1,0:T(8,128)(2,1)}, u32[]{:S(2)}, u32[]{:S(2)}) collective-permute-start(bf16[128,1024]{1,0:T(8,128)(2,1)} %x_ref.3), channel_id=1, source_target_pairs={{0,6},{2,0},{4,2},{6,4},{1,7},{3,1},{5,3},{7,5},{8,14},{10,8},{12,... | collective-permute-start | bytes 786440 | tf_op jit(solution)/shard_map/ppermute | solution.py:71
  17.0 26.2 %collective-permute-start.4 = (bf16[256,1024]{1,0:T(8,128)(2,1)S(1)}, bf16[256,1024]{1,0:T(8,128)(2,1)S(1)}, u32[]{:S(2)}, u32[]{:S(2)}) collective-permute-start(bf16[256,1024]{1,0:T(8,128)(2,1)S(1)} %constant_dynamic-update-slice_fusion), channel_id=1, source_target_pairs={{0,1},{1,0},{2,3},{3,2},{4,5},{5,4},{6,7},{7,6},{8,9},{9,8},{10,11... | collective-permute-start | bytes 1572872 | tf_op jit(solution)/shard_map/ppermute | solution.py:53
  18.6 23.8 %collective-permute-start.3 = (bf16[256,1024]{1,0:T(8,128)(2,1)S(1)}, bf16[256,1024]{1,0:T(8,128)(2,1)S(1)}, u32[]{:S(2)}, u32[]{:S(2)}) collective-permute-start(bf16[256,1024]{1,0:T(8,128)(2,1)S(1)} %constant_dynamic-update-slice_fusion), channel_id=1, source_target_pairs={{0,16},{16,0},{1,17},{17,1},{2,18},{18,2},{3,19},{19,3},{4,20},{20... | collective-permute-start | bytes 1572872 | tf_op jit(solution)/shard_map/ppermute | solution.py:53
  22.8 25.2 %all-to-all-start = ((bf16[32,32,192]{2,1,0:T(8,128)(2,1)}), bf16[32,32,192]{2,1,0:T(8,128)(2,1)S(1)}, u32[]{:S(2)}, u32[]{:S(2)}) async-start(bf16[32,32,192]{2,1,0:T(8,128)(2,1)} %bitcast.20), calls=%async_computation | async-start | bytes 1048576 | tf_op jit(solution)/shard_map/all_to_all | solution.py:829
  25.4 76.4 %all-gather.5.cloned.1.call-start = ((), (), s32[]{:S(2)}) async-start(), calls=%async_computation.8 | async-start | bytes 2162688 | tf_op jit(solution)/shard_map/all_gather | solution.py:823
  60.2 24.8 %collective-permute-start.7 = (bf16[384,1024]{1,0:T(8,128)(2,1)}, bf16[384,1024]{1,0:T(8,128)(2,1)}, u32[]{:S(2)}, u32[]{:S(2)}) collective-permute-start(bf16[384,1024]{1,0:T(8,128)(2,1)} %get-tuple-element.165), channel_id=1, source_target_pairs={{0,1},{1,0},{2,3},{3,2},{4,5},{5,4},{6,7},{7,6},{8,9},{9,8},{10,11... | collective-permute-start | bytes 2359304 | tf_op jit(solution)/shard_map/ppermute | solution.py:53
  61.6 26.6 %collective-permute-start.6 = (bf16[384,1024]{1,0:T(8,128)(2,1)}, bf16[384,1024]{1,0:T(8,128)(2,1)}, u32[]{:S(2)}, u32[]{:S(2)}) collective-permute-start(bf16[384,1024]{1,0:T(8,128)(2,1)} %get-tuple-element.165), channel_id=1, source_target_pairs={{0,16},{16,0},{1,17},{17,1},{2,18},{18,2},{3,19},{19,3},{4,20},{20... | collective-permute-start | bytes 2359304 | tf_op jit(solution)/shard_map/ppermute | solution.py:53
  64.4 27.2 %all-to-all-start.1 = ((bf16[8,32,1024]{2,1,0:T(8,128)(2,1)}), bf16[8,32,1024]{2,1,0:T(8,128)(2,1)S(1)}, u32[]{:S(2)}, u32[]{:S(2)}) async-start(bf16[8,32,1024]{2,1,0:T(8,128)(2,1)} %reshape.348), calls=%async_computation.1 | async-start | bytes 1048576 | tf_op jit(solution)/shard_map/all_to_all | solution.py:836
  67.9 119.0 %all-gather.9.cloned.1.call-start = ((), (), s32[]{:S(2)}) async-start(), calls=%async_computation.12 | async-start | bytes 3932160 | tf_op jit(solution)/shard_map/all_gather | solution.py:876
  145.4 19.9 %all-to-all-start.2 = ((bf16[16,128,64]{1,2,0:T(8,128)(2,1)}), bf16[16,128,64]{1,2,0:T(8,128)(2,1)S(1)}, u32[]{:S(2)}, u32[]{:S(2)}) async-start(bf16[16,128,64]{1,2,0:T(8,128)(2,1)} %copy.51), calls=%async_computation.2 | async-start | bytes 524288 | tf_op jit(solution)/shard_map/all_to_all | solution.py:884
  151.0 155.2 %reduce-scatter.3.cloned.1.call-start = ((), (), s32[]{:S(2)}) async-start(), calls=%async_computation.9 | async-start | bytes 3932160 | tf_op jit(solution)/shard_map/reduce_scatter | solution.py:892
  151.3 20.3 %collective-permute-start.16 = (bf16[128,1024]{1,0:T(8,128)(2,1)S(1)}, bf16[128,1024]{1,0:T(8,128)(2,1)S(1)}, u32[]{:S(2)}, u32[]{:S(2)}) collective-permute-start(bf16[128,1024]{1,0:T(8,128)(2,1)S(1)} %get-tuple-element.163), channel_id=1, source_target_pairs={{0,1},{1,0},{2,3},{3,2},{4,5},{5,4},{6,7},{7,6},{8,9},{9,8},{10,11... | collective-permute-start | bytes 786440 | tf_op jit(solution)/shard_map/ppermute | solution.py:53
  171.6 12.5 %collective-permute-start.17 = (bf16[512,1024]{1,0:T(8,128)(2,1)S(1)}, bf16[512,1024]{1,0:T(8,128)(2,1)S(1)}, u32[]{:S(2)}, u32[]{:S(2)}) collective-permute-start(bf16[512,1024]{1,0:T(8,128)(2,1)S(1)} %pad_maximum_fusion.1.grad_mine_ref), channel_id=1, source_target_pairs={{0,8},{8,0},{1,9},{9,1},{2,10},{10,2},{3,11},{11,3},{4,12},{12,4},... | collective-permute-start | bytes 3145736 | tf_op jit(solution)/shard_map/ppermute | solution.py:53
  236.6 22.2 %collective-permute-start.23 = (bf16[512,2048]{1,0:T(8,128)(2,1)}, bf16[512,2048]{1,0:T(8,128)(2,1)}, u32[]{:S(2)}, u32[]{:S(2)}) collective-permute-start(bf16[512,2048]{1,0:T(8,128)(2,1)} %get-tuple-element.102), channel_id=1, source_target_pairs={{0,8},{8,0},{1,9},{9,1},{2,10},{10,2},{3,11},{11,3},{4,12},{12,4},... | collective-permute-start | bytes 6291464 | tf_op jit(solution)/shard_map/ppermute | solution.py:53
  263.6 42.6 %collective-permute-start.24 = (bf16[256,2048]{1,0:T(8,128)(2,1)S(1)}, bf16[256,2048]{1,0:T(8,128)(2,1)S(1)}, u32[]{:S(2)}, u32[]{:S(2)}) collective-permute-start(bf16[256,2048]{1,0:T(8,128)(2,1)S(1)} %pad_maximum_fusion.2), channel_id=1, source_target_pairs={{0,16},{16,0},{1,17},{17,1},{2,18},{18,2},{3,19},{19,3},{4,20},{20... | collective-permute-start | bytes 3145736 | tf_op jit(solution)/shard_map/ppermute | solution.py:53
  308.0 20.0 %collective-permute-start.26 = (bf16[128,2048]{1,0:T(8,128)(2,1)S(1)}, bf16[128,2048]{1,0:T(8,128)(2,1)}, u32[]{:S(2)}, u32[]{:S(2)}) collective-permute-start(bf16[128,2048]{1,0:T(8,128)(2,1)S(1)} %fusion.4), channel_id=1, source_target_pairs={{0,1},{1,0},{2,3},{3,2},{4,5},{5,4},{6,7},{7,6},{8,9},{9,8},{10,11... | collective-permute-start | bytes 1572872 | tf_op jit(solution)/shard_map/ppermute | solution.py:53
  309.6 18.4 %all-to-all-start.4 = ((bf16[8,32,1024]{2,1,0:T(8,128)(2,1)}), bf16[8,32,1024]{2,1,0:T(8,128)(2,1)S(1)}, u32[]{:S(2)}, u32[]{:S(2)}) async-start(bf16[8,32,1024]{2,1,0:T(8,128)(2,1)} %bitcast.41), calls=%async_computation.5 | async-start | bytes 1048576 | tf_op jit(solution)/shard_map/all_to_all | solution.py:918
  313.4 73.5 %reduce-scatter.5.cloned.1.call-start = ((), (), s32[]{:S(2)}) async-start(), calls=%async_computation.11 | async-start | bytes 327680 | tf_op jit(solution)/shard_map/reduce_scatter | solution.py:938
  331.2 99.7 %all-gather.7.cloned.1.call-start = ((), (), s32[]{:S(2)}) async-start(), calls=%async_computation.10 | async-start | bytes 6488064 | tf_op jit(solution)/shard_map/all_gather | solution.py:896
  341.8 46.5 %all-to-all-start.5 = ((bf16[16,160,192]{2,1,0:T(8,128)(2,1)}), bf16[16,160,192]{2,1,0:T(8,128)(2,1)S(1)}, u32[]{:S(2)}, u32[]{:S(2)}) async-start(bf16[16,160,192]{2,1,0:T(8,128)(2,1)} %pad_maximum_fusion), calls=%async_computation.6 | async-start | bytes 2621440 | tf_op jit(solution)/shard_map/all_to_all | solution.py:963
  360.5 14.7 %collective-permute-start.31 = (f32[18,128]{1,0:T(8,128)S(1)}, f32[18,128]{1,0:T(8,128)S(1)}, u32[]{:S(2)}, u32[]{:S(2)}) collective-permute-start(f32[18,128]{1,0:T(8,128)S(1)} %add.305), channel_id=1, source_target_pairs={{0,2},{2,0},{4,6},{6,4},{1,3},{3,1},{5,7},{7,5},{8,10},{10,8},{12,... | collective-permute-start | bytes 27656 | tf_op jit(solution)/shard_map/ppermute | solution.py:92
  375.2 11.6 %collective-permute-start.32 = (f32[18,128]{1,0:T(8,128)S(1)}, f32[18,128]{1,0:T(8,128)S(1)}, u32[]{:S(2)}, u32[]{:S(2)}) collective-permute-start(f32[18,128]{1,0:T(8,128)S(1)} %add.306), channel_id=1, source_target_pairs={{0,4},{2,6},{4,0},{6,2},{1,5},{3,7},{5,1},{7,3},{8,12},{10,14},{12... | collective-permute-start | bytes 27656 | tf_op jit(solution)/shard_map/ppermute | solution.py:92
  (46 other events, 356.0 us)
Sparse Core Ops, SparseCore 0:
  29.0 60.3 all-gather.4
  102.0 68.8 all-gather.8
  204.9 65.4 reduce-scatter.2
  331.4 22.7 reduce-scatter.4
  356.9 74.0 all-gather.6

commit v4 on v3

--- a/solution.py
+++ b/solution.py
@@ -23,9 +23,10 @@
 
 SEGMENT_LANE = 64
 VARIATE_LANE = 76
+OWN_VARIATE_LANE = 88
 MASK = -512.0
-QUERY_TILE = 256
-KEY_TILE = 256
+QUERY_TILE = 512
+KEY_TILE = 512
 PROJECT_BLOCKS = 4
 
 bf16 = jnp.bfloat16
@@ -58,29 +59,30 @@
     return mine, swap(mine, "core")
 
 
-def chip_gather(shard, rider, tables):
+def chip_gather(shard, rider, late):
     depth = lax.axis_size("bz")
     chips = depth * 4
-    rows = shard.shape[0]
     z, y, x = lax.axis_index("bz"), lax.axis_index("by"), lax.axis_index("hx")
     at = jnp.arange(chips, dtype=jnp.int32)
     if depth > 4:
-        gathered = lax.all_gather(shard, CHIPS, axis=0, tiled=True).reshape(chips, rows, D)
-        return gathered, at, jnp.concatenate(quarters(rider), axis=0), tables
-    shifted = [
+        pieces = lax.all_gather(shard, CHIPS, axis=0)
+        return list(pieces), at, (swap(rider, "hx"), swap(rider, "by")), late
+    column = [
         lax.ppermute(shard, "bz", [(i, (i + by) % depth) for i in range(depth)])
         for by in range(1, depth)
     ]
-    near = quarters(jnp.concatenate([shard, rider], axis=0))
-    shifted, tables = lax.optimization_barrier((shifted, tables))
-    pieces = [near[0][:rows], near[1][:rows], near[2][:rows], near[3]]
-    riders = [near[0][rows:], near[1][rows:], near[2][rows:], near[4]]
-    pieces = pieces + quarters(jnp.concatenate(shifted, axis=0))
+    across_x, across_y = [swap(shard, "hx")], [swap(shard, "by")]
+    across_x += [swap(piece, "hx") for piece in column]
+    across_y += [swap(piece, "by") for piece in column]
+    across_x, across_y, late = lax.optimization_barrier((across_x, across_y, late))
+    corner = [swap(across_x[i], "by") if i > 1 else swap(across_y[i], "hx") for i in range(depth)]
+    riders = swap(rider, "hx"), swap(rider, "by")
+    pieces = [shard, across_x[0], across_y[0], corner[0]]
+    pieces += column + across_x[1:] + across_y[1:] + corner[1:]
     back = (z - at // 4) % depth
     flips = ((at % 2) ^ x) + 2 * (((at // 2) % 2) ^ y)
     where = jnp.where(back == 0, flips, 4 + flips * (depth - 1) + back - 1).astype(jnp.int32)
-    gathered = jnp.concatenate(pieces, axis=0).reshape(chips, rows, D)
-    return gathered, where, jnp.concatenate(riders, axis=0), tables
+    return pieces, where, riders, late
 
 
 def sum_everywhere(values):
@@ -142,11 +144,26 @@
     )
 
 
-def project_kernel(where_ref, *refs):
-    x_refs = refs[:PROJECT_BLOCKS]
-    gain_ref, weight_ref, cosine_ref, sine_ref, gains_ref, hot_ref = refs[PROJECT_BLOCKS:-4]
-    normed_ref, raw_ref, query_ref, kv_ref = refs[-4:]
-    x = jnp.concatenate([x_ref[0] for x_ref in x_refs], axis=0).astype(f32)
+def project_kernel(where_ref, *refs, chips):
+    piece_refs, refs = refs[:chips], refs[chips:]
+    gain_ref, weight_ref, cosine_ref, sine_ref, gains_ref, hot_ref, mask_ref = refs[:7]
+    normed_ref, raw_ref, query_ref, kv_ref, out_ref, x_ref, arrived = refs[7:]
+    step = pl.program_id(0)
+
+    @pl.when(step == 0)
+    def _():
+        copies = [
+            pltpu.make_async_copy(piece_refs[i], x_ref.at[i], arrived.at[i]) for i in range(chips)
+        ]
+        for copy in copies:
+            copy.start()
+        for copy in copies:
+            copy.wait()
+
+    places = [where_ref[step * PROJECT_BLOCKS + i] for i in range(PROJECT_BLOCKS)]
+    for i, place in enumerate(places):
+        out_ref[i] = x_ref[place, BLOCK:]
+    x = jnp.concatenate([x_ref[place, :BLOCK] for place in places], axis=0).astype(f32)
     normed = norm_rows(x, gain_ref[...]).astype(bf16)
     normed_ref[...] = normed
     project = dot(normed, weight_ref[...], ((1,), (0,)))
@@ -158,72 +175,65 @@
     turned = scaled * cosine_ref[...] + swap_halves(scaled, lane) * sine_ref[...]
     turned = turned.astype(bf16).astype(f32)
     query_ref[...] = jnp.where(lane < HD, turned, hot_ref[...].astype(f32)).astype(bf16)
-    kv_ref[...] = jnp.where(lane < HD, value, turned * HD ** (-0.5)).astype(bf16)
-
-
-def project(where, gathered, gain, weight, cosine, sine, gains, hot):
-    blocks = gathered.shape[0]
+    key = pltpu.roll(turned * HD ** (-0.5), HD, 1)
+    ones = jnp.where((lane >= HD) & (lane < HD + 3), 1.0, 0.0)
+    kv_ref[:, :128] = jnp.where(lane < HD, key, mask_ref[...].astype(f32)).astype(bf16)
+    kv_ref[:, 128:] = jnp.where(lane < HD, value, ones).astype(bf16)
+
+
+def project(where, pieces, gain, weight, cosine, sine, gains, hot, mask):
+    blocks = len(pieces)
     rows = blocks * BLOCK
     step_rows = PROJECT_BLOCKS * BLOCK
-    row_spec = lambda width: pl.BlockSpec((step_rows, width), lambda j, where: (j, 0))
-    whole = lambda array: pl.BlockSpec(array.shape, lambda j, where: (0, 0))
-    block = lambda i: pl.BlockSpec(
-        (1, BLOCK, D), lambda j, where: (where[j * PROJECT_BLOCKS + i], 0, 0)
-    )
+    out_rows = pieces[0].shape[0] - BLOCK
+    row_spec = lambda width: pl.BlockSpec((step_rows, width), lambda j, *unused: (j, 0))
+    whole = lambda array: pl.BlockSpec(array.shape, lambda j, *unused: (0, 0))
+    anywhere = pl.BlockSpec(memory_space=pl.ANY)
+    tables = [whole(gain), whole(weight), row_spec(128), row_spec(128), whole(gains)]
     return pl.pallas_call(
-        project_kernel,
+        partial(project_kernel, chips=blocks),
         grid_spec=pltpu.PrefetchScalarGridSpec(
             num_scalar_prefetch=1,
             grid=(blocks // PROJECT_BLOCKS,),
-            in_specs=[block(i) for i in range(PROJECT_BLOCKS)]
-            + [
-                whole(gain),
-                whole(weight),
+            in_specs=[anywhere] * blocks + tables + [row_spec(128), row_spec(128)],
+            out_specs=[
+                row_spec(D),
                 row_spec(128),
                 row_spec(128),
-                whole(gains),
-                row_spec(128),
+                row_spec(256),
+                pl.BlockSpec((PROJECT_BLOCKS, out_rows, D), lambda j, *unused: (j, 0, 0)),
             ],
-            out_specs=[row_spec(D), row_spec(128), row_spec(128), row_spec(128)],
+            scratch_shapes=[
+                pltpu.VMEM((blocks, BLOCK + out_rows, D), bf16),
+                pltpu.SemaphoreType.DMA((blocks,)),
+            ],
         ),
         out_shape=[
             jax.ShapeDtypeStruct((rows, D), bf16),
             jax.ShapeDtypeStruct((rows, 128), f32),
             jax.ShapeDtypeStruct((rows, 128), bf16),
-            jax.ShapeDtypeStruct((rows, 128), bf16),
+            jax.ShapeDtypeStruct((rows, 256), bf16),
+            jax.ShapeDtypeStruct((blocks, out_rows, D), bf16),
         ],
         name="project",
-    )(where, *[gathered] * PROJECT_BLOCKS, gain, weight, cosine, sine, gains, hot)
-
-
-def sort_keys(place_ref, own_ref, other_ref, mask_ref, key_ref, value_ref):
+    )(where, *pieces, gain, weight, cosine, sine, gains, hot, mask)
+
+
+def sort_keys(place_ref, own_ref, other_ref, keys_ref):
     blocks = own_ref.shape[0] // BLOCK
-    lane = lanes((BLOCK, 128))
-    ones = jnp.where((lane >= HD) & (lane < HD + 3), 1.0, 0.0)
     for half, source_ref in ((0, own_ref), (1, other_ref)):
 
         def put(j, unused, half=half, source_ref=source_ref):
             source = pl.multiple_of(j * BLOCK, BLOCK)
-            tail = pl.multiple_of((half * blocks + j) * BLOCK, BLOCK)
             target = pl.multiple_of(place_ref[half * blocks + j] * BLOCK, BLOCK)
-            both = source_ref[pl.ds(source, BLOCK), :].astype(f32)
-            mask = mask_ref[pl.ds(tail, BLOCK), :].astype(f32)
-            key_ref[pl.ds(target, BLOCK), :] = jnp.where(
-                lane < HD, pltpu.roll(both, HD, 1), mask
-            ).astype(bf16)
-            value_ref[pl.ds(target, BLOCK), :] = jnp.where(lane < HD, both, ones).astype(bf16)
+            keys_ref[pl.ds(target, BLOCK), :] = source_ref[pl.ds(source, BLOCK), :]
             return unused
 
-        lax.fori_loop(0, blocks, put, 0)
-
-
-def tile_rows(order_ref, tile):
-    count = QUERY_TILE // BLOCK
-    return [pl.multiple_of(order_ref[tile * count + i] * BLOCK, BLOCK) for i in range(count)]
-
-
-def load_rows(ref, starts):
-    return jnp.concatenate([ref[pl.ds(start, BLOCK), :] for start in starts], axis=0)
+        lax.fori_loop(0, blocks, put, 0, unroll=4)
+
+
+def block_start(order_ref, index):
+    return pl.multiple_of(order_ref[index] * BLOCK, BLOCK)
 
 
 def attend_kernel(
@@ -234,29 +244,27 @@
     query_ref,
     own_ref,
     other_ref,
-    mask_ref,
     kept_ref,
     attended_ref,
-    key_ref,
-    value_ref,
+    keys_ref,
 ):
     tile = pl.program_id(0)
+    count = QUERY_TILE // BLOCK
 
     @pl.when(tile == 0)
     def _():
-        sort_keys(place_ref, own_ref, other_ref, mask_ref, key_ref, value_ref)
-        kept_ref[...] = jnp.zeros_like(kept_ref)
-        attended_ref[...] = jnp.zeros_like(attended_ref)
-
-    starts = tile_rows(order_ref, tile)
-    query = load_rows(query_ref, starts)
+        sort_keys(place_ref, own_ref, other_ref, keys_ref)
+        if order_ref.shape[0] * BLOCK != query_ref.shape[0]:
+            kept_ref[...] = jnp.zeros_like(kept_ref)
+            attended_ref[...] = jnp.zeros_like(attended_ref)
+
+    starts = [block_start(order_ref, tile * count + i) for i in range(count)]
+    query = jnp.concatenate([query_ref[pl.ds(start, BLOCK), :] for start in starts], axis=0)
 
     def chunk(index, accumulated):
-        first = pl.multiple_of(index * KEY_TILE, KEY_TILE)
-        key = key_ref[pl.ds(first, KEY_TILE), :]
-        value = value_ref[pl.ds(first, KEY_TILE), :]
-        expo = jnp.exp(dot(query, key, ((1,), (1,))))
-        return accumulated + dot(expo.astype(bf16), value, ((1,), (0,)))
+        window = pl.ds(pl.multiple_of(index * KEY_TILE, KEY_TILE), KEY_TILE)
+        expo = jnp.exp(dot(query, keys_ref[window, :128], ((1,), (1,))))
+        return accumulated + dot(expo.astype(bf16), keys_ref[window, 128:], ((1,), (0,)))
 
     accumulated = lax.fori_loop(
         low_ref[tile], high_ref[tile], chunk, jnp.zeros((QUERY_TILE, 128), f32)
@@ -267,7 +275,7 @@
     for i, start in enumerate(starts):
         piece = kept[i * BLOCK : (i + 1) * BLOCK]
         kept_ref[pl.ds(start, BLOCK), :] = piece
-        attended_ref[pl.ds(start, BLOCK), :] = piece[:, :HD].astype(bf16)
+        attended_ref[order_ref[tile * count + i]] = piece.T[:HD].astype(bf16)
 
 
 def fixed(array):
@@ -276,10 +284,13 @@
     )
 
 
-def attend(order, place, low, high, query, own, other, mask):
+def attend(order, place, low, high, query, own, other):
     rows = query.shape[0]
-    operands = (query, own, other, mask)
-    outs = (jax.ShapeDtypeStruct((rows, 128), f32), jax.ShapeDtypeStruct((rows, HD), bf16))
+    operands = (query, own, other)
+    outs = (
+        jax.ShapeDtypeStruct((rows, 128), f32),
+        jax.ShapeDtypeStruct((rows // BLOCK, HD, BLOCK), bf16),
+    )
     return pl.pallas_call(
         attend_kernel,
         grid_spec=pltpu.PrefetchScalarGridSpec(
@@ -287,7 +298,7 @@
             grid=(low.shape[0],),
             in_specs=[fixed(array) for array in operands],
             out_specs=[fixed(array) for array in outs],
-            scratch_shapes=[pltpu.VMEM((2 * rows, 128), bf16), pltpu.VMEM((2 * rows, 128), bf16)],
+            scratch_shapes=[pltpu.VMEM((2 * rows, 256), bf16)],
         ),
         out_shape=list(outs),
         name="attend",
@@ -297,119 +308,142 @@
 def attend_back_kernel(
     order_ref,
     place_ref,
+    source_ref,
     low_ref,
     high_ref,
     query_ref,
     own_ref,
     other_ref,
-    mask_ref,
-    hot_ref,
     kept_ref,
     grad_ref,
     query_grad_ref,
     own_grad_ref,
     other_grad_ref,
     bias_ref,
-    key_ref,
-    value_ref,
-    key_grad_ref,
-    value_grad_ref,
+    keys_ref,
+    sorted_ref,
+    wide_ref,
+    sums_ref,
+    every_ref,
+    same_ref,
 ):
-    tile = pl.program_id(0)
-
-    @pl.when(tile == 0)
+    step = pl.program_id(0)
+    own_rows = own_ref.shape[0]
+    taken = order_ref.shape[0]
+
+    @pl.when(step == 0)
     def _():
-        sort_keys(place_ref, own_ref, other_ref, mask_ref, key_ref, value_ref)
-        query_grad_ref[...] = jnp.zeros_like(query_grad_ref)
-        key_grad_ref[...] = jnp.zeros_like(key_grad_ref)
-        value_grad_ref[...] = jnp.zeros_like(value_grad_ref)
-
-    starts = tile_rows(order_ref, tile)
-    query = load_rows(query_ref, starts)
-    kept = load_rows(kept_ref, starts)
-    grad = load_rows(grad_ref, starts).astype(f32)
-    grad = jnp.concatenate([grad, jnp.zeros_like(grad)], axis=1)
-    lane = lanes(kept.shape)
-    totals = kept[:, HD : HD + 1]
-    center = jnp.sum(jnp.where(lane < HD, grad * kept, 0.0), axis=1, keepdims=True) / totals
-    center_high = center.astype(bf16).astype(f32)
-    center_rest = center - center_high
-    center_mid = center_rest.astype(bf16).astype(f32)
-    center_low = center_rest - center_mid
-    wide = jnp.where(lane == HD, -center_high, 0.0)
-    wide = jnp.where(lane == HD + 1, -center_mid, wide)
-    wide = jnp.where(lane == HD + 2, -center_low, wide)
-    wide = jnp.where(lane < HD, grad / totals, wide).astype(bf16)
-
-    def chunk(index, query_grad):
-        first = pl.multiple_of(index * KEY_TILE, KEY_TILE)
-        window = pl.ds(first, KEY_TILE)
-        key = key_ref[window, :]
-        value = value_ref[window, :]
+        sort_keys(place_ref, own_ref, other_ref, keys_ref)
+        every_ref[...] = jnp.zeros_like(every_ref)
+        same_ref[...] = jnp.zeros_like(same_ref)
+        sums_ref[...] = jnp.zeros_like(sums_ref)
+        if taken * BLOCK != own_rows:
+            query_grad_ref[...] = jnp.zeros_like(query_grad_ref)
+        lane = lanes((BLOCK, 128))
+
+        def put(i, unused):
+            source = pl.ds(block_start(order_ref, i), BLOCK)
+            target = pl.ds(pl.multiple_of(i * BLOCK, BLOCK), BLOCK)
+            sorted_ref[target, :] = query_ref[source, :]
+            kept = kept_ref[source, :]
+            grad = grad_ref[order_ref[i]].astype(f32)
+            grad = jnp.concatenate([grad, jnp.zeros_like(grad)], axis=0).T
+            inverse = 1.0 / kept[:, HD : HD + 1]
+            center = jnp.sum(grad * kept, axis=1, keepdims=True) * inverse
+            center_high = center.astype(bf16).astype(f32)
+            center_rest = center - center_high
+            center_mid = center_rest.astype(bf16).astype(f32)
+            center_low = center_rest - center_mid
+            wide = jnp.where(lane == HD, -center_high, 0.0)
+            wide = jnp.where(lane == HD + 1, -center_mid, wide)
+            wide = jnp.where(lane == HD + 2, -center_low, wide)
+            wide_ref[target, :] = jnp.where(lane < HD, grad * inverse, wide).astype(bf16)
+            return unused
+
+        lax.fori_loop(0, taken, put, 0, unroll=4)
+
+    window = pl.ds(pl.multiple_of(step * KEY_TILE, KEY_TILE), KEY_TILE)
+    key = keys_ref[window, :128]
+    value = keys_ref[window, 128:]
+
+    def tile(index, grads):
+        rows = pl.ds(pl.multiple_of(index * QUERY_TILE, QUERY_TILE), QUERY_TILE)
+        query = sorted_ref[rows, :]
+        wide = wide_ref[rows, :]
         expo = jnp.exp(dot(key, query, ((1,), (1,))))
-        score_grad = expo * dot(value, wide, ((1,), (1,)))
-        score_low = score_grad.astype(bf16)
-        value_grad_ref[window, :] += dot(expo.astype(bf16), wide, ((1,), (0,)))
-        key_grad_ref[window, :] += dot(score_low, query, ((1,), (0,)))
-        return query_grad + dot(score_low, key, ((0,), (0,)))
-
-    query_grad = lax.fori_loop(
-        low_ref[tile], high_ref[tile], chunk, jnp.zeros((QUERY_TILE, 128), f32)
-    )
-    for i, start in enumerate(starts):
-        query_grad_ref[pl.ds(start, BLOCK), :] = query_grad[i * BLOCK : (i + 1) * BLOCK]
-
-    @pl.when(tile == pl.num_programs(0) - 1)
+        score_low = (expo * dot(value, wide, ((1,), (1,)))).astype(bf16)
+        sums_ref[rows, :] += dot(score_low, key, ((0,), (0,)))
+        return (
+            grads[0] + dot(score_low, query, ((1,), (0,))),
+            grads[1] + dot(expo.astype(bf16), wide, ((1,), (0,))),
+        )
+
+    empty = jnp.zeros((KEY_TILE, 128), f32)
+    key_grad, value_grad = lax.fori_loop(low_ref[step], high_ref[step], tile, (empty, empty))
+    lane = lanes(key_grad.shape)
+    joined = jnp.where(lane < HD, value_grad, pltpu.roll(key_grad, HD, 1) * HD ** (-0.5))
+    joined = joined.astype(bf16)
+    for i in range(KEY_TILE // BLOCK):
+        source = source_ref[step * (KEY_TILE // BLOCK) + i] * BLOCK
+        piece = joined[i * BLOCK : (i + 1) * BLOCK]
+
+        @pl.when(source < own_rows)
+        def _(source=source, piece=piece):
+            own_grad_ref[pl.ds(pl.multiple_of(source, BLOCK), BLOCK), :] = piece
+
+        @pl.when(source >= own_rows)
+        def _(source=source, piece=piece):
+            other_grad_ref[pl.ds(pl.multiple_of(source - own_rows, BLOCK), BLOCK), :] = piece
+
+    every = jnp.where((lane >= VARIATE_LANE) & (lane < VARIATE_LANE + NVAR), key_grad, 0.0)
+    shift = 128 + VARIATE_LANE - OWN_VARIATE_LANE
+    same = every * pltpu.roll(key.astype(f32), shift, 1)
+    every_ref[...] += jnp.sum(every.reshape(-1, 8, 128), axis=0)
+    same_ref[...] += jnp.sum(same.reshape(-1, 8, 128), axis=0)
+
+    @pl.when(step == pl.num_programs(0) - 1)
     def _():
-        blocks = own_ref.shape[0] // BLOCK
-        block_lane = lanes((BLOCK, 128))
-        variate = (block_lane >= VARIATE_LANE) & (block_lane < VARIATE_LANE + NVAR)
-        sums = (jnp.zeros((BLOCK, 128), f32), jnp.zeros((BLOCK, 128), f32))
-        for half, target_ref in ((0, own_grad_ref), (1, other_grad_ref)):
-
-            def take(j, sums, half=half, target_ref=target_ref):
-                target = pl.multiple_of(j * BLOCK, BLOCK)
-                tail = pl.multiple_of((half * blocks + j) * BLOCK, BLOCK)
-                source = pl.multiple_of(place_ref[half * blocks + j] * BLOCK, BLOCK)
-                key_grad = key_grad_ref[pl.ds(source, BLOCK), :]
-                value_grad = value_grad_ref[pl.ds(source, BLOCK), :]
-                target_ref[pl.ds(target, BLOCK), :] = jnp.where(
-                    block_lane < HD, value_grad, pltpu.roll(key_grad, HD, 1) * HD ** (-0.5)
-                )
-                every = jnp.where(variate, key_grad, 0.0)
-                hot = hot_ref[pl.ds(tail, BLOCK), :].astype(f32)
-                return (sums[0] + every, sums[1] + every * hot)
-
-            sums = lax.fori_loop(0, blocks, take, sums)
-        every = jnp.sum(sums[0], keepdims=True)
-        same = jnp.sum(sums[1], keepdims=True)
+        def put(i, unused):
+            target = pl.ds(block_start(order_ref, i), BLOCK)
+            rows = pl.ds(pl.multiple_of(i * BLOCK, BLOCK), BLOCK)
+            query_grad_ref[target, :] = sums_ref[rows, :].astype(bf16)
+            return unused
+
+        lax.fori_loop(0, taken, put, 0, unroll=4)
+        every = jnp.sum(every_ref[...], keepdims=True)
+        same = jnp.sum(same_ref[...], keepdims=True)
         bias_lane = lanes((8, 128))
-        bias_ref[...] = jnp.where(bias_lane == 0, every - same, jnp.where(bias_lane == 1, same, 0.0))
-
-
-def attend_back(order, place, low, high, query, own, other, mask, hot, kept, grad):
+        bias_ref[...] = jnp.where(
+            bias_lane == 0, every - same, jnp.where(bias_lane == 1, same, 0.0)
+        )
+
+
+def attend_back(order, place, source, low, high, query, own, other, kept, grad):
     rows = query.shape[0]
-    operands = (query, own, other, mask, hot, kept, grad)
-    outs = tuple(jax.ShapeDtypeStruct((rows, 128), f32) for _ in range(3)) + (
+    taken = order.shape[0] * BLOCK
+    operands = (query, own, other, kept, grad)
+    outs = tuple(jax.ShapeDtypeStruct((rows, 128), bf16) for _ in range(3)) + (
         jax.ShapeDtypeStruct((8, 128), f32),
     )
     return pl.pallas_call(
         attend_back_kernel,
         grid_spec=pltpu.PrefetchScalarGridSpec(
-            num_scalar_prefetch=4,
+            num_scalar_prefetch=5,
             grid=(low.shape[0],),
             in_specs=[fixed(array) for array in operands],
             out_specs=[fixed(array) for array in outs],
             scratch_shapes=[
-                pltpu.VMEM((2 * rows, 128), bf16),
-                pltpu.VMEM((2 * rows, 128), bf16),
-                pltpu.VMEM((2 * rows, 128), f32),
-                pltpu.VMEM((2 * rows, 128), f32),
+                pltpu.VMEM((2 * rows, 256), bf16),
+                pltpu.VMEM((taken, 128), bf16),
+                pltpu.VMEM((taken, 128), bf16),
+                pltpu.VMEM((taken, 128), f32),
+                pltpu.VMEM((8, 128), f32),
+                pltpu.VMEM((8, 128), f32),
             ],
         ),
         out_shape=list(outs),
         name="attend_back",
-    )(order, place, low, high, *operands)
+    )(order, place, source, low, high, *operands)
 
 
 def project_back_kernel(
@@ -436,9 +470,10 @@
         weight_ref[...] = jnp.zeros_like(weight_ref)
         gain_ref[...] = jnp.zeros_like(gain_ref)
 
-    kv_grad = (own_ref[...] + other_ref[...]).astype(bf16).astype(f32)
+    kv_grad = own_ref[...].astype(f32) + other_ref[...].astype(f32)
+    kv_grad = kv_grad.astype(bf16).astype(f32)
     lane = lanes(kv_grad.shape)
-    turned = jnp.where(lane < HD, query_grad_ref[...].astype(bf16).astype(f32), kv_grad)
+    turned = jnp.where(lane < HD, query_grad_ref[...].astype(f32), kv_grad)
     grad = turned * cosine_ref[...] - swap_halves(turned, lane) * sine_ref[...]
     raw = raw_ref[...]
     factor = lax.rsqrt(half_mean(raw * raw, lane) + EPSILON)
@@ -462,7 +497,7 @@
 
 def project_back(query_grad, own, other, raw, cosine, sine, gains, normed, forward):
     rows = query_grad.shape[0]
-    step_rows = 2 * BLOCK
+    step_rows = 4 * BLOCK
     row_spec = lambda width: pl.BlockSpec((step_rows, width), lambda j: (j, 0))
     whole = lambda shape: pl.BlockSpec(shape, lambda j: (0, 0))
     return pl.pallas_call(
@@ -573,15 +608,8 @@
     )(*second, *grad, weight)
 
 
-def out_kernel(
-    parts_ref, x_ref, weight_ref, gain_ref, merged_ref, middle_ref, second_ref, squares_ref
-):
-    heads = parts_ref.shape[0]
-    for pair in range(heads // 2):
-        merged_ref[:, pair * 2 * HD : (pair + 1) * 2 * HD] = jnp.concatenate(
-            [parts_ref[2 * pair], parts_ref[2 * pair + 1]], axis=1
-        )
-    branch = dot(merged_ref[...], weight_ref[...], ((1,), (0,)))
+def out_kernel(parts_ref, x_ref, weight_ref, gain_ref, middle_ref, second_ref, squares_ref):
+    branch = dot(parts_ref[...], weight_ref[...], ((0,), (0,)))
     x = x_ref[...].astype(f32)
     middle = x + branch
     middle_ref[...] = middle
@@ -597,7 +625,6 @@
     return pl.pallas_call(
         out_kernel,
         out_shape=[
-            jax.ShapeDtypeStruct((rows, D), bf16),
             jax.ShapeDtypeStruct((rows, D), f32),
             jax.ShapeDtypeStruct((rows, D), bf16),
             jax.ShapeDtypeStruct((8, 128), f32),
@@ -625,9 +652,7 @@
     grad_middle_ref[...] = grad_middle
     branch = grad_middle.astype(bf16)
     branch_ref[...] = branch
-    merged = dot(branch, weight_ref[...], ((1,), (1,))).astype(bf16)
-    for head in range(parts_ref.shape[0]):
-        parts_ref[head] = merged[:, head * HD : (head + 1) * HD]
+    parts_ref[...] = dot(weight_ref[...], branch, ((1,), (1,))).astype(bf16)
     gain_grad_ref[...] = jnp.broadcast_to(
         jnp.sum(gain_rows, axis=0, keepdims=True), gain_grad_ref.shape
     )
@@ -640,7 +665,7 @@
         out_shape=[
             jax.ShapeDtypeStruct((rows, D), f32),
             jax.ShapeDtypeStruct((rows, D), bf16),
-            jax.ShapeDtypeStruct((H, rows, HD), bf16),
+            jax.ShapeDtypeStruct((D, rows), bf16),
             jax.ShapeDtypeStruct((8, D), f32),
         ],
         name="middle_back",
@@ -660,7 +685,7 @@
 ):
     shard = mine_ref.shape[0] // 4
     rows = shard // depth
-    grad_ref[...] = dot(merged_ref[...], branch_ref[...], ((0,), (0,)))
+    grad_ref[...] = dot(merged_ref[...], branch_ref[...], ((1,), (0,)))
     mine_ref[:, :D] = ffn_mine_ref[...]
     other_ref[:, :D] = ffn_other_ref[...]
     for place in range(8):
@@ -753,12 +778,9 @@
     return (segment, packed_at - begin, ends)
 
 
-def both_cores(array, core):
-    pairs = array.reshape((-1, 2, BLOCK) + array.shape[1:])
-    shape = (-1,) + array.shape[1:]
-    own = lax.dynamic_index_in_dim(pairs, core, 1, keepdims=False).reshape(shape)
-    other = lax.dynamic_index_in_dim(pairs, 1 - core, 1, keepdims=False).reshape(shape)
-    return own, other
+def own_rows(array, core):
+    pairs = array.reshape(-1, 2, BLOCK)
+    return lax.dynamic_index_in_dim(pairs, core, 1, keepdims=False).reshape(-1)
 
 
 def one_hot_rows(segment, variate):
@@ -782,6 +804,7 @@
         here = lane - VARIATE_LANE - copy * NVAR
         value = jnp.where(here == variate[:, None], part[1], part[0])
         rows = jnp.where((here >= 0) & (here < NVAR), value, rows)
+    rows = jnp.where(lane == OWN_VARIATE_LANE + variate[:, None], 1.0, rows)
     return rows.astype(bf16)
 
 
@@ -820,30 +843,27 @@
     segments = seq_lengths.shape[0] + 1
     tokens = variate_ids.shape[0]
 
-    out_full = lax.all_gather(out_weight, DEVICES, axis=0, tiled=True)
-
     by_head = qkv_weight.reshape(rows, 3, H, HD)
     to_heads = jnp.repeat(
         by_head.transpose(2, 0, 1, 3).reshape(H, rows, 3 * HD), 2 * sharers, axis=0
     )
-    own_qkv = lax.all_to_all(to_heads, DEVICES, 0, 0, tiled=True).reshape(D, 3 * HD)
-    own_qkv = jnp.pad(own_qkv, ((0, 0), (0, HD)))
+    own_qkv = lax.all_to_all(to_heads, DEVICES, 0, 0, tiled=True)
+    own_qkv = jnp.pad(own_qkv.reshape(D, 3 * HD), ((0, 0), (0, HD)))
     to_plane = (
         expand_weight.reshape(rows, 2, depth, 8, hidden_rows)
         .transpose(3, 0, 1, 2, 4)
         .reshape(8, rows, 2 * depth * hidden_rows)
     )
-    expand_part = lax.all_to_all(to_plane, PLANE, 0, 0, tiled=True).reshape(8 * rows, -1)
+    expand_part = lax.all_to_all(to_plane, PLANE, 0, 0, tiled=True)
+    expand_part = expand_part.reshape(8 * rows, -1)
 
     segment, position, ends = token_meta(seq_lengths, block_order)
-    own_segment, other_segment = both_cores(segment, core)
-    own_variate, other_variate = both_cores(variate_ids, core)
-    own_position = both_cores(position, core)[0]
-    all_segment = jnp.concatenate([own_segment, other_segment])
-    all_variate = jnp.concatenate([own_variate, other_variate])
+    own_segment = own_rows(segment, core)
+    own_variate = own_rows(variate_ids, core)
+    own_position = own_rows(position, core)
     bias = lax.dynamic_index_in_dim(variate_bias, head, 1, keepdims=False)
-    hot = one_hot_rows(all_segment, all_variate)
-    mask = mask_rows(all_segment, all_variate, segments, bias)
+    hot = one_hot_rows(own_segment, own_variate)
+    mask = mask_rows(own_segment, own_variate, segments, bias)
     freqs = THETA ** (-jnp.arange(HD // 2, dtype=f32) / (HD // 2))
     angles = own_position.astype(f32)[:, None] * freqs[None, :]
     cosine = jnp.tile(jnp.cos(angles), (1, 4))
@@ -865,56 +885,78 @@
     finish = jnp.min(jnp.where(ends[None, :] > last_token[:, None], ends[None, :], tokens), axis=1)
     low = begins // KEY_TILE
     high = (finish + KEY_TILE - 1) // KEY_TILE
+    slots = jnp.arange(2 * chips, dtype=jnp.int32)
+    source = jnp.sum(
+        jnp.where(place[None, :] == slots[:, None], slots[None, :], 0), axis=1, dtype=jnp.int32
+    )
+    chunks = jnp.arange(tokens // KEY_TILE, dtype=jnp.int32)[:, None]
+    low_tile = jnp.sum((high[None, :] <= chunks).astype(jnp.int32), axis=1)
+    high_tile = jnp.sum((low[None, :] <= chunks).astype(jnp.int32), axis=1)
     gains = jnp.concatenate([query_gain, key_gain])[None, :]
 
-    tables = (hot, mask, cosine, sine, place, order, low, high, own_qkv)
-    gathered, where, cotangent_mine, tables = chip_gather(inputs, cotangent, tables)
-    hot, mask, cosine, sine, place, order, low, high, own_qkv = tables
+    late = (hot, mask, cosine, sine, own_qkv, place, order, low, high, source, low_tile, high_tile)
+    pieces, where, riders, late = chip_gather(
+        jnp.concatenate([inputs, out_weight], axis=0), cotangent, late
+    )
+    hot, mask, cosine, sine, own_qkv, place, order, low, high, source, low_tile, high_tile = late
 
     feed_part = jnp.concatenate([expand_part, down_weight], axis=0)
-    gathered, out_full, feed_part = lax.optimization_barrier((gathered, out_full, feed_part))
     feed_own = lax.all_gather(feed_part[None], "bz", axis=0, tiled=True)
-    cotangent_plane = (cotangent_mine, swap(cotangent_mine, "core"))
-
-    normed_low, raw, query, own_kv = project(
-        where, gathered, attn_gain[None], own_qkv, cosine, sine, gains, hot
-    )
+
+    normed_low, raw, query, own_kv, out_mine = project(
+        where, pieces, attn_gain[None], own_qkv, cosine, sine, gains, hot, mask
+    )
+    own_kv, riders = lax.optimization_barrier((own_kv, riders))
     other_kv = swap(own_kv, "core")
-    kept, attended = attend(order, place, low, high, query, own_kv, other_kv, mask)
-    parts = lax.all_to_all(attended.reshape(chips, BLOCK, HD), CHIPS, 0, 0, tiled=True)
-    parts = over_sharers(parts, sharers)
-    merged, middle, second, squares = out_project(parts, inputs, out_full, ffn_gain[None])
+    rider_corner = swap(riders[0], "by")
+    kept, attended = attend(order, place, low, high, query, own_kv, other_kv)
+    attended, rider_corner = lax.optimization_barrier((attended, rider_corner))
+    cotangent_mine = jnp.concatenate([cotangent, *riders, rider_corner], axis=0)
+    cotangent_other = swap(cotangent_mine, "core")
+    out_other = swap(out_mine, "core")
+    out_full = jnp.stack(
+        [jnp.where(core == 0, out_mine, out_other), jnp.where(core == 0, out_other, out_mine)],
+        axis=1,
+    ).reshape(D, D)
+    merged = lax.all_to_all(attended, CHIPS, 0, 0, tiled=True)
+    merged, cotangent_other = lax.optimization_barrier((merged, cotangent_other))
+    cotangent_plane = (cotangent_mine, cotangent_other)
+    merged = over_sharers(merged, sharers).reshape(D, BLOCK)
+    middle, second, squares = out_project(merged, inputs, out_full, ffn_gain[None])
     second_plane = plane_gather(second)
 
     ffn_mine, ffn_other, back_mine, back_other, feed_grad = feed(
         second_plane, cotangent_plane, feed_own, hidden_rows
     )
-    feed_grad = lax.psum_scatter(feed_grad, "bz", scatter_dimension=0, tiled=True)[0]
-    ffn_mine, late_qkv = lax.optimization_barrier(
-        (ffn_mine, by_head.transpose(0, 2, 1, 3).reshape(rows, 3 * D))
-    )
-    qkv_full = lax.all_gather(late_qkv, DEVICES, axis=0, tiled=True)
+    feed_grad = lax.psum_scatter(feed_grad, "bz", scatter_dimension=0, tiled=True)
+    feed_grad = feed_grad[0]
+
+    qkv_full = lax.all_gather(
+        by_head.transpose(0, 2, 1, 3).reshape(rows, 3 * D), DEVICES, axis=0, tiled=True
+    )
     grad_middle, branch_grad, to_chips, grad_ffn = middle_back(
         *plane_scatter(back_mine, back_other), middle, cotangent, ffn_gain[None], out_full
     )
-    grad_attended = lax.all_to_all(jnp.repeat(to_chips, sharers, axis=0), CHIPS, 0, 0, tiled=True)
-    grad_attended = grad_attended.reshape(-1, HD)
+    grad_attended = lax.all_to_all(
+        jnp.repeat(to_chips.reshape(H, HD, BLOCK), sharers, axis=0), CHIPS, 0, 0, tiled=True
+    )
 
     joined_mine, joined_other = out_grad(
         jnp.stack(plane_members()), merged, branch_grad, ffn_mine, ffn_other, depth
     )
-    joined = joined_mine.astype(f32) + swap(joined_other, "core").astype(f32)
+    joined_other = swap(joined_other, "core")
+    joined = (joined_mine.astype(f32) + joined_other.astype(f32)).astype(bf16)
     joined = joined.reshape(4, BLOCK, 2 * D)
-    to_x = jnp.concatenate([joined[1], joined[3]], axis=0).astype(bf16)
+    to_x = jnp.concatenate([joined[1], joined[3]], axis=0)
     grad_attended, to_x = lax.optimization_barrier((grad_attended, to_x))
     from_x = swap(to_x, "hx")
 
     query_grad, own_grad, other_grad, bias_grad = attend_back(
-        order, place, low, high, query, own_kv, other_kv, mask, hot, kept, grad_attended
+        order, place, source, low_tile, high_tile, query, own_kv, other_kv, kept, grad_attended
     )
     query_grad, from_x, feed_grad = lax.optimization_barrier((query_grad, from_x, feed_grad))
     from_x = from_x.astype(f32)
-    from_y = swap((joined[2] + from_x[BLOCK:]).astype(bf16), "by")
+    from_y = swap((joined[2].astype(f32) + from_x[BLOCK:]).astype(bf16), "by")
     expand_grad = lax.all_to_all(
         feed_grad[: 8 * rows].reshape(8, rows, -1), PLANE, 0, 0, tiled=True
     )
@@ -932,7 +974,7 @@
     grad_qkv_part, from_y, expand_grad = lax.optimization_barrier(
         (grad_qkv_part, from_y, expand_grad)
     )
-    joined = joined[0] + from_x[:BLOCK] + from_y.astype(f32)
+    joined = joined[0].astype(f32) + from_x[:BLOCK] + from_y.astype(f32)
     ffn_branch = joined[:, :D]
     outputs = (middle + ffn_branch).astype(bf16)
     grad_out = lax.psum_scatter(joined[:, D:].astype(bf16), "bz", scatter_dimension=0, tiled=True)
@@ -959,7 +1001,6 @@
             jnp.zeros((93,), f32),
         ]
     )
-    joined, packed = lax.optimization_barrier((joined, packed))
     joined = lax.all_to_all(joined, CHIPS, 0, 0, tiled=True)
     summed = sum_everywhere(packed.reshape(-1, 128))
     grad_down = feed_grad[8 * rows :].astype(f32)

time: 446 us -> 393 us (0.88)
  Pallas kernels: 126 us -> 101 us
  blocking collectives: 21 us -> 0 us
  local copies, waits for them, and re-layouts: 52.6 us -> 35.8 us
  starting transfers between devices: 63 us -> 75.5 us
  waiting for transfers between devices: 130 us -> 125 us
    all_to_all x1 -> x0, blocking collectives: 21 us -> none  [body(): lax.all_to_all(jnp.repeat(to_chips, sharers, axis=0), CHIPS, 0, 0, tiled=...]
    all_gather x2 -> x1, waiting for transfers between devices: 40.1 us -> 25.5 us  [body(): lax.all_gather(by_head.transpose(0, 2, 1, 3).reshape(rows, 3 * D), DEVICE...]
    pallas_call x1, Pallas kernels: 26.4 us -> 13.2 us  [attend(): pl.pallas_call(attend_kernel, grid_spec=pltpu.PrefetchScalarGridSpec(num_...]
    pallas_call x1, Pallas kernels: 41.1 us -> 29.5 us  [attend_back(): pl.pallas_call(attend_back_kernel, grid_spec=pltpu.PrefetchScalarGridSpec...]
    ppermute x28 -> x36, starting transfers between devices: 25.4 us -> 36.5 us  [swap(): return lax.ppermute(shard, axis, [(0, 1), (1, 0)])]
    ppermute x2, waiting for transfers between devices: 15.9 us -> 21 us  [sum_everywhere(): lax.ppermute(values, 'bz', [(i, i ^ step) for i in range(depth)])]
    add x2 -> x3, other arithmetic: 6.18 us -> 1.56 us  [the longest x1 1.55 us: body(): joined = joined[0].astype(f32) + from_x[:BLOCK] + from_y.astype(f32)]
    all_to_all x3 -> x4, starting transfers between devices: 11.7 us -> 15.8 us  [the longest x1 4.81 us: body(): merged = lax.all_to_all(attended, CHIPS, 0, 0, tiled=True)]
  transfers between devices with their start and end apart: 43 -> 51, of which waited for: 24 -> 27; matrix products, arithmetic and copies ran while one was open for 19% -> 16% of each run, Pallas kernels for 23% -> 20%
where the time goes in v4:
time: 393 us; the launch traced here: 391 us
  waiting for transfers between devices  125 us (32%)
  Pallas kernels  101 us (26%)
  starting transfers between devices  75.5 us (19%)
  other arithmetic  38.1 us (10%)
  local copies, waits for them, and re-layouts  35.8 us (9%)
  between operations  16 us (4%)
    ppermute x36, waiting for transfers between devices, swap(): return lax.ppermute(shard, axis, [(0, 1), (1, 0)])  54.7 us
    ppermute x36, starting transfers between devices, swap(): return lax.ppermute(shard, axis, [(0, 1), (1, 0)])  36.5 us
    pallas_call x1, Pallas kernels, attend_back(): pl.pallas_call(attend_back_kernel, grid_spec=pltpu.PrefetchScalarGridSpec...  29.5 us
    all_gather x1, waiting for transfers between devices, body(): lax.all_gather(by_head.transpose(0, 2, 1, 3).reshape(rows, 3 * D), DEVICE...  25.5 us
    ppermute x2, waiting for transfers between devices, sum_everywhere(): lax.ppermute(values, 'bz', [(i, i ^ step) for i in range(depth)])  21 us
    pallas_call x1, Pallas kernels, feed(): pl.pallas_call(feed_kernel, grid=(2 * steps,), in_specs=[mine, other, min...  17.7 us
    pallas_call x1, Pallas kernels, attend(): pl.pallas_call(attend_kernel, grid_spec=pltpu.PrefetchScalarGridSpec(num_...  13.2 us
    unnamed x79, local copies, waits for them, and re-layouts  13.2 us
  transfers between devices with their start and end apart: 51, of which 27 were waited for; matrix products, arithmetic and copies ran while one was open for 16% of the time, Pallas kernels for 20%

profile of v4, /device:TPU:0, one launch (start us, length us, event | category | flops | bytes accessed | tf_op | source)
XLA Modules:
  0.0 391.5 jit_solution(13288537252258906993)
XLA Ops:
  32.8 6.4 %select_convert_fusion.refs_22_ = bf16[2048,128]{1,0:T(8,128)(2,1)} fusion(s32[128]{0:T(128)S(1)} %get-tuple-element.206, bf16[]{:T(256)} %bitcast.12, bf16[]{:T(256)} %bitcast.11, s32[128]{0:T(128)S(1)} %get-tuple-element.207, bf16[]{:T(256)} %bitcast.10, bf16[]{:T(256)} %bitcast.9, s32[128]{0:T(128)S(1)} %get-tuple-element.208, bf16[]{:T(256)} %bitcast.8, ...), kind=kLoop, calls=%fused_computation.11 | loop fusion | flops 3670016 | bytes 551436 | tf_op jit(solution)/shard_map/convert_element_type | solution.py:808
  52.7 8.8 %collective-permute-done.2.refs_7_ = bf16[160,1024]{1,0:T(8,128)(2,1)S(1)} collective-permute-done((bf16[160,1024]{1,0:T(8,128)(2,1)}, bf16[160,1024]{1,0:T(8,128)(2,1)S(1)}, u32[]{:S(2)}, u32[]{:S(2)}) %collective-permute-start.2) | collective-permute-done | bytes 327712 | tf_op jit(solution)/shard_map/ppermute | solution.py:54
  68.6 6.3 %collective-permute-done.6.refs_9_ = bf16[160,1024]{1,0:T(8,128)(2,1)S(1)} collective-permute-done((bf16[160,1024]{1,0:T(8,128)(2,1)}, bf16[160,1024]{1,0:T(8,128)(2,1)S(1)}, u32[]{:S(2)}, u32[]{:S(2)}) %collective-permute-start.6) | collective-permute-done | bytes 327712 | tf_op jit(solution)/shard_map/ppermute | solution.py:54
  81.5 6.2 %collective-permute-done.11.refs_3_ = bf16[160,1024]{1,0:T(8,128)(2,1)S(1)} collective-permute-done((bf16[160,1024]{1,0:T(8,128)(2,1)}, bf16[160,1024]{1,0:T(8,128)(2,1)S(1)}, u32[]{:S(2)}, u32[]{:S(2)}) %collective-permute-start.11) | collective-permute-done | bytes 327712 | tf_op jit(solution)/shard_map/ppermute | solution.py:54
  96.8 11.6 %project.1 = (bf16[2048,1024]{1,0:T(8,128)(2,1)}, f32[2048,128]{1,0:T(8,128)}, bf16[2048,128]{1,0:T(8,128)(2,1)}, bf16[2048,256]{1,0:T(8,128)(2,1)}, bf16[16,32,1024]{2,1,0:T(8,128)(2,1)}) custom-call(s32[16]{0:T(128)} %compare_select_fusion.5.where_ref, bf16[160,1024]{1,0:T(8,128)(2,1)} %copy-done.10, bf16[160,1024]{1,0:T(8,128)(2,1)} %collective-permute-done.refs_1_, ...), custom_call_target="tpu_custom_call" | custom-call | tf_op jit(solution)/shard_map/project/pallas_call | solution.py:193
  113.2 13.2 %attend.1 = (f32[2048,128]{1,0:T(8,128)}, bf16[16,64,128]{2,1,0:T(8,128)(2,1)}) custom-call(s32[16]{0:T(128)} %get-tuple-element.82.order_ref, s32[32]{0:T(128)} %copy-done.31, s32[4]{0:T(128)} %copy-done.29, s32[4]{0:T(128)} %copy-done.30, bf16[2048,128]{1,0:T(8,128)(2,1)} %get-tuple-element.99.query_ref, bf16[2048,256]{1,0:T(8,128)(2,1)} %get-tuple-element.101.own_ref, ...), custom_call_target="tpu_custom_call" | custom-call | tf_op jit(solution)/shard_map/attend/pallas_call | solution.py:294
  126.6 4.8 %all-to-all-start.1 = ((bf16[16,64,128]{2,1,0:T(8,128)(2,1)}), bf16[16,64,128]{2,1,0:T(8,128)(2,1)S(1)}, u32[]{:S(2)}, u32[]{:S(2)}) async-start(bf16[16,64,128]{2,1,0:T(8,128)(2,1)} %get-tuple-element.104), calls=%async_computation.1 | async-start | bytes 524288 | tf_op jit(solution)/shard_map/all_to_all | solution.py:921
  135.1 6.8 %all-to-all-done.1 = bf16[16,64,128]{2,1,0:T(8,128)(2,1)S(1)} async-done(((bf16[16,64,128]{2,1,0:T(8,128)(2,1)}), bf16[16,64,128]{2,1,0:T(8,128)(2,1)S(1)}, u32[]{:S(2)}, u32[]{:S(2)}) %all-to-all-start.1) | async-done | bytes 262176 | tf_op jit(solution)/shard_map/all_to_all | solution.py:921
  148.3 4.6 %collective-permute-done.22 = bf16[128,1024]{1,0:T(8,128)(2,1)S(1)} collective-permute-done((bf16[128,1024]{1,0:T(8,128)(2,1)}, bf16[128,1024]{1,0:T(8,128)(2,1)S(1)}, u32[]{:S(2)}, u32[]{:S(2)}) %collective-permute-start.22) | collective-permute-done | bytes 262176 | tf_op jit(solution)/shard_map/ppermute | solution.py:54
  162.9 17.7 %feed.1 = (bf16[512,1024]{1,0:T(8,128)(2,1)}, bf16[512,1024]{1,0:T(8,128)(2,1)}, bf16[512,1024]{1,0:T(8,128)(2,1)}, bf16[512,1024]{1,0:T(8,128)(2,1)}, bf16[4,384,1024]{2,1,0:T(8,128)(2,1)}) custom-call(bf16[512,1024]{1,0:T(8,128)(2,1)} %copy-done.8, bf16[512,1024]{1,0:T(8,128)(2,1)} %copy-done.12, bf16[512,1024]{1,0:T(8,128)(2,1)} %copy-done.9, ...), custom_call_target="tpu_custom_call" | custom-call | tf_op jit(solution)/shard_map/feed/pallas_call | solution.py:595
  203.3 3.9 middle_back.1
  207.1 5.3 %out_grad.1 = (bf16[512,2048]{1,0:T(8,128)(2,1)}, bf16[512,2048]{1,0:T(8,128)(2,1)}) custom-call(s32[8]{0:T(128)} %stack.47.members_ref, bf16[1024,128]{1,0:T(8,128)(2,1)} %bitcast.85, bf16[128,1024]{1,0:T(8,128)(2,1)} %get-tuple-element.114.branch_ref, bf16[512,1024]{1,0:T(8,128)(2,1)} %get-tuple-element.115.ffn_mine_ref, ...), custom_call_target="tpu_custom_call" | custom-call | tf_op jit(solution)/shard_map/out_grad/pallas_call | solution.py:702
  212.4 4.2 %all-to-all-start.3 = ((bf16[16,64,128]{2,1,0:T(8,128)(2,1)}), bf16[16,64,128]{2,1,0:T(8,128)(2,1)}, u32[]{:S(2)}, u32[]{:S(2)}) async-start(bf16[16,64,128]{2,1,0:T(8,128)(2,1)} %bitcast.38), calls=%async_computation.3 | async-start | bytes 524288 | tf_op jit(solution)/shard_map/all_to_all | solution.py:940
  221.1 10.8 %all-to-all-done.3.grad_ref = bf16[16,64,128]{2,1,0:T(8,128)(2,1)} async-done(((bf16[16,64,128]{2,1,0:T(8,128)(2,1)}), bf16[16,64,128]{2,1,0:T(8,128)(2,1)}, u32[]{:S(2)}, u32[]{:S(2)}) %all-to-all-start.3) | async-done | bytes 262176 | tf_op jit(solution)/shard_map/all_to_all | solution.py:940
  232.8 29.5 %attend_back.1 = (bf16[2048,128]{1,0:T(8,128)(2,1)}, bf16[2048,128]{1,0:T(8,128)(2,1)}, bf16[2048,128]{1,0:T(8,128)(2,1)}, f32[8,128]{1,0:T(8,128)}) custom-call(s32[16]{0:T(128)} %get-tuple-element.82.order_ref, s32[32]{0:T(128)} %copy-done.31, s32[32]{0:T(128)} %select_reduce_fusion.source_ref, s32[8]{0:T(128)} %get-tuple-element.120.low_ref, ...), custom_call_target="tpu_custom_call" | custom-call | tf_op jit(solution)/shard_map/attend_back/pallas_call | solution.py:428
  266.9 3.7 all-to-all-start.4
  270.7 8.0 %project_back.1 = (bf16[2048,192]{1,0:T(8,128)(2,1)}, bf16[1024,192]{1,0:T(8,128)(2,1)}, f32[8,128]{1,0:T(8,128)}, f32[1024,128]{1,0:T(8,128)}) custom-call(bf16[2048,128]{1,0:T(8,128)(2,1)} %get-tuple-element.129.query_grad_ref, bf16[2048,128]{1,0:T(8,128)(2,1)} %get-tuple-element.130.own_ref, bf16[2048,128]{1,0:T(8,128)(2,1)} %collective-permute-done.33.other_ref, ...), custom_call_target="tpu_custom_call" | custom-call | tf_op jit(solution)/shard_map/project_back/pallas_call | solution.py:503
  278.7 6.3 %all-to-all-done.4.parts_ref = bf16[8,32,1024]{2,1,0:T(8,128)(2,1)S(1)} async-done(((bf16[8,32,1024]{2,1,0:T(8,128)(2,1)}), bf16[8,32,1024]{2,1,0:T(8,128)(2,1)S(1)}, u32[]{:S(2)}, u32[]{:S(2)}) %all-to-all-start.4) | async-done | bytes 524320 | tf_op jit(solution)/shard_map/all_to_all | solution.py:960
  294.5 8.1 %all-to-all-start.5 = ((bf16[16,160,192]{2,1,0:T(8,128)(2,1)}), bf16[16,160,192]{2,1,0:T(8,128)(2,1)S(1)}, u32[]{:S(2)}, u32[]{:S(2)}) async-start(bf16[16,160,192]{2,1,0:T(8,128)(2,1)} %pad_maximum_fusion.1), calls=%async_computation.6 | async-start | bytes 2621440 | tf_op jit(solution)/shard_map/all_to_all | solution.py:1004
  319.5 11.1 %collective-permute-done.39 = f32[18,128]{1,0:T(8,128)S(1)} collective-permute-done((f32[18,128]{1,0:T(8,128)S(1)}, f32[18,128]{1,0:T(8,128)S(1)}, u32[]{:S(2)}, u32[]{:S(2)}) %collective-permute-start.39) | collective-permute-done | bytes 9248 | tf_op jit(solution)/shard_map/ppermute | solution.py:94
  330.6 3.8 collective-permute-start.40
  338.3 9.9 %collective-permute-done.40 = f32[18,128]{1,0:T(8,128)S(1)} collective-permute-done((f32[18,128]{1,0:T(8,128)S(1)}, f32[18,128]{1,0:T(8,128)S(1)}, u32[]{:S(2)}, u32[]{:S(2)}) %collective-permute-start.40) | collective-permute-done | bytes 9248 | tf_op jit(solution)/shard_map/ppermute | solution.py:94
  352.3 25.5 %all-gather.4.cloned.1.call-done.weight_ref = bf16[1024,3072]{1,0:T(8,128)(2,1)} async-done(((bf16[32,3072]{1,0:T(8,128)(2,1)}), bf16[1024,3072]{1,0:T(8,128)(2,1)}) %all-gather.4.cloned.1.call-update) | async-done | bytes 6291472 | tf_op jit(solution)/shard_map/all_gather | solution.py:934
  377.8 6.6 %input_back.1 = (f32[128,1024]{1,0:T(8,128)}, f32[32,3072]{1,0:T(8,128)}) custom-call(bf16[16,160,192]{2,1,0:T(8,128)(2,1)} %copy-done.3, bf16[1024,3072]{1,0:T(8,128)(2,1)} %all-gather.4.cloned.1.call-done.weight_ref, bf16[128,1024]{1,0:T(8,128)(2,1)} %x_ref.3, f32[1,1024]{1,0:T(1,128)} %bitcast.106, f32[128,1024]{1,0:T(8,128)} %get-tuple-element.146.middle_ref), custom_call_target="tpu_custom_call" | custom-call | tf_op jit(solution)/shard_map/input_back/pallas_call | solution.py:740
  (272 shorter events, 152.7 us)
Async XLA Ops:
  9.9 38.7 %collective-permute-start = (bf16[160,1024]{1,0:T(8,128)(2,1)S(1)}, bf16[160,1024]{1,0:T(8,128)(2,1)}, u32[]{:S(2)}, u32[]{:S(2)}) collective-permute-start(bf16[160,1024]{1,0:T(8,128)(2,1)S(1)} %constant_dynamic-update-slice_fusion.refs_0_), channel_id=1, source_target_pairs={{0,16},{16,0},{1,17},{17,1},{2,18},{18,2},{3,19},{19,3},{4,20},{20... | collective-permute-start | bytes 983048 | tf_op jit(solution)/shard_map/ppermute | solution.py:54
  12.8 32.7 %collective-permute-start.1 = (bf16[160,1024]{1,0:T(8,128)(2,1)S(1)}, bf16[160,1024]{1,0:T(8,128)(2,1)}, u32[]{:S(2)}, u32[]{:S(2)}) collective-permute-start(bf16[160,1024]{1,0:T(8,128)(2,1)S(1)} %constant_dynamic-update-slice_fusion.refs_0_), channel_id=1, source_target_pairs={{0,2},{2,4},{4,6},{6,0},{1,3},{3,5},{5,7},{7,1},{8,10},{10,12},{12... | collective-permute-start | bytes 983048 | tf_op jit(solution)/shard_map/ppermute | solution.py:71
  14.4 35.7 %collective-permute-start.3 = (bf16[160,1024]{1,0:T(8,128)(2,1)S(1)}, bf16[160,1024]{1,0:T(8,128)(2,1)}, u32[]{:S(2)}, u32[]{:S(2)}) collective-permute-start(bf16[160,1024]{1,0:T(8,128)(2,1)S(1)} %constant_dynamic-update-slice_fusion.refs_0_), channel_id=1, source_target_pairs={{0,4},{2,6},{4,0},{6,2},{1,5},{3,7},{5,1},{7,3},{8,12},{10,14},{12... | collective-permute-start | bytes 983048 | tf_op jit(solution)/shard_map/ppermute | solution.py:71
  17.0 33.7 %collective-permute-start.5 = (bf16[160,1024]{1,0:T(8,128)(2,1)S(1)}, bf16[160,1024]{1,0:T(8,128)(2,1)}, u32[]{:S(2)}, u32[]{:S(2)}) collective-permute-start(bf16[160,1024]{1,0:T(8,128)(2,1)S(1)} %constant_dynamic-update-slice_fusion.refs_0_), channel_id=1, source_target_pairs={{0,6},{2,0},{4,2},{6,4},{1,7},{3,1},{5,3},{7,5},{8,14},{10,8},{12,... | collective-permute-start | bytes 983048 | tf_op jit(solution)/shard_map/ppermute | solution.py:71
  18.3 32.6 %collective-permute-start.7 = (bf16[160,1024]{1,0:T(8,128)(2,1)S(1)}, bf16[160,1024]{1,0:T(8,128)(2,1)}, u32[]{:S(2)}, u32[]{:S(2)}) collective-permute-start(bf16[160,1024]{1,0:T(8,128)(2,1)S(1)} %constant_dynamic-update-slice_fusion.refs_0_), channel_id=1, source_target_pairs={{0,1},{1,0},{2,3},{3,2},{4,5},{5,4},{6,7},{7,6},{8,9},{9,8},{10,11... | collective-permute-start | bytes 983048 | tf_op jit(solution)/shard_map/ppermute | solution.py:54
  22.4 18.8 %all-to-all-start.2 = ((bf16[8,32,1024]{2,1,0:T(8,128)(2,1)}), bf16[8,32,1024]{2,1,0:T(8,128)(2,1)S(1)}, u32[]{:S(2)}, u32[]{:S(2)}) async-start(bf16[8,32,1024]{2,1,0:T(8,128)(2,1)} %reshape.339), calls=%async_computation.2 | async-start | bytes 1048576 | tf_op jit(solution)/shard_map/all_to_all | solution.py:857
  42.1 24.1 %all-to-all-start = ((bf16[32,32,192]{2,1,0:T(8,128)(2,1)}), bf16[32,32,192]{2,1,0:T(8,128)(2,1)S(1)}, u32[]{:S(2)}, u32[]{:S(2)}) async-start(bf16[32,32,192]{2,1,0:T(8,128)(2,1)} %bitcast.18), calls=%async_computation | async-start | bytes 1048576 | tf_op jit(solution)/shard_map/all_to_all | solution.py:850
  45.5 116.4 %all-gather.6.cloned.1.call-start = ((), (), s32[]{:S(2)}) async-start(), calls=%async_computation.11 | async-start | bytes 3932160 | tf_op jit(solution)/shard_map/all_gather | solution.py:904
  48.5 26.4 %collective-permute-start.8 = (bf16[160,1024]{1,0:T(8,128)(2,1)}, bf16[160,1024]{1,0:T(8,128)(2,1)}, u32[]{:S(2)}, u32[]{:S(2)}) collective-permute-start(bf16[160,1024]{1,0:T(8,128)(2,1)} %collective-permute-done.1.refs_4_), channel_id=1, source_target_pairs={{0,1},{1,0},{2,3},{3,2},{4,5},{5,4},{6,7},{7,6},{8,9},{9,8},{10,11... | collective-permute-start | bytes 983048 | tf_op jit(solution)/shard_map/ppermute | solution.py:54
  50.1 18.6 %collective-permute-start.4 = (bf16[160,1024]{1,0:T(8,128)(2,1)}, bf16[160,1024]{1,0:T(8,128)(2,1)}, u32[]{:S(2)}, u32[]{:S(2)}) collective-permute-start(bf16[160,1024]{1,0:T(8,128)(2,1)} %collective-permute-done.3.refs_5_), channel_id=1, source_target_pairs={{0,16},{16,0},{1,17},{17,1},{2,18},{18,2},{3,19},{19,3},{4,20},{20... | collective-permute-start | bytes 983048 | tf_op jit(solution)/shard_map/ppermute | solution.py:54
  50.6 24.3 %collective-permute-start.9 = (bf16[160,1024]{1,0:T(8,128)(2,1)}, bf16[160,1024]{1,0:T(8,128)(2,1)}, u32[]{:S(2)}, u32[]{:S(2)}) collective-permute-start(bf16[160,1024]{1,0:T(8,128)(2,1)} %collective-permute-done.3.refs_5_), channel_id=1, source_target_pairs={{0,1},{1,0},{2,3},{3,2},{4,5},{5,4},{6,7},{7,6},{8,9},{9,8},{10,11... | collective-permute-start | bytes 983048 | tf_op jit(solution)/shard_map/ppermute | solution.py:54
  50.9 24.1 %collective-permute-start.6 = (bf16[160,1024]{1,0:T(8,128)(2,1)}, bf16[160,1024]{1,0:T(8,128)(2,1)S(1)}, u32[]{:S(2)}, u32[]{:S(2)}) collective-permute-start(bf16[160,1024]{1,0:T(8,128)(2,1)} %collective-permute-done.5.refs_6_), channel_id=1, source_target_pairs={{0,16},{16,0},{1,17},{17,1},{2,18},{18,2},{3,19},{19,3},{4,20},{20... | collective-permute-start | bytes 983048 | tf_op jit(solution)/shard_map/ppermute | solution.py:54
  80.9 27.5 %collective-permute-start.15 = (bf16[128,1024]{1,0:T(8,128)(2,1)}, bf16[128,1024]{1,0:T(8,128)(2,1)}, u32[]{:S(2)}, u32[]{:S(2)}) collective-permute-start(bf16[128,1024]{1,0:T(8,128)(2,1)} %cotangent_ref.1), channel_id=1, source_target_pairs={{0,16},{16,0},{1,17},{17,1},{2,18},{18,2},{3,19},{19,3},{4,20},{20... | collective-permute-start | bytes 786440 | tf_op jit(solution)/shard_map/ppermute | solution.py:54
  87.6 20.8 %collective-permute-start.16 = (bf16[128,1024]{1,0:T(8,128)(2,1)}, bf16[128,1024]{1,0:T(8,128)(2,1)}, u32[]{:S(2)}, u32[]{:S(2)}) collective-permute-start(bf16[128,1024]{1,0:T(8,128)(2,1)} %cotangent_ref.1), channel_id=1, source_target_pairs={{0,1},{1,0},{2,3},{3,2},{4,5},{5,4},{6,7},{7,6},{8,9},{9,8},{10,11... | collective-permute-start | bytes 786440 | tf_op jit(solution)/shard_map/ppermute | solution.py:54
  108.5 23.2 %collective-permute-start.20 = (bf16[16,32,1024]{2,1,0:T(8,128)(2,1)}, bf16[16,32,1024]{2,1,0:T(8,128)(2,1)}, u32[]{:S(2)}, u32[]{:S(2)}) collective-permute-start(bf16[16,32,1024]{2,1,0:T(8,128)(2,1)} %get-tuple-element.108), channel_id=1, source_target_pairs={{0,8},{8,0},{1,9},{9,1},{2,10},{10,2},{3,11},{11,3},{4,12},{12,4},... | collective-permute-start | bytes 3145736 | tf_op jit(solution)/shard_map/ppermute | solution.py:54
  131.4 130.9 %reduce-scatter.3.cloned.1.call-start = ((), (), s32[]{:S(2)}) async-start(), calls=%async_computation.8 | async-start | bytes 3932160 | tf_op jit(solution)/shard_map/reduce_scatter | solution.py:931
  212.4 19.4 %all-to-all-start.3 = ((bf16[16,64,128]{2,1,0:T(8,128)(2,1)}), bf16[16,64,128]{2,1,0:T(8,128)(2,1)}, u32[]{:S(2)}, u32[]{:S(2)}) async-start(bf16[16,64,128]{2,1,0:T(8,128)(2,1)} %bitcast.38), calls=%async_computation.3 | async-start | bytes 524288 | tf_op jit(solution)/shard_map/all_to_all | solution.py:940
  231.9 30.4 %collective-permute-start.32 = (bf16[256,2048]{1,0:T(8,128)(2,1)}, bf16[256,2048]{1,0:T(8,128)(2,1)S(1)}, u32[]{:S(2)}, u32[]{:S(2)}) collective-permute-start(bf16[256,2048]{1,0:T(8,128)(2,1)} %pad_maximum_fusion.2), channel_id=1, source_target_pairs={{0,16},{16,0},{1,17},{17,1},{2,18},{18,2},{3,19},{19,3},{4,20},{20... | collective-permute-start | bytes 3145736 | tf_op jit(solution)/shard_map/ppermute | solution.py:54
  264.9 20.1 %collective-permute-start.34 = (bf16[128,2048]{1,0:T(8,128)(2,1)}, bf16[128,2048]{1,0:T(8,128)(2,1)S(1)}, u32[]{:S(2)}, u32[]{:S(2)}) collective-permute-start(bf16[128,2048]{1,0:T(8,128)(2,1)} %fusion), channel_id=1, source_target_pairs={{0,1},{1,0},{2,3},{3,2},{4,5},{5,4},{6,7},{7,6},{8,9},{9,8},{10,11... | collective-permute-start | bytes 1572872 | tf_op jit(solution)/shard_map/ppermute | solution.py:54
  266.9 18.1 %all-to-all-start.4 = ((bf16[8,32,1024]{2,1,0:T(8,128)(2,1)}), bf16[8,32,1024]{2,1,0:T(8,128)(2,1)S(1)}, u32[]{:S(2)}, u32[]{:S(2)}) async-start(bf16[8,32,1024]{2,1,0:T(8,128)(2,1)} %bitcast.40), calls=%async_computation.5 | async-start | bytes 1048576 | tf_op jit(solution)/shard_map/all_to_all | solution.py:960
  270.6 77.6 %reduce-scatter.5.cloned.1.call-start = ((), (), s32[]{:S(2)}) async-start(), calls=%async_computation.10 | async-start | bytes 327680 | tf_op jit(solution)/shard_map/reduce_scatter | solution.py:980
  288.9 88.8 %all-gather.4.cloned.1.call-start = ((), (), s32[]{:S(2)}) async-start(), calls=%async_computation.9 | async-start | bytes 6488064 | tf_op jit(solution)/shard_map/all_gather | solution.py:934
  294.5 55.3 %all-to-all-start.5 = ((bf16[16,160,192]{2,1,0:T(8,128)(2,1)}), bf16[16,160,192]{2,1,0:T(8,128)(2,1)S(1)}, u32[]{:S(2)}, u32[]{:S(2)}) async-start(bf16[16,160,192]{2,1,0:T(8,128)(2,1)} %pad_maximum_fusion.1), calls=%async_computation.6 | async-start | bytes 2621440 | tf_op jit(solution)/shard_map/all_to_all | solution.py:1004
  330.6 17.6 %collective-permute-start.40 = (f32[18,128]{1,0:T(8,128)S(1)}, f32[18,128]{1,0:T(8,128)S(1)}, u32[]{:S(2)}, u32[]{:S(2)}) collective-permute-start(f32[18,128]{1,0:T(8,128)S(1)} %add.332), channel_id=1, source_target_pairs={{0,4},{2,6},{4,0},{6,2},{1,5},{3,7},{5,1},{7,3},{8,12},{10,14},{12... | collective-permute-start | bytes 27656 | tf_op jit(solution)/shard_map/ppermute | solution.py:94
  (62 other events, 538.2 us)
Sparse Core Ops, SparseCore 0:
  65.1 62.3 all-gather.5
  180.9 63.5 reduce-scatter.2
  289.0 27.2 reduce-scatter.4
Sparse Core Ops, SparseCore 1:
  292.3 85.4 all-gather.3

commit v5 on v4

--- a/solution.py
+++ b/solution.py
@@ -67,10 +67,7 @@
     if depth > 4:
         pieces = lax.all_gather(shard, CHIPS, axis=0)
         return list(pieces), at, (swap(rider, "hx"), swap(rider, "by")), late
-    column = [
-        lax.ppermute(shard, "bz", [(i, (i + by) % depth) for i in range(depth)])
-        for by in range(1, depth)
-    ]
+    column = z_shifts([shard] * (depth - 1))
     across_x, across_y = [swap(shard, "hx")], [swap(shard, "by")]
     across_x += [swap(piece, "hx") for piece in column]
     across_y += [swap(piece, "by") for piece in column]
@@ -89,11 +86,37 @@
     for axis in ("core", "hx", "by"):
         values = values + swap(values, axis)
     depth = lax.axis_size("bz")
-    step = 1
-    while step < depth:
-        values = values + lax.ppermute(values, "bz", [(i, i ^ step) for i in range(depth)])
-        step *= 2
-    return values
+    if depth > 4:
+        step = 1
+        while step < depth:
+            values = values + lax.ppermute(values, "bz", [(i, i ^ step) for i in range(depth)])
+            step *= 2
+        return values
+    shifted = z_shifts([values] * (depth - 1))
+    copies = jnp.stack([values] + shifted)
+    back = (lax.axis_index("bz") - jnp.arange(depth, dtype=jnp.int32)) % depth
+    return sum(lax.dynamic_index_in_dim(copies, back[z], 0, keepdims=False) for z in range(depth))
+
+
+def z_shifts(values):
+    depth = lax.axis_size("bz")
+    return [
+        lax.ppermute(value, "bz", [(i, (i + by + 1) % depth) for i in range(depth)])
+        for by, value in enumerate(values)
+    ]
+
+
+def sum_along_z(parts):
+    depth = lax.axis_size("bz")
+    if depth > 4:
+        parts = parts.reshape(-1, parts.shape[2]).astype(bf16)
+        return lax.psum_scatter(parts, "bz", scatter_dimension=0, tiled=True).astype(f32)
+    z = lax.axis_index("bz")
+    parts = [
+        lax.dynamic_index_in_dim(parts, (z + by) % depth, 0, keepdims=False) for by in range(depth)
+    ]
+    arrived = z_shifts([part.astype(bf16) for part in parts[1:]])
+    return sum([part.astype(f32) for part in arrived], parts[0])
 
 
 def quarters(shard):
@@ -479,12 +502,12 @@
     factor = lax.rsqrt(half_mean(raw * raw, lane) + EPSILON)
     scaled = grad * gains_ref[...]
     inner = half_mean(scaled * raw, lane)
-    both = (factor * (scaled - raw * (factor * factor) * inner)).astype(bf16)
+    both = factor * (scaled - raw * (factor * factor) * inner)
     gain_ref[...] += jnp.sum(grad * raw * factor, axis=0, keepdims=True)
-    value = jnp.where(lane < HD, kv_grad, 0.0).astype(bf16)
-    full = jnp.concatenate([both, value], axis=1)
-    grad_ref[...] = full[:, : 3 * HD]
-    weight_ref[...] += dot(normed_ref[...], full, ((0,), (0,)))
+    full = jnp.concatenate([both, jnp.where(lane < HD, kv_grad, 0.0)], axis=1)
+    for i in range(grad_ref.shape[0]):
+        grad_ref[i] = full[i * BLOCK : (i + 1) * BLOCK].T[: 3 * HD].astype(bf16)
+    weight_ref[...] += dot(normed_ref[...], full.astype(bf16), ((0,), (0,)))
 
     @pl.when(step == pl.num_programs(0) - 1)
     def _():
@@ -504,9 +527,14 @@
         project_back_kernel,
         grid=(rows // step_rows,),
         in_specs=[row_spec(128)] * 6 + [whole(gains.shape), row_spec(D), whole(forward.shape)],
-        out_specs=[row_spec(3 * HD), whole((D, 3 * HD)), whole((8, 128)), whole((D, 128))],
+        out_specs=[
+            pl.BlockSpec((step_rows // BLOCK, 3 * HD, BLOCK), lambda j: (j, 0, 0)),
+            whole((D, 3 * HD)),
+            whole((8, 128)),
+            whole((D, 128)),
+        ],
         out_shape=[
-            jax.ShapeDtypeStruct((rows, 3 * HD), bf16),
+            jax.ShapeDtypeStruct((rows // BLOCK, 3 * HD, BLOCK), bf16),
             jax.ShapeDtypeStruct((D, 3 * HD), bf16),
             jax.ShapeDtypeStruct((8, 128), f32),
             jax.ShapeDtypeStruct((D, 128), f32),
@@ -717,20 +745,20 @@
     joined_ref, weight_ref, x_ref, gain_ref, middle_ref, grad_ref, qkv_ref, wide_ref
 ):
     heads = joined_ref.shape[0]
-    rows = x_ref.shape[0]
+    rows = qkv_ref.shape[0]
+    for head in range(heads):
+        wide_ref[head * 3 * HD : (head + 1) * 3 * HD] = joined_ref[head, : 3 * HD]
     for pair in range(heads // 2):
-        left = joined_ref[2 * pair]
-        right = joined_ref[2 * pair + 1]
-        wide_ref[:, pair * 6 * HD : (pair + 1) * 6 * HD] = jnp.concatenate(
-            [left[:rows], right[:rows]], axis=1
-        )
-        for part in range(3):
-            at = part * D + pair * 2 * HD
-            window = slice(part * HD, (part + 1) * HD)
-            qkv_ref[:, at : at + 2 * HD] = jnp.concatenate(
-                [left[rows:, window], right[rows:, window]], axis=1
-            ).astype(f32)
-    grad_normed = dot(wide_ref[...], weight_ref[...], ((1,), (1,)))
+        left = joined_ref[2 * pair, 3 * HD :].astype(f32)
+        right = joined_ref[2 * pair + 1, 3 * HD :].astype(f32)
+        at = pair * 2 * HD
+        low = jnp.concatenate([left[:, :HD], right[:, :HD]], axis=1)
+        high = jnp.concatenate([left[:, HD:], right[:, HD:]], axis=1)
+        qkv_ref[:, at : at + 2 * HD] = low[:rows]
+        qkv_ref[:, D + at : D + at + 2 * HD] = high[:rows]
+        qkv_ref[: rows // 2, 2 * D + at : 2 * D + at + 2 * HD] = low[rows:]
+        qkv_ref[rows // 2 :, 2 * D + at : 2 * D + at + 2 * HD] = high[rows:]
+    grad_normed = dot(wide_ref[...], weight_ref[...], ((0,), (1,)))
     grad, _ = norm_back(x_ref[...].astype(f32), gain_ref[...], grad_normed)
     grad_ref[...] = middle_ref[...] + grad
 
@@ -741,9 +769,9 @@
         input_back_kernel,
         out_shape=[
             jax.ShapeDtypeStruct((rows, D), f32),
-            jax.ShapeDtypeStruct((joined.shape[1] - rows, 3 * D), f32),
+            jax.ShapeDtypeStruct(((joined.shape[1] - 3 * HD) * 2 // 3, 3 * D), f32),
         ],
-        scratch_shapes=[pltpu.VMEM((rows, 3 * D), bf16)],
+        scratch_shapes=[pltpu.VMEM((3 * D, rows), bf16)],
         name="input_back",
     )(joined, weight, x, gain, middle)
 
@@ -954,7 +982,7 @@
     query_grad, own_grad, other_grad, bias_grad = attend_back(
         order, place, source, low_tile, high_tile, query, own_kv, other_kv, kept, grad_attended
     )
-    query_grad, from_x, feed_grad = lax.optimization_barrier((query_grad, from_x, feed_grad))
+    query_grad, from_x = lax.optimization_barrier((query_grad, from_x))
     from_x = from_x.astype(f32)
     from_y = swap((joined[2].astype(f32) + from_x[BLOCK:]).astype(bf16), "by")
     expand_grad = lax.all_to_all(
@@ -971,21 +999,22 @@
         normed_low,
         own_qkv,
     )
-    grad_qkv_part, from_y, expand_grad = lax.optimization_barrier(
-        (grad_qkv_part, from_y, expand_grad)
-    )
+    grad_qkv_part, from_y = lax.optimization_barrier((grad_qkv_part, from_y))
     joined = joined[0].astype(f32) + from_x[:BLOCK] + from_y.astype(f32)
     ffn_branch = joined[:, :D]
     outputs = (middle + ffn_branch).astype(bf16)
-    grad_out = lax.psum_scatter(joined[:, D:].astype(bf16), "bz", scatter_dimension=0, tiled=True)
-    grad_out = grad_out.astype(f32)
+    grad_out = sum_along_z(joined[:, D:].reshape(depth, rows, D))
+    grad_qkv_part, expand_grad = lax.optimization_barrier((grad_qkv_part, expand_grad))
     grad_qkv_part = grad_qkv_part.reshape(chips, 2, rows, 3 * HD)
     grad_qkv_own = lax.dynamic_index_in_dim(grad_qkv_part, core, 1, keepdims=False)
     grad_qkv_other = lax.dynamic_index_in_dim(grad_qkv_part, 1 - core, 1, keepdims=False)
     grad_qkv_own = grad_qkv_own.astype(f32) + swap(grad_qkv_other, "core").astype(f32)
+    values = grad_qkv_own[:, :, 2 * HD :]
+    values = jnp.concatenate([values[:, : rows // 2], values[:, rows // 2 :]], axis=2)
     joined = jnp.concatenate(
-        [grad_project.reshape(chips, BLOCK, 3 * HD), grad_qkv_own.astype(bf16)], axis=1
-    )
+        [grad_project, grad_qkv_own[:, :, : 2 * HD].astype(bf16), values.astype(bf16)], axis=1
+    )
+    joined = lax.all_to_all(joined, CHIPS, 0, 0, tiled=True)
 
     bias_part = jnp.where(
         jnp.arange(H)[None, :] == head, bias_grad[0, :2][:, None], jnp.zeros((2, H), f32)
@@ -1001,15 +1030,13 @@
             jnp.zeros((93,), f32),
         ]
     )
-    joined = lax.all_to_all(joined, CHIPS, 0, 0, tiled=True)
     summed = sum_everywhere(packed.reshape(-1, 128))
     grad_down = feed_grad[8 * rows :].astype(f32)
     grad_expand = widen(expand_grad, depth, hidden_rows)
-    joined, summed, grad_down, grad_expand = lax.optimization_barrier(
-        (joined, summed, grad_down, grad_expand)
-    )
-    joined = over_sharers(joined, sharers)
-    grad_inputs, grad_qkv = input_back(joined, qkv_full, inputs, attn_gain[None], grad_middle)
+    joined, grad_down, grad_expand = lax.optimization_barrier((joined, grad_down, grad_expand))
+    grad_inputs, grad_qkv = input_back(
+        over_sharers(joined, sharers), qkv_full, inputs, attn_gain[None], grad_middle
+    )
     summed = summed.reshape(-1)
     at = 2 * D + 2 * HD
     root_means = jnp.sqrt(summed[at + 2 * H : at + 2 * H + 3] / (tokens * D))

time: 393 us -> 363 us (0.924)
  waiting for transfers between devices: 125 us -> 77.9 us
  starting transfers between devices: 75.5 us -> 91.2 us
  between operations: 16 us -> 24.1 us
  other arithmetic: 38.1 us -> 32.2 us
    all_gather x1, waiting for transfers between devices: 25.5 us -> 0.01 us  [body(): lax.all_gather(by_head.transpose(0, 2, 1, 3).reshape(rows, 3 * D), DEVICE...]
    ppermute x5 -> x9, waiting for transfers between devices: 21 us -> 0.02 us  [z_shifts(): lax.ppermute(value, 'bz', [(i, (i + by + 1) % depth) for i in range(depth)])]
    ppermute x5 -> x9, starting transfers between devices: 11.1 us -> 24.8 us  [z_shifts(): lax.ppermute(value, 'bz', [(i, (i + by + 1) % depth) for i in range(depth)])]
  transfers between devices with their start and end apart: 51 -> 54, of which waited for: 27 -> 21; matrix products, arithmetic and copies ran while one was open for 16% -> 16% of each run, Pallas kernels for 20% -> 21%
where the time goes in v5:
time: 363 us; the launch traced here: 361 us
  Pallas kernels  101 us (28%)
  starting transfers between devices  91.2 us (25%)
  waiting for transfers between devices  77.9 us (21%)
  local copies, waits for them, and re-layouts  35 us (10%)
  other arithmetic  32.2 us (9%)
  between operations  24.1 us (7%)
    ppermute x36, waiting for transfers between devices, swap(): return lax.ppermute(shard, axis, [(0, 1), (1, 0)])  56.6 us
    ppermute x36, starting transfers between devices, swap(): return lax.ppermute(shard, axis, [(0, 1), (1, 0)])  37.5 us
    pallas_call x1, Pallas kernels, attend_back(): pl.pallas_call(attend_back_kernel, grid_spec=pltpu.PrefetchScalarGridSpec...  29.5 us
    ppermute x9, starting transfers between devices, z_shifts(): lax.ppermute(value, 'bz', [(i, (i + by + 1) % depth) for i in range(depth)])  24.8 us
    pallas_call x1, Pallas kernels, feed(): pl.pallas_call(feed_kernel, grid=(2 * steps,), in_specs=[mine, other, min...  17.6 us
    pallas_call x1, Pallas kernels, attend(): pl.pallas_call(attend_kernel, grid_spec=pltpu.PrefetchScalarGridSpec(num_...  13.2 us
    unnamed x79, local copies, waits for them, and re-layouts  11.5 us
    pallas_call x1, Pallas kernels, project(): pl.pallas_call(partial(project_kernel, chips=blocks), grid_spec=pltpu.Pre...  11.4 us
  transfers between devices with their start and end apart: 54, of which 21 were waited for; matrix products, arithmetic and copies ran while one was open for 16% of the time, Pallas kernels for 21%

profile of v5, /device:TPU:0, one launch (start us, length us, event | category | flops | bytes accessed | tf_op | source)
XLA Modules:
  0.0 361.2 jit_solution(12034811909947302197)
XLA Ops:
  22.4 3.5 all-to-all-start.2
  32.1 6.4 %select_convert_fusion.refs_22_ = bf16[2048,128]{1,0:T(8,128)(2,1)} fusion(s32[128]{0:T(128)S(1)} %get-tuple-element.214, bf16[]{:T(256)} %bitcast.12, bf16[]{:T(256)} %bitcast.11, s32[128]{0:T(128)S(1)} %get-tuple-element.215, bf16[]{:T(256)} %bitcast.10, bf16[]{:T(256)} %bitcast.9, s32[128]{0:T(128)S(1)} %get-tuple-element.216, bf16[]{:T(256)} %bitcast.8, ...), kind=kLoop, calls=%fused_computation.10 | loop fusion | flops 3670016 | bytes 551436 | tf_op jit(solution)/shard_map/convert_element_type | solution.py:836
  50.9 10.0 %collective-permute-done.2.refs_7_ = bf16[160,1024]{1,0:T(8,128)(2,1)} collective-permute-done((bf16[160,1024]{1,0:T(8,128)(2,1)}, bf16[160,1024]{1,0:T(8,128)(2,1)}, u32[]{:S(2)}, u32[]{:S(2)}) %collective-permute-start.2) | collective-permute-done | bytes 327712 | tf_op jit(solution)/shard_map/ppermute | solution.py:54
  67.8 6.5 %collective-permute-done.6.refs_9_ = bf16[160,1024]{1,0:T(8,128)(2,1)} collective-permute-done((bf16[160,1024]{1,0:T(8,128)(2,1)}, bf16[160,1024]{1,0:T(8,128)(2,1)}, u32[]{:S(2)}, u32[]{:S(2)}) %collective-permute-start.6) | collective-permute-done | bytes 327712 | tf_op jit(solution)/shard_map/ppermute | solution.py:54
  80.1 5.9 %collective-permute-done.11.refs_3_ = bf16[160,1024]{1,0:T(8,128)(2,1)S(1)} collective-permute-done((bf16[160,1024]{1,0:T(8,128)(2,1)}, bf16[160,1024]{1,0:T(8,128)(2,1)S(1)}, u32[]{:S(2)}, u32[]{:S(2)}) %collective-permute-start.11) | collective-permute-done | bytes 327712 | tf_op jit(solution)/shard_map/ppermute | solution.py:54
  95.2 11.4 %project.1 = (bf16[2048,1024]{1,0:T(8,128)(2,1)}, f32[2048,128]{1,0:T(8,128)}, bf16[2048,128]{1,0:T(8,128)(2,1)}, bf16[2048,256]{1,0:T(8,128)(2,1)}, bf16[16,32,1024]{2,1,0:T(8,128)(2,1)}) custom-call(s32[16]{0:T(128)} %compare_select_fusion.7.where_ref, bf16[160,1024]{1,0:T(8,128)(2,1)} %copy-done.11, bf16[160,1024]{1,0:T(8,128)(2,1)} %collective-permute-done.refs_1_, ...), custom_call_target="tpu_custom_call" | custom-call | tf_op jit(solution)/shard_map/project/pallas_call | solution.py:216
  110.7 13.2 %attend.1 = (f32[2048,128]{1,0:T(8,128)}, bf16[16,64,128]{2,1,0:T(8,128)(2,1)}) custom-call(s32[16]{0:T(128)} %get-tuple-element.81.order_ref, s32[32]{0:T(128)} %copy-done.30, s32[4]{0:T(128)} %copy-done.28, s32[4]{0:T(128)} %copy-done.29, bf16[2048,128]{1,0:T(8,128)(2,1)} %get-tuple-element.98.query_ref, bf16[2048,256]{1,0:T(8,128)(2,1)} %get-tuple-element.100.own_ref, ...), custom_call_target="tpu_custom_call" | custom-call | tf_op jit(solution)/shard_map/attend/pallas_call | solution.py:317
  124.1 5.5 %all-to-all-start.1 = ((bf16[16,64,128]{2,1,0:T(8,128)(2,1)}), bf16[16,64,128]{2,1,0:T(8,128)(2,1)S(1)}, u32[]{:S(2)}, u32[]{:S(2)}) async-start(bf16[16,64,128]{2,1,0:T(8,128)(2,1)} %get-tuple-element.103), calls=%async_computation.1 | async-start | bytes 524288 | tf_op jit(solution)/shard_map/all_to_all | solution.py:949
  133.2 6.8 %all-to-all-done.1 = bf16[16,64,128]{2,1,0:T(8,128)(2,1)S(1)} async-done(((bf16[16,64,128]{2,1,0:T(8,128)(2,1)}), bf16[16,64,128]{2,1,0:T(8,128)(2,1)S(1)}, u32[]{:S(2)}, u32[]{:S(2)}) %all-to-all-start.1) | async-done | bytes 262176 | tf_op jit(solution)/shard_map/all_to_all | solution.py:949
  146.4 4.5 %collective-permute-done.22 = bf16[128,1024]{1,0:T(8,128)(2,1)S(1)} collective-permute-done((bf16[128,1024]{1,0:T(8,128)(2,1)}, bf16[128,1024]{1,0:T(8,128)(2,1)S(1)}, u32[]{:S(2)}, u32[]{:S(2)}) %collective-permute-start.22) | collective-permute-done | bytes 262176 | tf_op jit(solution)/shard_map/ppermute | solution.py:54
  160.9 17.6 %feed.1 = (bf16[512,1024]{1,0:T(8,128)(2,1)}, bf16[512,1024]{1,0:T(8,128)(2,1)}, bf16[512,1024]{1,0:T(8,128)(2,1)}, bf16[512,1024]{1,0:T(8,128)(2,1)}, bf16[4,384,1024]{2,1,0:T(8,128)(2,1)}) custom-call(bf16[512,1024]{1,0:T(8,128)(2,1)} %copy-done.9, bf16[512,1024]{1,0:T(8,128)(2,1)} %copy-done.14, bf16[512,1024]{1,0:T(8,128)(2,1)} %copy-done.10, ...), custom_call_target="tpu_custom_call" | custom-call | tf_op jit(solution)/shard_map/feed/pallas_call | solution.py:623
  194.3 4.5 %collective-permute-done.28.from_x_ref = bf16[128,1024]{1,0:T(8,128)(2,1)S(1)} collective-permute-done((bf16[128,1024]{1,0:T(8,128)(2,1)S(1)}, bf16[128,1024]{1,0:T(8,128)(2,1)S(1)}, u32[]{:S(2)}, u32[]{:S(2)}) %collective-permute-start.28) | collective-permute-done | bytes 262176 | tf_op jit(solution)/shard_map/ppermute | solution.py:54
  200.0 3.9 %middle_back.1 = (f32[128,1024]{1,0:T(8,128)}, bf16[128,1024]{1,0:T(8,128)(2,1)}, bf16[1024,128]{1,0:T(8,128)(2,1)}, f32[8,1024]{1,0:T(8,128)}) custom-call(f32[128,1024]{1,0:T(8,128)} %slice.217.own_ref, bf16[128,1024]{1,0:T(8,128)(2,1)} %copy-done.23, bf16[128,1024]{1,0:T(8,128)(2,1)} %copy-done.24, f32[128,1024]{1,0:T(8,128)} %get-tuple-element.108.middle_ref, ...), custom_call_target="tpu_custom_call" | custom-call | tf_op jit(solution)/shard_map/middle_back/pallas_call | solution.py:691
  203.9 5.2 %out_grad.1 = (bf16[512,2048]{1,0:T(8,128)(2,1)}, bf16[512,2048]{1,0:T(8,128)(2,1)}) custom-call(s32[8]{0:T(128)} %stack.62.members_ref, bf16[1024,128]{1,0:T(8,128)(2,1)} %bitcast.110, bf16[128,1024]{1,0:T(8,128)(2,1)} %get-tuple-element.113.branch_ref, bf16[512,1024]{1,0:T(8,128)(2,1)} %get-tuple-element.114.ffn_mine_ref, ...), custom_call_target="tpu_custom_call" | custom-call | tf_op jit(solution)/shard_map/out_grad/pallas_call | solution.py:730
  209.0 4.9 %all-to-all-start.3 = ((bf16[16,64,128]{2,1,0:T(8,128)(2,1)}), bf16[16,64,128]{2,1,0:T(8,128)(2,1)S(1)}, u32[]{:S(2)}, u32[]{:S(2)}) async-start(bf16[16,64,128]{2,1,0:T(8,128)(2,1)} %bitcast.38), calls=%async_computation.3 | async-start | bytes 524288 | tf_op jit(solution)/shard_map/all_to_all | solution.py:968
  219.5 9.0 %all-to-all-done.3.grad_ref = bf16[16,64,128]{2,1,0:T(8,128)(2,1)S(1)} async-done(((bf16[16,64,128]{2,1,0:T(8,128)(2,1)}), bf16[16,64,128]{2,1,0:T(8,128)(2,1)S(1)}, u32[]{:S(2)}, u32[]{:S(2)}) %all-to-all-start.3) | async-done | bytes 262176 | tf_op jit(solution)/shard_map/all_to_all | solution.py:968
  231.6 29.5 %attend_back.1 = (bf16[2048,128]{1,0:T(8,128)(2,1)}, bf16[2048,128]{1,0:T(8,128)(2,1)}, bf16[2048,128]{1,0:T(8,128)(2,1)}, f32[8,128]{1,0:T(8,128)}) custom-call(s32[16]{0:T(128)} %get-tuple-element.81.order_ref, s32[32]{0:T(128)} %copy-done.30, s32[32]{0:T(128)} %select_reduce_fusion.source_ref, s32[8]{0:T(128)} %get-tuple-element.119.low_ref, ...), custom_call_target="tpu_custom_call" | custom-call | tf_op jit(solution)/shard_map/attend_back/pallas_call | solution.py:451
  265.0 8.0 %project_back.1 = (bf16[16,192,128]{2,1,0:T(8,128)(2,1)}, bf16[1024,192]{1,0:T(8,128)(2,1)}, f32[8,128]{1,0:T(8,128)}, f32[1024,128]{1,0:T(8,128)}) custom-call(bf16[2048,128]{1,0:T(8,128)(2,1)} %get-tuple-element.127.query_grad_ref, bf16[2048,128]{1,0:T(8,128)(2,1)} %get-tuple-element.128.own_ref, bf16[2048,128]{1,0:T(8,128)(2,1)} %collective-permute-done.33.other_ref, ...), custom_call_target="tpu_custom_call" | custom-call | tf_op jit(solution)/shard_map/project_back/pallas_call | solution.py:526
  275.0 7.0 %collective-permute-done.34 = bf16[128,2048]{1,0:T(8,128)(2,1)S(1)} collective-permute-done((bf16[128,2048]{1,0:T(8,128)(2,1)S(1)}, bf16[128,2048]{1,0:T(8,128)(2,1)S(1)}, u32[]{:S(2)}, u32[]{:S(2)}) %collective-permute-start.34) | collective-permute-done | bytes 524320 | tf_op jit(solution)/shard_map/ppermute | solution.py:54
  284.1 4.5 %all-to-all-start.4 = ((bf16[8,32,1024]{2,1,0:T(8,128)(2,1)}), bf16[8,32,1024]{2,1,0:T(8,128)(2,1)S(1)}, u32[]{:S(2)}, u32[]{:S(2)}) async-start(bf16[8,32,1024]{2,1,0:T(8,128)(2,1)} %bitcast.115), calls=%async_computation.5 | async-start | bytes 1048576 | tf_op jit(solution)/shard_map/all_to_all | solution.py:988
  292.9 5.4 %all-to-all-done.4.parts_ref = bf16[8,32,1024]{2,1,0:T(8,128)(2,1)S(1)} async-done(((bf16[8,32,1024]{2,1,0:T(8,128)(2,1)}), bf16[8,32,1024]{2,1,0:T(8,128)(2,1)S(1)}, u32[]{:S(2)}, u32[]{:S(2)}) %all-to-all-start.4) | async-done | bytes 524320 | tf_op jit(solution)/shard_map/all_to_all | solution.py:988
  302.5 6.8 %all-to-all-start.5 = ((bf16[16,240,128]{2,1,0:T(8,128)(2,1)}), bf16[16,240,128]{2,1,0:T(8,128)(2,1)S(1)}, u32[]{:S(2)}, u32[]{:S(2)}) async-start(bf16[16,240,128]{2,1,0:T(8,128)(2,1)} %maximum_maximum_fusion), calls=%async_computation.6 | async-start | bytes 1966080 | tf_op jit(solution)/shard_map/all_to_all | solution.py:1017
  328.1 11.0 %collective-permute-start.36 = (bf16[32,1024]{1,0:T(8,128)(2,1)S(1)}, bf16[32,1024]{1,0:T(8,128)(2,1)S(1)}, u32[]{:S(2)}, u32[]{:S(2)}) collective-permute-start(bf16[32,1024]{1,0:T(8,128)(2,1)S(1)} %get-tuple-element.175), channel_id=1, source_target_pairs={{0,2},{2,4},{4,6},{6,0},{1,3},{3,5},{5,7},{7,1},{8,10},{10,12},{12... | collective-permute-start | bytes 196616 | tf_op jit(solution)/shard_map/ppermute | solution.py:104
  347.2 6.5 %input_back.1 = (f32[128,1024]{1,0:T(8,128)}, f32[32,3072]{1,0:T(8,128)}) custom-call(bf16[16,240,128]{2,1,0:T(8,128)(2,1)} %copy-done.4, bf16[1024,3072]{1,0:T(8,128)(2,1)} %all-gather.4.cloned.1.call-done.weight_ref, bf16[128,1024]{1,0:T(8,128)(2,1)} %x_ref.3, f32[1,1024]{1,0:T(1,128)} %bitcast.130, f32[128,1024]{1,0:T(8,128)} %get-tuple-element.140.middle_ref), custom_call_target="tpu_custom_call" | custom-call | tf_op jit(solution)/shard_map/input_back/pallas_call | solution.py:768
  (282 shorter events, 139.4 us)
Async XLA Ops:
  9.9 36.9 %collective-permute-start = (bf16[160,1024]{1,0:T(8,128)(2,1)S(1)}, bf16[160,1024]{1,0:T(8,128)(2,1)}, u32[]{:S(2)}, u32[]{:S(2)}) collective-permute-start(bf16[160,1024]{1,0:T(8,128)(2,1)S(1)} %constant_dynamic-update-slice_fusion.refs_0_), channel_id=1, source_target_pairs={{0,16},{16,0},{1,17},{17,1},{2,18},{18,2},{3,19},{19,3},{4,20},{20... | collective-permute-start | bytes 983048 | tf_op jit(solution)/shard_map/ppermute | solution.py:54
  12.8 32.0 %collective-permute-start.1 = (bf16[160,1024]{1,0:T(8,128)(2,1)S(1)}, bf16[160,1024]{1,0:T(8,128)(2,1)}, u32[]{:S(2)}, u32[]{:S(2)}) collective-permute-start(bf16[160,1024]{1,0:T(8,128)(2,1)S(1)} %constant_dynamic-update-slice_fusion.refs_0_), channel_id=1, source_target_pairs={{0,2},{2,4},{4,6},{6,0},{1,3},{3,5},{5,7},{7,1},{8,10},{10,12},{12... | collective-permute-start | bytes 983048 | tf_op jit(solution)/shard_map/ppermute | solution.py:104
  14.4 33.9 %collective-permute-start.3 = (bf16[160,1024]{1,0:T(8,128)(2,1)S(1)}, bf16[160,1024]{1,0:T(8,128)(2,1)}, u32[]{:S(2)}, u32[]{:S(2)}) collective-permute-start(bf16[160,1024]{1,0:T(8,128)(2,1)S(1)} %constant_dynamic-update-slice_fusion.refs_0_), channel_id=1, source_target_pairs={{0,4},{2,6},{4,0},{6,2},{1,5},{3,7},{5,1},{7,3},{8,12},{10,14},{12... | collective-permute-start | bytes 983048 | tf_op jit(solution)/shard_map/ppermute | solution.py:104
  17.0 31.9 %collective-permute-start.5 = (bf16[160,1024]{1,0:T(8,128)(2,1)S(1)}, bf16[160,1024]{1,0:T(8,128)(2,1)}, u32[]{:S(2)}, u32[]{:S(2)}) collective-permute-start(bf16[160,1024]{1,0:T(8,128)(2,1)S(1)} %constant_dynamic-update-slice_fusion.refs_0_), channel_id=1, source_target_pairs={{0,6},{2,0},{4,2},{6,4},{1,7},{3,1},{5,3},{7,5},{8,14},{10,8},{12,... | collective-permute-start | bytes 983048 | tf_op jit(solution)/shard_map/ppermute | solution.py:104
  18.3 30.8 %collective-permute-start.7 = (bf16[160,1024]{1,0:T(8,128)(2,1)S(1)}, bf16[160,1024]{1,0:T(8,128)(2,1)}, u32[]{:S(2)}, u32[]{:S(2)}) collective-permute-start(bf16[160,1024]{1,0:T(8,128)(2,1)S(1)} %constant_dynamic-update-slice_fusion.refs_0_), channel_id=1, source_target_pairs={{0,1},{1,0},{2,3},{3,2},{4,5},{5,4},{6,7},{7,6},{8,9},{9,8},{10,11... | collective-permute-start | bytes 983048 | tf_op jit(solution)/shard_map/ppermute | solution.py:54
  22.4 18.1 %all-to-all-start.2 = ((bf16[8,32,1024]{2,1,0:T(8,128)(2,1)}), bf16[8,32,1024]{2,1,0:T(8,128)(2,1)S(1)}, u32[]{:S(2)}, u32[]{:S(2)}) async-start(bf16[8,32,1024]{2,1,0:T(8,128)(2,1)} %reshape.365), calls=%async_computation.2 | async-start | bytes 1048576 | tf_op jit(solution)/shard_map/all_to_all | solution.py:885
  41.4 24.2 %all-to-all-start = ((bf16[32,32,192]{2,1,0:T(8,128)(2,1)}), bf16[32,32,192]{2,1,0:T(8,128)(2,1)S(1)}, u32[]{:S(2)}, u32[]{:S(2)}) async-start(bf16[32,32,192]{2,1,0:T(8,128)(2,1)} %bitcast.18), calls=%async_computation | async-start | bytes 1048576 | tf_op jit(solution)/shard_map/all_to_all | solution.py:878
  44.7 115.2 %all-gather.6.cloned.1.call-start = ((), (), s32[]{:S(2)}) async-start(), calls=%async_computation.9 | async-start | bytes 3932160 | tf_op jit(solution)/shard_map/all_gather | solution.py:932
  46.8 27.6 %collective-permute-start.8 = (bf16[160,1024]{1,0:T(8,128)(2,1)}, bf16[160,1024]{1,0:T(8,128)(2,1)S(1)}, u32[]{:S(2)}, u32[]{:S(2)}) collective-permute-start(bf16[160,1024]{1,0:T(8,128)(2,1)} %collective-permute-done.1.refs_4_), channel_id=1, source_target_pairs={{0,1},{1,0},{2,3},{3,2},{4,5},{5,4},{6,7},{7,6},{8,9},{9,8},{10,11... | collective-permute-start | bytes 983048 | tf_op jit(solution)/shard_map/ppermute | solution.py:54
  48.3 19.5 %collective-permute-start.4 = (bf16[160,1024]{1,0:T(8,128)(2,1)}, bf16[160,1024]{1,0:T(8,128)(2,1)S(1)}, u32[]{:S(2)}, u32[]{:S(2)}) collective-permute-start(bf16[160,1024]{1,0:T(8,128)(2,1)} %collective-permute-done.3.refs_5_), channel_id=1, source_target_pairs={{0,16},{16,0},{1,17},{17,1},{2,18},{18,2},{3,19},{19,3},{4,20},{20... | collective-permute-start | bytes 983048 | tf_op jit(solution)/shard_map/ppermute | solution.py:54
  48.9 25.5 %collective-permute-start.9 = (bf16[160,1024]{1,0:T(8,128)(2,1)}, bf16[160,1024]{1,0:T(8,128)(2,1)}, u32[]{:S(2)}, u32[]{:S(2)}) collective-permute-start(bf16[160,1024]{1,0:T(8,128)(2,1)} %collective-permute-done.3.refs_5_), channel_id=1, source_target_pairs={{0,1},{1,0},{2,3},{3,2},{4,5},{5,4},{6,7},{7,6},{8,9},{9,8},{10,11... | collective-permute-start | bytes 983048 | tf_op jit(solution)/shard_map/ppermute | solution.py:54
  49.1 25.2 %collective-permute-start.6 = (bf16[160,1024]{1,0:T(8,128)(2,1)}, bf16[160,1024]{1,0:T(8,128)(2,1)}, u32[]{:S(2)}, u32[]{:S(2)}) collective-permute-start(bf16[160,1024]{1,0:T(8,128)(2,1)} %collective-permute-done.5.refs_6_), channel_id=1, source_target_pairs={{0,16},{16,0},{1,17},{17,1},{2,18},{18,2},{3,19},{19,3},{4,20},{20... | collective-permute-start | bytes 983048 | tf_op jit(solution)/shard_map/ppermute | solution.py:54
  76.1 17.1 %collective-permute-start.12 = (bf16[160,1024]{1,0:T(8,128)(2,1)}, bf16[160,1024]{1,0:T(8,128)(2,1)}, u32[]{:S(2)}, u32[]{:S(2)}) collective-permute-start(bf16[160,1024]{1,0:T(8,128)(2,1)} %copy-done.20), channel_id=1, source_target_pairs={{0,16},{16,0},{1,17},{17,1},{2,18},{18,2},{3,19},{19,3},{4,20},{20... | collective-permute-start | bytes 983048 | tf_op jit(solution)/shard_map/ppermute | solution.py:54
  79.3 27.3 %collective-permute-start.15 = (bf16[128,1024]{1,0:T(8,128)(2,1)S(1)}, bf16[128,1024]{1,0:T(8,128)(2,1)S(1)}, u32[]{:S(2)}, u32[]{:S(2)}) collective-permute-start(bf16[128,1024]{1,0:T(8,128)(2,1)S(1)} %copy-done.15), channel_id=1, source_target_pairs={{0,16},{16,0},{1,17},{17,1},{2,18},{18,2},{3,19},{19,3},{4,20},{20... | collective-permute-start | bytes 786440 | tf_op jit(solution)/shard_map/ppermute | solution.py:54
  86.0 20.6 %collective-permute-start.16 = (bf16[128,1024]{1,0:T(8,128)(2,1)S(1)}, bf16[128,1024]{1,0:T(8,128)(2,1)}, u32[]{:S(2)}, u32[]{:S(2)}) collective-permute-start(bf16[128,1024]{1,0:T(8,128)(2,1)S(1)} %copy-done.15), channel_id=1, source_target_pairs={{0,1},{1,0},{2,3},{3,2},{4,5},{5,4},{6,7},{7,6},{8,9},{9,8},{10,11... | collective-permute-start | bytes 786440 | tf_op jit(solution)/shard_map/ppermute | solution.py:54
  106.7 23.1 %collective-permute-start.20 = (bf16[16,32,1024]{2,1,0:T(8,128)(2,1)}, bf16[16,32,1024]{2,1,0:T(8,128)(2,1)}, u32[]{:S(2)}, u32[]{:S(2)}) collective-permute-start(bf16[16,32,1024]{2,1,0:T(8,128)(2,1)} %get-tuple-element.107), channel_id=1, source_target_pairs={{0,8},{8,0},{1,9},{9,1},{2,10},{10,2},{3,11},{11,3},{4,12},{12,4},... | collective-permute-start | bytes 3145736 | tf_op jit(solution)/shard_map/ppermute | solution.py:54
  107.2 16.7 %collective-permute-start.18 = (bf16[128,1024]{1,0:T(8,128)(2,1)S(1)}, bf16[128,1024]{1,0:T(8,128)(2,1)S(1)}, u32[]{:S(2)}, u32[]{:S(2)}) collective-permute-start(bf16[128,1024]{1,0:T(8,128)(2,1)S(1)} %collective-permute-done.15), channel_id=1, source_target_pairs={{0,1},{1,0},{2,3},{3,2},{4,5},{5,4},{6,7},{7,6},{8,9},{9,8},{10,11... | collective-permute-start | bytes 786440 | tf_op jit(solution)/shard_map/ppermute | solution.py:54
  129.6 152.4 %reduce-scatter.2.cloned.1.call-start = ((), (), s32[]{:S(2)}) async-start(), calls=%async_computation.7 | async-start | bytes 3932160 | tf_op jit(solution)/shard_map/reduce_scatter | solution.py:959
  178.6 167.6 %all-gather.4.cloned.1.call-start = ((), (), s32[]{:S(2)}) async-start(), calls=%async_computation.8 | async-start | bytes 6488064 | tf_op jit(solution)/shard_map/all_gather | solution.py:962
  209.0 19.5 %all-to-all-start.3 = ((bf16[16,64,128]{2,1,0:T(8,128)(2,1)}), bf16[16,64,128]{2,1,0:T(8,128)(2,1)S(1)}, u32[]{:S(2)}, u32[]{:S(2)}) async-start(bf16[16,64,128]{2,1,0:T(8,128)(2,1)} %bitcast.38), calls=%async_computation.3 | async-start | bytes 524288 | tf_op jit(solution)/shard_map/all_to_all | solution.py:968
  228.5 33.2 %collective-permute-start.32 = (bf16[256,2048]{1,0:T(8,128)(2,1)}, bf16[256,2048]{1,0:T(8,128)(2,1)S(1)}, u32[]{:S(2)}, u32[]{:S(2)}) collective-permute-start(bf16[256,2048]{1,0:T(8,128)(2,1)} %pad_maximum_fusion.1), channel_id=1, source_target_pairs={{0,16},{16,0},{1,17},{17,1},{2,18},{18,2},{3,19},{19,3},{4,20},{20... | collective-permute-start | bytes 3145736 | tf_op jit(solution)/shard_map/ppermute | solution.py:54
  263.4 18.7 %collective-permute-start.34 = (bf16[128,2048]{1,0:T(8,128)(2,1)S(1)}, bf16[128,2048]{1,0:T(8,128)(2,1)S(1)}, u32[]{:S(2)}, u32[]{:S(2)}) collective-permute-start(bf16[128,2048]{1,0:T(8,128)(2,1)S(1)} %fusion), channel_id=1, source_target_pairs={{0,1},{1,0},{2,3},{3,2},{4,5},{5,4},{6,7},{7,6},{8,9},{9,8},{10,11... | collective-permute-start | bytes 1572872 | tf_op jit(solution)/shard_map/ppermute | solution.py:54
  302.5 43.7 %all-to-all-start.5 = ((bf16[16,240,128]{2,1,0:T(8,128)(2,1)}), bf16[16,240,128]{2,1,0:T(8,128)(2,1)S(1)}, u32[]{:S(2)}, u32[]{:S(2)}) async-start(bf16[16,240,128]{2,1,0:T(8,128)(2,1)} %maximum_maximum_fusion), calls=%async_computation.6 | async-start | bytes 1966080 | tf_op jit(solution)/shard_map/all_to_all | solution.py:1017
  324.2 17.4 %collective-permute-start.38 = (bf16[32,1024]{1,0:T(8,128)(2,1)S(1)}, bf16[32,1024]{1,0:T(8,128)(2,1)S(1)}, u32[]{:S(2)}, u32[]{:S(2)}) collective-permute-start(bf16[32,1024]{1,0:T(8,128)(2,1)S(1)} %get-tuple-element.176), channel_id=1, source_target_pairs={{0,6},{2,0},{4,2},{6,4},{1,7},{3,1},{5,3},{7,5},{8,14},{10,8},{12,... | collective-permute-start | bytes 196616 | tf_op jit(solution)/shard_map/ppermute | solution.py:104
  (65 other events, 564.6 us)
Sparse Core Ops, SparseCore 0:
  64.4 62.3 all-gather.5
  178.7 66.5 reduce-scatter.1
Sparse Core Ops, SparseCore 1:
  181.9 118.9 all-gather.3

commit v6 on v5

--- a/solution.py
+++ b/solution.py
@@ -167,10 +167,31 @@
     )
 
 
-def project_kernel(where_ref, *refs, chips):
+def mask_matrix(segments, bias_ref):
+    shape = (128, 128)
+    row = lax.broadcasted_iota(jnp.int32, shape, 0)
+    lane = lax.broadcasted_iota(jnp.int32, shape, 1)
+    segment = row - SEGMENT_LANE
+    here = lane - SEGMENT_LANE
+    apart = (segment >= 0) & (segment < segments) & (here >= 0) & (here < segments)
+    matrix = jnp.where(apart & (here != segment), MASK, 0.0)
+    variate = row - VARIATE_LANE
+    known = (variate >= 0) & (variate < NVAR)
+    copy = (lane - VARIATE_LANE) // NVAR
+    same = (lane - VARIATE_LANE) % NVAR == variate
+    bias = jnp.where(same, bias_ref[1], bias_ref[0])
+    high = bias.astype(bf16).astype(f32)
+    mid = (bias - high).astype(bf16).astype(f32)
+    value = jnp.where(copy == 0, high, jnp.where(copy == 1, mid, bias - high - mid))
+    biased = known & (lane >= VARIATE_LANE) & (lane < VARIATE_LANE + 3 * NVAR)
+    matrix = jnp.where(biased, value, matrix)
+    return jnp.where(known & (lane == OWN_VARIATE_LANE + variate), 1.0, matrix).astype(bf16)
+
+
+def project_kernel(where_ref, bias_ref, *refs, chips, segments):
     piece_refs, refs = refs[:chips], refs[chips:]
-    gain_ref, weight_ref, cosine_ref, sine_ref, gains_ref, hot_ref, mask_ref = refs[:7]
-    normed_ref, raw_ref, query_ref, kv_ref, out_ref, x_ref, arrived = refs[7:]
+    gain_ref, weight_ref, cosine_ref, sine_ref, gains_ref, hot_ref = refs[:6]
+    normed_ref, raw_ref, query_ref, kv_ref, out_ref, x_ref, mask_ref, arrived = refs[6:]
     step = pl.program_id(0)
 
     @pl.when(step == 0)
@@ -180,6 +201,7 @@
         ]
         for copy in copies:
             copy.start()
+        mask_ref[...] = mask_matrix(segments, bias_ref)
         for copy in copies:
             copy.wait()
 
@@ -197,14 +219,15 @@
     scaled = both * lax.rsqrt(half_mean(both * both, lane) + EPSILON) * gains_ref[...]
     turned = scaled * cosine_ref[...] + swap_halves(scaled, lane) * sine_ref[...]
     turned = turned.astype(bf16).astype(f32)
-    query_ref[...] = jnp.where(lane < HD, turned, hot_ref[...].astype(f32)).astype(bf16)
+    hot = hot_ref[...]
+    query_ref[...] = jnp.where(lane < HD, turned, hot.astype(f32)).astype(bf16)
     key = pltpu.roll(turned * HD ** (-0.5), HD, 1)
     ones = jnp.where((lane >= HD) & (lane < HD + 3), 1.0, 0.0)
-    kv_ref[:, :128] = jnp.where(lane < HD, key, mask_ref[...].astype(f32)).astype(bf16)
+    kv_ref[:, :128] = jnp.where(lane < HD, key, dot(hot, mask_ref[...], ((1,), (0,)))).astype(bf16)
     kv_ref[:, 128:] = jnp.where(lane < HD, value, ones).astype(bf16)
 
 
-def project(where, pieces, gain, weight, cosine, sine, gains, hot, mask):
+def project(where, bias, pieces, gain, weight, cosine, sine, gains, hot, segments):
     blocks = len(pieces)
     rows = blocks * BLOCK
     step_rows = PROJECT_BLOCKS * BLOCK
@@ -214,11 +237,11 @@
     anywhere = pl.BlockSpec(memory_space=pl.ANY)
     tables = [whole(gain), whole(weight), row_spec(128), row_spec(128), whole(gains)]
     return pl.pallas_call(
-        partial(project_kernel, chips=blocks),
+        partial(project_kernel, chips=blocks, segments=segments),
         grid_spec=pltpu.PrefetchScalarGridSpec(
-            num_scalar_prefetch=1,
+            num_scalar_prefetch=2,
             grid=(blocks // PROJECT_BLOCKS,),
-            in_specs=[anywhere] * blocks + tables + [row_spec(128), row_spec(128)],
+            in_specs=[anywhere] * blocks + tables + [row_spec(128)],
             out_specs=[
                 row_spec(D),
                 row_spec(128),
@@ -228,6 +251,7 @@
             ],
             scratch_shapes=[
                 pltpu.VMEM((blocks, BLOCK + out_rows, D), bf16),
+                pltpu.VMEM((128, 128), bf16),
                 pltpu.SemaphoreType.DMA((blocks,)),
             ],
         ),
@@ -239,7 +263,7 @@
             jax.ShapeDtypeStruct((blocks, out_rows, D), bf16),
         ],
         name="project",
-    )(where, *pieces, gain, weight, cosine, sine, gains, hot, mask)
+    )(where, bias, *pieces, gain, weight, cosine, sine, gains, hot)
 
 
 def sort_keys(place_ref, own_ref, other_ref, keys_ref):
@@ -554,7 +578,8 @@
     ffn_other_ref,
     back_mine_ref,
     back_other_ref,
-    weight_grad_ref,
+    expand_out_ref,
+    down_out_ref,
     expand_ref,
     down_ref,
     expand_grad_ref,
@@ -602,13 +627,8 @@
 
     @pl.when(step == pl.num_programs(0) - 1)
     def _():
-        for z in range(depth):
-            weight_grad_ref[z, :expand_rows] = expand_grad_ref[
-                z * expand_rows : (z + 1) * expand_rows
-            ].astype(bf16)
-            weight_grad_ref[z, expand_rows:] = down_grad_ref[
-                z * down_rows : (z + 1) * down_rows
-            ].astype(bf16)
+        expand_out_ref[...] = expand_grad_ref[...].astype(bf16)
+        down_out_ref[...] = down_grad_ref[...].astype(bf16)
 
 
 def feed(second, grad, weight, down_rows):
@@ -620,12 +640,14 @@
     other = pl.BlockSpec((tile, D), lambda i: (jnp.maximum(i - steps, 0), 0))
     whole = pl.BlockSpec(weight.shape, lambda i: (0, 0, 0), pipeline_mode=pl.Buffered(1))
     token_rows = jax.ShapeDtypeStruct((rows, D), bf16)
+    expand_out = jax.ShapeDtypeStruct((depth * (both_rows - down_rows), width), bf16)
+    down_out = jax.ShapeDtypeStruct((depth * down_rows, D), bf16)
     return pl.pallas_call(
         feed_kernel,
         grid=(2 * steps,),
         in_specs=[mine, other, mine, other, whole],
-        out_specs=[mine, other, mine, other, whole],
-        out_shape=[token_rows] * 4 + [jax.ShapeDtypeStruct(weight.shape, bf16)],
+        out_specs=[mine, other, mine, other, fixed(expand_out), fixed(down_out)],
+        out_shape=[token_rows] * 4 + [expand_out, down_out],
         scratch_shapes=[
             pltpu.VMEM((depth * (both_rows - down_rows), width), bf16),
             pltpu.VMEM((depth * down_rows, D), bf16),
@@ -817,23 +839,6 @@
     for copy in range(3):
         hot = hot | (lane == VARIATE_LANE + copy * NVAR + variate[:, None])
     return hot.astype(bf16)
-
-
-def mask_rows(segment, variate, segments, bias):
-    lane = jnp.arange(128, dtype=jnp.int32)[None, :]
-    here = lane - SEGMENT_LANE
-    rows = jnp.where(
-        (here >= 0) & (here < segments) & (here != segment[:, None]), jnp.float32(MASK), 0.0
-    )
-    high = lax.reduce_precision(bias, 8, 7)
-    mid = lax.reduce_precision(bias - high, 8, 7)
-    low = bias - high - mid
-    for copy, part in enumerate((high, mid, low)):
-        here = lane - VARIATE_LANE - copy * NVAR
-        value = jnp.where(here == variate[:, None], part[1], part[0])
-        rows = jnp.where((here >= 0) & (here < NVAR), value, rows)
-    rows = jnp.where(lane == OWN_VARIATE_LANE + variate[:, None], 1.0, rows)
-    return rows.astype(bf16)
 
 
 def over_sharers(parts, sharers):
@@ -891,7 +896,6 @@
     own_position = own_rows(position, core)
     bias = lax.dynamic_index_in_dim(variate_bias, head, 1, keepdims=False)
     hot = one_hot_rows(own_segment, own_variate)
-    mask = mask_rows(own_segment, own_variate, segments, bias)
     freqs = THETA ** (-jnp.arange(HD // 2, dtype=f32) / (HD // 2))
     angles = own_position.astype(f32)[:, None] * freqs[None, :]
     cosine = jnp.tile(jnp.cos(angles), (1, 4))
@@ -922,17 +926,17 @@
     high_tile = jnp.sum((low[None, :] <= chunks).astype(jnp.int32), axis=1)
     gains = jnp.concatenate([query_gain, key_gain])[None, :]
 
-    late = (hot, mask, cosine, sine, own_qkv, place, order, low, high, source, low_tile, high_tile)
+    late = (hot, cosine, sine, place, order, low, high, source, low_tile, high_tile)
     pieces, where, riders, late = chip_gather(
         jnp.concatenate([inputs, out_weight], axis=0), cotangent, late
     )
-    hot, mask, cosine, sine, own_qkv, place, order, low, high, source, low_tile, high_tile = late
+    hot, cosine, sine, place, order, low, high, source, low_tile, high_tile = late
 
     feed_part = jnp.concatenate([expand_part, down_weight], axis=0)
     feed_own = lax.all_gather(feed_part[None], "bz", axis=0, tiled=True)
 
     normed_low, raw, query, own_kv, out_mine = project(
-        where, pieces, attn_gain[None], own_qkv, cosine, sine, gains, hot, mask
+        where, bias, pieces, attn_gain[None], own_qkv, cosine, sine, gains, hot, segments
     )
     own_kv, riders = lax.optimization_barrier((own_kv, riders))
     other_kv = swap(own_kv, "core")
@@ -953,11 +957,11 @@
     middle, second, squares = out_project(merged, inputs, out_full, ffn_gain[None])
     second_plane = plane_gather(second)
 
-    ffn_mine, ffn_other, back_mine, back_other, feed_grad = feed(
+    ffn_mine, ffn_other, back_mine, back_other, expand_grad, down_grad = feed(
         second_plane, cotangent_plane, feed_own, hidden_rows
     )
-    feed_grad = lax.psum_scatter(feed_grad, "bz", scatter_dimension=0, tiled=True)
-    feed_grad = feed_grad[0]
+    expand_grad = lax.psum_scatter(expand_grad, "bz", scatter_dimension=0, tiled=True)
+    down_grad = lax.psum_scatter(down_grad, "bz", scatter_dimension=0, tiled=True)
 
     qkv_full = lax.all_gather(
         by_head.transpose(0, 2, 1, 3).reshape(rows, 3 * D), DEVICES, axis=0, tiled=True
@@ -983,10 +987,9 @@
         order, place, source, low_tile, high_tile, query, own_kv, other_kv, kept, grad_attended
     )
     query_grad, from_x = lax.optimization_barrier((query_grad, from_x))
-    from_x = from_x.astype(f32)
-    from_y = swap((joined[2].astype(f32) + from_x[BLOCK:]).astype(bf16), "by")
+    from_y = swap((joined[2].astype(f32) + from_x[BLOCK:].astype(f32)).astype(bf16), "by")
     expand_grad = lax.all_to_all(
-        feed_grad[: 8 * rows].reshape(8, rows, -1), PLANE, 0, 0, tiled=True
+        expand_grad.reshape(8, rows, -1), PLANE, 0, 0, tiled=True
     )
     grad_project, grad_qkv_part, gain_grad, attn_grad = project_back(
         query_grad,
@@ -1000,7 +1003,7 @@
         own_qkv,
     )
     grad_qkv_part, from_y = lax.optimization_barrier((grad_qkv_part, from_y))
-    joined = joined[0].astype(f32) + from_x[:BLOCK] + from_y.astype(f32)
+    joined = joined[0].astype(f32) + from_x[:BLOCK].astype(f32) + from_y.astype(f32)
     ffn_branch = joined[:, :D]
     outputs = (middle + ffn_branch).astype(bf16)
     grad_out = sum_along_z(joined[:, D:].reshape(depth, rows, D))
@@ -1031,7 +1034,7 @@
         ]
     )
     summed = sum_everywhere(packed.reshape(-1, 128))
-    grad_down = feed_grad[8 * rows :].astype(f32)
+    grad_down = down_grad.astype(f32)
     grad_expand = widen(expand_grad, depth, hidden_rows)
     joined, grad_down, grad_expand = lax.optimization_barrier((joined, grad_down, grad_expand))
     grad_inputs, grad_qkv = input_back(

time: 363 us -> 363 us (level)
  waiting for transfers between devices: 77.9 us -> 90 us
  starting transfers between devices: 91.2 us -> 84.7 us
  other arithmetic: 32.2 us -> 27.4 us
    ppermute x36, waiting for transfers between devices: 56.6 us -> 68.7 us  [swap(): return lax.ppermute(shard, axis, [(0, 1), (1, 0)])]
    ppermute x9, starting transfers between devices: 24.8 us -> 15.6 us  [z_shifts(): lax.ppermute(value, 'bz', [(i, (i + by + 1) % depth) for i in range(depth)])]
    all_to_all x1, waiting for transfers between devices: 5.41 us -> 0.01 us  [body(): lax.all_to_all(expand_grad.reshape(8, rows, -1), PLANE, 0, 0, tiled=True)]
    convert_element_type x4 -> x2, other arithmetic: 8.49 us -> 3.79 us  [the longest x1 2 us: body(): (joined[2].astype(f32) + from_x[BLOCK:].astype(f32)).astype(bf16)]
    all_to_all x1, starting transfers between devices: 3.31 us -> 7.45 us  [body(): own_qkv = lax.all_to_all(to_heads, DEVICES, 0, 0, tiled=True)]
    unnamed x79 -> x73, local copies, waits for them, and re-layouts: 11.5 us -> 12.5 us
  transfers between devices with their start and end apart: 54 -> 55, of which waited for: 21 -> 23; matrix products, arithmetic and copies ran while one was open for 16% -> 15% of each run, Pallas kernels for 21% -> 21%
where the time goes in v6:
time: 363 us; the launch traced here: 361 us
  Pallas kernels  101 us (28%)
  waiting for transfers between devices  90 us (25%)
  starting transfers between devices  84.7 us (23%)
  local copies, waits for them, and re-layouts  34.5 us (10%)
  other arithmetic  27.4 us (8%)
  between operations  23.7 us (7%)
    ppermute x36, waiting for transfers between devices, swap(): return lax.ppermute(shard, axis, [(0, 1), (1, 0)])  68.7 us
    ppermute x36, starting transfers between devices, swap(): return lax.ppermute(shard, axis, [(0, 1), (1, 0)])  38.5 us
    pallas_call x1, Pallas kernels, attend_back(): pl.pallas_call(attend_back_kernel, grid_spec=pltpu.PrefetchScalarGridSpec...  29.5 us
    pallas_call x1, Pallas kernels, feed(): pl.pallas_call(feed_kernel, grid=(2 * steps,), in_specs=[mine, other, min...  17.7 us
    ppermute x9, starting transfers between devices, z_shifts(): lax.ppermute(value, 'bz', [(i, (i + by + 1) % depth) for i in range(depth)])  15.6 us
    pallas_call x1, Pallas kernels, attend(): pl.pallas_call(attend_kernel, grid_spec=pltpu.PrefetchScalarGridSpec(num_...  13.2 us
    unnamed x73, local copies, waits for them, and re-layouts  12.5 us
    pallas_call x1, Pallas kernels, project(): pl.pallas_call(partial(project_kernel, chips=blocks, segments=segments),...  11.5 us
  transfers between devices with their start and end apart: 55, of which 23 were waited for; matrix products, arithmetic and copies ran while one was open for 15% of the time, Pallas kernels for 21%

profile of v6, /device:TPU:0, one launch (start us, length us, event | category | flops | bytes accessed | tf_op | source)
XLA Modules:
  0.0 361.2 jit_solution(13997676410617282306)
XLA Ops:
  22.4 3.5 all-to-all-start.2
  36.5 7.5 %all-to-all-start = ((bf16[32,32,192]{2,1,0:T(8,128)(2,1)}), bf16[32,32,192]{2,1,0:T(8,128)(2,1)S(1)}, u32[]{:S(2)}, u32[]{:S(2)}) async-start(bf16[32,32,192]{2,1,0:T(8,128)(2,1)} %bitcast.15), calls=%async_computation | async-start | bytes 1048576 | tf_op jit(solution)/shard_map/all_to_all | solution.py:883
  53.2 7.0 %collective-permute-done.4.refs_8_ = bf16[160,1024]{1,0:T(8,128)(2,1)} collective-permute-done((bf16[160,1024]{1,0:T(8,128)(2,1)}, bf16[160,1024]{1,0:T(8,128)(2,1)}, u32[]{:S(2)}, u32[]{:S(2)}) %collective-permute-start.4) | collective-permute-done | bytes 327712 | tf_op jit(solution)/shard_map/ppermute | solution.py:54
  60.2 6.3 %collective-permute-done.6.refs_9_ = bf16[160,1024]{1,0:T(8,128)(2,1)} collective-permute-done((bf16[160,1024]{1,0:T(8,128)(2,1)}, bf16[160,1024]{1,0:T(8,128)(2,1)}, u32[]{:S(2)}, u32[]{:S(2)}) %collective-permute-start.6) | collective-permute-done | bytes 327712 | tf_op jit(solution)/shard_map/ppermute | solution.py:54
  67.1 6.4 %collective-permute-done.10.refs_12_ = bf16[160,1024]{1,0:T(8,128)(2,1)S(1)} collective-permute-done((bf16[160,1024]{1,0:T(8,128)(2,1)}, bf16[160,1024]{1,0:T(8,128)(2,1)S(1)}, u32[]{:S(2)}, u32[]{:S(2)}) %collective-permute-start.10) | collective-permute-done | bytes 327712 | tf_op jit(solution)/shard_map/ppermute | solution.py:54
  80.0 5.3 %collective-permute-done.11.refs_3_ = bf16[160,1024]{1,0:T(8,128)(2,1)S(1)} collective-permute-done((bf16[160,1024]{1,0:T(8,128)(2,1)}, bf16[160,1024]{1,0:T(8,128)(2,1)S(1)}, u32[]{:S(2)}, u32[]{:S(2)}) %collective-permute-start.11) | collective-permute-done | bytes 327712 | tf_op jit(solution)/shard_map/ppermute | solution.py:54
  94.4 11.5 %project.1 = (bf16[2048,1024]{1,0:T(8,128)(2,1)}, f32[2048,128]{1,0:T(8,128)}, bf16[2048,128]{1,0:T(8,128)(2,1)}, bf16[2048,256]{1,0:T(8,128)(2,1)}, bf16[16,32,1024]{2,1,0:T(8,128)(2,1)}) custom-call(s32[16]{0:T(128)} %compare_select_fusion.7.where_ref, f32[2]{0:T(128)} %fusion.16.bias_ref, bf16[160,1024]{1,0:T(8,128)(2,1)} %copy-done.10, ...), custom_call_target="tpu_custom_call" | custom-call | tf_op jit(solution)/shard_map/project/pallas_call | solution.py:239
  110.4 13.2 %attend.1 = (f32[2048,128]{1,0:T(8,128)}, bf16[16,64,128]{2,1,0:T(8,128)(2,1)}) custom-call(s32[16]{0:T(128)} %get-tuple-element.80.order_ref, s32[32]{0:T(128)} %copy-done.28, s32[4]{0:T(128)} %copy-done.26, s32[4]{0:T(128)} %copy-done.27, bf16[2048,128]{1,0:T(8,128)(2,1)} %get-tuple-element.95.query_ref, bf16[2048,256]{1,0:T(8,128)(2,1)} %get-tuple-element.97.own_ref, ...), custom_call_target="tpu_custom_call" | custom-call | tf_op jit(solution)/shard_map/attend/pallas_call | solution.py:341
  123.7 6.1 %all-to-all-start.1 = ((bf16[16,64,128]{2,1,0:T(8,128)(2,1)}), bf16[16,64,128]{2,1,0:T(8,128)(2,1)S(1)}, u32[]{:S(2)}, u32[]{:S(2)}) async-start(bf16[16,64,128]{2,1,0:T(8,128)(2,1)} %get-tuple-element.100), calls=%async_computation.1 | async-start | bytes 524288 | tf_op jit(solution)/shard_map/all_to_all | solution.py:953
  133.5 6.8 %all-to-all-done.1 = bf16[16,64,128]{2,1,0:T(8,128)(2,1)S(1)} async-done(((bf16[16,64,128]{2,1,0:T(8,128)(2,1)}), bf16[16,64,128]{2,1,0:T(8,128)(2,1)S(1)}, u32[]{:S(2)}, u32[]{:S(2)}) %all-to-all-start.1) | async-done | bytes 262176 | tf_op jit(solution)/shard_map/all_to_all | solution.py:953
  146.7 4.6 %collective-permute-done.22 = bf16[128,1024]{1,0:T(8,128)(2,1)S(1)} collective-permute-done((bf16[128,1024]{1,0:T(8,128)(2,1)}, bf16[128,1024]{1,0:T(8,128)(2,1)S(1)}, u32[]{:S(2)}, u32[]{:S(2)}) %collective-permute-start.22) | collective-permute-done | bytes 262176 | tf_op jit(solution)/shard_map/ppermute | solution.py:54
  161.3 17.7 %feed.1 = (bf16[512,1024]{1,0:T(8,128)(2,1)}, bf16[512,1024]{1,0:T(8,128)(2,1)}, bf16[512,1024]{1,0:T(8,128)(2,1)}, bf16[512,1024]{1,0:T(8,128)(2,1)}, bf16[1024...) custom-call(bf16[512,1024]{1,0:T(8,128)(2,1)} %copy-done.8, bf16[512,1024]{1,0:T(8,128)(2,1)} %copy-done.13, ...), custom_call_target="tpu_custom_call" | custom-call | tf_op jit(solution)/shard_map/feed/pallas_call | solution.py:645
  195.4 4.3 %collective-permute-done.28.from_x_ref = bf16[128,1024]{1,0:T(8,128)(2,1)S(1)} collective-permute-done((bf16[128,1024]{1,0:T(8,128)(2,1)S(1)}, bf16[128,1024]{1,0:T(8,128)(2,1)S(1)}, u32[]{:S(2)}, u32[]{:S(2)}) %collective-permute-start.28) | collective-permute-done | bytes 262176 | tf_op jit(solution)/shard_map/ppermute | solution.py:54
  201.1 3.9 %middle_back.1 = (f32[128,1024]{1,0:T(8,128)}, bf16[128,1024]{1,0:T(8,128)(2,1)}, bf16[1024,128]{1,0:T(8,128)(2,1)}, f32[8,1024]{1,0:T(8,128)}) custom-call(f32[128,1024]{1,0:T(8,128)} %slice.183.own_ref, bf16[128,1024]{1,0:T(8,128)(2,1)} %copy-done.21, bf16[128,1024]{1,0:T(8,128)(2,1)} %copy-done.22, f32[128,1024]{1,0:T(8,128)} %get-tuple-element.105.middle_ref, ...), custom_call_target="tpu_custom_call" | custom-call | tf_op jit(solution)/shard_map/middle_back/pallas_call | solution.py:713
  205.0 5.3 %out_grad.1 = (bf16[512,2048]{1,0:T(8,128)(2,1)}, bf16[512,2048]{1,0:T(8,128)(2,1)}) custom-call(s32[8]{0:T(128)} %stack.62.members_ref, bf16[1024,128]{1,0:T(8,128)(2,1)} %bitcast.101, bf16[128,1024]{1,0:T(8,128)(2,1)} %get-tuple-element.110.branch_ref, bf16[512,1024]{1,0:T(8,128)(2,1)} %get-tuple-element.111.ffn_mine_ref, ...), custom_call_target="tpu_custom_call" | custom-call | tf_op jit(solution)/shard_map/out_grad/pallas_call | solution.py:752
  210.2 4.7 %all-to-all-start.3 = ((bf16[16,64,128]{2,1,0:T(8,128)(2,1)}), bf16[16,64,128]{2,1,0:T(8,128)(2,1)S(1)}, u32[]{:S(2)}, u32[]{:S(2)}) async-start(bf16[16,64,128]{2,1,0:T(8,128)(2,1)} %bitcast.34), calls=%async_computation.3 | async-start | bytes 524288 | tf_op jit(solution)/shard_map/all_to_all | solution.py:972
  220.5 9.3 %all-to-all-done.3.grad_ref = bf16[16,64,128]{2,1,0:T(8,128)(2,1)S(1)} async-done(((bf16[16,64,128]{2,1,0:T(8,128)(2,1)}), bf16[16,64,128]{2,1,0:T(8,128)(2,1)S(1)}, u32[]{:S(2)}, u32[]{:S(2)}) %all-to-all-start.3) | async-done | bytes 262176 | tf_op jit(solution)/shard_map/all_to_all | solution.py:972
  232.6 29.5 %attend_back.1 = (bf16[2048,128]{1,0:T(8,128)(2,1)}, bf16[2048,128]{1,0:T(8,128)(2,1)}, bf16[2048,128]{1,0:T(8,128)(2,1)}, f32[8,128]{1,0:T(8,128)}) custom-call(s32[16]{0:T(128)} %get-tuple-element.80.order_ref, s32[32]{0:T(128)} %copy-done.28, s32[32]{0:T(128)} %select_reduce_fusion.source_ref, s32[8]{0:T(128)} %get-tuple-element.116.low_ref, ...), custom_call_target="tpu_custom_call" | custom-call | tf_op jit(solution)/shard_map/attend_back/pallas_call | solution.py:475
  262.8 3.5 all-to-all-start.4
  271.2 8.0 %project_back.1 = (bf16[16,192,128]{2,1,0:T(8,128)(2,1)}, bf16[1024,192]{1,0:T(8,128)(2,1)}, f32[8,128]{1,0:T(8,128)}, f32[1024,128]{1,0:T(8,128)}) custom-call(bf16[2048,128]{1,0:T(8,128)(2,1)} %get-tuple-element.124.query_grad_ref, bf16[2048,128]{1,0:T(8,128)(2,1)} %get-tuple-element.125.own_ref, bf16[2048,128]{1,0:T(8,128)(2,1)} %copy-done.17, ...), custom_call_target="tpu_custom_call" | custom-call | tf_op jit(solution)/shard_map/project_back/pallas_call | solution.py:550
  281.2 16.3 %collective-permute-done.34 = bf16[128,2048]{1,0:T(8,128)(2,1)} collective-permute-done((bf16[128,2048]{1,0:T(8,128)(2,1)}, bf16[128,2048]{1,0:T(8,128)(2,1)}, u32[]{:S(2)}, u32[]{:S(2)}) %collective-permute-start.34) | collective-permute-done | bytes 524320 | tf_op jit(solution)/shard_map/ppermute | solution.py:54
  305.4 5.0 %all-to-all-start.5 = ((bf16[16,240,128]{2,1,0:T(8,128)(2,1)}), bf16[16,240,128]{2,1,0:T(8,128)(2,1)S(1)}, u32[]{:S(2)}, u32[]{:S(2)}) async-start(bf16[16,240,128]{2,1,0:T(8,128)(2,1)} %maximum_maximum_fusion), calls=%async_computation.6 | async-start | bytes 1966080 | tf_op jit(solution)/shard_map/all_to_all | solution.py:1020
  327.5 5.2 %collective-permute-start.44 = (f32[18,128]{1,0:T(8,128)S(1)}, f32[18,128]{1,0:T(8,128)S(1)}, u32[]{:S(2)}, u32[]{:S(2)}) collective-permute-start(f32[18,128]{1,0:T(8,128)S(1)} %add.388), channel_id=1, source_target_pairs={{0,6},{2,0},{4,2},{6,4},{1,7},{3,1},{5,3},{7,5},{8,14},{10,8},{12,... | collective-permute-start | bytes 27656 | tf_op jit(solution)/shard_map/ppermute | solution.py:104
  347.6 6.5 %input_back.1 = (f32[128,1024]{1,0:T(8,128)}, f32[32,3072]{1,0:T(8,128)}) custom-call(bf16[16,240,128]{2,1,0:T(8,128)(2,1)} %copy-done.3, bf16[1024,3072]{1,0:T(8,128)(2,1)} %all-gather.4.cloned.1.call-done.weight_ref, bf16[128,1024]{1,0:T(8,128)(2,1)} %x_ref.3, f32[1,1024]{1,0:T(1,128)} %bitcast.117, f32[128,1024]{1,0:T(8,128)} %get-tuple-element.138.middle_ref), custom_call_target="tpu_custom_call" | custom-call | tf_op jit(solution)/shard_map/input_back/pallas_call | solution.py:790
  (267 shorter events, 140.2 us)
Async XLA Ops:
  9.9 34.1 %collective-permute-start = (bf16[160,1024]{1,0:T(8,128)(2,1)S(1)}, bf16[160,1024]{1,0:T(8,128)(2,1)}, u32[]{:S(2)}, u32[]{:S(2)}) collective-permute-start(bf16[160,1024]{1,0:T(8,128)(2,1)S(1)} %constant_dynamic-update-slice_fusion.refs_0_), channel_id=1, source_target_pairs={{0,16},{16,0},{1,17},{17,1},{2,18},{18,2},{3,19},{19,3},{4,20},{20... | collective-permute-start | bytes 983048 | tf_op jit(solution)/shard_map/ppermute | solution.py:54
  12.8 19.8 %collective-permute-start.1 = (bf16[160,1024]{1,0:T(8,128)(2,1)S(1)}, bf16[160,1024]{1,0:T(8,128)(2,1)}, u32[]{:S(2)}, u32[]{:S(2)}) collective-permute-start(bf16[160,1024]{1,0:T(8,128)(2,1)S(1)} %constant_dynamic-update-slice_fusion.refs_0_), channel_id=1, source_target_pairs={{0,2},{2,4},{4,6},{6,0},{1,3},{3,5},{5,7},{7,1},{8,10},{10,12},{12... | collective-permute-start | bytes 983048 | tf_op jit(solution)/shard_map/ppermute | solution.py:104
  14.4 31.4 %collective-permute-start.3 = (bf16[160,1024]{1,0:T(8,128)(2,1)S(1)}, bf16[160,1024]{1,0:T(8,128)(2,1)}, u32[]{:S(2)}, u32[]{:S(2)}) collective-permute-start(bf16[160,1024]{1,0:T(8,128)(2,1)S(1)} %constant_dynamic-update-slice_fusion.refs_0_), channel_id=1, source_target_pairs={{0,4},{2,6},{4,0},{6,2},{1,5},{3,7},{5,1},{7,3},{8,12},{10,14},{12... | collective-permute-start | bytes 983048 | tf_op jit(solution)/shard_map/ppermute | solution.py:104
  17.0 30.3 %collective-permute-start.5 = (bf16[160,1024]{1,0:T(8,128)(2,1)S(1)}, bf16[160,1024]{1,0:T(8,128)(2,1)}, u32[]{:S(2)}, u32[]{:S(2)}) collective-permute-start(bf16[160,1024]{1,0:T(8,128)(2,1)S(1)} %constant_dynamic-update-slice_fusion.refs_0_), channel_id=1, source_target_pairs={{0,6},{2,0},{4,2},{6,4},{1,7},{3,1},{5,3},{7,5},{8,14},{10,8},{12,... | collective-permute-start | bytes 983048 | tf_op jit(solution)/shard_map/ppermute | solution.py:104
  18.3 29.5 %collective-permute-start.7 = (bf16[160,1024]{1,0:T(8,128)(2,1)S(1)}, bf16[160,1024]{1,0:T(8,128)(2,1)}, u32[]{:S(2)}, u32[]{:S(2)}) collective-permute-start(bf16[160,1024]{1,0:T(8,128)(2,1)S(1)} %constant_dynamic-update-slice_fusion.refs_0_), channel_id=1, source_target_pairs={{0,1},{1,0},{2,3},{3,2},{4,5},{5,4},{6,7},{7,6},{8,9},{9,8},{10,11... | collective-permute-start | bytes 983048 | tf_op jit(solution)/shard_map/ppermute | solution.py:54
  36.5 54.9 %all-to-all-start = ((bf16[32,32,192]{2,1,0:T(8,128)(2,1)}), bf16[32,32,192]{2,1,0:T(8,128)(2,1)S(1)}, u32[]{:S(2)}, u32[]{:S(2)}) async-start(bf16[32,32,192]{2,1,0:T(8,128)(2,1)} %bitcast.15), calls=%async_computation | async-start | bytes 1048576 | tf_op jit(solution)/shard_map/all_to_all | solution.py:883
  43.9 116.4 %all-gather.6.cloned.1.call-start = ((), (), s32[]{:S(2)}) async-start(), calls=%async_computation.11 | async-start | bytes 3932160 | tf_op jit(solution)/shard_map/all_gather | solution.py:936
  44.0 22.5 %collective-permute-start.8 = (bf16[160,1024]{1,0:T(8,128)(2,1)}, bf16[160,1024]{1,0:T(8,128)(2,1)}, u32[]{:S(2)}, u32[]{:S(2)}) collective-permute-start(bf16[160,1024]{1,0:T(8,128)(2,1)} %collective-permute-done.1.refs_4_), channel_id=1, source_target_pairs={{0,1},{1,0},{2,3},{3,2},{4,5},{5,4},{6,7},{7,6},{8,9},{9,8},{10,11... | collective-permute-start | bytes 983048 | tf_op jit(solution)/shard_map/ppermute | solution.py:54
  47.3 19.8 %collective-permute-start.9 = (bf16[160,1024]{1,0:T(8,128)(2,1)}, bf16[160,1024]{1,0:T(8,128)(2,1)}, u32[]{:S(2)}, u32[]{:S(2)}) collective-permute-start(bf16[160,1024]{1,0:T(8,128)(2,1)} %collective-permute-done.3.refs_5_), channel_id=1, source_target_pairs={{0,1},{1,0},{2,3},{3,2},{4,5},{5,4},{6,7},{7,6},{8,9},{9,8},{10,11... | collective-permute-start | bytes 983048 | tf_op jit(solution)/shard_map/ppermute | solution.py:54
  47.8 18.7 %collective-permute-start.6 = (bf16[160,1024]{1,0:T(8,128)(2,1)}, bf16[160,1024]{1,0:T(8,128)(2,1)}, u32[]{:S(2)}, u32[]{:S(2)}) collective-permute-start(bf16[160,1024]{1,0:T(8,128)(2,1)} %collective-permute-done.5.refs_6_), channel_id=1, source_target_pairs={{0,16},{16,0},{1,17},{17,1},{2,18},{18,2},{3,19},{19,3},{4,20},{20... | collective-permute-start | bytes 983048 | tf_op jit(solution)/shard_map/ppermute | solution.py:54
  48.1 25.3 %collective-permute-start.10 = (bf16[160,1024]{1,0:T(8,128)(2,1)}, bf16[160,1024]{1,0:T(8,128)(2,1)S(1)}, u32[]{:S(2)}, u32[]{:S(2)}) collective-permute-start(bf16[160,1024]{1,0:T(8,128)(2,1)} %collective-permute-done.5.refs_6_), channel_id=1, source_target_pairs={{0,1},{1,0},{2,3},{3,2},{4,5},{5,4},{6,7},{7,6},{8,9},{9,8},{10,11... | collective-permute-start | bytes 983048 | tf_op jit(solution)/shard_map/ppermute | solution.py:54
  77.4 17.0 %collective-permute-start.14 = (bf16[160,1024]{1,0:T(8,128)(2,1)}, bf16[160,1024]{1,0:T(8,128)(2,1)}, u32[]{:S(2)}, u32[]{:S(2)}) collective-permute-start(bf16[160,1024]{1,0:T(8,128)(2,1)} %collective-permute-done.6.refs_9_), channel_id=1, source_target_pairs={{0,1},{1,0},{2,3},{3,2},{4,5},{5,4},{6,7},{7,6},{8,9},{9,8},{10,11... | collective-permute-start | bytes 983048 | tf_op jit(solution)/shard_map/ppermute | solution.py:54
  78.5 27.4 %collective-permute-start.15 = (bf16[128,1024]{1,0:T(8,128)(2,1)}, bf16[128,1024]{1,0:T(8,128)(2,1)}, u32[]{:S(2)}, u32[]{:S(2)}) collective-permute-start(bf16[128,1024]{1,0:T(8,128)(2,1)} %cotangent_ref.1), channel_id=1, source_target_pairs={{0,16},{16,0},{1,17},{17,1},{2,18},{18,2},{3,19},{19,3},{4,20},{20... | collective-permute-start | bytes 786440 | tf_op jit(solution)/shard_map/ppermute | solution.py:54
  85.2 20.6 %collective-permute-start.16 = (bf16[128,1024]{1,0:T(8,128)(2,1)}, bf16[128,1024]{1,0:T(8,128)(2,1)}, u32[]{:S(2)}, u32[]{:S(2)}) collective-permute-start(bf16[128,1024]{1,0:T(8,128)(2,1)} %cotangent_ref.1), channel_id=1, source_target_pairs={{0,1},{1,0},{2,3},{3,2},{4,5},{5,4},{6,7},{7,6},{8,9},{9,8},{10,11... | collective-permute-start | bytes 786440 | tf_op jit(solution)/shard_map/ppermute | solution.py:54
  106.0 24.1 %collective-permute-start.20 = (bf16[16,32,1024]{2,1,0:T(8,128)(2,1)}, bf16[16,32,1024]{2,1,0:T(8,128)(2,1)}, u32[]{:S(2)}, u32[]{:S(2)}) collective-permute-start(bf16[16,32,1024]{2,1,0:T(8,128)(2,1)} %get-tuple-element.104), channel_id=1, source_target_pairs={{0,8},{8,0},{1,9},{9,1},{2,10},{10,2},{3,11},{11,3},{4,12},{12,4},... | collective-permute-start | bytes 3145736 | tf_op jit(solution)/shard_map/ppermute | solution.py:54
  106.5 17.1 %collective-permute-start.18 = (bf16[128,1024]{1,0:T(8,128)(2,1)}, bf16[128,1024]{1,0:T(8,128)(2,1)S(1)}, u32[]{:S(2)}, u32[]{:S(2)}) collective-permute-start(bf16[128,1024]{1,0:T(8,128)(2,1)} %collective-permute-done.15), channel_id=1, source_target_pairs={{0,1},{1,0},{2,3},{3,2},{4,5},{5,4},{6,7},{7,6},{8,9},{9,8},{10,11... | collective-permute-start | bytes 786440 | tf_op jit(solution)/shard_map/ppermute | solution.py:54
  129.8 132.9 %reduce-scatter.3.cloned.1.call-start = ((), (), s32[]{:S(2)}) async-start(), calls=%async_computation.8 | async-start | bytes 2621440 | tf_op jit(solution)/shard_map/reduce_scatter | solution.py:963
  179.1 146.6 %reduce-scatter.5.cloned.1.call-start = ((), (), s32[]{:S(2)}) async-start(), calls=%async_computation.9 | async-start | bytes 1310720 | tf_op jit(solution)/shard_map/reduce_scatter | solution.py:964
  179.8 166.8 %all-gather.4.cloned.1.call-start = ((), (), s32[]{:S(2)}) async-start(), calls=%async_computation.10 | async-start | bytes 6488064 | tf_op jit(solution)/shard_map/all_gather | solution.py:966
  210.2 19.6 %all-to-all-start.3 = ((bf16[16,64,128]{2,1,0:T(8,128)(2,1)}), bf16[16,64,128]{2,1,0:T(8,128)(2,1)S(1)}, u32[]{:S(2)}, u32[]{:S(2)}) async-start(bf16[16,64,128]{2,1,0:T(8,128)(2,1)} %bitcast.34), calls=%async_computation.3 | async-start | bytes 524288 | tf_op jit(solution)/shard_map/all_to_all | solution.py:972
  229.8 36.4 %collective-permute-start.32 = (bf16[256,2048]{1,0:T(8,128)(2,1)}, bf16[256,2048]{1,0:T(8,128)(2,1)}, u32[]{:S(2)}, u32[]{:S(2)}) collective-permute-start(bf16[256,2048]{1,0:T(8,128)(2,1)} %pad_maximum_fusion.1), channel_id=1, source_target_pairs={{0,16},{16,0},{1,17},{17,1},{2,18},{18,2},{3,19},{19,3},{4,20},{20... | collective-permute-start | bytes 3145736 | tf_op jit(solution)/shard_map/ppermute | solution.py:54
  262.8 34.8 %all-to-all-start.4 = ((bf16[8,32,1024]{2,1,0:T(8,128)(2,1)}), bf16[8,32,1024]{2,1,0:T(8,128)(2,1)S(1)}, u32[]{:S(2)}, u32[]{:S(2)}) async-start(bf16[8,32,1024]{2,1,0:T(8,128)(2,1)} %bitcast.111), calls=%async_computation.5 | async-start | bytes 1048576 | tf_op jit(solution)/shard_map/all_to_all | solution.py:991
  268.3 29.3 %collective-permute-start.34 = (bf16[128,2048]{1,0:T(8,128)(2,1)}, bf16[128,2048]{1,0:T(8,128)(2,1)}, u32[]{:S(2)}, u32[]{:S(2)}) collective-permute-start(bf16[128,2048]{1,0:T(8,128)(2,1)} %add_convert_fusion.1), channel_id=1, source_target_pairs={{0,1},{1,0},{2,3},{3,2},{4,5},{5,4},{6,7},{7,6},{8,9},{9,8},{10,11... | collective-permute-start | bytes 1572872 | tf_op jit(solution)/shard_map/ppermute | solution.py:54
  305.4 41.2 %all-to-all-start.5 = ((bf16[16,240,128]{2,1,0:T(8,128)(2,1)}), bf16[16,240,128]{2,1,0:T(8,128)(2,1)S(1)}, u32[]{:S(2)}, u32[]{:S(2)}) async-start(bf16[16,240,128]{2,1,0:T(8,128)(2,1)} %maximum_maximum_fusion), calls=%async_computation.6 | async-start | bytes 1966080 | tf_op jit(solution)/shard_map/all_to_all | solution.py:1020
  (63 other events, 580.9 us)
Sparse Core Ops, SparseCore 0:
  52.0 63.5 all-gather.5
  179.2 48.8 reduce-scatter.2
  230.3 34.4 reduce-scatter.4
Sparse Core Ops, SparseCore 1:
  183.2 121.5 all-gather.3

commit v7 on v6

--- a/solution.py
+++ b/solution.py
@@ -25,7 +25,7 @@
 VARIATE_LANE = 76
 OWN_VARIATE_LANE = 88
 MASK = -512.0
-QUERY_TILE = 512
+QUERY_TILE = 1024
 KEY_TILE = 512
 PROJECT_BLOCKS = 4
 
@@ -93,9 +93,11 @@
             step *= 2
         return values
     shifted = z_shifts([values] * (depth - 1))
-    copies = jnp.stack([values] + shifted)
-    back = (lax.axis_index("bz") - jnp.arange(depth, dtype=jnp.int32)) % depth
-    return sum(lax.dynamic_index_in_dim(copies, back[z], 0, keepdims=False) for z in range(depth))
+    shifted = [values] + shifted
+    while len(shifted) > 1:
+        half = len(shifted) // 2
+        shifted = [shifted[i] + shifted[half + i] for i in range(half)]
+    return shifted[0]
 
 
 def z_shifts(values):
@@ -111,10 +113,8 @@
     if depth > 4:
         parts = parts.reshape(-1, parts.shape[2]).astype(bf16)
         return lax.psum_scatter(parts, "bz", scatter_dimension=0, tiled=True).astype(f32)
-    z = lax.axis_index("bz")
-    parts = [
-        lax.dynamic_index_in_dim(parts, (z + by) % depth, 0, keepdims=False) for by in range(depth)
-    ]
+    z = lax.axis_index("bz").astype(jnp.uint32)
+    parts = [pick(parts, (z + jnp.uint32(by)) & jnp.uint32(depth - 1), 0) for by in range(depth)]
     arrived = z_shifts([part.astype(bf16) for part in parts[1:]])
     return sum([part.astype(f32) for part in arrived], parts[0])
 
@@ -143,12 +143,12 @@
 
 
 def plane_members():
-    by, hx, core = lax.axis_index("by"), lax.axis_index("hx"), lax.axis_index("core")
-    members = []
-    for core_flip in (0, 1):
-        for x_flip, y_flip in ((0, 0), (1, 0), (0, 1), (1, 1)):
-            members.append((by ^ y_flip) * 4 + (hx ^ x_flip) * 2 + (core ^ core_flip))
-    return members
+    here = (lax.axis_index("by") * 2 + lax.axis_index("hx")) * 2 + lax.axis_index("core")
+    return here ^ jnp.array([0, 2, 4, 6, 1, 3, 5, 7], jnp.int32)
+
+
+def pick(array, index, axis):
+    return lax.dynamic_index_in_dim(array, index.astype(jnp.uint32), axis, keepdims=False)
 
 
 def lanes(shape):
@@ -830,7 +830,7 @@
 
 def own_rows(array, core):
     pairs = array.reshape(-1, 2, BLOCK)
-    return lax.dynamic_index_in_dim(pairs, core, 1, keepdims=False).reshape(-1)
+    return pick(pairs, core, 1).reshape(-1)
 
 
 def one_hot_rows(segment, variate):
@@ -894,7 +894,7 @@
     own_segment = own_rows(segment, core)
     own_variate = own_rows(variate_ids, core)
     own_position = own_rows(position, core)
-    bias = lax.dynamic_index_in_dim(variate_bias, head, 1, keepdims=False)
+    bias = pick(variate_bias, head, 1)
     hot = one_hot_rows(own_segment, own_variate)
     freqs = THETA ** (-jnp.arange(HD // 2, dtype=f32) / (HD // 2))
     angles = own_position.astype(f32)[:, None] * freqs[None, :]
@@ -902,8 +902,8 @@
     sine = jnp.sin(angles)
     sine = jnp.tile(jnp.concatenate([-sine, sine], axis=1), (1, 2))
     pairs = block_order.reshape(chips, 2)
-    own_place = lax.dynamic_index_in_dim(pairs, core, 1, keepdims=False)
-    other_place = lax.dynamic_index_in_dim(pairs, 1 - core, 1, keepdims=False)
+    own_place = pick(pairs, core, 1)
+    other_place = pick(pairs, 1 - core, 1)
     place = jnp.concatenate([own_place, other_place])
     rank = jnp.sum((own_place[None, :] < own_place[:, None]).astype(jnp.int32), axis=1)
     taken = chips // sharers
@@ -974,7 +974,7 @@
     )
 
     joined_mine, joined_other = out_grad(
-        jnp.stack(plane_members()), merged, branch_grad, ffn_mine, ffn_other, depth
+        plane_members(), merged, branch_grad, ffn_mine, ffn_other, depth
     )
     joined_other = swap(joined_other, "core")
     joined = (joined_mine.astype(f32) + joined_other.astype(f32)).astype(bf16)
@@ -1002,15 +1002,14 @@
         normed_low,
         own_qkv,
     )
-    grad_qkv_part, from_y = lax.optimization_barrier((grad_qkv_part, from_y))
     joined = joined[0].astype(f32) + from_x[:BLOCK].astype(f32) + from_y.astype(f32)
     ffn_branch = joined[:, :D]
     outputs = (middle + ffn_branch).astype(bf16)
     grad_out = sum_along_z(joined[:, D:].reshape(depth, rows, D))
     grad_qkv_part, expand_grad = lax.optimization_barrier((grad_qkv_part, expand_grad))
     grad_qkv_part = grad_qkv_part.reshape(chips, 2, rows, 3 * HD)
-    grad_qkv_own = lax.dynamic_index_in_dim(grad_qkv_part, core, 1, keepdims=False)
-    grad_qkv_other = lax.dynamic_index_in_dim(grad_qkv_part, 1 - core, 1, keepdims=False)
+    grad_qkv_own = pick(grad_qkv_part, core, 1)
+    grad_qkv_other = pick(grad_qkv_part, 1 - core, 1)
     grad_qkv_own = grad_qkv_own.astype(f32) + swap(grad_qkv_other, "core").astype(f32)
     values = grad_qkv_own[:, :, 2 * HD :]
     values = jnp.concatenate([values[:, : rows // 2], values[:, rows // 2 :]], axis=2)

time: 363 us -> 347 us (0.956)
  between operations: 23.7 us -> 15.9 us
  starting transfers between devices: 84.7 us -> 80.1 us
  waiting for transfers between devices: 90 us -> 86 us
    ppermute x36, waiting for transfers between devices: 68.7 us -> 64.7 us  [swap(): return lax.ppermute(shard, axis, [(0, 1), (1, 0)])]
    unnamed x73 -> x75, local copies, waits for them, and re-layouts: 12.5 us -> 11.6 us
  transfers between devices with their start and end apart: 55 -> 55, of which waited for: 23 -> 26; matrix products, arithmetic and copies ran while one was open for 15% -> 15% of each run, Pallas kernels for 21% -> 23%
where the time goes in v7:
time: 347 us; the launch traced here: 345 us
  Pallas kernels  103 us (30%)
  waiting for transfers between devices  86 us (25%)
  starting transfers between devices  80.1 us (23%)
  local copies, waits for them, and re-layouts  32.3 us (9%)
  other arithmetic  28.5 us (8%)
  between operations  15.9 us (5%)
    ppermute x36, waiting for transfers between devices, swap(): return lax.ppermute(shard, axis, [(0, 1), (1, 0)])  64.7 us
    ppermute x36, starting transfers between devices, swap(): return lax.ppermute(shard, axis, [(0, 1), (1, 0)])  36 us
    pallas_call x1, Pallas kernels, attend_back(): pl.pallas_call(attend_back_kernel, grid_spec=pltpu.PrefetchScalarGridSpec...  30.5 us
    pallas_call x1, Pallas kernels, feed(): pl.pallas_call(feed_kernel, grid=(2 * steps,), in_specs=[mine, other, min...  17.6 us
    ppermute x9, starting transfers between devices, z_shifts(): lax.ppermute(value, 'bz', [(i, (i + by + 1) % depth) for i in range(depth)])  14.3 us
    pallas_call x1, Pallas kernels, attend(): pl.pallas_call(attend_kernel, grid_spec=pltpu.PrefetchScalarGridSpec(num_...  14.1 us
    unnamed x75, local copies, waits for them, and re-layouts  11.6 us
    pallas_call x1, Pallas kernels, project(): pl.pallas_call(partial(project_kernel, chips=blocks, segments=segments),...  11.4 us
  transfers between devices with their start and end apart: 55, of which 26 were waited for; matrix products, arithmetic and copies ran while one was open for 15% of the time, Pallas kernels for 23%

profile of v7, /device:TPU:0, one launch (start us, length us, event | category | flops | bytes accessed | tf_op | source)
XLA Modules:
  0.0 345.5 jit_solution(9525869296177698583)
XLA Ops:
  22.4 3.5 %all-to-all-start.2 = ((bf16[8,32,1024]{2,1,0:T(8,128)(2,1)}), bf16[8,32,1024]{2,1,0:T(8,128)(2,1)S(1)}, u32[]{:S(2)}, u32[]{:S(2)}) async-start(bf16[8,32,1024]{2,1,0:T(8,128)(2,1)} %reshape.295), calls=%async_computation.2 | async-start | bytes 1048576 | tf_op jit(solution)/shard_map/all_to_all | solution.py:890
  36.5 7.4 %all-to-all-start = ((bf16[32,32,192]{2,1,0:T(8,128)(2,1)}), bf16[32,32,192]{2,1,0:T(8,128)(2,1)S(1)}, u32[]{:S(2)}, u32[]{:S(2)}) async-start(bf16[32,32,192]{2,1,0:T(8,128)(2,1)} %bitcast.15), calls=%async_computation | async-start | bytes 1048576 | tf_op jit(solution)/shard_map/all_to_all | solution.py:883
  53.2 7.0 %collective-permute-done.4.refs_8_ = bf16[160,1024]{1,0:T(8,128)(2,1)} collective-permute-done((bf16[160,1024]{1,0:T(8,128)(2,1)}, bf16[160,1024]{1,0:T(8,128)(2,1)}, u32[]{:S(2)}, u32[]{:S(2)}) %collective-permute-start.4) | collective-permute-done | bytes 327712 | tf_op jit(solution)/shard_map/ppermute | solution.py:54
  60.2 6.3 %collective-permute-done.6.refs_9_ = bf16[160,1024]{1,0:T(8,128)(2,1)} collective-permute-done((bf16[160,1024]{1,0:T(8,128)(2,1)}, bf16[160,1024]{1,0:T(8,128)(2,1)}, u32[]{:S(2)}, u32[]{:S(2)}) %collective-permute-start.6) | collective-permute-done | bytes 327712 | tf_op jit(solution)/shard_map/ppermute | solution.py:54
  67.0 6.5 %collective-permute-done.10.refs_12_ = bf16[160,1024]{1,0:T(8,128)(2,1)S(1)} collective-permute-done((bf16[160,1024]{1,0:T(8,128)(2,1)}, bf16[160,1024]{1,0:T(8,128)(2,1)S(1)}, u32[]{:S(2)}, u32[]{:S(2)}) %collective-permute-start.10) | collective-permute-done | bytes 327712 | tf_op jit(solution)/shard_map/ppermute | solution.py:54
  80.0 5.3 %collective-permute-done.11.refs_3_ = bf16[160,1024]{1,0:T(8,128)(2,1)S(1)} collective-permute-done((bf16[160,1024]{1,0:T(8,128)(2,1)}, bf16[160,1024]{1,0:T(8,128)(2,1)S(1)}, u32[]{:S(2)}, u32[]{:S(2)}) %collective-permute-start.11) | collective-permute-done | bytes 327712 | tf_op jit(solution)/shard_map/ppermute | solution.py:54
  94.4 11.4 %project.1 = (bf16[2048,1024]{1,0:T(8,128)(2,1)}, f32[2048,128]{1,0:T(8,128)}, bf16[2048,128]{1,0:T(8,128)(2,1)}, bf16[2048,256]{1,0:T(8,128)(2,1)}, bf16[16,32,1024]{2,1,0:T(8,128)(2,1)}) custom-call(s32[16]{0:T(128)} %compare_select_fusion.5.where_ref, f32[2]{0:T(128)} %fusion.20.bias_ref, bf16[160,1024]{1,0:T(8,128)(2,1)} %copy-done.10, ...), custom_call_target="tpu_custom_call" | custom-call | tf_op jit(solution)/shard_map/project/pallas_call | solution.py:239
  110.3 14.1 %attend.1 = (f32[2048,128]{1,0:T(8,128)}, bf16[16,64,128]{2,1,0:T(8,128)(2,1)}) custom-call(s32[16]{0:T(128)} %get-tuple-element.78.order_ref, s32[32]{0:T(128)} %copy-done.27, s32[2]{0:T(128)} %copy-done.26, s32[2]{0:T(128)} %copy-done.25, bf16[2048,128]{1,0:T(8,128)(2,1)} %get-tuple-element.93.query_ref, bf16[2048,256]{1,0:T(8,128)(2,1)} %get-tuple-element.95.own_ref, ...), custom_call_target="tpu_custom_call" | custom-call | tf_op jit(solution)/shard_map/attend/pallas_call | solution.py:341
  124.6 6.1 %all-to-all-start.1 = ((bf16[16,64,128]{2,1,0:T(8,128)(2,1)}), bf16[16,64,128]{2,1,0:T(8,128)(2,1)S(1)}, u32[]{:S(2)}, u32[]{:S(2)}) async-start(bf16[16,64,128]{2,1,0:T(8,128)(2,1)} %get-tuple-element.98), calls=%async_computation.1 | async-start | bytes 524288 | tf_op jit(solution)/shard_map/all_to_all | solution.py:953
  134.3 6.9 %all-to-all-done.1 = bf16[16,64,128]{2,1,0:T(8,128)(2,1)S(1)} async-done(((bf16[16,64,128]{2,1,0:T(8,128)(2,1)}), bf16[16,64,128]{2,1,0:T(8,128)(2,1)S(1)}, u32[]{:S(2)}, u32[]{:S(2)}) %all-to-all-start.1) | async-done | bytes 262176 | tf_op jit(solution)/shard_map/all_to_all | solution.py:953
  147.6 4.6 %collective-permute-done.22 = bf16[128,1024]{1,0:T(8,128)(2,1)S(1)} collective-permute-done((bf16[128,1024]{1,0:T(8,128)(2,1)}, bf16[128,1024]{1,0:T(8,128)(2,1)S(1)}, u32[]{:S(2)}, u32[]{:S(2)}) %collective-permute-start.22) | collective-permute-done | bytes 262176 | tf_op jit(solution)/shard_map/ppermute | solution.py:54
  162.2 17.6 %feed.1 = (bf16[512,1024]{1,0:T(8,128)(2,1)}, bf16[512,1024]{1,0:T(8,128)(2,1)}, bf16[512,1024]{1,0:T(8,128)(2,1)}, bf16[512,1024]{1,0:T(8,128)(2,1)}, bf16[1024...) custom-call(bf16[512,1024]{1,0:T(8,128)(2,1)} %copy-done.8, bf16[512,1024]{1,0:T(8,128)(2,1)} %copy-done.13, ...), custom_call_target="tpu_custom_call" | custom-call | tf_op jit(solution)/shard_map/feed/pallas_call | solution.py:645
  196.1 4.4 %collective-permute-done.28.from_x_ref = bf16[128,1024]{1,0:T(8,128)(2,1)S(1)} collective-permute-done((bf16[128,1024]{1,0:T(8,128)(2,1)S(1)}, bf16[128,1024]{1,0:T(8,128)(2,1)S(1)}, u32[]{:S(2)}, u32[]{:S(2)}) %collective-permute-start.28) | collective-permute-done | bytes 262176 | tf_op jit(solution)/shard_map/ppermute | solution.py:54
  201.8 3.9 %middle_back.1 = (f32[128,1024]{1,0:T(8,128)}, bf16[128,1024]{1,0:T(8,128)(2,1)}, bf16[1024,128]{1,0:T(8,128)(2,1)}, f32[8,1024]{1,0:T(8,128)}) custom-call(f32[128,1024]{1,0:T(8,128)} %slice.168.own_ref, bf16[128,1024]{1,0:T(8,128)(2,1)} %copy-done.20, bf16[128,1024]{1,0:T(8,128)(2,1)} %copy-done.21, f32[128,1024]{1,0:T(8,128)} %get-tuple-element.103.middle_ref, ...), custom_call_target="tpu_custom_call" | custom-call | tf_op jit(solution)/shard_map/middle_back/pallas_call | solution.py:713
  205.7 5.2 %out_grad.1 = (bf16[512,2048]{1,0:T(8,128)(2,1)}, bf16[512,2048]{1,0:T(8,128)(2,1)}) custom-call(s32[8]{0:T(128)} %broadcast_xor_fusion.members_ref, bf16[1024,128]{1,0:T(8,128)(2,1)} %bitcast.84, bf16[128,1024]{1,0:T(8,128)(2,1)} %get-tuple-element.108.branch_ref, bf16[512,1024]{1,0:T(8,128)(2,1)} %get-tuple-element.109.ffn_mine_ref, ...), custom_call_target="tpu_custom_call" | custom-call | tf_op jit(solution)/shard_map/out_grad/pallas_call | solution.py:752
  210.9 4.7 %all-to-all-start.3 = ((bf16[16,64,128]{2,1,0:T(8,128)(2,1)}), bf16[16,64,128]{2,1,0:T(8,128)(2,1)S(1)}, u32[]{:S(2)}, u32[]{:S(2)}) async-start(bf16[16,64,128]{2,1,0:T(8,128)(2,1)} %bitcast.26), calls=%async_computation.3 | async-start | bytes 524288 | tf_op jit(solution)/shard_map/all_to_all | solution.py:972
  221.2 9.4 %all-to-all-done.3.grad_ref = bf16[16,64,128]{2,1,0:T(8,128)(2,1)S(1)} async-done(((bf16[16,64,128]{2,1,0:T(8,128)(2,1)}), bf16[16,64,128]{2,1,0:T(8,128)(2,1)S(1)}, u32[]{:S(2)}, u32[]{:S(2)}) %all-to-all-start.3) | async-done | bytes 262176 | tf_op jit(solution)/shard_map/all_to_all | solution.py:972
  233.3 30.5 %attend_back.1 = (bf16[2048,128]{1,0:T(8,128)(2,1)}, bf16[2048,128]{1,0:T(8,128)(2,1)}, bf16[2048,128]{1,0:T(8,128)(2,1)}, f32[8,128]{1,0:T(8,128)}) custom-call(s32[16]{0:T(128)} %get-tuple-element.78.order_ref, s32[32]{0:T(128)} %copy-done.27, s32[32]{0:T(128)} %select_reduce_fusion.source_ref, s32[8]{0:T(128)} %fusion.18.low_ref, s32[8]{0:T(128)} %fusion.19.high_ref, ...), custom_call_target="tpu_custom_call" | custom-call | tf_op jit(solution)/shard_map/attend_back/pallas_call | solution.py:475
  264.6 3.5 %all-to-all-start.4 = ((bf16[8,32,1024]{2,1,0:T(8,128)(2,1)}), bf16[8,32,1024]{2,1,0:T(8,128)(2,1)S(1)}, u32[]{:S(2)}, u32[]{:S(2)}) async-start(bf16[8,32,1024]{2,1,0:T(8,128)(2,1)} %bitcast.94), calls=%async_computation.5 | async-start | bytes 1048576 | tf_op jit(solution)/shard_map/all_to_all | solution.py:991
  272.3 8.0 %project_back.1 = (bf16[16,192,128]{2,1,0:T(8,128)(2,1)}, bf16[1024,192]{1,0:T(8,128)(2,1)}, f32[8,128]{1,0:T(8,128)}, f32[1024,128]{1,0:T(8,128)}) custom-call(bf16[2048,128]{1,0:T(8,128)(2,1)} %get-tuple-element.122.query_grad_ref, bf16[2048,128]{1,0:T(8,128)(2,1)} %get-tuple-element.123.own_ref, bf16[2048,128]{1,0:T(8,128)(2,1)} %collective-permute-done.34.other_ref, ...), custom_call_target="tpu_custom_call" | custom-call | tf_op jit(solution)/shard_map/project_back/pallas_call | solution.py:550
  288.5 4.2 %all-to-all-start.5 = ((bf16[16,240,128]{2,1,0:T(8,128)(2,1)}), bf16[16,240,128]{2,1,0:T(8,128)(2,1)S(1)}, u32[]{:S(2)}, u32[]{:S(2)}) async-start(bf16[16,240,128]{2,1,0:T(8,128)(2,1)} %maximum_maximum_fusion), calls=%async_computation.6 | async-start | bytes 1966080 | tf_op jit(solution)/shard_map/all_to_all | solution.py:1019
  292.7 10.5 %collective-permute-done.33 = bf16[128,2048]{1,0:T(8,128)(2,1)} collective-permute-done((bf16[128,2048]{1,0:T(8,128)(2,1)}, bf16[128,2048]{1,0:T(8,128)(2,1)}, u32[]{:S(2)}, u32[]{:S(2)}) %collective-permute-start.33) | collective-permute-done | bytes 524320 | tf_op jit(solution)/shard_map/ppermute | solution.py:54
  317.4 3.4 collective-permute-start.44
  331.8 6.5 %input_back.1 = (f32[128,1024]{1,0:T(8,128)}, f32[32,3072]{1,0:T(8,128)}) custom-call(bf16[16,240,128]{2,1,0:T(8,128)(2,1)} %copy-done.3, bf16[1024,3072]{1,0:T(8,128)(2,1)} %all-gather.4.cloned.1.call-done.weight_ref, bf16[128,1024]{1,0:T(8,128)(2,1)} %x_ref.3, f32[1,1024]{1,0:T(1,128)} %bitcast.101, f32[128,1024]{1,0:T(8,128)} %get-tuple-element.134.middle_ref), custom_call_target="tpu_custom_call" | custom-call | tf_op jit(solution)/shard_map/input_back/pallas_call | solution.py:790
  (265 shorter events, 138.6 us)
Async XLA Ops:
  9.9 34.1 %collective-permute-start = (bf16[160,1024]{1,0:T(8,128)(2,1)S(1)}, bf16[160,1024]{1,0:T(8,128)(2,1)}, u32[]{:S(2)}, u32[]{:S(2)}) collective-permute-start(bf16[160,1024]{1,0:T(8,128)(2,1)S(1)} %constant_dynamic-update-slice_fusion.refs_0_), channel_id=1, source_target_pairs={{0,16},{16,0},{1,17},{17,1},{2,18},{18,2},{3,19},{19,3},{4,20},{20... | collective-permute-start | bytes 983048 | tf_op jit(solution)/shard_map/ppermute | solution.py:54
  12.8 20.5 %collective-permute-start.1 = (bf16[160,1024]{1,0:T(8,128)(2,1)S(1)}, bf16[160,1024]{1,0:T(8,128)(2,1)}, u32[]{:S(2)}, u32[]{:S(2)}) collective-permute-start(bf16[160,1024]{1,0:T(8,128)(2,1)S(1)} %constant_dynamic-update-slice_fusion.refs_0_), channel_id=1, source_target_pairs={{0,2},{2,4},{4,6},{6,0},{1,3},{3,5},{5,7},{7,1},{8,10},{10,12},{12... | collective-permute-start | bytes 983048 | tf_op jit(solution)/shard_map/ppermute | solution.py:106
  14.4 31.4 %collective-permute-start.3 = (bf16[160,1024]{1,0:T(8,128)(2,1)S(1)}, bf16[160,1024]{1,0:T(8,128)(2,1)}, u32[]{:S(2)}, u32[]{:S(2)}) collective-permute-start(bf16[160,1024]{1,0:T(8,128)(2,1)S(1)} %constant_dynamic-update-slice_fusion.refs_0_), channel_id=1, source_target_pairs={{0,4},{2,6},{4,0},{6,2},{1,5},{3,7},{5,1},{7,3},{8,12},{10,14},{12... | collective-permute-start | bytes 983048 | tf_op jit(solution)/shard_map/ppermute | solution.py:106
  17.0 30.3 %collective-permute-start.5 = (bf16[160,1024]{1,0:T(8,128)(2,1)S(1)}, bf16[160,1024]{1,0:T(8,128)(2,1)}, u32[]{:S(2)}, u32[]{:S(2)}) collective-permute-start(bf16[160,1024]{1,0:T(8,128)(2,1)S(1)} %constant_dynamic-update-slice_fusion.refs_0_), channel_id=1, source_target_pairs={{0,6},{2,0},{4,2},{6,4},{1,7},{3,1},{5,3},{7,5},{8,14},{10,8},{12,... | collective-permute-start | bytes 983048 | tf_op jit(solution)/shard_map/ppermute | solution.py:106
  18.3 29.5 %collective-permute-start.7 = (bf16[160,1024]{1,0:T(8,128)(2,1)S(1)}, bf16[160,1024]{1,0:T(8,128)(2,1)}, u32[]{:S(2)}, u32[]{:S(2)}) collective-permute-start(bf16[160,1024]{1,0:T(8,128)(2,1)S(1)} %constant_dynamic-update-slice_fusion.refs_0_), channel_id=1, source_target_pairs={{0,1},{1,0},{2,3},{3,2},{4,5},{5,4},{6,7},{7,6},{8,9},{9,8},{10,11... | collective-permute-start | bytes 983048 | tf_op jit(solution)/shard_map/ppermute | solution.py:54
  36.5 54.9 %all-to-all-start = ((bf16[32,32,192]{2,1,0:T(8,128)(2,1)}), bf16[32,32,192]{2,1,0:T(8,128)(2,1)S(1)}, u32[]{:S(2)}, u32[]{:S(2)}) async-start(bf16[32,32,192]{2,1,0:T(8,128)(2,1)} %bitcast.15), calls=%async_computation | async-start | bytes 1048576 | tf_op jit(solution)/shard_map/all_to_all | solution.py:883
  43.9 117.3 %all-gather.6.cloned.1.call-start = ((), (), s32[]{:S(2)}) async-start(), calls=%async_computation.11 | async-start | bytes 3932160 | tf_op jit(solution)/shard_map/all_gather | solution.py:936
  44.0 22.5 %collective-permute-start.8 = (bf16[160,1024]{1,0:T(8,128)(2,1)}, bf16[160,1024]{1,0:T(8,128)(2,1)}, u32[]{:S(2)}, u32[]{:S(2)}) collective-permute-start(bf16[160,1024]{1,0:T(8,128)(2,1)} %collective-permute-done.1.refs_4_), channel_id=1, source_target_pairs={{0,1},{1,0},{2,3},{3,2},{4,5},{5,4},{6,7},{7,6},{8,9},{9,8},{10,11... | collective-permute-start | bytes 983048 | tf_op jit(solution)/shard_map/ppermute | solution.py:54
  47.3 19.7 %collective-permute-start.9 = (bf16[160,1024]{1,0:T(8,128)(2,1)}, bf16[160,1024]{1,0:T(8,128)(2,1)S(1)}, u32[]{:S(2)}, u32[]{:S(2)}) collective-permute-start(bf16[160,1024]{1,0:T(8,128)(2,1)} %collective-permute-done.3.refs_5_), channel_id=1, source_target_pairs={{0,1},{1,0},{2,3},{3,2},{4,5},{5,4},{6,7},{7,6},{8,9},{9,8},{10,11... | collective-permute-start | bytes 983048 | tf_op jit(solution)/shard_map/ppermute | solution.py:54
  47.8 18.7 %collective-permute-start.6 = (bf16[160,1024]{1,0:T(8,128)(2,1)}, bf16[160,1024]{1,0:T(8,128)(2,1)}, u32[]{:S(2)}, u32[]{:S(2)}) collective-permute-start(bf16[160,1024]{1,0:T(8,128)(2,1)} %collective-permute-done.5.refs_6_), channel_id=1, source_target_pairs={{0,16},{16,0},{1,17},{17,1},{2,18},{18,2},{3,19},{19,3},{4,20},{20... | collective-permute-start | bytes 983048 | tf_op jit(solution)/shard_map/ppermute | solution.py:54
  48.1 25.3 %collective-permute-start.10 = (bf16[160,1024]{1,0:T(8,128)(2,1)}, bf16[160,1024]{1,0:T(8,128)(2,1)S(1)}, u32[]{:S(2)}, u32[]{:S(2)}) collective-permute-start(bf16[160,1024]{1,0:T(8,128)(2,1)} %collective-permute-done.5.refs_6_), channel_id=1, source_target_pairs={{0,1},{1,0},{2,3},{3,2},{4,5},{5,4},{6,7},{7,6},{8,9},{9,8},{10,11... | collective-permute-start | bytes 983048 | tf_op jit(solution)/shard_map/ppermute | solution.py:54
  77.4 17.0 %collective-permute-start.14 = (bf16[160,1024]{1,0:T(8,128)(2,1)}, bf16[160,1024]{1,0:T(8,128)(2,1)}, u32[]{:S(2)}, u32[]{:S(2)}) collective-permute-start(bf16[160,1024]{1,0:T(8,128)(2,1)} %collective-permute-done.6.refs_9_), channel_id=1, source_target_pairs={{0,1},{1,0},{2,3},{3,2},{4,5},{5,4},{6,7},{7,6},{8,9},{9,8},{10,11... | collective-permute-start | bytes 983048 | tf_op jit(solution)/shard_map/ppermute | solution.py:54
  78.5 27.3 %collective-permute-start.15 = (bf16[128,1024]{1,0:T(8,128)(2,1)}, bf16[128,1024]{1,0:T(8,128)(2,1)}, u32[]{:S(2)}, u32[]{:S(2)}) collective-permute-start(bf16[128,1024]{1,0:T(8,128)(2,1)} %cotangent_ref.1), channel_id=1, source_target_pairs={{0,16},{16,0},{1,17},{17,1},{2,18},{18,2},{3,19},{19,3},{4,20},{20... | collective-permute-start | bytes 786440 | tf_op jit(solution)/shard_map/ppermute | solution.py:54
  85.2 20.6 %collective-permute-start.16 = (bf16[128,1024]{1,0:T(8,128)(2,1)}, bf16[128,1024]{1,0:T(8,128)(2,1)}, u32[]{:S(2)}, u32[]{:S(2)}) collective-permute-start(bf16[128,1024]{1,0:T(8,128)(2,1)} %cotangent_ref.1), channel_id=1, source_target_pairs={{0,1},{1,0},{2,3},{3,2},{4,5},{5,4},{6,7},{7,6},{8,9},{9,8},{10,11... | collective-permute-start | bytes 786440 | tf_op jit(solution)/shard_map/ppermute | solution.py:54
  105.9 25.0 %collective-permute-start.20 = (bf16[16,32,1024]{2,1,0:T(8,128)(2,1)}, bf16[16,32,1024]{2,1,0:T(8,128)(2,1)}, u32[]{:S(2)}, u32[]{:S(2)}) collective-permute-start(bf16[16,32,1024]{2,1,0:T(8,128)(2,1)} %get-tuple-element.102), channel_id=1, source_target_pairs={{0,8},{8,0},{1,9},{9,1},{2,10},{10,2},{3,11},{11,3},{4,12},{12,4},... | collective-permute-start | bytes 3145736 | tf_op jit(solution)/shard_map/ppermute | solution.py:54
  106.4 18.0 %collective-permute-start.18 = (bf16[128,1024]{1,0:T(8,128)(2,1)}, bf16[128,1024]{1,0:T(8,128)(2,1)S(1)}, u32[]{:S(2)}, u32[]{:S(2)}) collective-permute-start(bf16[128,1024]{1,0:T(8,128)(2,1)} %collective-permute-done.15), channel_id=1, source_target_pairs={{0,1},{1,0},{2,3},{3,2},{4,5},{5,4},{6,7},{7,6},{8,9},{9,8},{10,11... | collective-permute-start | bytes 786440 | tf_op jit(solution)/shard_map/ppermute | solution.py:54
  130.7 134.0 %reduce-scatter.3.cloned.1.call-start = ((), (), s32[]{:S(2)}) async-start(), calls=%async_computation.8 | async-start | bytes 2621440 | tf_op jit(solution)/shard_map/reduce_scatter | solution.py:963
  179.8 133.1 %reduce-scatter.5.cloned.1.call-start = ((), (), s32[]{:S(2)}) async-start(), calls=%async_computation.9 | async-start | bytes 1310720 | tf_op jit(solution)/shard_map/reduce_scatter | solution.py:964
  180.6 150.3 %all-gather.4.cloned.1.call-start = ((), (), s32[]{:S(2)}) async-start(), calls=%async_computation.10 | async-start | bytes 6488064 | tf_op jit(solution)/shard_map/all_gather | solution.py:966
  210.9 19.7 %all-to-all-start.3 = ((bf16[16,64,128]{2,1,0:T(8,128)(2,1)}), bf16[16,64,128]{2,1,0:T(8,128)(2,1)S(1)}, u32[]{:S(2)}, u32[]{:S(2)}) async-start(bf16[16,64,128]{2,1,0:T(8,128)(2,1)} %bitcast.26), calls=%async_computation.3 | async-start | bytes 524288 | tf_op jit(solution)/shard_map/all_to_all | solution.py:972
  230.6 37.6 %collective-permute-start.32 = (bf16[256,2048]{1,0:T(8,128)(2,1)}, bf16[256,2048]{1,0:T(8,128)(2,1)}, u32[]{:S(2)}, u32[]{:S(2)}) collective-permute-start(bf16[256,2048]{1,0:T(8,128)(2,1)} %pad_maximum_fusion.1), channel_id=1, source_target_pairs={{0,16},{16,0},{1,17},{17,1},{2,18},{18,2},{3,19},{19,3},{4,20},{20... | collective-permute-start | bytes 3145736 | tf_op jit(solution)/shard_map/ppermute | solution.py:54
  264.6 18.9 %all-to-all-start.4 = ((bf16[8,32,1024]{2,1,0:T(8,128)(2,1)}), bf16[8,32,1024]{2,1,0:T(8,128)(2,1)S(1)}, u32[]{:S(2)}, u32[]{:S(2)}) async-start(bf16[8,32,1024]{2,1,0:T(8,128)(2,1)} %bitcast.94), calls=%async_computation.5 | async-start | bytes 1048576 | tf_op jit(solution)/shard_map/all_to_all | solution.py:991
  270.4 32.9 %collective-permute-start.33 = (bf16[128,2048]{1,0:T(8,128)(2,1)}, bf16[128,2048]{1,0:T(8,128)(2,1)}, u32[]{:S(2)}, u32[]{:S(2)}) collective-permute-start(bf16[128,2048]{1,0:T(8,128)(2,1)} %add_convert_fusion.1), channel_id=1, source_target_pairs={{0,1},{1,0},{2,3},{3,2},{4,5},{5,4},{6,7},{7,6},{8,9},{9,8},{10,11... | collective-permute-start | bytes 1572872 | tf_op jit(solution)/shard_map/ppermute | solution.py:54
  288.5 42.4 %all-to-all-start.5 = ((bf16[16,240,128]{2,1,0:T(8,128)(2,1)}), bf16[16,240,128]{2,1,0:T(8,128)(2,1)S(1)}, u32[]{:S(2)}, u32[]{:S(2)}) async-start(bf16[16,240,128]{2,1,0:T(8,128)(2,1)} %maximum_maximum_fusion), calls=%async_computation.6 | async-start | bytes 1966080 | tf_op jit(solution)/shard_map/all_to_all | solution.py:1019
  (64 other events, 570.4 us)
Sparse Core Ops, SparseCore 0:
  51.9 63.4 all-gather.5
  179.9 48.8 reduce-scatter.2
  231.1 34.4 reduce-scatter.4
Sparse Core Ops, SparseCore 1:
  183.9 133.5 all-gather.3

commit v8 on v7

--- a/solution.py
+++ b/solution.py
@@ -25,7 +25,7 @@
 VARIATE_LANE = 76
 OWN_VARIATE_LANE = 88
 MASK = -512.0
-QUERY_TILE = 1024
+QUERY_TILE = 512
 KEY_TILE = 512
 PROJECT_BLOCKS = 4
 
@@ -276,7 +276,7 @@
             keys_ref[pl.ds(target, BLOCK), :] = source_ref[pl.ds(source, BLOCK), :]
             return unused
 
-        lax.fori_loop(0, blocks, put, 0, unroll=4)
+        lax.fori_loop(0, blocks, put, 0, unroll=8)
 
 
 def block_start(order_ref, index):
@@ -407,7 +407,7 @@
             wide_ref[target, :] = jnp.where(lane < HD, grad * inverse, wide).astype(bf16)
             return unused
 
-        lax.fori_loop(0, taken, put, 0, unroll=4)
+        lax.fori_loop(0, taken, put, 0, unroll=8)
 
     window = pl.ds(pl.multiple_of(step * KEY_TILE, KEY_TILE), KEY_TILE)
     key = keys_ref[window, :128]
@@ -456,7 +456,7 @@
             query_grad_ref[target, :] = sums_ref[rows, :].astype(bf16)
             return unused
 
-        lax.fori_loop(0, taken, put, 0, unroll=4)
+        lax.fori_loop(0, taken, put, 0, unroll=8)
         every = jnp.sum(every_ref[...], keepdims=True)
         same = jnp.sum(same_ref[...], keepdims=True)
         bias_lane = lanes((8, 128))

time: 347 us -> 346 us (level)
  transfers between devices with their start and end apart: 55 -> 55, of which waited for: 26 -> 27; matrix products, arithmetic and copies ran while one was open for 15% -> 15% of each run, Pallas kernels for 23% -> 22%
where the time goes in v8:
time: 346 us; the launch traced here: 344 us
  Pallas kernels  101 us (29%)
  waiting for transfers between devices  88.1 us (25%)
  starting transfers between devices  79.3 us (23%)
  local copies, waits for them, and re-layouts  32.3 us (9%)
  other arithmetic  28.4 us (8%)
  between operations  15.9 us (5%)
    ppermute x36, waiting for transfers between devices, swap(): return lax.ppermute(shard, axis, [(0, 1), (1, 0)])  65.9 us
    ppermute x36, starting transfers between devices, swap(): return lax.ppermute(shard, axis, [(0, 1), (1, 0)])  35.2 us
    pallas_call x1, Pallas kernels, attend_back(): pl.pallas_call(attend_back_kernel, grid_spec=pltpu.PrefetchScalarGridSpec...  29.3 us
    pallas_call x1, Pallas kernels, feed(): pl.pallas_call(feed_kernel, grid=(2 * steps,), in_specs=[mine, other, min...  17.6 us
    ppermute x9, starting transfers between devices, z_shifts(): lax.ppermute(value, 'bz', [(i, (i + by + 1) % depth) for i in range(depth)])  14.6 us
    pallas_call x1, Pallas kernels, attend(): pl.pallas_call(attend_kernel, grid_spec=pltpu.PrefetchScalarGridSpec(num_...  13.2 us
    unnamed x75, local copies, waits for them, and re-layouts  11.6 us
    pallas_call x1, Pallas kernels, project(): pl.pallas_call(partial(project_kernel, chips=blocks, segments=segments),...  11.4 us
  transfers between devices with their start and end apart: 55, of which 27 were waited for; matrix products, arithmetic and copies ran while one was open for 15% of the time, Pallas kernels for 22%

profile of v8, /device:TPU:0, one launch (start us, length us, event | category | flops | bytes accessed | tf_op | source)
XLA Modules:
  0.0 344.5 jit_solution(3145436012119343584)
XLA Ops:
  22.4 3.5 %all-to-all-start.2 = ((bf16[8,32,1024]{2,1,0:T(8,128)(2,1)}), bf16[8,32,1024]{2,1,0:T(8,128)(2,1)S(1)}, u32[]{:S(2)}, u32[]{:S(2)}) async-start(bf16[8,32,1024]{2,1,0:T(8,128)(2,1)} %reshape.295), calls=%async_computation.2 | async-start | bytes 1048576 | tf_op jit(solution)/shard_map/all_to_all | solution.py:890
  36.5 7.4 %all-to-all-start = ((bf16[32,32,192]{2,1,0:T(8,128)(2,1)}), bf16[32,32,192]{2,1,0:T(8,128)(2,1)S(1)}, u32[]{:S(2)}, u32[]{:S(2)}) async-start(bf16[32,32,192]{2,1,0:T(8,128)(2,1)} %bitcast.15), calls=%async_computation | async-start | bytes 1048576 | tf_op jit(solution)/shard_map/all_to_all | solution.py:883
  53.2 7.0 %collective-permute-done.4.refs_8_ = bf16[160,1024]{1,0:T(8,128)(2,1)} collective-permute-done((bf16[160,1024]{1,0:T(8,128)(2,1)}, bf16[160,1024]{1,0:T(8,128)(2,1)}, u32[]{:S(2)}, u32[]{:S(2)}) %collective-permute-start.4) | collective-permute-done | bytes 327712 | tf_op jit(solution)/shard_map/ppermute | solution.py:54
  60.2 6.3 %collective-permute-done.6.refs_9_ = bf16[160,1024]{1,0:T(8,128)(2,1)} collective-permute-done((bf16[160,1024]{1,0:T(8,128)(2,1)}, bf16[160,1024]{1,0:T(8,128)(2,1)}, u32[]{:S(2)}, u32[]{:S(2)}) %collective-permute-start.6) | collective-permute-done | bytes 327712 | tf_op jit(solution)/shard_map/ppermute | solution.py:54
  67.0 6.5 %collective-permute-done.10.refs_12_ = bf16[160,1024]{1,0:T(8,128)(2,1)S(1)} collective-permute-done((bf16[160,1024]{1,0:T(8,128)(2,1)}, bf16[160,1024]{1,0:T(8,128)(2,1)S(1)}, u32[]{:S(2)}, u32[]{:S(2)}) %collective-permute-start.10) | collective-permute-done | bytes 327712 | tf_op jit(solution)/shard_map/ppermute | solution.py:54
  80.0 5.3 %collective-permute-done.11.refs_3_ = bf16[160,1024]{1,0:T(8,128)(2,1)S(1)} collective-permute-done((bf16[160,1024]{1,0:T(8,128)(2,1)}, bf16[160,1024]{1,0:T(8,128)(2,1)S(1)}, u32[]{:S(2)}, u32[]{:S(2)}) %collective-permute-start.11) | collective-permute-done | bytes 327712 | tf_op jit(solution)/shard_map/ppermute | solution.py:54
  94.4 11.4 %project.1 = (bf16[2048,1024]{1,0:T(8,128)(2,1)}, f32[2048,128]{1,0:T(8,128)}, bf16[2048,128]{1,0:T(8,128)(2,1)}, bf16[2048,256]{1,0:T(8,128)(2,1)}, bf16[16,32,1024]{2,1,0:T(8,128)(2,1)}) custom-call(s32[16]{0:T(128)} %compare_select_fusion.5.where_ref, f32[2]{0:T(128)} %fusion.16.bias_ref, bf16[160,1024]{1,0:T(8,128)(2,1)} %copy-done.10, ...), custom_call_target="tpu_custom_call" | custom-call | tf_op jit(solution)/shard_map/project/pallas_call | solution.py:239
  110.3 13.2 %attend.1 = (f32[2048,128]{1,0:T(8,128)}, bf16[16,64,128]{2,1,0:T(8,128)(2,1)}) custom-call(s32[16]{0:T(128)} %get-tuple-element.78.order_ref, s32[32]{0:T(128)} %copy-done.27, s32[4]{0:T(128)} %copy-done.26, s32[4]{0:T(128)} %copy-done.25, bf16[2048,128]{1,0:T(8,128)(2,1)} %get-tuple-element.93.query_ref, bf16[2048,256]{1,0:T(8,128)(2,1)} %get-tuple-element.95.own_ref, ...), custom_call_target="tpu_custom_call" | custom-call | tf_op jit(solution)/shard_map/attend/pallas_call | solution.py:341
  123.7 6.1 %all-to-all-start.1 = ((bf16[16,64,128]{2,1,0:T(8,128)(2,1)}), bf16[16,64,128]{2,1,0:T(8,128)(2,1)S(1)}, u32[]{:S(2)}, u32[]{:S(2)}) async-start(bf16[16,64,128]{2,1,0:T(8,128)(2,1)} %get-tuple-element.98), calls=%async_computation.1 | async-start | bytes 524288 | tf_op jit(solution)/shard_map/all_to_all | solution.py:953
  133.4 6.9 %all-to-all-done.1 = bf16[16,64,128]{2,1,0:T(8,128)(2,1)S(1)} async-done(((bf16[16,64,128]{2,1,0:T(8,128)(2,1)}), bf16[16,64,128]{2,1,0:T(8,128)(2,1)S(1)}, u32[]{:S(2)}, u32[]{:S(2)}) %all-to-all-start.1) | async-done | bytes 262176 | tf_op jit(solution)/shard_map/all_to_all | solution.py:953
  141.0 3.2 out_project.1
  146.7 4.6 %collective-permute-done.22 = bf16[128,1024]{1,0:T(8,128)(2,1)S(1)} collective-permute-done((bf16[128,1024]{1,0:T(8,128)(2,1)}, bf16[128,1024]{1,0:T(8,128)(2,1)S(1)}, u32[]{:S(2)}, u32[]{:S(2)}) %collective-permute-start.22) | collective-permute-done | bytes 262176 | tf_op jit(solution)/shard_map/ppermute | solution.py:54
  161.3 17.6 %feed.1 = (bf16[512,1024]{1,0:T(8,128)(2,1)}, bf16[512,1024]{1,0:T(8,128)(2,1)}, bf16[512,1024]{1,0:T(8,128)(2,1)}, bf16[512,1024]{1,0:T(8,128)(2,1)}, bf16[1024...) custom-call(bf16[512,1024]{1,0:T(8,128)(2,1)} %copy-done.8, bf16[512,1024]{1,0:T(8,128)(2,1)} %copy-done.13, ...), custom_call_target="tpu_custom_call" | custom-call | tf_op jit(solution)/shard_map/feed/pallas_call | solution.py:645
  195.3 4.4 %collective-permute-done.28.from_x_ref = bf16[128,1024]{1,0:T(8,128)(2,1)S(1)} collective-permute-done((bf16[128,1024]{1,0:T(8,128)(2,1)S(1)}, bf16[128,1024]{1,0:T(8,128)(2,1)S(1)}, u32[]{:S(2)}, u32[]{:S(2)}) %collective-permute-start.28) | collective-permute-done | bytes 262176 | tf_op jit(solution)/shard_map/ppermute | solution.py:54
  201.0 3.9 %middle_back.1 = (f32[128,1024]{1,0:T(8,128)}, bf16[128,1024]{1,0:T(8,128)(2,1)}, bf16[1024,128]{1,0:T(8,128)(2,1)}, f32[8,1024]{1,0:T(8,128)}) custom-call(f32[128,1024]{1,0:T(8,128)} %slice.168.own_ref, bf16[128,1024]{1,0:T(8,128)(2,1)} %copy-done.20, bf16[128,1024]{1,0:T(8,128)(2,1)} %copy-done.21, f32[128,1024]{1,0:T(8,128)} %get-tuple-element.103.middle_ref, ...), custom_call_target="tpu_custom_call" | custom-call | tf_op jit(solution)/shard_map/middle_back/pallas_call | solution.py:713
  204.9 5.2 %out_grad.1 = (bf16[512,2048]{1,0:T(8,128)(2,1)}, bf16[512,2048]{1,0:T(8,128)(2,1)}) custom-call(s32[8]{0:T(128)} %broadcast_xor_fusion.members_ref, bf16[1024,128]{1,0:T(8,128)(2,1)} %bitcast.84, bf16[128,1024]{1,0:T(8,128)(2,1)} %get-tuple-element.108.branch_ref, bf16[512,1024]{1,0:T(8,128)(2,1)} %get-tuple-element.109.ffn_mine_ref, ...), custom_call_target="tpu_custom_call" | custom-call | tf_op jit(solution)/shard_map/out_grad/pallas_call | solution.py:752
  210.1 4.7 %all-to-all-start.3 = ((bf16[16,64,128]{2,1,0:T(8,128)(2,1)}), bf16[16,64,128]{2,1,0:T(8,128)(2,1)S(1)}, u32[]{:S(2)}, u32[]{:S(2)}) async-start(bf16[16,64,128]{2,1,0:T(8,128)(2,1)} %bitcast.26), calls=%async_computation.3 | async-start | bytes 524288 | tf_op jit(solution)/shard_map/all_to_all | solution.py:972
  220.3 9.5 %all-to-all-done.3.grad_ref = bf16[16,64,128]{2,1,0:T(8,128)(2,1)S(1)} async-done(((bf16[16,64,128]{2,1,0:T(8,128)(2,1)}), bf16[16,64,128]{2,1,0:T(8,128)(2,1)S(1)}, u32[]{:S(2)}, u32[]{:S(2)}) %all-to-all-start.3) | async-done | bytes 262176 | tf_op jit(solution)/shard_map/all_to_all | solution.py:972
  232.4 29.3 %attend_back.1 = (bf16[2048,128]{1,0:T(8,128)(2,1)}, bf16[2048,128]{1,0:T(8,128)(2,1)}, bf16[2048,128]{1,0:T(8,128)(2,1)}, f32[8,128]{1,0:T(8,128)}) custom-call(s32[16]{0:T(128)} %get-tuple-element.78.order_ref, s32[32]{0:T(128)} %copy-done.27, s32[32]{0:T(128)} %select_reduce_fusion.source_ref, s32[8]{0:T(128)} %convert_reduce_fusion.2.low_ref, ...), custom_call_target="tpu_custom_call" | custom-call | tf_op jit(solution)/shard_map/attend_back/pallas_call | solution.py:475
  262.6 3.5 %all-to-all-start.4 = ((bf16[8,32,1024]{2,1,0:T(8,128)(2,1)}), bf16[8,32,1024]{2,1,0:T(8,128)(2,1)S(1)}, u32[]{:S(2)}, u32[]{:S(2)}) async-start(bf16[8,32,1024]{2,1,0:T(8,128)(2,1)} %bitcast.94), calls=%async_computation.5 | async-start | bytes 1048576 | tf_op jit(solution)/shard_map/all_to_all | solution.py:991
  270.0 8.0 %project_back.1 = (bf16[16,192,128]{2,1,0:T(8,128)(2,1)}, bf16[1024,192]{1,0:T(8,128)(2,1)}, f32[8,128]{1,0:T(8,128)}, f32[1024,128]{1,0:T(8,128)}) custom-call(bf16[2048,128]{1,0:T(8,128)(2,1)} %get-tuple-element.122.query_grad_ref, bf16[2048,128]{1,0:T(8,128)(2,1)} %get-tuple-element.123.own_ref, bf16[2048,128]{1,0:T(8,128)(2,1)} %collective-permute-done.34.other_ref, ...), custom_call_target="tpu_custom_call" | custom-call | tf_op jit(solution)/shard_map/project_back/pallas_call | solution.py:550
  286.5 3.9 %all-to-all-start.5 = ((bf16[16,240,128]{2,1,0:T(8,128)(2,1)}), bf16[16,240,128]{2,1,0:T(8,128)(2,1)S(1)}, u32[]{:S(2)}, u32[]{:S(2)}) async-start(bf16[16,240,128]{2,1,0:T(8,128)(2,1)} %maximum_maximum_fusion), calls=%async_computation.6 | async-start | bytes 1966080 | tf_op jit(solution)/shard_map/all_to_all | solution.py:1019
  290.4 11.7 %collective-permute-done.33 = bf16[128,2048]{1,0:T(8,128)(2,1)} collective-permute-done((bf16[128,2048]{1,0:T(8,128)(2,1)}, bf16[128,2048]{1,0:T(8,128)(2,1)}, u32[]{:S(2)}, u32[]{:S(2)}) %collective-permute-start.33) | collective-permute-done | bytes 524320 | tf_op jit(solution)/shard_map/ppermute | solution.py:54
  330.8 6.5 %input_back.1 = (f32[128,1024]{1,0:T(8,128)}, f32[32,3072]{1,0:T(8,128)}) custom-call(bf16[16,240,128]{2,1,0:T(8,128)(2,1)} %copy-done.3, bf16[1024,3072]{1,0:T(8,128)(2,1)} %all-gather.4.cloned.1.call-done.weight_ref, bf16[128,1024]{1,0:T(8,128)(2,1)} %x_ref.3, f32[1,1024]{1,0:T(1,128)} %bitcast.101, f32[128,1024]{1,0:T(8,128)} %get-tuple-element.134.middle_ref), custom_call_target="tpu_custom_call" | custom-call | tf_op jit(solution)/shard_map/input_back/pallas_call | solution.py:790
  (265 shorter events, 139.0 us)
Async XLA Ops:
  9.9 34.1 %collective-permute-start = (bf16[160,1024]{1,0:T(8,128)(2,1)S(1)}, bf16[160,1024]{1,0:T(8,128)(2,1)}, u32[]{:S(2)}, u32[]{:S(2)}) collective-permute-start(bf16[160,1024]{1,0:T(8,128)(2,1)S(1)} %constant_dynamic-update-slice_fusion.refs_0_), channel_id=1, source_target_pairs={{0,16},{16,0},{1,17},{17,1},{2,18},{18,2},{3,19},{19,3},{4,20},{20... | collective-permute-start | bytes 983048 | tf_op jit(solution)/shard_map/ppermute | solution.py:54
  12.8 20.5 %collective-permute-start.1 = (bf16[160,1024]{1,0:T(8,128)(2,1)S(1)}, bf16[160,1024]{1,0:T(8,128)(2,1)}, u32[]{:S(2)}, u32[]{:S(2)}) collective-permute-start(bf16[160,1024]{1,0:T(8,128)(2,1)S(1)} %constant_dynamic-update-slice_fusion.refs_0_), channel_id=1, source_target_pairs={{0,2},{2,4},{4,6},{6,0},{1,3},{3,5},{5,7},{7,1},{8,10},{10,12},{12... | collective-permute-start | bytes 983048 | tf_op jit(solution)/shard_map/ppermute | solution.py:106
  14.4 31.4 %collective-permute-start.3 = (bf16[160,1024]{1,0:T(8,128)(2,1)S(1)}, bf16[160,1024]{1,0:T(8,128)(2,1)}, u32[]{:S(2)}, u32[]{:S(2)}) collective-permute-start(bf16[160,1024]{1,0:T(8,128)(2,1)S(1)} %constant_dynamic-update-slice_fusion.refs_0_), channel_id=1, source_target_pairs={{0,4},{2,6},{4,0},{6,2},{1,5},{3,7},{5,1},{7,3},{8,12},{10,14},{12... | collective-permute-start | bytes 983048 | tf_op jit(solution)/shard_map/ppermute | solution.py:106
  17.0 30.3 %collective-permute-start.5 = (bf16[160,1024]{1,0:T(8,128)(2,1)S(1)}, bf16[160,1024]{1,0:T(8,128)(2,1)}, u32[]{:S(2)}, u32[]{:S(2)}) collective-permute-start(bf16[160,1024]{1,0:T(8,128)(2,1)S(1)} %constant_dynamic-update-slice_fusion.refs_0_), channel_id=1, source_target_pairs={{0,6},{2,0},{4,2},{6,4},{1,7},{3,1},{5,3},{7,5},{8,14},{10,8},{12,... | collective-permute-start | bytes 983048 | tf_op jit(solution)/shard_map/ppermute | solution.py:106
  18.3 29.5 %collective-permute-start.7 = (bf16[160,1024]{1,0:T(8,128)(2,1)S(1)}, bf16[160,1024]{1,0:T(8,128)(2,1)}, u32[]{:S(2)}, u32[]{:S(2)}) collective-permute-start(bf16[160,1024]{1,0:T(8,128)(2,1)S(1)} %constant_dynamic-update-slice_fusion.refs_0_), channel_id=1, source_target_pairs={{0,1},{1,0},{2,3},{3,2},{4,5},{5,4},{6,7},{7,6},{8,9},{9,8},{10,11... | collective-permute-start | bytes 983048 | tf_op jit(solution)/shard_map/ppermute | solution.py:54
  36.5 54.9 %all-to-all-start = ((bf16[32,32,192]{2,1,0:T(8,128)(2,1)}), bf16[32,32,192]{2,1,0:T(8,128)(2,1)S(1)}, u32[]{:S(2)}, u32[]{:S(2)}) async-start(bf16[32,32,192]{2,1,0:T(8,128)(2,1)} %bitcast.15), calls=%async_computation | async-start | bytes 1048576 | tf_op jit(solution)/shard_map/all_to_all | solution.py:883
  43.9 116.4 %all-gather.6.cloned.1.call-start = ((), (), s32[]{:S(2)}) async-start(), calls=%async_computation.11 | async-start | bytes 3932160 | tf_op jit(solution)/shard_map/all_gather | solution.py:936
  44.0 22.5 %collective-permute-start.8 = (bf16[160,1024]{1,0:T(8,128)(2,1)}, bf16[160,1024]{1,0:T(8,128)(2,1)}, u32[]{:S(2)}, u32[]{:S(2)}) collective-permute-start(bf16[160,1024]{1,0:T(8,128)(2,1)} %collective-permute-done.1.refs_4_), channel_id=1, source_target_pairs={{0,1},{1,0},{2,3},{3,2},{4,5},{5,4},{6,7},{7,6},{8,9},{9,8},{10,11... | collective-permute-start | bytes 983048 | tf_op jit(solution)/shard_map/ppermute | solution.py:54
  47.3 19.7 %collective-permute-start.9 = (bf16[160,1024]{1,0:T(8,128)(2,1)}, bf16[160,1024]{1,0:T(8,128)(2,1)S(1)}, u32[]{:S(2)}, u32[]{:S(2)}) collective-permute-start(bf16[160,1024]{1,0:T(8,128)(2,1)} %collective-permute-done.3.refs_5_), channel_id=1, source_target_pairs={{0,1},{1,0},{2,3},{3,2},{4,5},{5,4},{6,7},{7,6},{8,9},{9,8},{10,11... | collective-permute-start | bytes 983048 | tf_op jit(solution)/shard_map/ppermute | solution.py:54
  47.8 18.7 %collective-permute-start.6 = (bf16[160,1024]{1,0:T(8,128)(2,1)}, bf16[160,1024]{1,0:T(8,128)(2,1)}, u32[]{:S(2)}, u32[]{:S(2)}) collective-permute-start(bf16[160,1024]{1,0:T(8,128)(2,1)} %collective-permute-done.5.refs_6_), channel_id=1, source_target_pairs={{0,16},{16,0},{1,17},{17,1},{2,18},{18,2},{3,19},{19,3},{4,20},{20... | collective-permute-start | bytes 983048 | tf_op jit(solution)/shard_map/ppermute | solution.py:54
  48.1 25.3 %collective-permute-start.10 = (bf16[160,1024]{1,0:T(8,128)(2,1)}, bf16[160,1024]{1,0:T(8,128)(2,1)S(1)}, u32[]{:S(2)}, u32[]{:S(2)}) collective-permute-start(bf16[160,1024]{1,0:T(8,128)(2,1)} %collective-permute-done.5.refs_6_), channel_id=1, source_target_pairs={{0,1},{1,0},{2,3},{3,2},{4,5},{5,4},{6,7},{7,6},{8,9},{9,8},{10,11... | collective-permute-start | bytes 983048 | tf_op jit(solution)/shard_map/ppermute | solution.py:54
  77.4 17.0 %collective-permute-start.14 = (bf16[160,1024]{1,0:T(8,128)(2,1)}, bf16[160,1024]{1,0:T(8,128)(2,1)}, u32[]{:S(2)}, u32[]{:S(2)}) collective-permute-start(bf16[160,1024]{1,0:T(8,128)(2,1)} %collective-permute-done.6.refs_9_), channel_id=1, source_target_pairs={{0,1},{1,0},{2,3},{3,2},{4,5},{5,4},{6,7},{7,6},{8,9},{9,8},{10,11... | collective-permute-start | bytes 983048 | tf_op jit(solution)/shard_map/ppermute | solution.py:54
  78.5 27.3 %collective-permute-start.15 = (bf16[128,1024]{1,0:T(8,128)(2,1)}, bf16[128,1024]{1,0:T(8,128)(2,1)}, u32[]{:S(2)}, u32[]{:S(2)}) collective-permute-start(bf16[128,1024]{1,0:T(8,128)(2,1)} %cotangent_ref.1), channel_id=1, source_target_pairs={{0,16},{16,0},{1,17},{17,1},{2,18},{18,2},{3,19},{19,3},{4,20},{20... | collective-permute-start | bytes 786440 | tf_op jit(solution)/shard_map/ppermute | solution.py:54
  85.2 20.6 %collective-permute-start.16 = (bf16[128,1024]{1,0:T(8,128)(2,1)}, bf16[128,1024]{1,0:T(8,128)(2,1)}, u32[]{:S(2)}, u32[]{:S(2)}) collective-permute-start(bf16[128,1024]{1,0:T(8,128)(2,1)} %cotangent_ref.1), channel_id=1, source_target_pairs={{0,1},{1,0},{2,3},{3,2},{4,5},{5,4},{6,7},{7,6},{8,9},{9,8},{10,11... | collective-permute-start | bytes 786440 | tf_op jit(solution)/shard_map/ppermute | solution.py:54
  105.9 24.2 %collective-permute-start.20 = (bf16[16,32,1024]{2,1,0:T(8,128)(2,1)}, bf16[16,32,1024]{2,1,0:T(8,128)(2,1)}, u32[]{:S(2)}, u32[]{:S(2)}) collective-permute-start(bf16[16,32,1024]{2,1,0:T(8,128)(2,1)} %get-tuple-element.102), channel_id=1, source_target_pairs={{0,8},{8,0},{1,9},{9,1},{2,10},{10,2},{3,11},{11,3},{4,12},{12,4},... | collective-permute-start | bytes 3145736 | tf_op jit(solution)/shard_map/ppermute | solution.py:54
  106.4 17.2 %collective-permute-start.18 = (bf16[128,1024]{1,0:T(8,128)(2,1)}, bf16[128,1024]{1,0:T(8,128)(2,1)S(1)}, u32[]{:S(2)}, u32[]{:S(2)}) collective-permute-start(bf16[128,1024]{1,0:T(8,128)(2,1)} %collective-permute-done.15), channel_id=1, source_target_pairs={{0,1},{1,0},{2,3},{3,2},{4,5},{5,4},{6,7},{7,6},{8,9},{9,8},{10,11... | collective-permute-start | bytes 786440 | tf_op jit(solution)/shard_map/ppermute | solution.py:54
  129.8 132.7 %reduce-scatter.3.cloned.1.call-start = ((), (), s32[]{:S(2)}) async-start(), calls=%async_computation.8 | async-start | bytes 2621440 | tf_op jit(solution)/shard_map/reduce_scatter | solution.py:963
  179.0 132.1 %reduce-scatter.5.cloned.1.call-start = ((), (), s32[]{:S(2)}) async-start(), calls=%async_computation.9 | async-start | bytes 1310720 | tf_op jit(solution)/shard_map/reduce_scatter | solution.py:964
  179.7 150.2 %all-gather.4.cloned.1.call-start = ((), (), s32[]{:S(2)}) async-start(), calls=%async_computation.10 | async-start | bytes 6488064 | tf_op jit(solution)/shard_map/all_gather | solution.py:966
  210.1 19.7 %all-to-all-start.3 = ((bf16[16,64,128]{2,1,0:T(8,128)(2,1)}), bf16[16,64,128]{2,1,0:T(8,128)(2,1)S(1)}, u32[]{:S(2)}, u32[]{:S(2)}) async-start(bf16[16,64,128]{2,1,0:T(8,128)(2,1)} %bitcast.26), calls=%async_computation.3 | async-start | bytes 524288 | tf_op jit(solution)/shard_map/all_to_all | solution.py:972
  229.7 36.3 %collective-permute-start.32 = (bf16[256,2048]{1,0:T(8,128)(2,1)}, bf16[256,2048]{1,0:T(8,128)(2,1)}, u32[]{:S(2)}, u32[]{:S(2)}) collective-permute-start(bf16[256,2048]{1,0:T(8,128)(2,1)} %pad_maximum_fusion.1), channel_id=1, source_target_pairs={{0,16},{16,0},{1,17},{17,1},{2,18},{18,2},{3,19},{19,3},{4,20},{20... | collective-permute-start | bytes 3145736 | tf_op jit(solution)/shard_map/ppermute | solution.py:54
  262.6 18.9 %all-to-all-start.4 = ((bf16[8,32,1024]{2,1,0:T(8,128)(2,1)}), bf16[8,32,1024]{2,1,0:T(8,128)(2,1)S(1)}, u32[]{:S(2)}, u32[]{:S(2)}) async-start(bf16[8,32,1024]{2,1,0:T(8,128)(2,1)} %bitcast.94), calls=%async_computation.5 | async-start | bytes 1048576 | tf_op jit(solution)/shard_map/all_to_all | solution.py:991
  268.1 34.0 %collective-permute-start.33 = (bf16[128,2048]{1,0:T(8,128)(2,1)}, bf16[128,2048]{1,0:T(8,128)(2,1)}, u32[]{:S(2)}, u32[]{:S(2)}) collective-permute-start(bf16[128,2048]{1,0:T(8,128)(2,1)} %add_convert_fusion.1), channel_id=1, source_target_pairs={{0,1},{1,0},{2,3},{3,2},{4,5},{5,4},{6,7},{7,6},{8,9},{9,8},{10,11... | collective-permute-start | bytes 1572872 | tf_op jit(solution)/shard_map/ppermute | solution.py:54
  286.5 43.3 %all-to-all-start.5 = ((bf16[16,240,128]{2,1,0:T(8,128)(2,1)}), bf16[16,240,128]{2,1,0:T(8,128)(2,1)S(1)}, u32[]{:S(2)}, u32[]{:S(2)}) async-start(bf16[16,240,128]{2,1,0:T(8,128)(2,1)} %maximum_maximum_fusion), calls=%async_computation.6 | async-start | bytes 1966080 | tf_op jit(solution)/shard_map/all_to_all | solution.py:1019
  (64 other events, 571.2 us)
Sparse Core Ops, SparseCore 0:
  51.9 63.4 all-gather.5
  179.1 48.8 reduce-scatter.2
  230.3 34.4 reduce-scatter.4
Sparse Core Ops, SparseCore 1:
  183.1 133.9 all-gather.3
